TPU v7x, 32 devices: a whole 2x2x4 slice. The times are simulated.
32 devices in a mesh: grp: 2 (over x), row: 8 (over z, y), col: 2 (over core).
Axes of the slice: x: 2, y: 2, z: 4, core: 2. Of those that a mesh axis runs over, the one named last changes fastest.
Arguments:
- embeddings: bfloat16 [16384, 128], P(('grp', 'row')), parts along dimension 0, may hold values from -6 to 6
- profiles: float32 [16384, 128], P(('grp', 'row')), parts along dimension 0, may hold values from -16 to 16
- seed_mask: int32 [16384], P(('grp', 'row')), parts along dimension 0, may hold values 0 or 1
- tile_cols: int32 [32, 13], P(('grp', 'row')), parts along dimension 0, may hold values from 0 to 15, as said below
- tile_count: int32 [32], P(('grp', 'row')), parts along dimension 0, may hold values from 1 to 13, as said below
Outputs:
- spread: float32 [16384, 128], P(('grp', 'row')), parts along dimension 0
There are 2 independent parts, one for each index of `grp`. A program takes and returns all parts, laid end to end along the dimension named above; each array names one. Nothing has to cross between parts.
Inputs may be any that keep to these rules, and one draw needn't show every extreme that they name: `tile_cols`: row block b lists itself in slot 0; slots 1 to tile_count[b] - 1 hold distinct other blocks c with |c - b| <= 6; later slots repeat b and are no tiles. `tile_count`: some row block lists 13 tiles and some lists one.
All inputs are finite; a program needn't handle non-finite values. No bound on the sum of `seed_mask` on one device may be relied on, other than what follows from the above.
Results may differ from a plain program's by a relative error of at most 0.00083.
Values may be sent and summed in bfloat16 or wider, within the bound.
No kernel may reach another device: no remote copies, remote signals or barrier semaphores. Data moves between devices by JAX's collectives and lax.ppermute only.
A program may use at most 64 MiB of HBM per device.

v0:
```python
import jax
import jax.numpy as jnp
from jax import lax
from jax.sharding import PartitionSpec as P

BAND = 6
ITERS = 2


KERNEL_SCALE = 12.5
ALPHA = 0.8
EPS = 1e-06


def passed_along(value, axis, by):
    peers = lax.axis_size(axis)
    pairs = [(i, i + by) for i in range(peers) if 0 <= i + by < peers]
    return lax.ppermute(value, axis, pairs)


def inverse_norms(tile_rows):
    values = tile_rows.astype(jnp.float32)
    return lax.rsqrt(jnp.mean(values * values, axis=-1) + EPS)


def neighbour_window(pieces, reach_devs):
    from_below = []
    from_above = []
    for distance in range(1, reach_devs + 1):
        from_below.append(passed_along(pieces, "row", distance))
        from_above.append(passed_along(pieces, "row", -distance))
    return jnp.concatenate(from_below[::-1] + [pieces] + from_above, axis=0)


def return_sums(window_sums, reach_devs):
    group = window_sums.shape[0] // (2 * reach_devs + 1)
    own_sums = window_sums[reach_devs * group : (reach_devs + 1) * group]
    for distance in range(1, reach_devs + 1):
        toward_above = window_sums[
            (reach_devs + distance) * group : (reach_devs + distance + 1) * group
        ]
        own_sums = own_sums + passed_along(toward_above, "row", distance)
        toward_below = window_sums[
            (reach_devs - distance) * group : (reach_devs - distance + 1) * group
        ]
        own_sums = own_sums + passed_along(toward_below, "row", -distance)
    return own_sums


def shards(embeddings, profiles, seed_mask, tile_cols, tile_count):
    local_blocks = tile_cols.shape[0]
    slot_total = tile_cols.shape[1]
    emb_width = embeddings.shape[1]
    block_rows = embeddings.shape[0] // local_blocks
    prof_width = profiles.shape[1]
    reach_devs = (BAND + local_blocks - 1) // local_blocks
    row_dev = lax.axis_index("row")
    col_dev = lax.axis_index("col")
    first_block = row_dev * local_blocks
    window_start = (row_dev - reach_devs) * local_blocks
    row_emb = embeddings.reshape(local_blocks, block_rows, emb_width)
    row_inv = inverse_norms(row_emb)
    seed_rows = (seed_mask.astype(jnp.float32)[:, None] * profiles).reshape(
        local_blocks, block_rows, prof_width
    )
    slot_ids = jnp.arange(slot_total, dtype=jnp.int32)
    slot_taken = slot_ids % 2 == col_dev
    window_emb = neighbour_window(row_emb, reach_devs)
    window_inv = inverse_norms(window_emb)
    window_blocks = window_emb.shape[0]
    col_local = jnp.arange(block_rows, dtype=jnp.int32)
    row_local = jnp.arange(block_rows, dtype=jnp.int32)
    flat_total = local_blocks * slot_total

    def tile_at(local_block, col_block):
        window_pos = col_block - window_start
        cosine_similarity = (
            lax.dot_general(
                row_emb[local_block],
                window_emb[window_pos],
                (((1,), (1,)), ((), ())),
                preferred_element_type=jnp.float32,
            )
            * row_inv[local_block][:, None]
            * window_inv[window_pos][None, :]
            / emb_width
        )
        edge_weight = jnp.exp((cosine_similarity - 1.0) * (2.0 * KERNEL_SCALE))
        row_ids = (first_block + local_block) * block_rows + row_local
        col_ids = col_block * block_rows + col_local
        return jnp.where(row_ids[:, None] == col_ids[None, :], 0.0, edge_weight)

    def slot_state(flat_index):
        local_block = flat_index // slot_total
        slot_index = flat_index % slot_total
        col_block = tile_cols[local_block, slot_index]
        is_live = jnp.logical_and(slot_index < tile_count[local_block], slot_taken[slot_index])
        return (local_block, col_block, is_live)

    def degree_step(flat_index, sums_carry):
        local_block, col_block, is_live = slot_state(flat_index)

        def degree_add_tile(inner):
            row_sums, col_sums, tile_store = inner
            edge_weight = tile_at(local_block, col_block)
            row_sums = row_sums.at[local_block].add(jnp.sum(edge_weight, axis=1))
            col_sums = col_sums.at[col_block - window_start].add(jnp.sum(edge_weight, axis=0))
            tile_store = lax.dynamic_update_index_in_dim(
                tile_store, edge_weight.astype(jnp.bfloat16), flat_index, 0
            )
            return (row_sums, col_sums, tile_store)

        return lax.cond(is_live, degree_add_tile, lambda unchanged: unchanged, sums_carry)

    start_sums = (
        jnp.zeros((local_blocks, block_rows), jnp.float32),
        jnp.zeros((window_blocks, block_rows), jnp.float32),
        jnp.zeros((flat_total, block_rows, block_rows), jnp.bfloat16),
    )
    row_sums, col_sums, tile_store = lax.fori_loop(0, flat_total, degree_step, start_sums)
    col_own = return_sums(col_sums, reach_devs)
    row_degree, col_degree = lax.psum((row_sums, col_own), "col")
    col_scale = lax.rsqrt(col_degree)
    row_scale = lax.rsqrt(row_degree)
    spread_state = seed_rows
    for iteration in range(ITERS):
        own_state = spread_state
        scaled = (own_state * col_scale[:, :, None]).astype(jnp.bfloat16)
        window_scaled = neighbour_window(scaled, reach_devs)

        def product_step(flat_index, row_total):
            local_block, col_block, is_live = slot_state(flat_index)

            def product_add_tile(inner):
                term = jnp.dot(
                    tile_store[flat_index],
                    window_scaled[col_block - window_start],
                    preferred_element_type=jnp.float32,
                )
                return inner.at[local_block].add(term)

            return lax.cond(is_live, product_add_tile, lambda unchanged: unchanged, row_total)

        start_total = jnp.zeros((local_blocks, block_rows, prof_width), jnp.float32)
        partial_sum = lax.fori_loop(0, flat_total, product_step, start_total)
        product = lax.psum(partial_sum, "col")
        spread_state = ALPHA * product * row_scale[:, :, None] + (1.0 - ALPHA) * seed_rows
    return spread_state.reshape(local_blocks * block_rows, prof_width)


def solution(mesh):
    placed = (
        P(("grp", "row"), None),
        P(("grp", "row"), None),
        P(("grp", "row")),
        P(("grp", "row"), None),
        P(("grp", "row")),
    )
    return jax.shard_map(
        shards, mesh=mesh, in_specs=placed, out_specs=P(("grp", "row"), None), check_vma=False
    )
```

profile of v0, /device:TPU:0, one launch (start us, length us, event | category | flops | bytes accessed | tf_op | source)
XLA Modules:
  0.0 602.2 jit_solution(14887365671108933601)
XLA Ops:
  6.5 6.0 collective-permute-start
  24.7 5.1 collective-permute-done.2
  29.9 5.5 collective-permute-done.4
  38.7 6.4 %broadcast_in_dim.21 = bf16[26,512,512]{2,1,0:T(8,128)(2,1)} broadcast(bf16[]{:T(256)} %constant.331.clone.1), dimensions={} | broadcast | bytes 13631490 | tf_op jit(solution)/shard_map/broadcast_in_dim | solution.py:118
  45.1 105.9 %while.63 = (s32[]{:T(128)}, f32[2,512]{1,0:T(2,128)S(1)}, f32[14,512]{1,0:T(8,128)S(1)}, bf16[26,512,512]{2,1,0:T(8,128)(2,1)}, s32[2]{0:T(128)S(1)}, /*index=5...) while((s32[]{:T(128)}, f32[2,512]{1,0:T(2,128)S(1)}, ...), condition=%wide.region_9.10_spmd.clone.clone, body=%wide.region_2.9_spmd.clone.clone.sunk | while | flops 69732400 | bytes 1887137 | solution.py:120
  47.7 6.4 %conditional.10 = ((f32[2,512]{1,0:T(2,128)S(1)}, f32[14,512]{1,0:T(8,128)S(1)}, bf16[26,512,512]{2,1,0:T(8,128)(2,1)})) conditional(s32[]{:T(128)} %convert_element_type.67, (f32[2,512]{1,0:T(2,128)S(1)}, f32[14,512]{1,0:T(8,128)S(1)}, bf16[26,512,512]{2,1,0:T(8,128)(2,1)}) %tuple.173, (s32[]{:T(128)}, f32[2,512]{1,0:T(2,128)S(1)}, s32[]{:T(128)}, ...), branch_computations={%region_3.3_spmd, %region_4.8_spmd} | conditional | flops 69732376 | bytes 1884554 | solution.py:113
  59.2 6.4 %conditional.10 = ((f32[2,512]{1,0:T(2,128)S(1)}, f32[14,512]{1,0:T(8,128)S(1)}, bf16[26,512,512]{2,1,0:T(8,128)(2,1)})) conditional(s32[]{:T(128)} %convert_element_type.67, (f32[2,512]{1,0:T(2,128)S(1)}, f32[14,512]{1,0:T(8,128)S(1)}, bf16[26,512,512]{2,1,0:T(8,128)(2,1)}) %tuple.173, (s32[]{:T(128)}, f32[2,512]{1,0:T(2,128)S(1)}, s32[]{:T(128)}, ...), branch_computations={%region_3.3_spmd, %region_4.8_spmd} | conditional | flops 69732376 | bytes 1884554 | solution.py:113
  70.8 6.4 %conditional.10 = ((f32[2,512]{1,0:T(2,128)S(1)}, f32[14,512]{1,0:T(8,128)S(1)}, bf16[26,512,512]{2,1,0:T(8,128)(2,1)})) conditional(s32[]{:T(128)} %convert_element_type.67, (f32[2,512]{1,0:T(2,128)S(1)}, f32[14,512]{1,0:T(8,128)S(1)}, bf16[26,512,512]{2,1,0:T(8,128)(2,1)}) %tuple.173, (s32[]{:T(128)}, f32[2,512]{1,0:T(2,128)S(1)}, s32[]{:T(128)}, ...), branch_computations={%region_3.3_spmd, %region_4.8_spmd} | conditional | flops 69732376 | bytes 1884554 | solution.py:113
  82.4 6.4 %conditional.10 = ((f32[2,512]{1,0:T(2,128)S(1)}, f32[14,512]{1,0:T(8,128)S(1)}, bf16[26,512,512]{2,1,0:T(8,128)(2,1)})) conditional(s32[]{:T(128)} %convert_element_type.67, (f32[2,512]{1,0:T(2,128)S(1)}, f32[14,512]{1,0:T(8,128)S(1)}, bf16[26,512,512]{2,1,0:T(8,128)(2,1)}) %tuple.173, (s32[]{:T(128)}, f32[2,512]{1,0:T(2,128)S(1)}, s32[]{:T(128)}, ...), branch_computations={%region_3.3_spmd, %region_4.8_spmd} | conditional | flops 69732376 | bytes 1884554 | solution.py:113
  107.0 6.4 %conditional.10 = ((f32[2,512]{1,0:T(2,128)S(1)}, f32[14,512]{1,0:T(8,128)S(1)}, bf16[26,512,512]{2,1,0:T(8,128)(2,1)})) conditional(s32[]{:T(128)} %convert_element_type.67, (f32[2,512]{1,0:T(2,128)S(1)}, f32[14,512]{1,0:T(8,128)S(1)}, bf16[26,512,512]{2,1,0:T(8,128)(2,1)}) %tuple.173, (s32[]{:T(128)}, f32[2,512]{1,0:T(2,128)S(1)}, s32[]{:T(128)}, ...), branch_computations={%region_3.3_spmd, %region_4.8_spmd} | conditional | flops 69732376 | bytes 1884554 | solution.py:113
  118.6 6.4 %conditional.10 = ((f32[2,512]{1,0:T(2,128)S(1)}, f32[14,512]{1,0:T(8,128)S(1)}, bf16[26,512,512]{2,1,0:T(8,128)(2,1)})) conditional(s32[]{:T(128)} %convert_element_type.67, (f32[2,512]{1,0:T(2,128)S(1)}, f32[14,512]{1,0:T(8,128)S(1)}, bf16[26,512,512]{2,1,0:T(8,128)(2,1)}) %tuple.173, (s32[]{:T(128)}, f32[2,512]{1,0:T(2,128)S(1)}, s32[]{:T(128)}, ...), branch_computations={%region_3.3_spmd, %region_4.8_spmd} | conditional | flops 69732376 | bytes 1884554 | solution.py:113
  151.0 26.1 %collective-permute-start.10 = (f32[2,512]{1,0:T(2,128)S(1)}, f32[2,512]{1,0:T(2,128)S(1)}, u32[]{:S(2)}, u32[]{:S(2)}) collective-permute-start(f32[2,512]{1,0:T(2,128)S(1)} %get-tuple-element.1123), channel_id=1, source_target_pairs={{0,6},{2,8},{4,10},{6,12},{8,14},{1,7},{3,9},{5,11},{7,13},{9,15},... | collective-permute-start | bytes 12296 | tf_op jit(solution)/shard_map/ppermute | solution.py:18
  178.5 26.0 %collective-permute-start.6 = (f32[2,512]{1,0:T(2,128)S(1)}, f32[2,512]{1,0:T(2,128)S(1)}, u32[]{:S(2)}, u32[]{:S(2)}) collective-permute-start(f32[2,512]{1,0:T(2,128)S(1)} %get-tuple-element.1118), channel_id=1, source_target_pairs={{0,2},{2,4},{4,6},{6,8},{8,10},{10,12},{12,14},{1,3},{3,5},{5,7},{... | collective-permute-start | bytes 12296 | tf_op jit(solution)/shard_map/ppermute | solution.py:18
  211.3 6.9 %collective-permute-done.9 = f32[2,512]{1,0:T(2,128)S(1)} collective-permute-done((f32[2,512]{1,0:T(2,128)S(1)}, f32[2,512]{1,0:T(2,128)S(1)}, u32[]{:S(2)}, u32[]{:S(2)}) %collective-permute-start.9) | collective-permute-done | bytes 4128 | tf_op jit(solution)/shard_map/ppermute | solution.py:18
  235.0 5.4 collective-permute-done.14
  247.7 97.7 %while.61 = (s32[]{:T(128)}, f32[2,512,128]{2,1,0:T(8,128)S(1)}, s32[2]{0:T(128)S(1)}, pred[13]{0:T(512)(128)(4,1)S(1)}, bf16[26,512,512]{2,1,0:T(8,128)(2,1)}, ...) while((s32[]{:T(128)}, f32[2,512,128]{2,1,0:T(8,128)S(1)}, ...), condition=%wide.region_15.16_spmd, body=%wide.region_11.15_spmd.sunk | while | flops 67239984 | bytes 1181250 | solution.py:145
  346.2 61.7 %all-reduce.4.cloned.1.call-done = f32[2,512,128]{2,1,0:T(8,128)} async-done(((f32[2,512,128]{2,1,0:T(8,128)}), f32[2,512,128]{2,1,0:T(8,128)}) %all-reduce.4.cloned.1.call-update) | async-done | bytes 524304 | tf_op jit(solution)/shard_map/psum | solution.py:146
  409.3 4.6 collective-permute-start.18
  425.6 6.1 %collective-permute-done.20 = bf16[2,512,128]{2,1,0:T(8,128)(2,1)S(1)} collective-permute-done((bf16[2,512,128]{2,1,0:T(8,128)(2,1)S(1)}, bf16[2,512,128]{2,1,0:T(8,128)(2,1)S(1)}, u32[]{:S(2)}, u32[]{:S(2)}) %collective-permute-start.20) | collective-permute-done | bytes 262176 | tf_op jit(solution)/shard_map/ppermute | solution.py:18
  431.8 5.0 collective-permute-done.22
  439.1 97.7 %while.62 = (s32[]{:T(128)}, f32[2,512,128]{2,1,0:T(8,128)S(1)}, s32[2]{0:T(128)S(1)}, pred[13]{0:T(512)(128)(4,1)S(1)}, bf16[26,512,512]{2,1,0:T(8,128)(2,1)}, ...) while((s32[]{:T(128)}, f32[2,512,128]{2,1,0:T(8,128)S(1)}, ...), condition=%wide.region_22.23_spmd, body=%wide.region_18.22_spmd.sunk | while | flops 67239984 | bytes 1181250 | solution.py:145
  471.7 4.6 conditional.9
  505.1 4.6 conditional.9
  537.6 55.7 %all-reduce.6.cloned.1.call-done = f32[2,512,128]{2,1,0:T(8,128)} async-done(((f32[2,512,128]{2,1,0:T(8,128)}), f32[2,512,128]{2,1,0:T(8,128)}) %all-reduce.6.cloned.1.call-update) | async-done | bytes 524304 | tf_op jit(solution)/shard_map/psum | solution.py:146
  (481 shorter events, 290.1 us)
Async XLA Ops:
  6.5 401.4 %all-reduce.4.cloned.1.call-start = ((), (), s32[]{:S(2)}) async-start(), calls=%async_computation | async-start | bytes 1048576 | tf_op jit(solution)/shard_map/psum | solution.py:146
  6.5 16.8 %collective-permute-start = (bf16[2,512,128]{2,1,0:T(8,128)(2,1)}, bf16[2,512,128]{2,1,0:T(8,128)(2,1)S(1)}, u32[]{:S(2)}, u32[]{:S(2)}) collective-permute-start(bf16[2,512,128]{2,1,0:T(8,128)(2,1)} %bitcast.76), channel_id=1, source_target_pairs={{0,6},{2,8},{4,10},{6,12},{8,14},{1,7},{3,9},{5,11},{7,13},{9,15},... | collective-permute-start | bytes 786440 | tf_op jit(solution)/shard_map/ppermute | solution.py:18
  12.6 12.1 %collective-permute-start.1 = (bf16[2,512,128]{2,1,0:T(8,128)(2,1)}, bf16[2,512,128]{2,1,0:T(8,128)(2,1)S(1)}, u32[]{:S(2)}, u32[]{:S(2)}) collective-permute-start(bf16[2,512,128]{2,1,0:T(8,128)(2,1)} %bitcast.77), channel_id=1, source_target_pairs={{0,4},{2,6},{4,8},{6,10},{8,12},{10,14},{1,5},{3,7},{5,9},{7,11},{... | collective-permute-start | bytes 786440 | tf_op jit(solution)/shard_map/ppermute | solution.py:18
  16.1 13.7 %collective-permute-start.2 = (bf16[2,512,128]{2,1,0:T(8,128)(2,1)}, bf16[2,512,128]{2,1,0:T(8,128)(2,1)S(1)}, u32[]{:S(2)}, u32[]{:S(2)}) collective-permute-start(bf16[2,512,128]{2,1,0:T(8,128)(2,1)} %bitcast.78), channel_id=1, source_target_pairs={{0,2},{2,4},{4,6},{6,8},{8,10},{10,12},{12,14},{1,3},{3,5},{5,7},{... | collective-permute-start | bytes 786440 | tf_op jit(solution)/shard_map/ppermute | solution.py:18
  19.5 10.4 %collective-permute-start.3 = (bf16[2,512,128]{2,1,0:T(8,128)(2,1)}, bf16[2,512,128]{2,1,0:T(8,128)(2,1)S(1)}, u32[]{:S(2)}, u32[]{:S(2)}) collective-permute-start(bf16[2,512,128]{2,1,0:T(8,128)(2,1)} %bitcast.79), channel_id=1, source_target_pairs={{2,0},{4,2},{6,4},{8,6},{10,8},{12,10},{14,12},{3,1},{5,3},{7,5},{... | collective-permute-start | bytes 786440 | tf_op jit(solution)/shard_map/ppermute | solution.py:18
  20.8 14.6 %collective-permute-start.4 = (bf16[2,512,128]{2,1,0:T(8,128)(2,1)}, bf16[2,512,128]{2,1,0:T(8,128)(2,1)S(1)}, u32[]{:S(2)}, u32[]{:S(2)}) collective-permute-start(bf16[2,512,128]{2,1,0:T(8,128)(2,1)} %bitcast.80), channel_id=1, source_target_pairs={{4,0},{6,2},{8,4},{10,6},{12,8},{14,10},{5,1},{7,3},{9,5},{11,7},{... | collective-permute-start | bytes 786440 | tf_op jit(solution)/shard_map/ppermute | solution.py:18
  23.3 14.2 %collective-permute-start.5 = (bf16[2,512,128]{2,1,0:T(8,128)(2,1)}, bf16[2,512,128]{2,1,0:T(8,128)(2,1)S(1)}, u32[]{:S(2)}, u32[]{:S(2)}) collective-permute-start(bf16[2,512,128]{2,1,0:T(8,128)(2,1)} %bitcast.81), channel_id=1, source_target_pairs={{6,0},{8,2},{10,4},{12,6},{14,8},{7,1},{9,3},{11,5},{13,7},{15,9},... | collective-permute-start | bytes 786440 | tf_op jit(solution)/shard_map/ppermute | solution.py:18
  151.0 58.8 %collective-permute-start.10 = (f32[2,512]{1,0:T(2,128)S(1)}, f32[2,512]{1,0:T(2,128)S(1)}, u32[]{:S(2)}, u32[]{:S(2)}) collective-permute-start(f32[2,512]{1,0:T(2,128)S(1)} %get-tuple-element.1123), channel_id=1, source_target_pairs={{0,6},{2,8},{4,10},{6,12},{8,14},{1,7},{3,9},{5,11},{7,13},{9,15},... | collective-permute-start | bytes 12296 | tf_op jit(solution)/shard_map/ppermute | solution.py:18
  177.2 34.1 %collective-permute-start.11 = (f32[2,512]{1,0:T(2,128)S(1)}, f32[2,512]{1,0:T(2,128)S(1)}, u32[]{:S(2)}, u32[]{:S(2)}) collective-permute-start(f32[2,512]{1,0:T(2,128)S(1)} %get-tuple-element.1122), channel_id=1, source_target_pairs={{6,0},{8,2},{10,4},{12,6},{14,8},{7,1},{9,3},{11,5},{13,7},{15,9},... | collective-permute-start | bytes 12296 | tf_op jit(solution)/shard_map/ppermute | solution.py:18
  178.5 32.8 %collective-permute-start.6 = (f32[2,512]{1,0:T(2,128)S(1)}, f32[2,512]{1,0:T(2,128)S(1)}, u32[]{:S(2)}, u32[]{:S(2)}) collective-permute-start(f32[2,512]{1,0:T(2,128)S(1)} %get-tuple-element.1118), channel_id=1, source_target_pairs={{0,2},{2,4},{4,6},{6,8},{8,10},{10,12},{12,14},{1,3},{3,5},{5,7},{... | collective-permute-start | bytes 12296 | tf_op jit(solution)/shard_map/ppermute | solution.py:18
  209.8 8.5 %collective-permute-start.9 = (f32[2,512]{1,0:T(2,128)S(1)}, f32[2,512]{1,0:T(2,128)S(1)}, u32[]{:S(2)}, u32[]{:S(2)}) collective-permute-start(f32[2,512]{1,0:T(2,128)S(1)} %get-tuple-element.1119), channel_id=1, source_target_pairs={{4,0},{6,2},{8,4},{10,6},{12,8},{14,10},{5,1},{7,3},{9,5},{11,7},{... | collective-permute-start | bytes 12296 | tf_op jit(solution)/shard_map/ppermute | solution.py:18
  221.0 11.0 %collective-permute-start.12 = (bf16[2,512,128]{2,1,0:T(8,128)(2,1)S(1)}, bf16[2,512,128]{2,1,0:T(8,128)(2,1)S(1)}, u32[]{:S(2)}, u32[]{:S(2)}) collective-permute-start(bf16[2,512,128]{2,1,0:T(8,128)(2,1)S(1)} %multiply_convert_fusion.1), channel_id=1, source_target_pairs={{0,6},{2,8},{4,10},{6,12},{8,14},{1,7},{3,9},{5,11},{7,13},{9,15},... | collective-permute-start | bytes 786440 | tf_op jit(solution)/shard_map/ppermute | solution.py:18
  223.5 11.5 %collective-permute-start.13 = (bf16[2,512,128]{2,1,0:T(8,128)(2,1)S(1)}, bf16[2,512,128]{2,1,0:T(8,128)(2,1)S(1)}, u32[]{:S(2)}, u32[]{:S(2)}) collective-permute-start(bf16[2,512,128]{2,1,0:T(8,128)(2,1)S(1)} %multiply_convert_fusion.1), channel_id=1, source_target_pairs={{0,4},{2,6},{4,8},{6,10},{8,12},{10,14},{1,5},{3,7},{5,9},{7,11},{... | collective-permute-start | bytes 786440 | tf_op jit(solution)/shard_map/ppermute | solution.py:18
  226.3 14.1 %collective-permute-start.14 = (bf16[2,512,128]{2,1,0:T(8,128)(2,1)S(1)}, bf16[2,512,128]{2,1,0:T(8,128)(2,1)S(1)}, u32[]{:S(2)}, u32[]{:S(2)}) collective-permute-start(bf16[2,512,128]{2,1,0:T(8,128)(2,1)S(1)} %multiply_convert_fusion.1), channel_id=1, source_target_pairs={{0,2},{2,4},{4,6},{6,8},{8,10},{10,12},{12,14},{1,3},{3,5},{5,7},{... | collective-permute-start | bytes 786440 | tf_op jit(solution)/shard_map/ppermute | solution.py:18
  229.4 11.3 %collective-permute-start.15 = (bf16[2,512,128]{2,1,0:T(8,128)(2,1)S(1)}, bf16[2,512,128]{2,1,0:T(8,128)(2,1)S(1)}, u32[]{:S(2)}, u32[]{:S(2)}) collective-permute-start(bf16[2,512,128]{2,1,0:T(8,128)(2,1)S(1)} %multiply_convert_fusion.1), channel_id=1, source_target_pairs={{2,0},{4,2},{6,4},{8,6},{10,8},{12,10},{14,12},{3,1},{5,3},{7,5},{... | collective-permute-start | bytes 786440 | tf_op jit(solution)/shard_map/ppermute | solution.py:18
  230.7 14.3 %collective-permute-start.16 = (bf16[2,512,128]{2,1,0:T(8,128)(2,1)S(1)}, bf16[2,512,128]{2,1,0:T(8,128)(2,1)S(1)}, u32[]{:S(2)}, u32[]{:S(2)}) collective-permute-start(bf16[2,512,128]{2,1,0:T(8,128)(2,1)S(1)} %multiply_convert_fusion.1), channel_id=1, source_target_pairs={{4,0},{6,2},{8,4},{10,6},{12,8},{14,10},{5,1},{7,3},{9,5},{11,7},{... | collective-permute-start | bytes 786440 | tf_op jit(solution)/shard_map/ppermute | solution.py:18
  232.1 15.5 %collective-permute-start.17 = (bf16[2,512,128]{2,1,0:T(8,128)(2,1)S(1)}, bf16[2,512,128]{2,1,0:T(8,128)(2,1)S(1)}, u32[]{:S(2)}, u32[]{:S(2)}) collective-permute-start(bf16[2,512,128]{2,1,0:T(8,128)(2,1)S(1)} %multiply_convert_fusion.1), channel_id=1, source_target_pairs={{6,0},{8,2},{10,4},{12,6},{14,8},{7,1},{9,3},{11,5},{13,7},{15,9},... | collective-permute-start | bytes 786440 | tf_op jit(solution)/shard_map/ppermute | solution.py:18
  346.2 247.2 %all-reduce.6.cloned.1.call-start = ((), (), s32[]{:S(2)}) async-start(), calls=%async_computation.1 | async-start | bytes 1048576 | tf_op jit(solution)/shard_map/psum | solution.py:146
  409.3 14.0 %collective-permute-start.18 = (bf16[2,512,128]{2,1,0:T(8,128)(2,1)S(1)}, bf16[2,512,128]{2,1,0:T(8,128)(2,1)S(1)}, u32[]{:S(2)}, u32[]{:S(2)}) collective-permute-start(bf16[2,512,128]{2,1,0:T(8,128)(2,1)S(1)} %multiply_convert_fusion), channel_id=1, source_target_pairs={{0,6},{2,8},{4,10},{6,12},{8,14},{1,7},{3,9},{5,11},{7,13},{9,15},... | collective-permute-start | bytes 786440 | tf_op jit(solution)/shard_map/ppermute | solution.py:18
  413.9 11.6 %collective-permute-start.19 = (bf16[2,512,128]{2,1,0:T(8,128)(2,1)S(1)}, bf16[2,512,128]{2,1,0:T(8,128)(2,1)S(1)}, u32[]{:S(2)}, u32[]{:S(2)}) collective-permute-start(bf16[2,512,128]{2,1,0:T(8,128)(2,1)S(1)} %multiply_convert_fusion), channel_id=1, source_target_pairs={{0,4},{2,6},{4,8},{6,10},{8,12},{10,14},{1,5},{3,7},{5,9},{7,11},{... | collective-permute-start | bytes 786440 | tf_op jit(solution)/shard_map/ppermute | solution.py:18
  417.3 14.3 %collective-permute-start.20 = (bf16[2,512,128]{2,1,0:T(8,128)(2,1)S(1)}, bf16[2,512,128]{2,1,0:T(8,128)(2,1)S(1)}, u32[]{:S(2)}, u32[]{:S(2)}) collective-permute-start(bf16[2,512,128]{2,1,0:T(8,128)(2,1)S(1)} %multiply_convert_fusion), channel_id=1, source_target_pairs={{0,2},{2,4},{4,6},{6,8},{8,10},{10,12},{12,14},{1,3},{3,5},{5,7},{... | collective-permute-start | bytes 786440 | tf_op jit(solution)/shard_map/ppermute | solution.py:18
  420.7 11.0 %collective-permute-start.21 = (bf16[2,512,128]{2,1,0:T(8,128)(2,1)S(1)}, bf16[2,512,128]{2,1,0:T(8,128)(2,1)S(1)}, u32[]{:S(2)}, u32[]{:S(2)}) collective-permute-start(bf16[2,512,128]{2,1,0:T(8,128)(2,1)S(1)} %multiply_convert_fusion), channel_id=1, source_target_pairs={{2,0},{4,2},{6,4},{8,6},{10,8},{12,10},{14,12},{3,1},{5,3},{7,5},{... | collective-permute-start | bytes 786440 | tf_op jit(solution)/shard_map/ppermute | solution.py:18
  422.0 14.8 %collective-permute-start.22 = (bf16[2,512,128]{2,1,0:T(8,128)(2,1)S(1)}, bf16[2,512,128]{2,1,0:T(8,128)(2,1)S(1)}, u32[]{:S(2)}, u32[]{:S(2)}) collective-permute-start(bf16[2,512,128]{2,1,0:T(8,128)(2,1)S(1)} %multiply_convert_fusion), channel_id=1, source_target_pairs={{4,0},{6,2},{8,4},{10,6},{12,8},{14,10},{5,1},{7,3},{9,5},{11,7},{... | collective-permute-start | bytes 786440 | tf_op jit(solution)/shard_map/ppermute | solution.py:18
  423.4 15.7 %collective-permute-start.23 = (bf16[2,512,128]{2,1,0:T(8,128)(2,1)S(1)}, bf16[2,512,128]{2,1,0:T(8,128)(2,1)S(1)}, u32[]{:S(2)}, u32[]{:S(2)}) collective-permute-start(bf16[2,512,128]{2,1,0:T(8,128)(2,1)S(1)} %multiply_convert_fusion), channel_id=1, source_target_pairs={{6,0},{8,2},{10,4},{12,6},{14,8},{7,1},{9,3},{11,5},{13,7},{15,9},... | collective-permute-start | bytes 786440 | tf_op jit(solution)/shard_map/ppermute | solution.py:18
  (21 other events, 371.1 us)
Sparse Core Ops, SparseCore 0:
  346.3 61.6 all-reduce.3
  537.7 55.5 all-reduce.5
where the time goes:
time: 606 us; the launch traced here: 602 us
  waiting for transfers between devices  165 us (27%)
  local copies, waits for them, and re-layouts  127 us (21%)
  loops' own time  124 us (20%)
  starting transfers between devices  104 us (17%)
  other arithmetic  39.3 us (6%)
  matrix products  26.8 us (4%)
  between operations  14 us (2%)
    psum x2, waiting for transfers between devices, shards(): product = lax.psum(partial_sum, 'col')  117 us
    ppermute x24, starting transfers between devices, passed_along(): return lax.ppermute(value, axis, pairs)  104 us
    another operation x2, loops' own time, shards(): partial_sum = lax.fori_loop(0, flat_total, product_step, start_total)  72 us
    dynamic_slice x78, local copies, waits for them, and re-layouts, slot_state(): slot_taken[slot_index]  51.3 us
    dynamic_slice x78, local copies, waits for them, and re-layouts, slot_state(): tile_count[local_block]  49.3 us
    ppermute x24, waiting for transfers between devices, passed_along(): return lax.ppermute(value, axis, pairs)  47.5 us
    another operation x1, loops' own time, shards(): lax.fori_loop(0, flat_total, degree_step, start_sums)  34.8 us
    another operation x30, other arithmetic  32.9 us
  transfers between devices with their start and end apart: 26, of which 14 were waited for; matrix products, arithmetic and copies ran while one was open for 0% of the time, Pallas kernels for 0%

commit v1 on v0

v1 whole, which is shorter than its diff:
```python
import jax
import jax.numpy as jnp
from jax import lax
from jax.experimental import pallas as pl
from jax.experimental.pallas import tpu as pltpu
from jax.sharding import PartitionSpec as P

BAND = 6
ITERS = 2

KERNEL_SCALE = 12.5
ALPHA = 0.8
EPS = 1e-06
LOG2E = 1.4426950408889634
LANES = 128
F32 = jnp.float32
BF16 = jnp.bfloat16

VMEM = pl.BlockSpec(memory_space=pltpu.VMEM)
SMEM = pl.BlockSpec(memory_space=pltpu.SMEM)


def peer_pairs(rows, cols, distance):
    pairs = []
    for low in range(rows - distance):
        core = (low // distance) % cols
        a, b = low * cols + core, (low + distance) * cols + core
        pairs += [(a, b), (b, a)]
    return pairs


def peer_sign(row_dev, col_dev, distance):
    return jnp.where(lax.rem(lax.div(row_dev, distance), 2) == col_dev, 1, -1)


def listed_bits(cols_ref, count_ref, local_block, own_block, slots):
    bits = jnp.int32(0)
    for s in range(slots):
        bit = lax.shift_left(jnp.int32(1), cols_ref[local_block, s] - own_block + BAND + 1)
        bits = bits | jnp.where(s < count_ref[local_block], bit, 0)
    return bits


def is_listed(bits, offset):
    return (lax.shift_right_logical(bits, offset + BAND + 1) & 1) == 1


def block_offsets(row_dev, col_dev, reach, blocks):
    offsets = [col_dev]
    for d in range(1, reach + 1):
        sign = peer_sign(row_dev, col_dev, d)
        offsets += [sign * (d * blocks) + k for k in range(blocks)]
    return offsets


def weights_kernel(dims, cols_ref, count_ref, own_ref, *rest):
    blocks, size, width, slots, reach, senders = dims
    peers = rest[:reach]
    w_ref, row_ref, col_ref, hl, ee, inv, col_acc, offs = rest[reach:]
    tiles = 1 + reach * blocks
    r, c = lax.axis_index("row"), lax.axis_index("col")
    bits = [listed_bits(cols_ref, count_ref, b, r * blocks + b, slots) for b in range(blocks)]
    for q, offset in enumerate(block_offsets(r, c, reach, blocks)):
        offs[q] = offset

    for b in range(blocks):
        x = own_ref[pl.ds(b * size, size), :].astype(F32)
        scale = lax.rsqrt(jnp.sum(x * x, axis=-1, keepdims=True) * (1.0 / width) + EPS)
        x = x * (scale * (2.0 * KERNEL_SCALE * LOG2E / width))
        high = x.astype(BF16)
        hl[pl.ds(b * size, size), :width] = high
        hl[pl.ds(b * size, size), width:] = (x - high.astype(F32)).astype(BF16)
    ones = jnp.ones((16, 2 * width), BF16)
    for q in range(tiles):
        if q == 0:
            e = own_ref[pl.ds(pl.multiple_of(c * size, size), size), :]
        else:
            e = peers[(q - 1) // blocks][pl.ds((q - 1) % blocks * size, size), :]
        ee[q, :, :width] = e
        ee[q, :, width:] = e
        x = e.astype(F32)
        x = x * x
        high = x.astype(BF16)
        both = jnp.concatenate([high, (x - high.astype(F32)).astype(BF16)], axis=1)
        total = lax.dot_general(ones, both, (((1,), (1,)), ((), ())), preferred_element_type=F32)
        inv[q] = lax.rsqrt(total[:8] * (1.0 / width) + EPS)
    row_ref[...] = jnp.zeros_like(row_ref)
    col_acc[...] = jnp.zeros_like(col_acc)

    def tile(b, q, diagonal):
        s = lax.dot_general(
            hl[pl.ds(pl.multiple_of(b * size, size), size), :],
            ee[q],
            (((1,), (1,)), ((), ())),
            preferred_element_type=F32,
        )
        w = jnp.exp2(s * inv[q, 0:1, :] - 2.0 * KERNEL_SCALE * LOG2E)
        if diagonal:
            ids = lax.broadcasted_iota(jnp.int32, (size, size), 0)
            w = jnp.where(ids == lax.broadcasted_iota(jnp.int32, (size, size), 1), 0.0, w)
        w_ref[b * tiles + q] = w.astype(BF16)
        part = w[:, :LANES]
        for k in range(1, size // LANES):
            part = part + w[:, k * LANES : (k + 1) * LANES]
        row_ref[pl.ds(pl.multiple_of(b * size, size), size), :] += part
        col_acc[q] += jnp.sum(w.reshape(size // 8, 8, size), axis=0)

    tile(c, 0, True)

    @pl.when(is_listed(jnp.where(c == 0, bits[1], bits[0]), 2 * c - 1))
    def _():
        tile(1 - c, 0, False)

    @pl.loop(1, tiles)
    def _(q):
        for b in range(blocks):

            @pl.when(is_listed(bits[b], offs[q] - b))
            def _():
                tile(b, q, False)

    sums = [jnp.sum(col_acc[q], axis=0, keepdims=True) for q in range(tiles)]
    sums += [jnp.zeros((1, size), F32)] * (8 - tiles)
    sums = jnp.concatenate(sums, axis=0).astype(BF16)
    for n in range(senders):
        col_ref[n] = sums


def product_kernel(dims, first, cols_ref, count_ref, *rest):
    blocks, size, width, slots, reach, rows = dims
    tiles = 1 + reach * blocks
    w_ref = rest[0]
    if first:
        sums_ref = rest[1]
        rest = rest[1:]
    own_ref, peers = rest[1], rest[2 : 2 + reach]
    if first:
        out_ref, scale_ref, scaled, scales, offs = rest[2 + reach :]
    else:
        out_ref, offs = rest[2 + reach :]
    r, c = lax.axis_index("row"), lax.axis_index("col")
    bits = [listed_bits(cols_ref, count_ref, b, r * blocks + b, slots) for b in range(blocks)]
    offsets = block_offsets(r, c, reach, blocks)

    if first:
        for n in range(reach + 1):
            chip = r if n == 0 else r + peer_sign(r, c, n) * n
            total = jnp.zeros((blocks, size), F32)
            for shift in range(-reach, reach + 1):
                other, d = chip + shift, abs(shift)
                valid = jnp.logical_and(
                    jnp.logical_and(other >= 0, other < rows), jnp.logical_and(chip >= 0, chip < rows)
                )
                if d == 0:
                    at = jnp.where(valid, other * blocks, 0)
                    term = jnp.concatenate([sums_ref[at + k].astype(F32)[0:1] for k in range(blocks)], axis=0)
                else:
                    core = lax.rem(lax.div(jnp.maximum(chip + min(shift, 0), 0), d), 2)
                    at = jnp.where(valid, other * 2 + core, 0)
                    term = sums_ref[at].astype(F32)[1 + (d - 1) * blocks : 1 + d * blocks]
                total = total + jnp.where(valid, term, 0.0)
            scales[n * blocks : (n + 1) * blocks] = jnp.where(total > 0.0, lax.rsqrt(total), 0.0)
        columns = scales[...].T
        for b in range(blocks):
            scale_ref[pl.ds(b * size, size), :] = jnp.broadcast_to(columns[:, b : b + 1], (size, width))
        s = own_ref[pl.ds(pl.multiple_of(c * size, size), size), :].astype(F32)
        scaled[0] = (s * scale_ref[pl.ds(pl.multiple_of(c * size, size), size), :]).astype(BF16)
        for q in range(1, tiles):
            s = peers[(q - 1) // blocks][pl.ds((q - 1) % blocks * size, size), :].astype(F32)
            scaled[q] = (s * columns[:, blocks + q - 1 : blocks + q]).astype(BF16)
    out_ref[...] = jnp.zeros_like(out_ref)
    for q in range(tiles):
        for b in range(blocks):

            @pl.when(is_listed(bits[b], offsets[q] - b))
            def _():
                if first:
                    s = scaled[q]
                elif q == 0:
                    s = own_ref[pl.ds(pl.multiple_of(c * size, size), size), :]
                else:
                    s = peers[(q - 1) // blocks][pl.ds((q - 1) % blocks * size, size), :]
                out_ref[pl.ds(b * size, size), :] += jnp.dot(
                    w_ref[b * tiles + q], s, preferred_element_type=F32
                )


def row_scale_kernel(own_ref, other_ref, out_ref):
    total = jnp.sum(own_ref[...] + other_ref[...], axis=-1, keepdims=True)
    out_ref[...] = jnp.broadcast_to(ALPHA * lax.rsqrt(total), out_ref.shape)


def state_kernel(own_ref, other_ref, rs_ref, seed_ref, cs_ref, out_ref):
    state = (own_ref[...] + other_ref[...]) * rs_ref[...] + (1.0 - ALPHA) * seed_ref[...]
    out_ref[...] = (state * cs_ref[...]).astype(BF16)


def shards(embeddings, profiles, seed_mask, tile_cols, tile_count):
    rows, cols = lax.axis_size("row"), lax.axis_size("col")
    blocks, slots = tile_cols.shape
    mols, width = embeddings.shape
    prof = profiles.shape[1]
    size = mols // blocks
    reach = (BAND + blocks - 1) // blocks
    tiles = 1 + reach * blocks
    senders = rows * cols
    assert blocks == 2 and cols == 2 and tiles <= 8
    params = pltpu.CompilerParams(vmem_limit_bytes=24 * 1024 * 1024)

    def from_peers(value):
        return [lax.ppermute(value, ("row", "col"), peer_pairs(rows, cols, d)) for d in range(1, reach + 1)]

    def other_core(value):
        return lax.ppermute(value, "col", [(0, 1), (1, 0)])

    peer_emb = from_peers(embeddings)
    seed_rows = seed_mask.astype(F32)[:, None] * profiles
    seeds = seed_rows.astype(BF16)
    peer_seeds = from_peers(seeds)

    weights, row_part, col_part = pl.pallas_call(
        lambda *refs: weights_kernel((blocks, size, width, slots, reach, senders), *refs),
        out_shape=(
            jax.ShapeDtypeStruct((blocks * tiles, size, size), BF16),
            jax.ShapeDtypeStruct((mols, LANES), F32),
            jax.ShapeDtypeStruct((senders, 8, size), BF16),
        ),
        in_specs=[SMEM, SMEM] + [VMEM] * (1 + reach),
        out_specs=(VMEM, VMEM, VMEM),
        scratch_shapes=[
            pltpu.VMEM((mols, 2 * width), BF16),
            pltpu.VMEM((tiles, size, 2 * width), BF16),
            pltpu.VMEM((tiles, 8, size), F32),
            pltpu.VMEM((tiles, 8, size), F32),
            pltpu.SMEM((tiles,), jnp.int32),
        ],
        compiler_params=params,
        name="weights",
    )(tile_cols, tile_count, embeddings, *peer_emb)

    col_sums = lax.all_to_all(col_part, ("row", "col"), 0, 0, tiled=True)
    row_scale = pl.pallas_call(
        row_scale_kernel,
        out_shape=jax.ShapeDtypeStruct((mols, LANES), F32),
        in_specs=[VMEM, VMEM],
        out_specs=VMEM,
        compiler_params=params,
        name="row_scale",
    )(row_part, other_core(row_part))

    dims = (blocks, size, prof, slots, reach, rows)
    partial, col_scale = pl.pallas_call(
        lambda *refs: product_kernel(dims, True, *refs),
        out_shape=(jax.ShapeDtypeStruct((mols, prof), F32), jax.ShapeDtypeStruct((mols, prof), F32)),
        in_specs=[SMEM, SMEM] + [VMEM] * (3 + reach),
        out_specs=(VMEM, VMEM),
        scratch_shapes=[
            pltpu.VMEM((tiles, size, prof), BF16),
            pltpu.VMEM((8, size), F32),
            pltpu.SMEM((tiles,), jnp.int32),
        ],
        compiler_params=params,
        name="first_product",
    )(tile_cols, tile_count, weights, col_sums, seeds, *peer_seeds)

    for iteration in range(1, ITERS):
        scaled = pl.pallas_call(
            state_kernel,
            out_shape=jax.ShapeDtypeStruct((mols, prof), BF16),
            in_specs=[VMEM] * 5,
            out_specs=VMEM,
            compiler_params=params,
            name="state",
        )(partial, other_core(partial), row_scale, seed_rows, col_scale)
        partial = pl.pallas_call(
            lambda *refs: product_kernel(dims, False, *refs),
            out_shape=jax.ShapeDtypeStruct((mols, prof), F32),
            in_specs=[SMEM, SMEM] + [VMEM] * (2 + reach),
            out_specs=VMEM,
            scratch_shapes=[pltpu.SMEM((tiles,), jnp.int32)],
            compiler_params=params,
            name="product",
        )(tile_cols, tile_count, weights, scaled, *from_peers(scaled))
    return (partial + other_core(partial)) * row_scale + (1.0 - ALPHA) * seed_rows


def solution(mesh):
    placed = (
        P(("grp", "row"), None),
        P(("grp", "row"), None),
        P(("grp", "row")),
        P(("grp", "row"), None),
        P(("grp", "row")),
    )
    return jax.shard_map(
        shards, mesh=mesh, in_specs=placed, out_specs=P(("grp", "row"), None), check_vma=False
    )
```

time: 606 us -> 81.2 us (0.13)
  waiting for transfers between devices: 165 us -> 16.4 us
  loops' own time: 124 us -> 0 us
  local copies, waits for them, and re-layouts: 127 us -> 9.64 us
  starting transfers between devices: 104 us -> 34.7 us
  other arithmetic: 39.3 us -> 2.86 us
  matrix products: 26.8 us -> 0 us
  Pallas kernels: 0 us -> 17.3 us
  between operations: 14 us -> 0.19 us
    another operation x81 -> x0, loops' own time: 124 us -> none  [the longest x2 72 us: shards(): partial_sum = lax.fori_loop(0, flat_total, product_step, start_total)]
    psum x2 -> x0, waiting for transfers between devices: 117 us -> none  [shards(): product = lax.psum(partial_sum, 'col')]
    dynamic_slice x186 -> x0, local copies, waits for them, and re-layouts: 112 us -> none  [the longest x78 51.3 us: slot_state(): slot_taken[slot_index]]
    ppermute x24 -> x12, starting transfers between devices: 104 us -> 31.2 us  [the longest x9 30.7 us: from_peers(): lax.ppermute(value, ('row', 'col'), peer_pairs(rows, cols, d))]
    ppermute x24 -> x12, waiting for transfers between devices: 47.5 us -> 8.79 us  [the longest x9 5.22 us: from_peers(): lax.ppermute(value, ('row', 'col'), peer_pairs(rows, cols, d))]
    another operation x30 -> x0, other arithmetic: 32.9 us -> none
    dot_general x18 -> x0, matrix products: 26.8 us -> none  [the longest x12 22.9 us: product_add_tile(): jnp.dot(tile_store[flat_index], window_scaled[col_block - window_start],...]
    pallas_call x0 -> x5, Pallas kernels: none -> 17.3 us  [the longest x1 7.17 us: shards(): pl.pallas_call(lambda *refs: weights_kernel((blocks, size, width, slots,...]
  transfers between devices with their start and end apart: 26 -> 13, of which waited for: 14 -> 5; matrix products, arithmetic and copies ran while one was open for 0% -> 2% of each run, Pallas kernels for 0% -> 16%
where the time goes in v1:
time: 81.2 us; the launch traced here: 81.1 us
  starting transfers between devices  34.7 us (43%)
  Pallas kernels  17.3 us (21%)
  waiting for transfers between devices  16.4 us (20%)
  local copies, waits for them, and re-layouts  9.64 us (12%)
  other arithmetic  2.86 us (4%)
    ppermute x9, starting transfers between devices, from_peers(): lax.ppermute(value, ('row', 'col'), peer_pairs(rows, cols, d))  30.7 us
    unnamed x16, local copies, waits for them, and re-layouts  9.64 us
    all_to_all x1, waiting for transfers between devices, shards(): col_sums = lax.all_to_all(col_part, ('row', 'col'), 0, 0, tiled=True)  7.59 us
    pallas_call x1, Pallas kernels, shards(): pl.pallas_call(lambda *refs: weights_kernel((blocks, size, width, slots,...  7.17 us
    pallas_call x1, Pallas kernels, shards(): pl.pallas_call(lambda *refs: product_kernel(dims, True, *refs), out_shape...  5.34 us
    ppermute x9, waiting for transfers between devices, from_peers(): lax.ppermute(value, ('row', 'col'), peer_pairs(rows, cols, d))  5.22 us
    pallas_call x1, Pallas kernels, shards(): pl.pallas_call(lambda *refs: product_kernel(dims, False, *refs), out_shap...  4.46 us
    ppermute x3, waiting for transfers between devices, other_core(): return lax.ppermute(value, 'col', [(0, 1), (1, 0)])  3.56 us
  transfers between devices with their start and end apart: 13, of which 5 were waited for; matrix products, arithmetic and copies ran while one was open for 2% of the time, Pallas kernels for 16%

profile of v1, /device:TPU:0, one launch (start us, length us, event | category | flops | bytes accessed | tf_op | source)
XLA Modules:
  0.0 81.1 jit_solution(16797630928959738339)
XLA Ops:
  0.0 4.9 %collective-permute-start = (bf16[1024,128]{1,0:T(8,128)(2,1)}, bf16[1024,128]{1,0:T(8,128)(2,1)S(1)}, u32[]{:S(2)}, u32[]{:S(2)}) collective-permute-start(bf16[1024,128]{1,0:T(8,128)(2,1)} %refs_2_.1), channel_id=1, source_target_pairs={{0,2},{2,0},{3,5},{5,3},{4,6},{6,4},{7,9},{9,7},{8,10},{10,8},{11,... | collective-permute-start | bytes 786440 | tf_op jit(solution)/shard_map/ppermute | solution.py:211
  4.9 3.5 %collective-permute-start.1 = (bf16[1024,128]{1,0:T(8,128)(2,1)}, bf16[1024,128]{1,0:T(8,128)(2,1)S(1)}, u32[]{:S(2)}, u32[]{:S(2)}) collective-permute-start(bf16[1024,128]{1,0:T(8,128)(2,1)} %refs_2_.1), channel_id=1, source_target_pairs={{0,4},{4,0},{2,6},{6,2},{5,9},{9,5},{7,11},{11,7},{8,12},{12,8},{1... | collective-permute-start | bytes 786440 | tf_op jit(solution)/shard_map/ppermute | solution.py:211
  8.4 1.9 %collective-permute-start.2 = (bf16[1024,128]{1,0:T(8,128)(2,1)}, bf16[1024,128]{1,0:T(8,128)(2,1)S(1)}, u32[]{:S(2)}, u32[]{:S(2)}) collective-permute-start(bf16[1024,128]{1,0:T(8,128)(2,1)} %refs_2_.1), channel_id=1, source_target_pairs={{0,6},{6,0},{2,8},{8,2},{4,10},{10,4},{7,13},{13,7},{9,15},{15,9},... | collective-permute-start | bytes 786440 | tf_op jit(solution)/shard_map/ppermute | solution.py:211
  10.3 0.7 convert_element_type.6
  11.0 1.2 %fusion = (bf16[1024,128]{1,0:T(8,128)(2,1)S(1)}, f32[1024,128]{1,0:T(8,128)S(1)}) fusion(f32[1024,128]{1,0:T(8,128)} %param.6, f32[1024]{0:T(1024)S(1)} %convert_element_type.6), kind=kLoop, calls=%fused_computation.2 | loop fusion | flops 262144 | bytes 1314816 | tf_op jit(solution)/shard_map/convert_element_type | solution.py:218
  12.2 5.9 %collective-permute-start.3 = (bf16[1024,128]{1,0:T(8,128)(2,1)S(1)}, bf16[1024,128]{1,0:T(8,128)(2,1)S(1)}, u32[]{:S(2)}, u32[]{:S(2)}) collective-permute-start(bf16[1024,128]{1,0:T(8,128)(2,1)S(1)} %get-tuple-element.15.refs_4_), channel_id=1, source_target_pairs={{0,2},{2,0},{3,5},{5,3},{4,6},{6,4},{7,9},{9,7},{8,10},{10,8},{11,... | collective-permute-start | bytes 786440 | tf_op jit(solution)/shard_map/ppermute | solution.py:211
  18.2 1.9 %collective-permute-start.4 = (bf16[1024,128]{1,0:T(8,128)(2,1)S(1)}, bf16[1024,128]{1,0:T(8,128)(2,1)S(1)}, u32[]{:S(2)}, u32[]{:S(2)}) collective-permute-start(bf16[1024,128]{1,0:T(8,128)(2,1)S(1)} %get-tuple-element.15.refs_4_), channel_id=1, source_target_pairs={{0,4},{4,0},{2,6},{6,2},{5,9},{9,5},{7,11},{11,7},{8,12},{12,8},{1... | collective-permute-start | bytes 786440 | tf_op jit(solution)/shard_map/ppermute | solution.py:211
  20.1 3.4 %collective-permute-start.5 = (bf16[1024,128]{1,0:T(8,128)(2,1)S(1)}, bf16[1024,128]{1,0:T(8,128)(2,1)S(1)}, u32[]{:S(2)}, u32[]{:S(2)}) collective-permute-start(bf16[1024,128]{1,0:T(8,128)(2,1)S(1)} %get-tuple-element.15.refs_4_), channel_id=1, source_target_pairs={{0,6},{6,0},{2,8},{8,2},{4,10},{10,4},{7,13},{13,7},{9,15},{15,9},... | collective-permute-start | bytes 786440 | tf_op jit(solution)/shard_map/ppermute | solution.py:211
  23.5 0.9 %copy-done.3 = bf16[1024,128]{1,0:T(8,128)(2,1)S(1)} copy-done((bf16[1024,128]{1,0:T(8,128)(2,1)S(1)}, bf16[1024,128]{1,0:T(8,128)(2,1)}, u32[]{:S(2)}) %copy-start.3) | copy-done | bytes 262168
  25.8 7.2 %weights.1 = (bf16[14,512,512]{2,1,0:T(8,128)(2,1)S(1)}, f32[1024,128]{1,0:T(8,128)S(1)}, bf16[16,8,512]{2,1,0:T(8,128)(2,1)}) custom-call(s32[2,13]{1,0:T(2,128)S(1)} %copy-done.4, s32[2]{0:T(128)S(1)} %copy-done.6, bf16[1024,128]{1,0:T(8,128)(2,1)S(1)} %copy-done.3, bf16[1024,128]{1,0:T(8,128)(2,1)S(1)} %collective-permute-done.refs_3_, ...), custom_call_target="tpu_custom_call" | custom-call | tf_op jit(solution)/shard_map/weights/pallas_call | solution.py:221
  33.0 2.9 %copy-done = bf16[14,512,512]{2,1,0:T(8,128)(2,1)} copy-done((bf16[14,512,512]{2,1,0:T(8,128)(2,1)}, bf16[14,512,512]{2,1,0:T(8,128)(2,1)S(1)}, u32[]{:S(2)}) %copy-start) | copy-done | bytes 7340056
  35.9 3.5 %all-to-all-start = ((bf16[16,8,512]{2,1,0:T(8,128)(2,1)}), bf16[16,8,512]{2,1,0:T(8,128)(2,1)S(1)}, u32[]{:S(2)}, u32[]{:S(2)}) async-start(bf16[16,8,512]{2,1,0:T(8,128)(2,1)} %get-tuple-element.11), calls=%async_computation | async-start | bytes 262144 | tf_op jit(solution)/shard_map/all_to_all | solution.py:241
  39.7 7.6 %all-to-all-done.refs_3_ = bf16[16,8,512]{2,1,0:T(8,128)(2,1)S(1)} async-done(((bf16[16,8,512]{2,1,0:T(8,128)(2,1)}), bf16[16,8,512]{2,1,0:T(8,128)(2,1)S(1)}, u32[]{:S(2)}, u32[]{:S(2)}) %all-to-all-start) | async-done | bytes 131104 | tf_op jit(solution)/shard_map/all_to_all | solution.py:241
  47.3 3.1 %copy-done.1 = bf16[14,512,512]{2,1,0:T(8,128)(2,1)S(1)} copy-done((bf16[14,512,512]{2,1,0:T(8,128)(2,1)S(1)}, bf16[14,512,512]{2,1,0:T(8,128)(2,1)}, u32[]{:S(2)}) %copy-start.1) | copy-done | bytes 7340056
  51.8 5.3 %first_product.1 = (f32[1024,128]{1,0:T(8,128)S(1)}, f32[1024,128]{1,0:T(8,128)S(1)}) custom-call(s32[2,13]{1,0:T(2,128)S(1)} %copy-done.5, s32[2]{0:T(128)S(1)} %copy-done.7, bf16[14,512,512]{2,1,0:T(8,128)(2,1)S(1)} %copy-done.1, bf16[16,8,512]{2,1,0:T(8,128)(2,1)S(1)} %all-to-all-done.refs_3_, bf16[1024,128]{1,0:T(8,128)(2,1)S(1)} %get-tuple-element.15.refs_4_, ...), custom_call_target="tpu_custom_call" | custom-call | tf_op jit(solution)/shard_map/first_product/pallas_call | solution.py:252
  57.4 1.7 %collective-permute-done.6.other_ref = f32[1024,128]{1,0:T(8,128)S(1)} collective-permute-done((f32[1024,128]{1,0:T(8,128)S(1)}, f32[1024,128]{1,0:T(8,128)S(1)}, u32[]{:S(2)}, u32[]{:S(2)}) %collective-permute-start.6) | collective-permute-done | bytes 524320 | tf_op jit(solution)/shard_map/ppermute | solution.py:214
  59.2 1.9 %collective-permute-start.8 = (bf16[1024,128]{1,0:T(8,128)(2,1)S(1)}, bf16[1024,128]{1,0:T(8,128)(2,1)S(1)}, u32[]{:S(2)}, u32[]{:S(2)}) collective-permute-start(bf16[1024,128]{1,0:T(8,128)(2,1)S(1)} %state.1.refs_3_), channel_id=1, source_target_pairs={{0,2},{2,0},{3,5},{5,3},{4,6},{6,4},{7,9},{9,7},{8,10},{10,8},{11,... | collective-permute-start | bytes 786440 | tf_op jit(solution)/shard_map/ppermute | solution.py:211
  61.2 2.0 %collective-permute-start.9 = (bf16[1024,128]{1,0:T(8,128)(2,1)S(1)}, bf16[1024,128]{1,0:T(8,128)(2,1)S(1)}, u32[]{:S(2)}, u32[]{:S(2)}) collective-permute-start(bf16[1024,128]{1,0:T(8,128)(2,1)S(1)} %state.1.refs_3_), channel_id=1, source_target_pairs={{0,4},{4,0},{2,6},{6,2},{5,9},{9,5},{7,11},{11,7},{8,12},{12,8},{1... | collective-permute-start | bytes 786440 | tf_op jit(solution)/shard_map/ppermute | solution.py:211
  63.2 5.3 %collective-permute-start.10 = (bf16[1024,128]{1,0:T(8,128)(2,1)S(1)}, bf16[1024,128]{1,0:T(8,128)(2,1)S(1)}, u32[]{:S(2)}, u32[]{:S(2)}) collective-permute-start(bf16[1024,128]{1,0:T(8,128)(2,1)S(1)} %state.1.refs_3_), channel_id=1, source_target_pairs={{0,6},{6,0},{2,8},{8,2},{4,10},{10,4},{7,13},{13,7},{9,15},{15,9},... | collective-permute-start | bytes 786440 | tf_op jit(solution)/shard_map/ppermute | solution.py:211
  68.5 0.9 %collective-permute-done.9.refs_5_ = bf16[1024,128]{1,0:T(8,128)(2,1)S(1)} collective-permute-done((bf16[1024,128]{1,0:T(8,128)(2,1)S(1)}, bf16[1024,128]{1,0:T(8,128)(2,1)S(1)}, u32[]{:S(2)}, u32[]{:S(2)}) %collective-permute-start.9) | collective-permute-done | bytes 262176 | tf_op jit(solution)/shard_map/ppermute | solution.py:211
  69.4 4.3 %collective-permute-done.10.refs_6_ = bf16[1024,128]{1,0:T(8,128)(2,1)S(1)} collective-permute-done((bf16[1024,128]{1,0:T(8,128)(2,1)S(1)}, bf16[1024,128]{1,0:T(8,128)(2,1)S(1)}, u32[]{:S(2)}, u32[]{:S(2)}) %collective-permute-start.10) | collective-permute-done | bytes 262176 | tf_op jit(solution)/shard_map/ppermute | solution.py:211
  73.7 4.5 %product.1 = f32[1024,128]{1,0:T(8,128)S(1)} custom-call(s32[2,13]{1,0:T(2,128)S(1)} %copy-done.5, s32[2]{0:T(128)S(1)} %copy-done.7, bf16[14,512,512]{2,1,0:T(8,128)(2,1)S(1)} %copy-done.2, bf16[1024,128]{1,0:T(8,128)(2,1)S(1)} %state.1.refs_3_, bf16[1024,128]{1,0:T(8,128)(2,1)S(1)} %collective-permute-done.8.refs_4_, ...), custom_call_target="tpu_custom_call" | custom-call | tf_op jit(solution)/shard_map/product/pallas_call | solution.py:275
  78.2 1.9 %collective-permute-done.11 = f32[1024,128]{1,0:T(8,128)S(1)} collective-permute-done((f32[1024,128]{1,0:T(8,128)S(1)}, f32[1024,128]{1,0:T(8,128)S(1)}, u32[]{:S(2)}, u32[]{:S(2)}) %collective-permute-start.11) | collective-permute-done | bytes 524320 | tf_op jit(solution)/shard_map/ppermute | solution.py:214
  80.1 0.9 %multiply_add_fusion = f32[1024,128]{1,0:T(8,128)} fusion(f32[1024,128]{1,0:T(8,128)S(1)} %get-tuple-element.16.seed_ref, f32[1024,128]{1,0:T(8,128)S(1)} %row_scale.1.rs_ref, f32[1024,128]{1,0:T(8,128)S(1)} %product.1, f32[1024,128]{1,0:T(8,128)S(1)} %collective-permute-done.11), kind=kLoop, calls=%fused_computation | loop fusion | flops 524288 | bytes 2621440 | tf_op jit(solution)/shard_map/add | solution.py:284
  (26 shorter events, 3.5 us)
Async XLA Ops:
  0.0 20.1 %collective-permute-start = (bf16[1024,128]{1,0:T(8,128)(2,1)}, bf16[1024,128]{1,0:T(8,128)(2,1)S(1)}, u32[]{:S(2)}, u32[]{:S(2)}) collective-permute-start(bf16[1024,128]{1,0:T(8,128)(2,1)} %refs_2_.1), channel_id=1, source_target_pairs={{0,2},{2,0},{3,5},{5,3},{4,6},{6,4},{7,9},{9,7},{8,10},{10,8},{11,... | collective-permute-start | bytes 786440 | tf_op jit(solution)/shard_map/ppermute | solution.py:211
  4.9 18.6 %collective-permute-start.1 = (bf16[1024,128]{1,0:T(8,128)(2,1)}, bf16[1024,128]{1,0:T(8,128)(2,1)S(1)}, u32[]{:S(2)}, u32[]{:S(2)}) collective-permute-start(bf16[1024,128]{1,0:T(8,128)(2,1)} %refs_2_.1), channel_id=1, source_target_pairs={{0,4},{4,0},{2,6},{6,2},{5,9},{9,5},{7,11},{11,7},{8,12},{12,8},{1... | collective-permute-start | bytes 786440 | tf_op jit(solution)/shard_map/ppermute | solution.py:211
  8.4 15.2 %collective-permute-start.2 = (bf16[1024,128]{1,0:T(8,128)(2,1)}, bf16[1024,128]{1,0:T(8,128)(2,1)S(1)}, u32[]{:S(2)}, u32[]{:S(2)}) collective-permute-start(bf16[1024,128]{1,0:T(8,128)(2,1)} %refs_2_.1), channel_id=1, source_target_pairs={{0,6},{6,0},{2,8},{8,2},{4,10},{10,4},{7,13},{13,7},{9,15},{15,9},... | collective-permute-start | bytes 786440 | tf_op jit(solution)/shard_map/ppermute | solution.py:211
  12.2 27.5 %collective-permute-start.3 = (bf16[1024,128]{1,0:T(8,128)(2,1)S(1)}, bf16[1024,128]{1,0:T(8,128)(2,1)S(1)}, u32[]{:S(2)}, u32[]{:S(2)}) collective-permute-start(bf16[1024,128]{1,0:T(8,128)(2,1)S(1)} %get-tuple-element.15.refs_4_), channel_id=1, source_target_pairs={{0,2},{2,0},{3,5},{5,3},{4,6},{6,4},{7,9},{9,7},{8,10},{10,8},{11,... | collective-permute-start | bytes 786440 | tf_op jit(solution)/shard_map/ppermute | solution.py:211
  18.2 21.6 %collective-permute-start.4 = (bf16[1024,128]{1,0:T(8,128)(2,1)S(1)}, bf16[1024,128]{1,0:T(8,128)(2,1)S(1)}, u32[]{:S(2)}, u32[]{:S(2)}) collective-permute-start(bf16[1024,128]{1,0:T(8,128)(2,1)S(1)} %get-tuple-element.15.refs_4_), channel_id=1, source_target_pairs={{0,4},{4,0},{2,6},{6,2},{5,9},{9,5},{7,11},{11,7},{8,12},{12,8},{1... | collective-permute-start | bytes 786440 | tf_op jit(solution)/shard_map/ppermute | solution.py:211
  20.1 19.6 %collective-permute-start.5 = (bf16[1024,128]{1,0:T(8,128)(2,1)S(1)}, bf16[1024,128]{1,0:T(8,128)(2,1)S(1)}, u32[]{:S(2)}, u32[]{:S(2)}) collective-permute-start(bf16[1024,128]{1,0:T(8,128)(2,1)S(1)} %get-tuple-element.15.refs_4_), channel_id=1, source_target_pairs={{0,6},{6,0},{2,8},{8,2},{4,10},{10,4},{7,13},{13,7},{9,15},{15,9},... | collective-permute-start | bytes 786440 | tf_op jit(solution)/shard_map/ppermute | solution.py:211
  23.5 1.0 %copy-start.3 = (bf16[1024,128]{1,0:T(8,128)(2,1)S(1)}, bf16[1024,128]{1,0:T(8,128)(2,1)}, u32[]{:S(2)}) copy-start(bf16[1024,128]{1,0:T(8,128)(2,1)} %refs_2_.1) | copy-start | bytes 786436
  24.5 0.7 copy-start.4
  25.2 0.7 copy-start.6
  33.0 2.9 %copy-start = (bf16[14,512,512]{2,1,0:T(8,128)(2,1)}, bf16[14,512,512]{2,1,0:T(8,128)(2,1)S(1)}, u32[]{:S(2)}) copy-start(bf16[14,512,512]{2,1,0:T(8,128)(2,1)S(1)} %get-tuple-element.10.refs_2_) | copy-start | bytes 22020100
  35.9 11.4 %all-to-all-start = ((bf16[16,8,512]{2,1,0:T(8,128)(2,1)}), bf16[16,8,512]{2,1,0:T(8,128)(2,1)S(1)}, u32[]{:S(2)}, u32[]{:S(2)}) async-start(bf16[16,8,512]{2,1,0:T(8,128)(2,1)} %get-tuple-element.11), calls=%async_computation | async-start | bytes 262144 | tf_op jit(solution)/shard_map/all_to_all | solution.py:241
  39.4 17.8 %collective-permute-start.7 = (f32[1024,128]{1,0:T(8,128)S(1)}, f32[1024,128]{1,0:T(8,128)S(1)}, u32[]{:S(2)}, u32[]{:S(2)}) collective-permute-start(f32[1024,128]{1,0:T(8,128)S(1)} %get-tuple-element.13.own_ref), channel_id=1, source_target_pairs={{0,1},{1,0},{2,3},{3,2},{4,5},{5,4},{6,7},{7,6},{8,9},{9,8},{10,11... | collective-permute-start | bytes 1572872 | tf_op jit(solution)/shard_map/ppermute | solution.py:214
  47.3 3.1 %copy-start.1 = (bf16[14,512,512]{2,1,0:T(8,128)(2,1)S(1)}, bf16[14,512,512]{2,1,0:T(8,128)(2,1)}, u32[]{:S(2)}) copy-start(bf16[14,512,512]{2,1,0:T(8,128)(2,1)} %copy-done) | copy-start | bytes 22020100
  50.4 0.7 copy-start.5
  51.1 0.7 copy-start.7
  51.8 21.9 %copy-start.2 = (bf16[14,512,512]{2,1,0:T(8,128)(2,1)S(1)}, bf16[14,512,512]{2,1,0:T(8,128)(2,1)}, u32[]{:S(2)}) copy-start(bf16[14,512,512]{2,1,0:T(8,128)(2,1)} %copy-done) | copy-start | bytes 22020100
  57.1 2.0 %collective-permute-start.6 = (f32[1024,128]{1,0:T(8,128)S(1)}, f32[1024,128]{1,0:T(8,128)S(1)}, u32[]{:S(2)}, u32[]{:S(2)}) collective-permute-start(f32[1024,128]{1,0:T(8,128)S(1)} %get-tuple-element.12.own_ref), channel_id=1, source_target_pairs={{0,1},{1,0},{2,3},{3,2},{4,5},{5,4},{6,7},{7,6},{8,9},{9,8},{10,11... | collective-permute-start | bytes 1572872 | tf_op jit(solution)/shard_map/ppermute | solution.py:214
  59.2 9.2 %collective-permute-start.8 = (bf16[1024,128]{1,0:T(8,128)(2,1)S(1)}, bf16[1024,128]{1,0:T(8,128)(2,1)S(1)}, u32[]{:S(2)}, u32[]{:S(2)}) collective-permute-start(bf16[1024,128]{1,0:T(8,128)(2,1)S(1)} %state.1.refs_3_), channel_id=1, source_target_pairs={{0,2},{2,0},{3,5},{5,3},{4,6},{6,4},{7,9},{9,7},{8,10},{10,8},{11,... | collective-permute-start | bytes 786440 | tf_op jit(solution)/shard_map/ppermute | solution.py:211
  61.2 8.3 %collective-permute-start.9 = (bf16[1024,128]{1,0:T(8,128)(2,1)S(1)}, bf16[1024,128]{1,0:T(8,128)(2,1)S(1)}, u32[]{:S(2)}, u32[]{:S(2)}) collective-permute-start(bf16[1024,128]{1,0:T(8,128)(2,1)S(1)} %state.1.refs_3_), channel_id=1, source_target_pairs={{0,4},{4,0},{2,6},{6,2},{5,9},{9,5},{7,11},{11,7},{8,12},{12,8},{1... | collective-permute-start | bytes 786440 | tf_op jit(solution)/shard_map/ppermute | solution.py:211
  63.2 10.5 %collective-permute-start.10 = (bf16[1024,128]{1,0:T(8,128)(2,1)S(1)}, bf16[1024,128]{1,0:T(8,128)(2,1)S(1)}, u32[]{:S(2)}, u32[]{:S(2)}) collective-permute-start(bf16[1024,128]{1,0:T(8,128)(2,1)S(1)} %state.1.refs_3_), channel_id=1, source_target_pairs={{0,6},{6,0},{2,8},{8,2},{4,10},{10,4},{7,13},{13,7},{9,15},{15,9},... | collective-permute-start | bytes 786440 | tf_op jit(solution)/shard_map/ppermute | solution.py:211
  78.2 2.0 %collective-permute-start.11 = (f32[1024,128]{1,0:T(8,128)S(1)}, f32[1024,128]{1,0:T(8,128)S(1)}, u32[]{:S(2)}, u32[]{:S(2)}) collective-permute-start(f32[1024,128]{1,0:T(8,128)S(1)} %product.1), channel_id=1, source_target_pairs={{0,1},{1,0},{2,3},{3,2},{4,5},{5,4},{6,7},{7,6},{8,9},{9,8},{10,11... | collective-permute-start | bytes 1572872 | tf_op jit(solution)/shard_map/ppermute | solution.py:214

commit v2 on v1

--- a/solution.py
+++ b/solution.py
@@ -17,7 +17,7 @@
 BF16 = jnp.bfloat16
 
 VMEM = pl.BlockSpec(memory_space=pltpu.VMEM)
-SMEM = pl.BlockSpec(memory_space=pltpu.SMEM)
+HBM = pl.BlockSpec(memory_space=pltpu.HBM)
 
 
 def peer_pairs(rows, cols, distance):
@@ -53,29 +53,25 @@
     return offsets
 
 
-def weights_kernel(dims, cols_ref, count_ref, own_ref, *rest):
+def weights_kernel(dims, cols_hbm, count_hbm, own_hbm, *rest):
     blocks, size, width, slots, reach, senders = dims
     peers = rest[:reach]
-    w_ref, row_ref, col_ref, hl, ee, inv, col_acc, offs = rest[reach:]
+    w_hbm, row_ref, col_ref, w_ref, own_ref, hl, ee, inv, col_acc, offs, cols_ref, count_ref, sems, w_sems = rest[reach:]
     tiles = 1 + reach * blocks
     r, c = lax.axis_index("row"), lax.axis_index("col")
-    bits = [listed_bits(cols_ref, count_ref, b, r * blocks + b, slots) for b in range(blocks)]
+    loads = [
+        pltpu.make_async_copy(own_hbm, own_ref, sems.at[0]),
+        pltpu.make_async_copy(cols_hbm, cols_ref, sems.at[1]),
+        pltpu.make_async_copy(count_hbm, count_ref, sems.at[2]),
+    ]
+    for load in loads:
+        load.start()
     for q, offset in enumerate(block_offsets(r, c, reach, blocks)):
         offs[q] = offset
 
-    for b in range(blocks):
-        x = own_ref[pl.ds(b * size, size), :].astype(F32)
-        scale = lax.rsqrt(jnp.sum(x * x, axis=-1, keepdims=True) * (1.0 / width) + EPS)
-        x = x * (scale * (2.0 * KERNEL_SCALE * LOG2E / width))
-        high = x.astype(BF16)
-        hl[pl.ds(b * size, size), :width] = high
-        hl[pl.ds(b * size, size), width:] = (x - high.astype(F32)).astype(BF16)
     ones = jnp.ones((16, 2 * width), BF16)
-    for q in range(tiles):
-        if q == 0:
-            e = own_ref[pl.ds(pl.multiple_of(c * size, size), size), :]
-        else:
-            e = peers[(q - 1) // blocks][pl.ds((q - 1) % blocks * size, size), :]
+
+    def column_side(q, e):
         ee[q, :, :width] = e
         ee[q, :, width:] = e
         x = e.astype(F32)
@@ -84,8 +80,25 @@
         both = jnp.concatenate([high, (x - high.astype(F32)).astype(BF16)], axis=1)
         total = lax.dot_general(ones, both, (((1,), (1,)), ((), ())), preferred_element_type=F32)
         inv[q] = lax.rsqrt(total[:8] * (1.0 / width) + EPS)
+
+    for q in range(1, tiles):
+        column_side(q, peers[(q - 1) // blocks][pl.ds((q - 1) % blocks * size, size), :])
     row_ref[...] = jnp.zeros_like(row_ref)
     col_acc[...] = jnp.zeros_like(col_acc)
+    for load in loads:
+        load.wait()
+    bits = [listed_bits(cols_ref, count_ref, b, r * blocks + b, slots) for b in range(blocks)]
+    column_side(0, own_ref[pl.ds(pl.multiple_of(c * size, size), size), :])
+    for b in range(blocks):
+        x = own_ref[pl.ds(b * size, size), :].astype(F32)
+        scale = lax.rsqrt(jnp.sum(x * x, axis=-1, keepdims=True) * (1.0 / width) + EPS)
+        x = x * (scale * (2.0 * KERNEL_SCALE * LOG2E / width))
+        high = x.astype(BF16)
+        hl[pl.ds(b * size, size), :width] = high
+        hl[pl.ds(b * size, size), width:] = (x - high.astype(F32)).astype(BF16)
+    def store(b, q):
+        at = b * tiles + q
+        return pltpu.make_async_copy(w_ref.at[at], w_hbm.at[at], w_sems.at[at])
 
     def tile(b, q, diagonal):
         s = lax.dot_general(
@@ -99,6 +112,7 @@
             ids = lax.broadcasted_iota(jnp.int32, (size, size), 0)
             w = jnp.where(ids == lax.broadcasted_iota(jnp.int32, (size, size), 1), 0.0, w)
         w_ref[b * tiles + q] = w.astype(BF16)
+        store(b, q).start()
         part = w[:, :LANES]
         for k in range(1, size // LANES):
             part = part + w[:, k * LANES : (k + 1) * LANES]
@@ -124,23 +138,49 @@
     sums = jnp.concatenate(sums, axis=0).astype(BF16)
     for n in range(senders):
         col_ref[n] = sums
-
-
-def product_kernel(dims, first, cols_ref, count_ref, *rest):
+    for q in range(tiles):
+        for b in range(blocks):
+
+            @pl.when(is_listed(bits[b], offs[q] - b))
+            def _():
+                store(b, q).wait()
+
+
+def product_kernel(dims, first, cols_hbm, count_hbm, w_src, *rest):
     blocks, size, width, slots, reach, rows = dims
     tiles = 1 + reach * blocks
-    w_ref = rest[0]
     if first:
-        sums_ref = rest[1]
-        rest = rest[1:]
-    own_ref, peers = rest[1], rest[2 : 2 + reach]
+        sums_ref, rest = rest[0], rest[1:]
+    own_ref, peers = rest[0], rest[1 : 1 + reach]
     if first:
-        out_ref, scale_ref, scaled, scales, offs = rest[2 + reach :]
+        out_ref, scale_ref, w_ref, scaled, scales, cols_ref, count_ref, sems, w_sems = rest[1 + reach :]
     else:
-        out_ref, offs = rest[2 + reach :]
+        out_ref, cols_ref, count_ref, sems = rest[1 + reach :]
+        w_ref = w_src
     r, c = lax.axis_index("row"), lax.axis_index("col")
+    loads = [
+        pltpu.make_async_copy(cols_hbm, cols_ref, sems.at[0]),
+        pltpu.make_async_copy(count_hbm, count_ref, sems.at[1]),
+    ]
+    for load in loads:
+        load.start()
+    offsets = block_offsets(r, c, reach, blocks)
+    out_ref[...] = jnp.zeros_like(out_ref)
+    for load in loads:
+        load.wait()
     bits = [listed_bits(cols_ref, count_ref, b, r * blocks + b, slots) for b in range(blocks)]
-    offsets = block_offsets(r, c, reach, blocks)
+
+    def fetch(b, q):
+        at = b * tiles + q
+        return pltpu.make_async_copy(w_src.at[at], w_ref.at[at], w_sems.at[at])
+
+    if first:
+        for q in range(tiles):
+            for b in range(blocks):
+
+                @pl.when(is_listed(bits[b], offsets[q] - b))
+                def _():
+                    fetch(b, q).start()
 
     if first:
         for n in range(reach + 1):
@@ -168,13 +208,13 @@
         for q in range(1, tiles):
             s = peers[(q - 1) // blocks][pl.ds((q - 1) % blocks * size, size), :].astype(F32)
             scaled[q] = (s * columns[:, blocks + q - 1 : blocks + q]).astype(BF16)
-    out_ref[...] = jnp.zeros_like(out_ref)
     for q in range(tiles):
         for b in range(blocks):
 
             @pl.when(is_listed(bits[b], offsets[q] - b))
             def _():
                 if first:
+                    fetch(b, q).wait()
                     s = scaled[q]
                 elif q == 0:
                     s = own_ref[pl.ds(pl.multiple_of(c * size, size), size), :]
@@ -207,6 +247,8 @@
     assert blocks == 2 and cols == 2 and tiles <= 8
     params = pltpu.CompilerParams(vmem_limit_bytes=24 * 1024 * 1024)
 
+    tables = [pltpu.SMEM(tile_cols.shape, jnp.int32), pltpu.SMEM(tile_count.shape, jnp.int32)]
+
     def from_peers(value):
         return [lax.ppermute(value, ("row", "col"), peer_pairs(rows, cols, d)) for d in range(1, reach + 1)]
 
@@ -214,29 +256,36 @@
         return lax.ppermute(value, "col", [(0, 1), (1, 0)])
 
     peer_emb = from_peers(embeddings)
-    seed_rows = seed_mask.astype(F32)[:, None] * profiles
+    tables_hbm = [pltpu.with_memory_space_constraint(t, pltpu.HBM) for t in (tile_cols, tile_count)]
+    emb_hbm = pltpu.with_memory_space_constraint(embeddings, pltpu.HBM)
+    seed_rows = jnp.where(seed_mask[:, None] > 0, profiles, 0.0)
     seeds = seed_rows.astype(BF16)
     peer_seeds = from_peers(seeds)
 
     weights, row_part, col_part = pl.pallas_call(
         lambda *refs: weights_kernel((blocks, size, width, slots, reach, senders), *refs),
         out_shape=(
-            jax.ShapeDtypeStruct((blocks * tiles, size, size), BF16),
+            pltpu.HBM((blocks * tiles, size, size), BF16),
             jax.ShapeDtypeStruct((mols, LANES), F32),
             jax.ShapeDtypeStruct((senders, 8, size), BF16),
         ),
-        in_specs=[SMEM, SMEM] + [VMEM] * (1 + reach),
-        out_specs=(VMEM, VMEM, VMEM),
+        in_specs=[HBM] * 3 + [VMEM] * reach,
+        out_specs=(HBM, VMEM, VMEM),
         scratch_shapes=[
+            pltpu.VMEM((blocks * tiles, size, size), BF16),
+            pltpu.VMEM((mols, width), BF16),
             pltpu.VMEM((mols, 2 * width), BF16),
             pltpu.VMEM((tiles, size, 2 * width), BF16),
             pltpu.VMEM((tiles, 8, size), F32),
             pltpu.VMEM((tiles, 8, size), F32),
             pltpu.SMEM((tiles,), jnp.int32),
+            *tables,
+            pltpu.SemaphoreType.DMA((3,)),
+            pltpu.SemaphoreType.DMA((blocks * tiles,)),
         ],
         compiler_params=params,
         name="weights",
-    )(tile_cols, tile_count, embeddings, *peer_emb)
+    )(*tables_hbm, emb_hbm, *peer_emb)
 
     col_sums = lax.all_to_all(col_part, ("row", "col"), 0, 0, tiled=True)
     row_scale = pl.pallas_call(
@@ -249,19 +298,25 @@
     )(row_part, other_core(row_part))
 
     dims = (blocks, size, prof, slots, reach, rows)
-    partial, col_scale = pl.pallas_call(
+    partial, col_scale, weights = pl.pallas_call(
         lambda *refs: product_kernel(dims, True, *refs),
-        out_shape=(jax.ShapeDtypeStruct((mols, prof), F32), jax.ShapeDtypeStruct((mols, prof), F32)),
-        in_specs=[SMEM, SMEM] + [VMEM] * (3 + reach),
-        out_specs=(VMEM, VMEM),
+        out_shape=(
+            jax.ShapeDtypeStruct((mols, prof), F32),
+            jax.ShapeDtypeStruct((mols, prof), F32),
+            jax.ShapeDtypeStruct((blocks * tiles, size, size), BF16),
+        ),
+        in_specs=[HBM] * 3 + [VMEM] * (2 + reach),
+        out_specs=(VMEM, VMEM, VMEM),
         scratch_shapes=[
             pltpu.VMEM((tiles, size, prof), BF16),
             pltpu.VMEM((8, size), F32),
-            pltpu.SMEM((tiles,), jnp.int32),
+            *tables,
+            pltpu.SemaphoreType.DMA((2,)),
+            pltpu.SemaphoreType.DMA((blocks * tiles,)),
         ],
         compiler_params=params,
         name="first_product",
-    )(tile_cols, tile_count, weights, col_sums, seeds, *peer_seeds)
+    )(*tables_hbm, pltpu.with_memory_space_constraint(weights, pltpu.HBM), col_sums, seeds, *peer_seeds)
 
     for iteration in range(1, ITERS):
         scaled = pl.pallas_call(
@@ -275,12 +330,12 @@
         partial = pl.pallas_call(
             lambda *refs: product_kernel(dims, False, *refs),
             out_shape=jax.ShapeDtypeStruct((mols, prof), F32),
-            in_specs=[SMEM, SMEM] + [VMEM] * (2 + reach),
+            in_specs=[HBM] * 2 + [VMEM] * (2 + reach),
             out_specs=VMEM,
-            scratch_shapes=[pltpu.SMEM((tiles,), jnp.int32)],
+            scratch_shapes=[*tables, pltpu.SemaphoreType.DMA((2,))],
             compiler_params=params,
             name="product",
-        )(tile_cols, tile_count, weights, scaled, *from_peers(scaled))
+        )(*tables_hbm, weights, scaled, *from_peers(scaled))
     return (partial + other_core(partial)) * row_scale + (1.0 - ALPHA) * seed_rows
 
 

time: 81.2 us -> 77.6 us (0.956)
  local copies, waits for them, and re-layouts: 9.64 us -> 0 us
  starting transfers between devices: 34.7 us -> 37.9 us
  Pallas kernels: 17.3 us -> 19.8 us
    unnamed x16 -> x0, local copies, waits for them, and re-layouts: 9.64 us -> none
    all_to_all x1, starting transfers between devices: 3.51 us -> 7.83 us  [shards(): col_sums = lax.all_to_all(col_part, ('row', 'col'), 0, 0, tiled=True)]
    ppermute x9, starting transfers between devices: 30.7 us -> 29.5 us  [from_peers(): lax.ppermute(value, ('row', 'col'), peer_pairs(rows, cols, d))]
    pallas_call x1, Pallas kernels: 7.17 us -> 8.35 us  [shards(): pl.pallas_call(lambda *refs: weights_kernel((blocks, size, width, slots,...]
    pallas_call x1, Pallas kernels: 5.34 us -> 6.49 us  [shards(): pl.pallas_call(lambda *refs: product_kernel(dims, True, *refs), out_shape...]
  transfers between devices with their start and end apart: 13 -> 13, of which waited for: 5 -> 4; matrix products, arithmetic and copies ran while one was open for 2% -> 2% of each run, Pallas kernels for 16% -> 19%
where the time goes in v2:
time: 77.6 us; the launch traced here: 77.4 us
  starting transfers between devices  37.9 us (49%)
  Pallas kernels  19.8 us (26%)
  waiting for transfers between devices  16.6 us (21%)
  other arithmetic  2.82 us (4%)
    ppermute x9, starting transfers between devices, from_peers(): lax.ppermute(value, ('row', 'col'), peer_pairs(rows, cols, d))  29.5 us
    pallas_call x1, Pallas kernels, shards(): pl.pallas_call(lambda *refs: weights_kernel((blocks, size, width, slots,...  8.35 us
    all_to_all x1, starting transfers between devices, shards(): col_sums = lax.all_to_all(col_part, ('row', 'col'), 0, 0, tiled=True)  7.83 us
    all_to_all x1, waiting for transfers between devices, shards(): col_sums = lax.all_to_all(col_part, ('row', 'col'), 0, 0, tiled=True)  7.51 us
    pallas_call x1, Pallas kernels, shards(): pl.pallas_call(lambda *refs: product_kernel(dims, True, *refs), out_shape...  6.49 us
    ppermute x9, waiting for transfers between devices, from_peers(): lax.ppermute(value, ('row', 'col'), peer_pairs(rows, cols, d))  5.56 us
    pallas_call x1, Pallas kernels, shards(): pl.pallas_call(lambda *refs: product_kernel(dims, False, *refs), out_shap...  4.65 us
    ppermute x3, waiting for transfers between devices, other_core(): return lax.ppermute(value, 'col', [(0, 1), (1, 0)])  3.56 us
  transfers between devices with their start and end apart: 13, of which 4 were waited for; matrix products, arithmetic and copies ran while one was open for 2% of the time, Pallas kernels for 19%

profile of v2, /device:TPU:0, one launch (start us, length us, event | category | flops | bytes accessed | tf_op | source)
XLA Modules:
  0.0 77.4 jit_solution(17700198074461949456)
XLA Ops:
  0.0 4.9 %collective-permute-start.1 = (bf16[1024,128]{1,0:T(8,128)(2,1)}, bf16[1024,128]{1,0:T(8,128)(2,1)S(1)}, u32[]{:S(2)}, u32[]{:S(2)}) collective-permute-start(bf16[1024,128]{1,0:T(8,128)(2,1)} %refs_2_.1), channel_id=1, source_target_pairs={{0,4},{4,0},{2,6},{6,2},{5,9},{9,5},{7,11},{11,7},{8,12},{12,8},{1... | collective-permute-start | bytes 786440 | tf_op jit(solution)/shard_map/ppermute | solution.py:253
  4.9 3.4 %collective-permute-start = (bf16[1024,128]{1,0:T(8,128)(2,1)}, bf16[1024,128]{1,0:T(8,128)(2,1)S(1)}, u32[]{:S(2)}, u32[]{:S(2)}) collective-permute-start(bf16[1024,128]{1,0:T(8,128)(2,1)} %refs_2_.1), channel_id=1, source_target_pairs={{0,2},{2,0},{3,5},{5,3},{4,6},{6,4},{7,9},{9,7},{8,10},{10,8},{11,... | collective-permute-start | bytes 786440 | tf_op jit(solution)/shard_map/ppermute | solution.py:253
  8.4 1.9 %collective-permute-start.2 = (bf16[1024,128]{1,0:T(8,128)(2,1)}, bf16[1024,128]{1,0:T(8,128)(2,1)S(1)}, u32[]{:S(2)}, u32[]{:S(2)}) collective-permute-start(bf16[1024,128]{1,0:T(8,128)(2,1)} %refs_2_.1), channel_id=1, source_target_pairs={{0,6},{6,0},{2,8},{8,2},{4,10},{10,4},{7,13},{13,7},{9,15},{15,9},... | collective-permute-start | bytes 786440 | tf_op jit(solution)/shard_map/ppermute | solution.py:253
  10.3 0.7 broadcast_compare_fusion
  11.0 1.2 %fusion = (bf16[1024,128]{1,0:T(8,128)(2,1)S(1)}, f32[1024,128]{1,0:T(8,128)S(1)}) fusion(f32[1024,128]{1,0:T(8,128)} %param.6, pred[1024]{0:T(1024)(128)(4,1)S(1)} %broadcast_compare_fusion), kind=kLoop, calls=%fused_computation.3 | loop fusion | flops 262144 | bytes 1311744 | tf_op jit(solution)/shard_map/convert_element_type | solution.py:262
  12.2 4.8 %collective-permute-start.5 = (bf16[1024,128]{1,0:T(8,128)(2,1)S(1)}, bf16[1024,128]{1,0:T(8,128)(2,1)S(1)}, u32[]{:S(2)}, u32[]{:S(2)}) collective-permute-start(bf16[1024,128]{1,0:T(8,128)(2,1)S(1)} %get-tuple-element.17.refs_4_), channel_id=1, source_target_pairs={{0,6},{6,0},{2,8},{8,2},{4,10},{10,4},{7,13},{13,7},{9,15},{15,9},... | collective-permute-start | bytes 786440 | tf_op jit(solution)/shard_map/ppermute | solution.py:253
  17.1 2.4 %collective-permute-start.4 = (bf16[1024,128]{1,0:T(8,128)(2,1)S(1)}, bf16[1024,128]{1,0:T(8,128)(2,1)S(1)}, u32[]{:S(2)}, u32[]{:S(2)}) collective-permute-start(bf16[1024,128]{1,0:T(8,128)(2,1)S(1)} %get-tuple-element.17.refs_4_), channel_id=1, source_target_pairs={{0,4},{4,0},{2,6},{6,2},{5,9},{9,5},{7,11},{11,7},{8,12},{12,8},{1... | collective-permute-start | bytes 786440 | tf_op jit(solution)/shard_map/ppermute | solution.py:253
  19.4 2.9 %collective-permute-start.3 = (bf16[1024,128]{1,0:T(8,128)(2,1)S(1)}, bf16[1024,128]{1,0:T(8,128)(2,1)S(1)}, u32[]{:S(2)}, u32[]{:S(2)}) collective-permute-start(bf16[1024,128]{1,0:T(8,128)(2,1)S(1)} %get-tuple-element.17.refs_4_), channel_id=1, source_target_pairs={{0,2},{2,0},{3,5},{5,3},{4,6},{6,4},{7,9},{9,7},{8,10},{10,8},{11,... | collective-permute-start | bytes 786440 | tf_op jit(solution)/shard_map/ppermute | solution.py:253
  22.4 8.3 %weights.1 = (bf16[14,512,512]{2,1,0:T(8,128)(2,1)}, f32[1024,128]{1,0:T(8,128)S(1)}, bf16[16,8,512]{2,1,0:T(8,128)(2,1)}) custom-call(s32[2,13]{1,0:T(2,128)} %refs_0_.5, s32[2]{0:T(128)} %refs_1_.5, bf16[1024,128]{1,0:T(8,128)(2,1)} %refs_2_.1, bf16[1024,128]{1,0:T(8,128)(2,1)S(1)} %collective-permute-done.refs_3_, ...), custom_call_target="tpu_custom_call" | custom-call | tf_op jit(solution)/shard_map/weights/pallas_call | solution.py:265
  30.7 7.8 %all-to-all-start = ((bf16[16,8,512]{2,1,0:T(8,128)(2,1)}), bf16[16,8,512]{2,1,0:T(8,128)(2,1)S(1)}, u32[]{:S(2)}, u32[]{:S(2)}) async-start(bf16[16,8,512]{2,1,0:T(8,128)(2,1)} %get-tuple-element.12), calls=%async_computation | async-start | bytes 262144 | tf_op jit(solution)/shard_map/all_to_all | solution.py:290
  38.5 0.4 collective-permute-start.7
  39.0 7.5 %all-to-all-done.refs_3_ = bf16[16,8,512]{2,1,0:T(8,128)(2,1)S(1)} async-done(((bf16[16,8,512]{2,1,0:T(8,128)(2,1)}), bf16[16,8,512]{2,1,0:T(8,128)(2,1)S(1)}, u32[]{:S(2)}, u32[]{:S(2)}) %all-to-all-start) | async-done | bytes 131104 | tf_op jit(solution)/shard_map/all_to_all | solution.py:290
  46.5 6.5 %first_product.1 = (f32[1024,128]{1,0:T(8,128)S(1)}, f32[1024,128]{1,0:T(8,128)S(1)}, bf16[14,512,512]{2,1,0:T(8,128)(2,1)S(1)}) custom-call(s32[2,13]{1,0:T(2,128)} %refs_0_.5, s32[2]{0:T(128)} %refs_1_.5, bf16[14,512,512]{2,1,0:T(8,128)(2,1)} %get-tuple-element.11.refs_2_, bf16[16,8,512]{2,1,0:T(8,128)(2,1)S(1)} %all-to-all-done.refs_3_, ...), custom_call_target="tpu_custom_call" | custom-call | tf_op jit(solution)/shard_map/first_product/pallas_call | solution.py:301
  53.0 0.1 collective-permute-start.6
  53.1 0.2 row_scale.1.rs_ref
  53.3 1.7 %collective-permute-done.6.other_ref = f32[1024,128]{1,0:T(8,128)S(1)} collective-permute-done((f32[1024,128]{1,0:T(8,128)S(1)}, f32[1024,128]{1,0:T(8,128)S(1)}, u32[]{:S(2)}, u32[]{:S(2)}) %collective-permute-start.6) | collective-permute-done | bytes 524320 | tf_op jit(solution)/shard_map/ppermute | solution.py:256
  55.0 0.1 state.1.refs_3_
  55.1 1.9 %collective-permute-start.10 = (bf16[1024,128]{1,0:T(8,128)(2,1)S(1)}, bf16[1024,128]{1,0:T(8,128)(2,1)S(1)}, u32[]{:S(2)}, u32[]{:S(2)}) collective-permute-start(bf16[1024,128]{1,0:T(8,128)(2,1)S(1)} %state.1.refs_3_), channel_id=1, source_target_pairs={{0,6},{6,0},{2,8},{8,2},{4,10},{10,4},{7,13},{13,7},{9,15},{15,9},... | collective-permute-start | bytes 786440 | tf_op jit(solution)/shard_map/ppermute | solution.py:253
  57.0 1.9 %collective-permute-start.9 = (bf16[1024,128]{1,0:T(8,128)(2,1)S(1)}, bf16[1024,128]{1,0:T(8,128)(2,1)S(1)}, u32[]{:S(2)}, u32[]{:S(2)}) collective-permute-start(bf16[1024,128]{1,0:T(8,128)(2,1)S(1)} %state.1.refs_3_), channel_id=1, source_target_pairs={{0,4},{4,0},{2,6},{6,2},{5,9},{9,5},{7,11},{11,7},{8,12},{12,8},{1... | collective-permute-start | bytes 786440 | tf_op jit(solution)/shard_map/ppermute | solution.py:253
  58.9 5.4 %collective-permute-start.8 = (bf16[1024,128]{1,0:T(8,128)(2,1)S(1)}, bf16[1024,128]{1,0:T(8,128)(2,1)S(1)}, u32[]{:S(2)}, u32[]{:S(2)}) collective-permute-start(bf16[1024,128]{1,0:T(8,128)(2,1)S(1)} %state.1.refs_3_), channel_id=1, source_target_pairs={{0,2},{2,0},{3,5},{5,3},{4,6},{6,4},{7,9},{9,7},{8,10},{10,8},{11,... | collective-permute-start | bytes 786440 | tf_op jit(solution)/shard_map/ppermute | solution.py:253
  64.3 5.5 %collective-permute-done.9.refs_5_ = bf16[1024,128]{1,0:T(8,128)(2,1)S(1)} collective-permute-done((bf16[1024,128]{1,0:T(8,128)(2,1)S(1)}, bf16[1024,128]{1,0:T(8,128)(2,1)S(1)}, u32[]{:S(2)}, u32[]{:S(2)}) %collective-permute-start.9) | collective-permute-done | bytes 262176 | tf_op jit(solution)/shard_map/ppermute | solution.py:253
  69.9 4.7 %product.1 = f32[1024,128]{1,0:T(8,128)S(1)} custom-call(s32[2,13]{1,0:T(2,128)} %refs_0_.5, s32[2]{0:T(128)} %refs_1_.5, bf16[14,512,512]{2,1,0:T(8,128)(2,1)S(1)} %get-tuple-element.13.refs_2_, bf16[1024,128]{1,0:T(8,128)(2,1)S(1)} %state.1.refs_3_, bf16[1024,128]{1,0:T(8,128)(2,1)S(1)} %collective-permute-done.8.refs_4_, ...), custom_call_target="tpu_custom_call" | custom-call | tf_op jit(solution)/shard_map/product/pallas_call | solution.py:330
  74.6 1.9 %collective-permute-done.11 = f32[1024,128]{1,0:T(8,128)S(1)} collective-permute-done((f32[1024,128]{1,0:T(8,128)S(1)}, f32[1024,128]{1,0:T(8,128)S(1)}, u32[]{:S(2)}, u32[]{:S(2)}) %collective-permute-start.11) | collective-permute-done | bytes 524320 | tf_op jit(solution)/shard_map/ppermute | solution.py:256
  76.5 0.9 %multiply_add_fusion = f32[1024,128]{1,0:T(8,128)} fusion(f32[1024,128]{1,0:T(8,128)S(1)} %get-tuple-element.18.seed_ref, f32[1024,128]{1,0:T(8,128)S(1)} %row_scale.1.rs_ref, f32[1024,128]{1,0:T(8,128)S(1)} %product.1, f32[1024,128]{1,0:T(8,128)S(1)} %collective-permute-done.11), kind=kLoop, calls=%fused_computation | loop fusion | flops 524288 | bytes 2621440 | tf_op jit(solution)/shard_map/add | solution.py:339
  (10 shorter events, 0.1 us)
Async XLA Ops:
  0.0 19.4 %collective-permute-start.1 = (bf16[1024,128]{1,0:T(8,128)(2,1)}, bf16[1024,128]{1,0:T(8,128)(2,1)S(1)}, u32[]{:S(2)}, u32[]{:S(2)}) collective-permute-start(bf16[1024,128]{1,0:T(8,128)(2,1)} %refs_2_.1), channel_id=1, source_target_pairs={{0,4},{4,0},{2,6},{6,2},{5,9},{9,5},{7,11},{11,7},{8,12},{12,8},{1... | collective-permute-start | bytes 786440 | tf_op jit(solution)/shard_map/ppermute | solution.py:253
  4.9 17.4 %collective-permute-start = (bf16[1024,128]{1,0:T(8,128)(2,1)}, bf16[1024,128]{1,0:T(8,128)(2,1)S(1)}, u32[]{:S(2)}, u32[]{:S(2)}) collective-permute-start(bf16[1024,128]{1,0:T(8,128)(2,1)} %refs_2_.1), channel_id=1, source_target_pairs={{0,2},{2,0},{3,5},{5,3},{4,6},{6,4},{7,9},{9,7},{8,10},{10,8},{11,... | collective-permute-start | bytes 786440 | tf_op jit(solution)/shard_map/ppermute | solution.py:253
  8.4 14.0 %collective-permute-start.2 = (bf16[1024,128]{1,0:T(8,128)(2,1)}, bf16[1024,128]{1,0:T(8,128)(2,1)S(1)}, u32[]{:S(2)}, u32[]{:S(2)}) collective-permute-start(bf16[1024,128]{1,0:T(8,128)(2,1)} %refs_2_.1), channel_id=1, source_target_pairs={{0,6},{6,0},{2,8},{8,2},{4,10},{10,4},{7,13},{13,7},{9,15},{15,9},... | collective-permute-start | bytes 786440 | tf_op jit(solution)/shard_map/ppermute | solution.py:253
  12.2 26.7 %collective-permute-start.5 = (bf16[1024,128]{1,0:T(8,128)(2,1)S(1)}, bf16[1024,128]{1,0:T(8,128)(2,1)S(1)}, u32[]{:S(2)}, u32[]{:S(2)}) collective-permute-start(bf16[1024,128]{1,0:T(8,128)(2,1)S(1)} %get-tuple-element.17.refs_4_), channel_id=1, source_target_pairs={{0,6},{6,0},{2,8},{8,2},{4,10},{10,4},{7,13},{13,7},{9,15},{15,9},... | collective-permute-start | bytes 786440 | tf_op jit(solution)/shard_map/ppermute | solution.py:253
  17.1 21.9 %collective-permute-start.4 = (bf16[1024,128]{1,0:T(8,128)(2,1)S(1)}, bf16[1024,128]{1,0:T(8,128)(2,1)S(1)}, u32[]{:S(2)}, u32[]{:S(2)}) collective-permute-start(bf16[1024,128]{1,0:T(8,128)(2,1)S(1)} %get-tuple-element.17.refs_4_), channel_id=1, source_target_pairs={{0,4},{4,0},{2,6},{6,2},{5,9},{9,5},{7,11},{11,7},{8,12},{12,8},{1... | collective-permute-start | bytes 786440 | tf_op jit(solution)/shard_map/ppermute | solution.py:253
  19.4 19.5 %collective-permute-start.3 = (bf16[1024,128]{1,0:T(8,128)(2,1)S(1)}, bf16[1024,128]{1,0:T(8,128)(2,1)S(1)}, u32[]{:S(2)}, u32[]{:S(2)}) collective-permute-start(bf16[1024,128]{1,0:T(8,128)(2,1)S(1)} %get-tuple-element.17.refs_4_), channel_id=1, source_target_pairs={{0,2},{2,0},{3,5},{5,3},{4,6},{6,4},{7,9},{9,7},{8,10},{10,8},{11,... | collective-permute-start | bytes 786440 | tf_op jit(solution)/shard_map/ppermute | solution.py:253
  30.7 15.8 %all-to-all-start = ((bf16[16,8,512]{2,1,0:T(8,128)(2,1)}), bf16[16,8,512]{2,1,0:T(8,128)(2,1)S(1)}, u32[]{:S(2)}, u32[]{:S(2)}) async-start(bf16[16,8,512]{2,1,0:T(8,128)(2,1)} %get-tuple-element.12), calls=%async_computation | async-start | bytes 262144 | tf_op jit(solution)/shard_map/all_to_all | solution.py:290
  38.5 14.5 %collective-permute-start.7 = (f32[1024,128]{1,0:T(8,128)S(1)}, f32[1024,128]{1,0:T(8,128)S(1)}, u32[]{:S(2)}, u32[]{:S(2)}) collective-permute-start(f32[1024,128]{1,0:T(8,128)S(1)} %get-tuple-element.15.own_ref), channel_id=1, source_target_pairs={{0,1},{1,0},{2,3},{3,2},{4,5},{5,4},{6,7},{7,6},{8,9},{9,8},{10,11... | collective-permute-start | bytes 1572872 | tf_op jit(solution)/shard_map/ppermute | solution.py:256
  53.0 2.0 %collective-permute-start.6 = (f32[1024,128]{1,0:T(8,128)S(1)}, f32[1024,128]{1,0:T(8,128)S(1)}, u32[]{:S(2)}, u32[]{:S(2)}) collective-permute-start(f32[1024,128]{1,0:T(8,128)S(1)} %get-tuple-element.14.own_ref), channel_id=1, source_target_pairs={{0,1},{1,0},{2,3},{3,2},{4,5},{5,4},{6,7},{7,6},{8,9},{9,8},{10,11... | collective-permute-start | bytes 1572872 | tf_op jit(solution)/shard_map/ppermute | solution.py:256
  55.1 9.2 %collective-permute-start.10 = (bf16[1024,128]{1,0:T(8,128)(2,1)S(1)}, bf16[1024,128]{1,0:T(8,128)(2,1)S(1)}, u32[]{:S(2)}, u32[]{:S(2)}) collective-permute-start(bf16[1024,128]{1,0:T(8,128)(2,1)S(1)} %state.1.refs_3_), channel_id=1, source_target_pairs={{0,6},{6,0},{2,8},{8,2},{4,10},{10,4},{7,13},{13,7},{9,15},{15,9},... | collective-permute-start | bytes 786440 | tf_op jit(solution)/shard_map/ppermute | solution.py:253
  57.0 12.9 %collective-permute-start.9 = (bf16[1024,128]{1,0:T(8,128)(2,1)S(1)}, bf16[1024,128]{1,0:T(8,128)(2,1)S(1)}, u32[]{:S(2)}, u32[]{:S(2)}) collective-permute-start(bf16[1024,128]{1,0:T(8,128)(2,1)S(1)} %state.1.refs_3_), channel_id=1, source_target_pairs={{0,4},{4,0},{2,6},{6,2},{5,9},{9,5},{7,11},{11,7},{8,12},{12,8},{1... | collective-permute-start | bytes 786440 | tf_op jit(solution)/shard_map/ppermute | solution.py:253
  58.9 10.9 %collective-permute-start.8 = (bf16[1024,128]{1,0:T(8,128)(2,1)S(1)}, bf16[1024,128]{1,0:T(8,128)(2,1)S(1)}, u32[]{:S(2)}, u32[]{:S(2)}) collective-permute-start(bf16[1024,128]{1,0:T(8,128)(2,1)S(1)} %state.1.refs_3_), channel_id=1, source_target_pairs={{0,2},{2,0},{3,5},{5,3},{4,6},{6,4},{7,9},{9,7},{8,10},{10,8},{11,... | collective-permute-start | bytes 786440 | tf_op jit(solution)/shard_map/ppermute | solution.py:253
  74.5 2.0 %collective-permute-start.11 = (f32[1024,128]{1,0:T(8,128)S(1)}, f32[1024,128]{1,0:T(8,128)S(1)}, u32[]{:S(2)}, u32[]{:S(2)}) collective-permute-start(f32[1024,128]{1,0:T(8,128)S(1)} %product.1), channel_id=1, source_target_pairs={{0,1},{1,0},{2,3},{3,2},{4,5},{5,4},{6,7},{7,6},{8,9},{9,8},{10,11... | collective-permute-start | bytes 1572872 | tf_op jit(solution)/shard_map/ppermute | solution.py:256

commit v3 on v0

v3 whole, which is shorter than its diff:
```python
import jax
import jax.numpy as jnp
from jax import lax
from jax.experimental import pallas as pl
from jax.experimental.pallas import tpu as pltpu
from jax.sharding import PartitionSpec as P

BAND = 6
ITERS = 2

KERNEL_SCALE = 12.5
ALPHA = 0.8
EPS = 1e-06
LOG2E = 1.4426950408889634
LANES = 128
TAIL = 16
F32 = jnp.float32
BF16 = jnp.bfloat16

VMEM = pl.BlockSpec(memory_space=pltpu.VMEM)
HBM = pl.BlockSpec(memory_space=pltpu.HBM)
PARAMS = pltpu.CompilerParams(vmem_limit_bytes=24 * 1024 * 1024)


def peer_pairs(rows, cols, distance):
    pairs = []
    for low in range(rows - distance):
        core = (low // distance) % cols
        a, b = low * cols + core, (low + distance) * cols + core
        pairs += [(a, b), (b, a)]
    busy = {a for a, _ in pairs}
    idle = [n for n in range(rows * cols) if n not in busy]
    for a, b in zip(idle[::2], idle[1::2]):
        pairs += [(a, b), (b, a)]
    return pairs


def peer_sign(distance):
    return jnp.where(lax.rem(lax.div(lax.axis_index("row"), distance), 2) == lax.axis_index("col"), 1, -1)


def table_entry(table, row, offset):
    lane = lax.broadcasted_iota(jnp.int32, (1, LANES), 1)
    return jnp.max(jnp.where(lane == offset + BAND, table[row : row + 1, :], 0.0), axis=-1, keepdims=True)


def lanes_sum(w):
    part = w[:, :LANES]
    for k in range(1, w.shape[1] // LANES):
        part = part + w[:, k * LANES : (k + 1) * LANES]
    return part


def pack_kernel(blocks, slots, emb_hbm, cols_hbm, count_hbm, out_ref, cols_ref, count_ref, sems):
    mols = emb_hbm.shape[0]
    loads = [
        pltpu.make_async_copy(emb_hbm, out_ref.at[pl.ds(0, mols), :], sems.at[0]),
        pltpu.make_async_copy(cols_hbm, cols_ref, sems.at[1]),
        pltpu.make_async_copy(count_hbm, count_ref, sems.at[2]),
    ]
    for load in loads:
        load.start()
    loads[1].wait()
    loads[2].wait()
    first = lax.axis_index("row") * blocks
    lane = lax.broadcasted_iota(jnp.int32, (TAIL, LANES), 1)
    row = lax.broadcasted_iota(jnp.int32, (TAIL, LANES), 0)
    table = jnp.zeros((TAIL, LANES), F32)
    for b in range(blocks):
        for s in range(slots):
            offset = jnp.where(s < count_ref[b], cols_ref[b, s] - (first + b) + BAND, -1)
            table = jnp.where(jnp.logical_and(lane == offset, row == b), 1.0, table)
    out_ref[pl.ds(mols, TAIL), :] = table.astype(BF16)
    loads[0].wait()


def tile_weights(hl, b, e, w_ref, at, s_ref, diagonal):
    size, width = e.shape
    x = e.astype(F32)
    x = x * x
    high = x.astype(BF16)
    both = jnp.concatenate([high, (x - high.astype(F32)).astype(BF16)], axis=1)
    nt = (((1,), (1,)), ((), ()))
    total = lax.dot_general(jnp.ones((TAIL, 2 * width), BF16), both, nt, preferred_element_type=F32)
    inv = lax.rsqrt(total[0:1] * (1.0 / width) + EPS)
    ee = jnp.concatenate([e, e], axis=1)
    s_ref[...] = lax.dot_general(hl[pl.ds(b * size, size), :], ee, nt, preferred_element_type=F32)
    parts = []
    rows = 32
    for k in range(size // rows):
        w = jnp.exp2(s_ref[pl.ds(k * rows, rows), :] * inv - 2.0 * KERNEL_SCALE * LOG2E)
        if diagonal is not None:
            i = lax.broadcasted_iota(jnp.int32, (rows, size), 0) + k * rows
            j = lax.broadcasted_iota(jnp.int32, (rows, size), 1)
            w = jnp.where(jnp.logical_and(i == j, diagonal), 0.0, w)
        w_ref[at, pl.ds(k * rows, rows), :] = w.astype(BF16)
        parts.append(lanes_sum(w))
    return parts


def add_parts(ref, first, parts, mask, start):
    rows = parts[0].shape[0]
    for k, part in enumerate(parts):
        at = pl.ds(first + k * rows, rows)
        value = part * mask
        ref[at, :] = value if start else ref[at, :] + value


def own_weights_kernel(blocks, pack_ref, hl, w_ref, row_ref, col_ref, s_ref):
    mols = hl.shape[0]
    size, width = mols // blocks, hl.shape[1] // 2
    c = lax.axis_index("col")
    table = pack_ref[pl.ds(mols, TAIL), :].astype(F32)
    for b in range(blocks):
        x = pack_ref[pl.ds(b * size, size), :].astype(F32)
        scale = lax.rsqrt(jnp.sum(x * x, axis=-1, keepdims=True) * (1.0 / width) + EPS)
        x = x * (scale * (2.0 * KERNEL_SCALE * LOG2E / width))
        high = x.astype(BF16)
        hl[pl.ds(b * size, size), :width] = high
        hl[pl.ds(b * size, size), width:] = (x - high.astype(F32)).astype(BF16)
    e = pack_ref[pl.ds(pl.multiple_of(c * size, size), size), :]
    for b in range(blocks):
        parts = tile_weights(hl, b, e, w_ref, b, s_ref, c == b)
        from_c = jnp.where(c == 0, table_entry(table, 0, b), table_entry(table, 1, b - 1))
        add_parts(row_ref, b * size, parts, table_entry(table, b, c - b), True)
        add_parts(col_ref, b * size, parts, from_c, True)


def peer_weights_kernel(dims, distance, pack_ref, peer_ref, hl, row_in, col_in, w_ref, *rest):
    blocks, rows, last = dims
    if last:
        deg_ref, row_ref, col_ref, s_ref = rest
    else:
        row_ref, col_ref, s_ref = rest
    mols = hl.shape[0]
    size = mols // blocks
    sign = peer_sign(distance)
    peer = lax.axis_index("row") + sign * distance
    valid = jnp.where(jnp.logical_and(peer >= 0, peer < rows), 1.0, 0.0)
    own_table = pack_ref[pl.ds(mols, TAIL), :].astype(F32)
    peer_table = peer_ref[pl.ds(mols, TAIL), :].astype(F32) * valid
    row_ref[...] = row_in[...]
    col_ref[...] = col_in[...]
    for k in range(blocks):
        e = peer_ref[pl.ds(k * size, size), :]
        for b in range(blocks):
            offset = sign * (distance * blocks) + (k - b)
            parts = tile_weights(hl, b, e, w_ref, k * blocks + b, s_ref, None)
            add_parts(row_ref, b * size, parts, table_entry(own_table, b, offset), False)
            add_parts(col_ref, b * size, parts, table_entry(peer_table, k, -offset), False)
    if last:
        lane = lax.broadcasted_iota(jnp.int32, (size, LANES), 1)
        for b in range(blocks):
            at = pl.ds(b * size, size)
            by_row = jnp.sum(row_ref[at, :], axis=-1, keepdims=True)
            by_col = jnp.sum(col_ref[at, :], axis=-1, keepdims=True)
            deg_ref[at, :] = jnp.where(lane < LANES // 2, by_row, by_col)


def scale_kernel(own_ref, other_ref, seed_ref, scaled_ref, rs_ref, cs_ref):
    total = lax.rsqrt(own_ref[...] + other_ref[...])
    by_col = jnp.broadcast_to(total[:, LANES // 2 : LANES // 2 + 1], total.shape)
    rs_ref[...] = jnp.broadcast_to(total[:, 0:1] * ALPHA, total.shape)
    cs_ref[...] = by_col
    scaled_ref[...] = (seed_ref[...] * by_col).astype(BF16)


def product_kernel(blocks, distance, pack_ref, w_ref, scaled_ref, *rest):
    out_ref = rest[-1]
    mols = scaled_ref.shape[0]
    size = mols // blocks
    table = pack_ref[pl.ds(mols, TAIL), :].astype(F32)
    c = lax.axis_index("col")
    for b in range(blocks):
        at = pl.ds(b * size, size)
        if distance == 0:
            s = scaled_ref[pl.ds(pl.multiple_of(c * size, size), size), :].astype(F32)
            s = (s * table_entry(table, b, c - b)).astype(BF16)
            out_ref[at, :] = jnp.dot(w_ref[b], s, preferred_element_type=F32)
            continue
        total = rest[0][at, :]
        for k in range(blocks):
            offset = peer_sign(distance) * (distance * blocks) + (k - b)
            s = scaled_ref[pl.ds(k * size, size), :].astype(F32)
            s = (s * table_entry(table, b, offset)).astype(BF16)
            total = total + jnp.dot(w_ref[k * blocks + b], s, preferred_element_type=F32)
        out_ref[at, :] = total


def state_kernel(own_ref, other_ref, rs_ref, seed_ref, cs_ref, out_ref):
    state = (own_ref[...] + other_ref[...]) * rs_ref[...] + (1.0 - ALPHA) * seed_ref[...]
    out_ref[...] = (state * cs_ref[...]).astype(BF16)


def kernel_call(body, name, ins, outs, flops, scratch=(), in_specs=None):
    return pl.pallas_call(
        body,
        out_shape=outs,
        in_specs=in_specs or [VMEM] * len(ins),
        out_specs=jax.tree.map(lambda _: VMEM, outs),
        scratch_shapes=scratch,
        compiler_params=PARAMS,
        cost_estimate=pl.CostEstimate(flops=flops, bytes_accessed=1 << 20, transcendentals=0),
        name=name,
    )(*ins)


def shards(embeddings, profiles, seed_mask, tile_cols, tile_count):
    rows, cols = lax.axis_size("row"), lax.axis_size("col")
    blocks, slots = tile_cols.shape
    mols, width = embeddings.shape
    prof = profiles.shape[1]
    size = mols // blocks
    reach = (BAND + blocks - 1) // blocks
    assert blocks == 2 and cols == 2 and width == LANES and prof == LANES
    f32_rows = jax.ShapeDtypeStruct((mols, LANES), F32)
    bf16_rows = jax.ShapeDtypeStruct((mols, LANES), BF16)
    tile_flops = 4 * size * size * width

    def from_peers(value):
        return [lax.ppermute(value, ("row", "col"), peer_pairs(rows, cols, d)) for d in range(1, reach + 1)]

    def other_core(value):
        return lax.ppermute(value, "col", [(0, 1), (1, 0)])

    def weights_of(tiles):
        return jax.ShapeDtypeStruct((tiles, size, size), BF16)

    held = [pltpu.with_memory_space_constraint(t, pltpu.HBM) for t in (embeddings, tile_cols, tile_count)]
    pack = kernel_call(
        lambda *refs: pack_kernel(blocks, slots, *refs),
        "pack",
        held,
        jax.ShapeDtypeStruct((mols + TAIL, LANES), BF16),
        1,
        [
            pltpu.SMEM(tile_cols.shape, jnp.int32),
            pltpu.SMEM(tile_count.shape, jnp.int32),
            pltpu.SemaphoreType.DMA((3,)),
        ],
        [HBM] * 3,
    )
    peer_packs = from_peers(pack)
    seed_rows = jnp.where(seed_mask[:, None] > 0, profiles, 0.0)
    one_tile = pltpu.VMEM((size, size), F32)
    hl, own_weights, row_sum, col_sum = kernel_call(
        lambda *refs: own_weights_kernel(blocks, *refs),
        "own_weights",
        [pack],
        (jax.ShapeDtypeStruct((mols, 2 * width), BF16), weights_of(blocks), f32_rows, f32_rows),
        blocks * tile_flops,
        [one_tile],
    )
    weights = [own_weights]
    for d in range(1, reach + 1):
        last = d == reach
        ins = [pack, peer_packs[d - 1], hl, row_sum, col_sum]
        out = kernel_call(
            lambda *refs, d=d, last=last: peer_weights_kernel((blocks, rows, last), d, *refs),
            "peer_weights",
            ins,
            (weights_of(blocks * blocks), f32_rows) if last else (weights_of(blocks * blocks), f32_rows, f32_rows),
            blocks * blocks * tile_flops,
            [pltpu.VMEM((mols, LANES), F32)] * 2 + [one_tile] if last else [one_tile],
        )
        weights.append(out[0])
        if last:
            degree = out[1]
        else:
            row_sum, col_sum = out[1:]
    scaled, row_scale, col_scale = kernel_call(
        scale_kernel, "scale", [degree, other_core(degree), seed_rows], (bf16_rows, f32_rows, f32_rows), 1
    )
    for iteration in range(ITERS):
        peers = from_peers(scaled)
        partial = kernel_call(
            lambda *refs: product_kernel(blocks, 0, *refs),
            "own_product",
            [pack, weights[0], scaled],
            f32_rows,
            blocks * tile_flops,
        )
        for d in range(1, reach + 1):
            partial = kernel_call(
                lambda *refs, d=d: product_kernel(blocks, d, *refs),
                "peer_product",
                [pack, weights[d], peers[d - 1], partial],
                f32_rows,
                blocks * blocks * tile_flops,
            )
        other = other_core(partial)
        if iteration + 1 < ITERS:
            scaled = kernel_call(
                state_kernel, "state", [partial, other, row_scale, seed_rows, col_scale], bf16_rows, 1
            )
    return (partial + other) * row_scale + (1.0 - ALPHA) * seed_rows


def solution(mesh):
    placed = (
        P(("grp", "row"), None),
        P(("grp", "row"), None),
        P(("grp", "row")),
        P(("grp", "row"), None),
        P(("grp", "row")),
    )
    return jax.shard_map(
        shards, mesh=mesh, in_specs=placed, out_specs=P(("grp", "row"), None), check_vma=False
    )
```

time: 606 us -> 63.9 us (0.11)
  waiting for transfers between devices: 165 us -> 30.3 us
  local copies, waits for them, and re-layouts: 127 us -> 0.01 us
  loops' own time: 124 us -> 0 us
  starting transfers between devices: 104 us -> 20.5 us
  other arithmetic: 39.3 us -> 1.25 us
  matrix products: 26.8 us -> 0 us
  between operations: 14 us -> 0.18 us
  Pallas kernels: 0 us -> 11.6 us
    another operation x81 -> x0, loops' own time: 124 us -> none  [the longest x2 72 us: shards(): partial_sum = lax.fori_loop(0, flat_total, product_step, start_total)]
    psum x2 -> x0, waiting for transfers between devices: 117 us -> none  [shards(): product = lax.psum(partial_sum, 'col')]
    dynamic_slice x186 -> x0, local copies, waits for them, and re-layouts: 112 us -> none  [the longest x78 51.3 us: slot_state(): slot_taken[slot_index]]
    ppermute x24 -> x12, starting transfers between devices: 104 us -> 20.5 us  [the longest x9 11.7 us: from_peers(): lax.ppermute(value, ('row', 'col'), peer_pairs(rows, cols, d))]
    another operation x30 -> x0, other arithmetic: 32.9 us -> none
    dot_general x18 -> x0, matrix products: 26.8 us -> none  [the longest x12 22.9 us: product_add_tile(): jnp.dot(tile_store[flat_index], window_scaled[col_block - window_start],...]
    ppermute x24 -> x12, waiting for transfers between devices: 47.5 us -> 30.3 us  [the longest x9 25.9 us: from_peers(): lax.ppermute(value, ('row', 'col'), peer_pairs(rows, cols, d))]
    pallas_call x0 -> x15, Pallas kernels: none -> 11.6 us  [kernel_call(): pl.pallas_call(body, out_shape=outs, in_specs=in_specs or [VMEM] * len(in...]
  transfers between devices with their start and end apart: 26 -> 12, of which waited for: 14 -> 6; matrix products, arithmetic and copies ran while one was open for 0% -> 0% of each run, Pallas kernels for 0% -> 11%
where the time goes in v3:
time: 63.9 us; the launch traced here: 63.8 us
  waiting for transfers between devices  30.3 us (47%)
  starting transfers between devices  20.5 us (32%)
  Pallas kernels  11.6 us (18%)
  other arithmetic  1.25 us (2%)
    ppermute x9, waiting for transfers between devices, from_peers(): lax.ppermute(value, ('row', 'col'), peer_pairs(rows, cols, d))  25.9 us
    ppermute x9, starting transfers between devices, from_peers(): lax.ppermute(value, ('row', 'col'), peer_pairs(rows, cols, d))  11.7 us
    pallas_call x15, Pallas kernels, kernel_call(): pl.pallas_call(body, out_shape=outs, in_specs=in_specs or [VMEM] * len(in...  11.6 us
    ppermute x3, starting transfers between devices, other_core(): return lax.ppermute(value, 'col', [(0, 1), (1, 0)])  8.74 us
    ppermute x3, waiting for transfers between devices, other_core(): return lax.ppermute(value, 'col', [(0, 1), (1, 0)])  4.39 us
  transfers between devices with their start and end apart: 12, of which 6 were waited for; matrix products, arithmetic and copies ran while one was open for 0% of the time, Pallas kernels for 11%

profile of v3, /device:TPU:0, one launch (start us, length us, event | category | flops | bytes accessed | tf_op | source)
XLA Modules:
  0.0 63.8 jit_solution(4945601789662054671)
XLA Ops:
  0.0 1.0 %pack.1.refs_0_ = bf16[1040,128]{1,0:T(8,128)(2,1)S(1)} custom-call(bf16[1024,128]{1,0:T(8,128)(2,1)} %refs_0_.1, s32[2,13]{1,0:T(2,128)} %refs_1_.1, s32[2]{0:T(128)} %refs_2_.1), custom_call_target="tpu_custom_call" | custom-call | flops 1 | bytes 1048576 | tf_op jit(solution)/shard_map/pack/pallas_call | solution.py:196
  1.0 3.0 %collective-permute-start.2 = (bf16[1040,128]{1,0:T(8,128)(2,1)S(1)}, bf16[1040,128]{1,0:T(8,128)(2,1)S(1)}, u32[]{:S(2)}, u32[]{:S(2)}) collective-permute-start(bf16[1040,128]{1,0:T(8,128)(2,1)S(1)} %pack.1.refs_0_), channel_id=1, source_target_pairs={{0,2},{2,0},{3,5},{5,3},{4,6},{6,4},{7,9},{9,7},{8,10},{10,8},{11,... | collective-permute-start | bytes 798728 | tf_op jit(solution)/shard_map/ppermute | solution.py:221
  4.0 1.6 %collective-permute-start.1 = (bf16[1040,128]{1,0:T(8,128)(2,1)S(1)}, bf16[1040,128]{1,0:T(8,128)(2,1)S(1)}, u32[]{:S(2)}, u32[]{:S(2)}) collective-permute-start(bf16[1040,128]{1,0:T(8,128)(2,1)S(1)} %pack.1.refs_0_), channel_id=1, source_target_pairs={{0,4},{4,0},{2,6},{6,2},{5,9},{9,5},{7,11},{11,7},{8,12},{12,8},{1... | collective-permute-start | bytes 798728 | tf_op jit(solution)/shard_map/ppermute | solution.py:221
  6.4 8.5 %collective-permute-done.2.refs_1_ = bf16[1040,128]{1,0:T(8,128)(2,1)S(1)} collective-permute-done((bf16[1040,128]{1,0:T(8,128)(2,1)S(1)}, bf16[1040,128]{1,0:T(8,128)(2,1)S(1)}, u32[]{:S(2)}, u32[]{:S(2)}) %collective-permute-start.2) | collective-permute-done | bytes 266272 | tf_op jit(solution)/shard_map/ppermute | solution.py:221
  14.9 1.1 %peer_weights.3 = (bf16[4,512,512]{2,1,0:T(8,128)(2,1)S(1)}, f32[1024,128]{1,0:T(8,128)S(1)}, f32[1024,128]{1,0:T(8,128)S(1)}) custom-call(bf16[1040,128]{1,0:T(8,128)(2,1)S(1)} %pack.1.refs_0_, bf16[1040,128]{1,0:T(8,128)(2,1)S(1)} %collective-permute-done.2.refs_1_, bf16[1024,256]{1,0:T(8,128)(2,1)S(1)} %get-tuple-element.20.refs_2_, ...), custom_call_target="tpu_custom_call" | custom-call | flops 536870912 | bytes 1048576 | tf_op jit(solution)/shard_map/peer_weights/pallas_call | solution.py:196
  16.1 1.1 %peer_weights.4 = (bf16[4,512,512]{2,1,0:T(8,128)(2,1)S(1)}, f32[1024,128]{1,0:T(8,128)S(1)}, f32[1024,128]{1,0:T(8,128)S(1)}) custom-call(bf16[1040,128]{1,0:T(8,128)(2,1)S(1)} %pack.1.refs_0_, bf16[1040,128]{1,0:T(8,128)(2,1)S(1)} %collective-permute-done.1.refs_1_, bf16[1024,256]{1,0:T(8,128)(2,1)S(1)} %get-tuple-element.20.refs_2_, ...), custom_call_target="tpu_custom_call" | custom-call | flops 536870912 | bytes 1048576 | tf_op jit(solution)/shard_map/peer_weights/pallas_call | solution.py:196
  17.2 1.2 %peer_weights.5 = (bf16[4,512,512]{2,1,0:T(8,128)(2,1)S(1)}, f32[1024,128]{1,0:T(8,128)S(1)}) custom-call(bf16[1040,128]{1,0:T(8,128)(2,1)S(1)} %pack.1.refs_0_, bf16[1040,128]{1,0:T(8,128)(2,1)S(1)} %collective-permute-done.refs_1_, bf16[1024,256]{1,0:T(8,128)(2,1)S(1)} %get-tuple-element.20.refs_2_, f32[1024,128]{1,0:T(8,128)S(1)} %get-tuple-element.25.refs_3_, ...), custom_call_target="tpu_custom_call" | custom-call | flops 536870912 | bytes 1048576 | tf_op jit(solution)/shard_map/peer_weights/pallas_call | solution.py:196
  18.4 2.5 %collective-permute-start.3 = (f32[1024,128]{1,0:T(8,128)S(1)}, f32[1024,128]{1,0:T(8,128)S(1)}, u32[]{:S(2)}, u32[]{:S(2)}) collective-permute-start(f32[1024,128]{1,0:T(8,128)S(1)} %get-tuple-element.28.own_ref), channel_id=1, source_target_pairs={{0,1},{1,0},{2,3},{3,2},{4,5},{5,4},{6,7},{7,6},{8,9},{9,8},{10,11... | collective-permute-start | bytes 1572872 | tf_op jit(solution)/shard_map/ppermute | solution.py:224
  21.1 1.3 %collective-permute-done.3.other_ref = f32[1024,128]{1,0:T(8,128)S(1)} collective-permute-done((f32[1024,128]{1,0:T(8,128)S(1)}, f32[1024,128]{1,0:T(8,128)S(1)}, u32[]{:S(2)}, u32[]{:S(2)}) %collective-permute-start.3) | collective-permute-done | bytes 524320 | tf_op jit(solution)/shard_map/ppermute | solution.py:224
  22.8 1.9 %collective-permute-start.6 = (bf16[1024,128]{1,0:T(8,128)(2,1)S(1)}, bf16[1024,128]{1,0:T(8,128)(2,1)S(1)}, u32[]{:S(2)}, u32[]{:S(2)}) collective-permute-start(bf16[1024,128]{1,0:T(8,128)(2,1)S(1)} %get-tuple-element.29.refs_2_), channel_id=1, source_target_pairs={{0,2},{2,0},{3,5},{5,3},{4,6},{6,4},{7,9},{9,7},{8,10},{10,8},{11,... | collective-permute-start | bytes 786440 | tf_op jit(solution)/shard_map/ppermute | solution.py:221
  24.7 1.7 %collective-permute-start.4 = (bf16[1024,128]{1,0:T(8,128)(2,1)S(1)}, bf16[1024,128]{1,0:T(8,128)(2,1)S(1)}, u32[]{:S(2)}, u32[]{:S(2)}) collective-permute-start(bf16[1024,128]{1,0:T(8,128)(2,1)S(1)} %get-tuple-element.29.refs_2_), channel_id=1, source_target_pairs={{0,6},{6,0},{2,8},{8,2},{4,10},{10,4},{7,13},{13,7},{9,15},{15,9},... | collective-permute-start | bytes 786440 | tf_op jit(solution)/shard_map/ppermute | solution.py:221
  26.9 8.7 %collective-permute-done.6.refs_2_ = bf16[1024,128]{1,0:T(8,128)(2,1)S(1)} collective-permute-done((bf16[1024,128]{1,0:T(8,128)(2,1)S(1)}, bf16[1024,128]{1,0:T(8,128)(2,1)S(1)}, u32[]{:S(2)}, u32[]{:S(2)}) %collective-permute-start.6) | collective-permute-done | bytes 262176 | tf_op jit(solution)/shard_map/ppermute | solution.py:221
  36.4 0.8 %peer_product.7.refs_3_ = f32[1024,128]{1,0:T(8,128)S(1)} custom-call(bf16[1040,128]{1,0:T(8,128)(2,1)S(1)} %pack.1.refs_0_, bf16[4,512,512]{2,1,0:T(8,128)(2,1)S(1)} %get-tuple-element.30.refs_1_, bf16[1024,128]{1,0:T(8,128)(2,1)S(1)} %collective-permute-done.5.refs_2_, f32[1024,128]{1,0:T(8,128)S(1)} %peer_product.6.refs_3_), custom_call_target="tpu_custom_call" | custom-call | flops 536870912 | bytes 1048576 | tf_op jit(solution)/shard_map/peer_product/pallas_call | solution.py:196
  37.2 0.8 %peer_product.8.own_ref = f32[1024,128]{1,0:T(8,128)S(1)} custom-call(bf16[1040,128]{1,0:T(8,128)(2,1)S(1)} %pack.1.refs_0_, bf16[4,512,512]{2,1,0:T(8,128)(2,1)S(1)} %get-tuple-element.27.refs_1_, bf16[1024,128]{1,0:T(8,128)(2,1)S(1)} %collective-permute-done.4.refs_2_, f32[1024,128]{1,0:T(8,128)S(1)} %peer_product.7.refs_3_), custom_call_target="tpu_custom_call" | custom-call | flops 536870912 | bytes 1048576 | tf_op jit(solution)/shard_map/peer_product/pallas_call | solution.py:196
  38.0 3.2 %collective-permute-start.7 = (f32[1024,128]{1,0:T(8,128)S(1)}, f32[1024,128]{1,0:T(8,128)S(1)}, u32[]{:S(2)}, u32[]{:S(2)}) collective-permute-start(f32[1024,128]{1,0:T(8,128)S(1)} %peer_product.8.own_ref), channel_id=1, source_target_pairs={{0,1},{1,0},{2,3},{3,2},{4,5},{5,4},{6,7},{7,6},{8,9},{9,8},{10,11... | collective-permute-start | bytes 1572872 | tf_op jit(solution)/shard_map/ppermute | solution.py:224
  41.2 1.5 %collective-permute-done.7.other_ref = f32[1024,128]{1,0:T(8,128)S(1)} collective-permute-done((f32[1024,128]{1,0:T(8,128)S(1)}, f32[1024,128]{1,0:T(8,128)S(1)}, u32[]{:S(2)}, u32[]{:S(2)}) %collective-permute-start.7) | collective-permute-done | bytes 524320 | tf_op jit(solution)/shard_map/ppermute | solution.py:224
  42.9 1.8 %collective-permute-start.10 = (bf16[1024,128]{1,0:T(8,128)(2,1)S(1)}, bf16[1024,128]{1,0:T(8,128)(2,1)S(1)}, u32[]{:S(2)}, u32[]{:S(2)}) collective-permute-start(bf16[1024,128]{1,0:T(8,128)(2,1)S(1)} %state.1.refs_2_), channel_id=1, source_target_pairs={{0,2},{2,0},{3,5},{5,3},{4,6},{6,4},{7,9},{9,7},{8,10},{10,8},{11,... | collective-permute-start | bytes 786440 | tf_op jit(solution)/shard_map/ppermute | solution.py:221
  44.7 1.7 %collective-permute-start.8 = (bf16[1024,128]{1,0:T(8,128)(2,1)S(1)}, bf16[1024,128]{1,0:T(8,128)(2,1)S(1)}, u32[]{:S(2)}, u32[]{:S(2)}) collective-permute-start(bf16[1024,128]{1,0:T(8,128)(2,1)S(1)} %state.1.refs_2_), channel_id=1, source_target_pairs={{0,6},{6,0},{2,8},{8,2},{4,10},{10,4},{7,13},{13,7},{9,15},{15,9},... | collective-permute-start | bytes 786440 | tf_op jit(solution)/shard_map/ppermute | solution.py:221
  46.9 8.7 %collective-permute-done.10.refs_2_ = bf16[1024,128]{1,0:T(8,128)(2,1)S(1)} collective-permute-done((bf16[1024,128]{1,0:T(8,128)(2,1)S(1)}, bf16[1024,128]{1,0:T(8,128)(2,1)S(1)}, u32[]{:S(2)}, u32[]{:S(2)}) %collective-permute-start.10) | collective-permute-done | bytes 262176 | tf_op jit(solution)/shard_map/ppermute | solution.py:221
  56.5 0.8 %peer_product.10.refs_3_ = f32[1024,128]{1,0:T(8,128)S(1)} custom-call(bf16[1040,128]{1,0:T(8,128)(2,1)S(1)} %pack.1.refs_0_, bf16[4,512,512]{2,1,0:T(8,128)(2,1)S(1)} %get-tuple-element.30.refs_1_, bf16[1024,128]{1,0:T(8,128)(2,1)S(1)} %collective-permute-done.9.refs_2_, f32[1024,128]{1,0:T(8,128)S(1)} %peer_product.9.refs_3_), custom_call_target="tpu_custom_call" | custom-call | flops 536870912 | bytes 1048576 | tf_op jit(solution)/shard_map/peer_product/pallas_call | solution.py:196
  57.3 0.8 %peer_product.11 = f32[1024,128]{1,0:T(8,128)S(1)} custom-call(bf16[1040,128]{1,0:T(8,128)(2,1)S(1)} %pack.1.refs_0_, bf16[4,512,512]{2,1,0:T(8,128)(2,1)S(1)} %get-tuple-element.27.refs_1_, bf16[1024,128]{1,0:T(8,128)(2,1)S(1)} %collective-permute-done.8.refs_2_, f32[1024,128]{1,0:T(8,128)S(1)} %peer_product.10.refs_3_), custom_call_target="tpu_custom_call" | custom-call | flops 536870912 | bytes 1048576 | tf_op jit(solution)/shard_map/peer_product/pallas_call | solution.py:196
  58.1 3.1 %collective-permute-start.11 = (f32[1024,128]{1,0:T(8,128)S(1)}, f32[1024,128]{1,0:T(8,128)S(1)}, u32[]{:S(2)}, u32[]{:S(2)}) collective-permute-start(f32[1024,128]{1,0:T(8,128)S(1)} %peer_product.11), channel_id=1, source_target_pairs={{0,1},{1,0},{2,3},{3,2},{4,5},{5,4},{6,7},{7,6},{8,9},{9,8},{10,11... | collective-permute-start | bytes 1572872 | tf_op jit(solution)/shard_map/ppermute | solution.py:224
  61.2 1.5 %collective-permute-done.11 = f32[1024,128]{1,0:T(8,128)S(1)} collective-permute-done((f32[1024,128]{1,0:T(8,128)S(1)}, f32[1024,128]{1,0:T(8,128)S(1)}, u32[]{:S(2)}, u32[]{:S(2)}) %collective-permute-start.11) | collective-permute-done | bytes 524320 | tf_op jit(solution)/shard_map/ppermute | solution.py:224
  62.8 1.0 %multiply_add_fusion = f32[1024,128]{1,0:T(8,128)} fusion(f32[1024,128]{1,0:T(8,128)S(1)} %get-tuple-element.33.rs_ref, f32[1024,128]{1,0:T(8,128)S(1)} %peer_product.11, f32[1024,128]{1,0:T(8,128)S(1)} %collective-permute-done.11, f32[1024,128]{1,0:T(8,128)S(1)} %copy-done, pred[1024]{0:T(1024)(128)(4,1)S(1)} %broadcast_compare_fusion), kind=kLoop, calls=%fused_computation | loop fusion | flops 655360 | bytes 2622464 | tf_op jit(solution)/shard_map/add | solution.py:296
  (22 shorter events, 4.2 us)
Async XLA Ops:
  1.0 13.9 %collective-permute-start.2 = (bf16[1040,128]{1,0:T(8,128)(2,1)S(1)}, bf16[1040,128]{1,0:T(8,128)(2,1)S(1)}, u32[]{:S(2)}, u32[]{:S(2)}) collective-permute-start(bf16[1040,128]{1,0:T(8,128)(2,1)S(1)} %pack.1.refs_0_), channel_id=1, source_target_pairs={{0,2},{2,0},{3,5},{5,3},{4,6},{6,4},{7,9},{9,7},{8,10},{10,8},{11,... | collective-permute-start | bytes 798728 | tf_op jit(solution)/shard_map/ppermute | solution.py:221
  4.0 12.0 %collective-permute-start.1 = (bf16[1040,128]{1,0:T(8,128)(2,1)S(1)}, bf16[1040,128]{1,0:T(8,128)(2,1)S(1)}, u32[]{:S(2)}, u32[]{:S(2)}) collective-permute-start(bf16[1040,128]{1,0:T(8,128)(2,1)S(1)} %pack.1.refs_0_), channel_id=1, source_target_pairs={{0,4},{4,0},{2,6},{6,2},{5,9},{9,5},{7,11},{11,7},{8,12},{12,8},{1... | collective-permute-start | bytes 798728 | tf_op jit(solution)/shard_map/ppermute | solution.py:221
  5.6 11.6 %collective-permute-start = (bf16[1040,128]{1,0:T(8,128)(2,1)S(1)}, bf16[1040,128]{1,0:T(8,128)(2,1)S(1)}, u32[]{:S(2)}, u32[]{:S(2)}) collective-permute-start(bf16[1040,128]{1,0:T(8,128)(2,1)S(1)} %pack.1.refs_0_), channel_id=1, source_target_pairs={{0,6},{6,0},{2,8},{8,2},{4,10},{10,4},{7,13},{13,7},{9,15},{15,9},... | collective-permute-start | bytes 798728 | tf_op jit(solution)/shard_map/ppermute | solution.py:221
  16.1 4.8 %copy-start.1 = (s32[1024]{0:T(1024)S(1)}, s32[1024]{0:T(1024)}, u32[]{:S(2)}) copy-start(s32[1024]{0:T(1024)} %param.7) | copy-start | bytes 12292
  16.1 4.8 %copy-start = (f32[1024,128]{1,0:T(8,128)S(1)}, f32[1024,128]{1,0:T(8,128)}, u32[]{:S(2)}) copy-start(f32[1024,128]{1,0:T(8,128)} %param.6) | copy-start | bytes 1572868
  18.4 4.0 %collective-permute-start.3 = (f32[1024,128]{1,0:T(8,128)S(1)}, f32[1024,128]{1,0:T(8,128)S(1)}, u32[]{:S(2)}, u32[]{:S(2)}) collective-permute-start(f32[1024,128]{1,0:T(8,128)S(1)} %get-tuple-element.28.own_ref), channel_id=1, source_target_pairs={{0,1},{1,0},{2,3},{3,2},{4,5},{5,4},{6,7},{7,6},{8,9},{9,8},{10,11... | collective-permute-start | bytes 1572872 | tf_op jit(solution)/shard_map/ppermute | solution.py:224
  22.8 12.8 %collective-permute-start.6 = (bf16[1024,128]{1,0:T(8,128)(2,1)S(1)}, bf16[1024,128]{1,0:T(8,128)(2,1)S(1)}, u32[]{:S(2)}, u32[]{:S(2)}) collective-permute-start(bf16[1024,128]{1,0:T(8,128)(2,1)S(1)} %get-tuple-element.29.refs_2_), channel_id=1, source_target_pairs={{0,2},{2,0},{3,5},{5,3},{4,6},{6,4},{7,9},{9,7},{8,10},{10,8},{11,... | collective-permute-start | bytes 786440 | tf_op jit(solution)/shard_map/ppermute | solution.py:221
  24.7 11.7 %collective-permute-start.5 = (bf16[1024,128]{1,0:T(8,128)(2,1)S(1)}, bf16[1024,128]{1,0:T(8,128)(2,1)S(1)}, u32[]{:S(2)}, u32[]{:S(2)}) collective-permute-start(bf16[1024,128]{1,0:T(8,128)(2,1)S(1)} %get-tuple-element.29.refs_2_), channel_id=1, source_target_pairs={{0,4},{4,0},{2,6},{6,2},{5,9},{9,5},{7,11},{11,7},{8,12},{12,8},{1... | collective-permute-start | bytes 786440 | tf_op jit(solution)/shard_map/ppermute | solution.py:221
  24.7 12.5 %collective-permute-start.4 = (bf16[1024,128]{1,0:T(8,128)(2,1)S(1)}, bf16[1024,128]{1,0:T(8,128)(2,1)S(1)}, u32[]{:S(2)}, u32[]{:S(2)}) collective-permute-start(bf16[1024,128]{1,0:T(8,128)(2,1)S(1)} %get-tuple-element.29.refs_2_), channel_id=1, source_target_pairs={{0,6},{6,0},{2,8},{8,2},{4,10},{10,4},{7,13},{13,7},{9,15},{15,9},... | collective-permute-start | bytes 786440 | tf_op jit(solution)/shard_map/ppermute | solution.py:221
  38.0 4.7 %collective-permute-start.7 = (f32[1024,128]{1,0:T(8,128)S(1)}, f32[1024,128]{1,0:T(8,128)S(1)}, u32[]{:S(2)}, u32[]{:S(2)}) collective-permute-start(f32[1024,128]{1,0:T(8,128)S(1)} %peer_product.8.own_ref), channel_id=1, source_target_pairs={{0,1},{1,0},{2,3},{3,2},{4,5},{5,4},{6,7},{7,6},{8,9},{9,8},{10,11... | collective-permute-start | bytes 1572872 | tf_op jit(solution)/shard_map/ppermute | solution.py:224
  42.9 12.8 %collective-permute-start.10 = (bf16[1024,128]{1,0:T(8,128)(2,1)S(1)}, bf16[1024,128]{1,0:T(8,128)(2,1)S(1)}, u32[]{:S(2)}, u32[]{:S(2)}) collective-permute-start(bf16[1024,128]{1,0:T(8,128)(2,1)S(1)} %state.1.refs_2_), channel_id=1, source_target_pairs={{0,2},{2,0},{3,5},{5,3},{4,6},{6,4},{7,9},{9,7},{8,10},{10,8},{11,... | collective-permute-start | bytes 786440 | tf_op jit(solution)/shard_map/ppermute | solution.py:221
  44.7 11.7 %collective-permute-start.9 = (bf16[1024,128]{1,0:T(8,128)(2,1)S(1)}, bf16[1024,128]{1,0:T(8,128)(2,1)S(1)}, u32[]{:S(2)}, u32[]{:S(2)}) collective-permute-start(bf16[1024,128]{1,0:T(8,128)(2,1)S(1)} %state.1.refs_2_), channel_id=1, source_target_pairs={{0,4},{4,0},{2,6},{6,2},{5,9},{9,5},{7,11},{11,7},{8,12},{12,8},{1... | collective-permute-start | bytes 786440 | tf_op jit(solution)/shard_map/ppermute | solution.py:221
  44.7 12.6 %collective-permute-start.8 = (bf16[1024,128]{1,0:T(8,128)(2,1)S(1)}, bf16[1024,128]{1,0:T(8,128)(2,1)S(1)}, u32[]{:S(2)}, u32[]{:S(2)}) collective-permute-start(bf16[1024,128]{1,0:T(8,128)(2,1)S(1)} %state.1.refs_2_), channel_id=1, source_target_pairs={{0,6},{6,0},{2,8},{8,2},{4,10},{10,4},{7,13},{13,7},{9,15},{15,9},... | collective-permute-start | bytes 786440 | tf_op jit(solution)/shard_map/ppermute | solution.py:221
  58.1 4.7 %collective-permute-start.11 = (f32[1024,128]{1,0:T(8,128)S(1)}, f32[1024,128]{1,0:T(8,128)S(1)}, u32[]{:S(2)}, u32[]{:S(2)}) collective-permute-start(f32[1024,128]{1,0:T(8,128)S(1)} %peer_product.11), channel_id=1, source_target_pairs={{0,1},{1,0},{2,3},{3,2},{4,5},{5,4},{6,7},{7,6},{8,9},{9,8},{10,11... | collective-permute-start | bytes 1572872 | tf_op jit(solution)/shard_map/ppermute | solution.py:224

commit v4 on v3

--- a/solution.py
+++ b/solution.py
@@ -1,3 +1,5 @@
+import itertools
+
 import jax
 import jax.numpy as jnp
 from jax import lax
@@ -22,21 +24,90 @@
 PARAMS = pltpu.CompilerParams(vmem_limit_bytes=24 * 1024 * 1024)
 
 
-def peer_pairs(rows, cols, distance):
-    pairs = []
-    for low in range(rows - distance):
-        core = (low // distance) % cols
-        a, b = low * cols + core, (low + distance) * cols + core
-        pairs += [(a, b), (b, a)]
-    busy = {a for a, _ in pairs}
-    idle = [n for n in range(rows * cols) if n not in busy]
-    for a, b in zip(idle[::2], idle[1::2]):
-        pairs += [(a, b), (b, a)]
-    return pairs
-
-
-def peer_sign(distance):
-    return jnp.where(lax.rem(lax.div(lax.axis_index("row"), distance), 2) == lax.axis_index("col"), 1, -1)
+def search_steps(rows, reach):
+    if reach != 3 or rows < 8:
+        return None
+    edges = [(a, a + d) for a in range(rows) for d in range(1, reach + 1) if a + d < rows]
+
+    def solve(room):
+        chosen = []
+
+        def place(n):
+            done = edges[n][0] if n < len(edges) else rows
+            if any(room[chip][step] for chip in range(max(done - reach, 0), done) for step in range(reach)):
+                return False
+            if n == len(edges):
+                return True
+            a, b = edges[n]
+            for k in range(reach):
+                step = (b - a - 1 + k) % reach
+                if room[a][step] and room[b][step]:
+                    room[a][step] -= 1
+                    room[b][step] -= 1
+                    chosen.append(step)
+                    if place(n + 1):
+                        return True
+                    room[a][step] += 1
+                    room[b][step] += 1
+                    chosen.pop()
+            return False
+
+        return chosen if place(0) else None
+
+    best, best_moved = None, None
+    orders = list(itertools.permutations(range(reach)))
+    for low, near_low, high, near_high in itertools.product(orders, range(reach), orders, range(reach)):
+        room = [[2] * reach for _ in range(rows)]
+        for chip, way, order, near in ((0, 1, low, near_low), (rows - 1, -1, high, near_high)):
+            for k in range(reach):
+                room[chip][order[k]] = k
+            room[chip + way][near] = 0
+            room[chip + 2 * way][order[1]] = 1
+        chosen = solve(room)
+        if chosen is not None:
+            moved = sum(step != b - a - 1 for (a, b), step in zip(edges, chosen))
+            if best is None or moved < best_moved:
+                best, best_moved = chosen, moved
+    if best is None:
+        return None
+    return [[e for e, s in zip(edges, best) if s == step] for step in range(reach)]
+
+
+def swap_steps(rows, cols, reach):
+    chip_steps = search_steps(rows, reach)
+    if chip_steps is None:
+        chip_steps = [[(a, a + d) for a in range(rows - d)] for d in range(1, reach + 1)]
+    steps = []
+    for chip_pairs in chip_steps:
+        free = [list(range(cols)) for _ in range(rows)]
+        offsets = [[0] * rows for _ in range(cols)]
+        swaps = []
+        for a, b in chip_pairs:
+            core_a, core_b = free[a].pop(0), free[b].pop(0)
+            swaps.append((a * cols + core_a, b * cols + core_b))
+            offsets[core_a][a], offsets[core_b][b] = b - a, a - b
+        idle = []
+        for chip, cores in enumerate(free):
+            if len(cores) == 2:
+                swaps.append((chip * cols + cores[0], chip * cols + cores[1]))
+            else:
+                idle += [chip * cols + core for core in cores]
+        swaps += list(zip(idle[::2], idle[1::2]))
+        steps.append((swaps + [(b, a) for a, b in swaps], offsets))
+    return steps
+
+
+def peer_offset(offsets):
+    r, c = lax.axis_index("row"), lax.axis_index("col")
+    value = jnp.int32(0)
+    for core, per_row in enumerate(offsets):
+        for word, first in enumerate(range(0, len(per_row), 8)):
+            code = sum((offset + 8) << (4 * n) for n, offset in enumerate(per_row[first : first + 8]))
+            code = jnp.int32(code - (1 << 32) if code >= 1 << 31 else code)
+            digit = (lax.shift_right_logical(code, 4 * lax.rem(r, 8)) & 15) - 8
+            here = jnp.logical_and(c == core, lax.div(r, 8) == word)
+            value = jnp.where(here, digit, value)
+    return value
 
 
 def table_entry(table, row, offset):
@@ -126,25 +197,24 @@
         add_parts(col_ref, b * size, parts, from_c, True)
 
 
-def peer_weights_kernel(dims, distance, pack_ref, peer_ref, hl, row_in, col_in, w_ref, *rest):
-    blocks, rows, last = dims
+def peer_weights_kernel(dims, offsets, pack_ref, peer_ref, hl, row_in, col_in, w_ref, *rest):
+    blocks, last = dims
     if last:
         deg_ref, row_ref, col_ref, s_ref = rest
     else:
         row_ref, col_ref, s_ref = rest
     mols = hl.shape[0]
     size = mols // blocks
-    sign = peer_sign(distance)
-    peer = lax.axis_index("row") + sign * distance
-    valid = jnp.where(jnp.logical_and(peer >= 0, peer < rows), 1.0, 0.0)
-    own_table = pack_ref[pl.ds(mols, TAIL), :].astype(F32)
+    chips = peer_offset(offsets)
+    valid = jnp.where(chips != 0, 1.0, 0.0)
+    own_table = pack_ref[pl.ds(mols, TAIL), :].astype(F32) * valid
     peer_table = peer_ref[pl.ds(mols, TAIL), :].astype(F32) * valid
     row_ref[...] = row_in[...]
     col_ref[...] = col_in[...]
     for k in range(blocks):
         e = peer_ref[pl.ds(k * size, size), :]
         for b in range(blocks):
-            offset = sign * (distance * blocks) + (k - b)
+            offset = chips * blocks + (k - b)
             parts = tile_weights(hl, b, e, w_ref, k * blocks + b, s_ref, None)
             add_parts(row_ref, b * size, parts, table_entry(own_table, b, offset), False)
             add_parts(col_ref, b * size, parts, table_entry(peer_table, k, -offset), False)
@@ -165,22 +235,25 @@
     scaled_ref[...] = (seed_ref[...] * by_col).astype(BF16)
 
 
-def product_kernel(blocks, distance, pack_ref, w_ref, scaled_ref, *rest):
+def product_kernel(blocks, offsets, pack_ref, w_ref, scaled_ref, *rest):
     out_ref = rest[-1]
     mols = scaled_ref.shape[0]
     size = mols // blocks
     table = pack_ref[pl.ds(mols, TAIL), :].astype(F32)
     c = lax.axis_index("col")
+    if offsets is not None:
+        chips = peer_offset(offsets)
+        table = table * jnp.where(chips != 0, 1.0, 0.0)
     for b in range(blocks):
         at = pl.ds(b * size, size)
-        if distance == 0:
+        if offsets is None:
             s = scaled_ref[pl.ds(pl.multiple_of(c * size, size), size), :].astype(F32)
             s = (s * table_entry(table, b, c - b)).astype(BF16)
             out_ref[at, :] = jnp.dot(w_ref[b], s, preferred_element_type=F32)
             continue
         total = rest[0][at, :]
         for k in range(blocks):
-            offset = peer_sign(distance) * (distance * blocks) + (k - b)
+            offset = chips * blocks + (k - b)
             s = scaled_ref[pl.ds(k * size, size), :].astype(F32)
             s = (s * table_entry(table, b, offset)).astype(BF16)
             total = total + jnp.dot(w_ref[k * blocks + b], s, preferred_element_type=F32)
@@ -213,12 +286,15 @@
     size = mols // blocks
     reach = (BAND + blocks - 1) // blocks
     assert blocks == 2 and cols == 2 and width == LANES and prof == LANES
+    steps = swap_steps(rows, cols, reach)
+    if len(steps) == 3:
+        steps = [steps[1], steps[0], steps[2]]
     f32_rows = jax.ShapeDtypeStruct((mols, LANES), F32)
     bf16_rows = jax.ShapeDtypeStruct((mols, LANES), BF16)
     tile_flops = 4 * size * size * width
 
     def from_peers(value):
-        return [lax.ppermute(value, ("row", "col"), peer_pairs(rows, cols, d)) for d in range(1, reach + 1)]
+        return [lax.ppermute(value, ("row", "col"), swaps) for swaps, _ in steps]
 
     def other_core(value):
         return lax.ppermute(value, "col", [(0, 1), (1, 0)])
@@ -252,11 +328,11 @@
         [one_tile],
     )
     weights = [own_weights]
-    for d in range(1, reach + 1):
-        last = d == reach
-        ins = [pack, peer_packs[d - 1], hl, row_sum, col_sum]
+    for step, (_, offsets) in enumerate(steps):
+        last = step + 1 == len(steps)
+        ins = [pack, peer_packs[step], hl, row_sum, col_sum]
         out = kernel_call(
-            lambda *refs, d=d, last=last: peer_weights_kernel((blocks, rows, last), d, *refs),
+            lambda *refs, offsets=offsets, last=last: peer_weights_kernel((blocks, last), offsets, *refs),
             "peer_weights",
             ins,
             (weights_of(blocks * blocks), f32_rows) if last else (weights_of(blocks * blocks), f32_rows, f32_rows),
@@ -274,17 +350,17 @@
     for iteration in range(ITERS):
         peers = from_peers(scaled)
         partial = kernel_call(
-            lambda *refs: product_kernel(blocks, 0, *refs),
+            lambda *refs: product_kernel(blocks, None, *refs),
             "own_product",
             [pack, weights[0], scaled],
             f32_rows,
             blocks * tile_flops,
         )
-        for d in range(1, reach + 1):
+        for step, (_, offsets) in enumerate(steps):
             partial = kernel_call(
-                lambda *refs, d=d: product_kernel(blocks, d, *refs),
+                lambda *refs, offsets=offsets: product_kernel(blocks, offsets, *refs),
                 "peer_product",
-                [pack, weights[d], peers[d - 1], partial],
+                [pack, weights[1 + step], peers[step], partial],
                 f32_rows,
                 blocks * blocks * tile_flops,
             )

time: 63.9 us -> 59.4 us (0.930)
  the two profiles are of different devices: /device:TPU:0 before, /device:TPU:17 now
where the time goes in v4:
time: 59.4 us; the launch traced here: 59.2 us
  waiting for transfers between devices  35 us (59%)
  Pallas kernels  11.6 us (20%)
  starting transfers between devices  11.2 us (19%)
  other arithmetic  1.25 us (2%)
    ppermute x9, waiting for transfers between devices, from_peers(): return [lax.ppermute(value, ('row', 'col'), swaps) for swaps, _ in steps]  30.2 us
    pallas_call x15, Pallas kernels, kernel_call(): pl.pallas_call(body, out_shape=outs, in_specs=in_specs or [VMEM] * len(in...  11.6 us
    ppermute x3, starting transfers between devices, other_core(): return lax.ppermute(value, 'col', [(0, 1), (1, 0)])  6.2 us
    ppermute x9, starting transfers between devices, from_peers(): return [lax.ppermute(value, ('row', 'col'), swaps) for swaps, _ in steps]  5.02 us
    ppermute x3, waiting for transfers between devices, other_core(): return lax.ppermute(value, 'col', [(0, 1), (1, 0)])  4.75 us
  transfers between devices with their start and end apart: 12, of which 10 were waited for; matrix products, arithmetic and copies ran while one was open for 0% of the time, Pallas kernels for 12%

profile of v4, /device:TPU:17, one launch (start us, length us, event | category | flops | bytes accessed | tf_op | source)
XLA Modules:
  0.0 59.2 jit_solution(12277601480517753205)
XLA Ops:
  0.0 1.0 %pack.1.refs_0_ = bf16[1040,128]{1,0:T(8,128)(2,1)S(1)} custom-call(bf16[1024,128]{1,0:T(8,128)(2,1)} %refs_0_.1, s32[2,13]{1,0:T(2,128)} %refs_1_.1, s32[2]{0:T(128)} %refs_2_.1), custom_call_target="tpu_custom_call" | custom-call | flops 1 | bytes 1048576 | tf_op jit(solution)/shard_map/pack/pallas_call | solution.py:269
  1.0 1.9 %collective-permute-start.2 = (bf16[1040,128]{1,0:T(8,128)(2,1)S(1)}, bf16[1040,128]{1,0:T(8,128)(2,1)S(1)}, u32[]{:S(2)}, u32[]{:S(2)}) collective-permute-start(bf16[1040,128]{1,0:T(8,128)(2,1)S(1)} %pack.1.refs_0_), channel_id=1, source_target_pairs={{0,2},{1,4},{3,6},{5,8},{7,10},{9,12},{11,14},{13,15},{2,0},{4,1},... | collective-permute-start | bytes 798728 | tf_op jit(solution)/shard_map/ppermute | solution.py:297
  2.9 1.1 %collective-permute-start = (bf16[1040,128]{1,0:T(8,128)(2,1)S(1)}, bf16[1040,128]{1,0:T(8,128)(2,1)S(1)}, u32[]{:S(2)}, u32[]{:S(2)}) collective-permute-start(bf16[1040,128]{1,0:T(8,128)(2,1)S(1)} %pack.1.refs_0_), channel_id=1, source_target_pairs={{0,6},{4,10},{7,8},{9,14},{2,3},{12,13},{1,5},{11,15},{6,0},{10,4}... | collective-permute-start | bytes 798728 | tf_op jit(solution)/shard_map/ppermute | solution.py:297
  4.0 0.8 %own_weights.1 = (bf16[1024,256]{1,0:T(8,128)(2,1)S(1)}, bf16[2,512,512]{2,1,0:T(8,128)(2,1)S(1)}, f32[1024,128]{1,0:T(8,128)S(1)}, f32[1024,128]{1,0:T(8,128)S(1)}) custom-call(bf16[1040,128]{1,0:T(8,128)(2,1)S(1)} %pack.1.refs_0_), custom_call_target="tpu_custom_call" | custom-call | flops 268435456 | bytes 1048576 | tf_op jit(solution)/shard_map/own_weights/pallas_call | solution.py:269
  4.8 2.9 %collective-permute-done.2.refs_1_ = bf16[1040,128]{1,0:T(8,128)(2,1)S(1)} collective-permute-done((bf16[1040,128]{1,0:T(8,128)(2,1)S(1)}, bf16[1040,128]{1,0:T(8,128)(2,1)S(1)}, u32[]{:S(2)}, u32[]{:S(2)}) %collective-permute-start.2) | collective-permute-done | bytes 266272 | tf_op jit(solution)/shard_map/ppermute | solution.py:297
  7.7 1.1 %peer_weights.3 = (bf16[4,512,512]{2,1,0:T(8,128)(2,1)S(1)}, f32[1024,128]{1,0:T(8,128)S(1)}, f32[1024,128]{1,0:T(8,128)S(1)}) custom-call(bf16[1040,128]{1,0:T(8,128)(2,1)S(1)} %pack.1.refs_0_, bf16[1040,128]{1,0:T(8,128)(2,1)S(1)} %collective-permute-done.2.refs_1_, bf16[1024,256]{1,0:T(8,128)(2,1)S(1)} %get-tuple-element.20.refs_2_, ...), custom_call_target="tpu_custom_call" | custom-call | flops 536870912 | bytes 1048576 | tf_op jit(solution)/shard_map/peer_weights/pallas_call | solution.py:269
  8.9 1.1 %peer_weights.4 = (bf16[4,512,512]{2,1,0:T(8,128)(2,1)S(1)}, f32[1024,128]{1,0:T(8,128)S(1)}, f32[1024,128]{1,0:T(8,128)S(1)}) custom-call(bf16[1040,128]{1,0:T(8,128)(2,1)S(1)} %pack.1.refs_0_, bf16[1040,128]{1,0:T(8,128)(2,1)S(1)} %collective-permute-done.1.refs_1_, bf16[1024,256]{1,0:T(8,128)(2,1)S(1)} %get-tuple-element.20.refs_2_, ...), custom_call_target="tpu_custom_call" | custom-call | flops 536870912 | bytes 1048576 | tf_op jit(solution)/shard_map/peer_weights/pallas_call | solution.py:269
  10.0 5.3 %collective-permute-done.refs_1_ = bf16[1040,128]{1,0:T(8,128)(2,1)S(1)} collective-permute-done((bf16[1040,128]{1,0:T(8,128)(2,1)S(1)}, bf16[1040,128]{1,0:T(8,128)(2,1)S(1)}, u32[]{:S(2)}, u32[]{:S(2)}) %collective-permute-start) | collective-permute-done | bytes 266272 | tf_op jit(solution)/shard_map/ppermute | solution.py:297
  15.3 1.2 %peer_weights.5 = (bf16[4,512,512]{2,1,0:T(8,128)(2,1)S(1)}, f32[1024,128]{1,0:T(8,128)S(1)}) custom-call(bf16[1040,128]{1,0:T(8,128)(2,1)S(1)} %pack.1.refs_0_, bf16[1040,128]{1,0:T(8,128)(2,1)S(1)} %collective-permute-done.refs_1_, bf16[1024,256]{1,0:T(8,128)(2,1)S(1)} %get-tuple-element.20.refs_2_, f32[1024,128]{1,0:T(8,128)S(1)} %get-tuple-element.25.refs_3_, ...), custom_call_target="tpu_custom_call" | custom-call | flops 536870912 | bytes 1048576 | tf_op jit(solution)/shard_map/peer_weights/pallas_call | solution.py:269
  16.5 3.5 %collective-permute-start.3 = (f32[1024,128]{1,0:T(8,128)S(1)}, f32[1024,128]{1,0:T(8,128)S(1)}, u32[]{:S(2)}, u32[]{:S(2)}) collective-permute-start(f32[1024,128]{1,0:T(8,128)S(1)} %get-tuple-element.28.own_ref), channel_id=1, source_target_pairs={{0,1},{1,0},{2,3},{3,2},{4,5},{5,4},{6,7},{7,6},{8,9},{9,8},{10,11... | collective-permute-start | bytes 1572872 | tf_op jit(solution)/shard_map/ppermute | solution.py:300
  20.3 1.3 %collective-permute-done.3.other_ref = f32[1024,128]{1,0:T(8,128)S(1)} collective-permute-done((f32[1024,128]{1,0:T(8,128)S(1)}, f32[1024,128]{1,0:T(8,128)S(1)}, u32[]{:S(2)}, u32[]{:S(2)}) %collective-permute-start.3) | collective-permute-done | bytes 524320 | tf_op jit(solution)/shard_map/ppermute | solution.py:300
  22.7 7.0 %collective-permute-done.6.refs_2_ = bf16[1024,128]{1,0:T(8,128)(2,1)S(1)} collective-permute-done((bf16[1024,128]{1,0:T(8,128)(2,1)S(1)}, bf16[1024,128]{1,0:T(8,128)(2,1)S(1)}, u32[]{:S(2)}, u32[]{:S(2)}) %collective-permute-start.6) | collective-permute-done | bytes 262176 | tf_op jit(solution)/shard_map/ppermute | solution.py:297
  29.7 0.8 %peer_product.6.refs_3_ = f32[1024,128]{1,0:T(8,128)S(1)} custom-call(bf16[1040,128]{1,0:T(8,128)(2,1)S(1)} %pack.1.refs_0_, bf16[4,512,512]{2,1,0:T(8,128)(2,1)S(1)} %get-tuple-element.31.refs_1_, bf16[1024,128]{1,0:T(8,128)(2,1)S(1)} %collective-permute-done.6.refs_2_, f32[1024,128]{1,0:T(8,128)S(1)} %own_product.2.refs_3_), custom_call_target="tpu_custom_call" | custom-call | flops 536870912 | bytes 1048576 | tf_op jit(solution)/shard_map/peer_product/pallas_call | solution.py:269
  30.5 5.8 %collective-permute-done.5.refs_2_ = bf16[1024,128]{1,0:T(8,128)(2,1)S(1)} collective-permute-done((bf16[1024,128]{1,0:T(8,128)(2,1)S(1)}, bf16[1024,128]{1,0:T(8,128)(2,1)S(1)}, u32[]{:S(2)}, u32[]{:S(2)}) %collective-permute-start.5) | collective-permute-done | bytes 262176 | tf_op jit(solution)/shard_map/ppermute | solution.py:297
  37.1 0.8 %peer_product.8.own_ref = f32[1024,128]{1,0:T(8,128)S(1)} custom-call(bf16[1040,128]{1,0:T(8,128)(2,1)S(1)} %pack.1.refs_0_, bf16[4,512,512]{2,1,0:T(8,128)(2,1)S(1)} %get-tuple-element.27.refs_1_, bf16[1024,128]{1,0:T(8,128)(2,1)S(1)} %collective-permute-done.4.refs_2_, f32[1024,128]{1,0:T(8,128)S(1)} %peer_product.7.refs_3_), custom_call_target="tpu_custom_call" | custom-call | flops 536870912 | bytes 1048576 | tf_op jit(solution)/shard_map/peer_product/pallas_call | solution.py:269
  38.0 1.9 %collective-permute-done.7.other_ref = f32[1024,128]{1,0:T(8,128)S(1)} collective-permute-done((f32[1024,128]{1,0:T(8,128)S(1)}, f32[1024,128]{1,0:T(8,128)S(1)}, u32[]{:S(2)}, u32[]{:S(2)}) %collective-permute-start.7) | collective-permute-done | bytes 524320 | tf_op jit(solution)/shard_map/ppermute | solution.py:300
  40.2 1.7 %collective-permute-start.9 = (bf16[1024,128]{1,0:T(8,128)(2,1)S(1)}, bf16[1024,128]{1,0:T(8,128)(2,1)S(1)}, u32[]{:S(2)}, u32[]{:S(2)}) collective-permute-start(bf16[1024,128]{1,0:T(8,128)(2,1)S(1)} %state.1.refs_2_), channel_id=1, source_target_pairs={{2,4},{3,8},{5,6},{7,12},{9,10},{11,13},{0,1},{14,15},{4,2},{8,3},... | collective-permute-start | bytes 786440 | tf_op jit(solution)/shard_map/ppermute | solution.py:297
  42.4 5.5 %collective-permute-done.10.refs_2_ = bf16[1024,128]{1,0:T(8,128)(2,1)S(1)} collective-permute-done((bf16[1024,128]{1,0:T(8,128)(2,1)S(1)}, bf16[1024,128]{1,0:T(8,128)(2,1)S(1)}, u32[]{:S(2)}, u32[]{:S(2)}) %collective-permute-start.10) | collective-permute-done | bytes 262176 | tf_op jit(solution)/shard_map/ppermute | solution.py:297
  48.7 1.0 %collective-permute-done.9.refs_2_ = bf16[1024,128]{1,0:T(8,128)(2,1)S(1)} collective-permute-done((bf16[1024,128]{1,0:T(8,128)(2,1)S(1)}, bf16[1024,128]{1,0:T(8,128)(2,1)S(1)}, u32[]{:S(2)}, u32[]{:S(2)}) %collective-permute-start.9) | collective-permute-done | bytes 262176 | tf_op jit(solution)/shard_map/ppermute | solution.py:297
  49.7 0.8 %peer_product.10.refs_3_ = f32[1024,128]{1,0:T(8,128)S(1)} custom-call(bf16[1040,128]{1,0:T(8,128)(2,1)S(1)} %pack.1.refs_0_, bf16[4,512,512]{2,1,0:T(8,128)(2,1)S(1)} %get-tuple-element.30.refs_1_, bf16[1024,128]{1,0:T(8,128)(2,1)S(1)} %collective-permute-done.9.refs_2_, f32[1024,128]{1,0:T(8,128)S(1)} %peer_product.9.refs_3_), custom_call_target="tpu_custom_call" | custom-call | flops 536870912 | bytes 1048576 | tf_op jit(solution)/shard_map/peer_product/pallas_call | solution.py:269
  50.5 2.7 %collective-permute-done.8.refs_2_ = bf16[1024,128]{1,0:T(8,128)(2,1)S(1)} collective-permute-done((bf16[1024,128]{1,0:T(8,128)(2,1)S(1)}, bf16[1024,128]{1,0:T(8,128)(2,1)S(1)}, u32[]{:S(2)}, u32[]{:S(2)}) %collective-permute-start.8) | collective-permute-done | bytes 262176 | tf_op jit(solution)/shard_map/ppermute | solution.py:297
  54.0 2.6 %collective-permute-start.11 = (f32[1024,128]{1,0:T(8,128)S(1)}, f32[1024,128]{1,0:T(8,128)S(1)}, u32[]{:S(2)}, u32[]{:S(2)}) collective-permute-start(f32[1024,128]{1,0:T(8,128)S(1)} %peer_product.11), channel_id=1, source_target_pairs={{0,1},{1,0},{2,3},{3,2},{4,5},{5,4},{6,7},{7,6},{8,9},{9,8},{10,11... | collective-permute-start | bytes 1572872 | tf_op jit(solution)/shard_map/ppermute | solution.py:300
  56.6 1.5 %collective-permute-done.11 = f32[1024,128]{1,0:T(8,128)S(1)} collective-permute-done((f32[1024,128]{1,0:T(8,128)S(1)}, f32[1024,128]{1,0:T(8,128)S(1)}, u32[]{:S(2)}, u32[]{:S(2)}) %collective-permute-start.11) | collective-permute-done | bytes 524320 | tf_op jit(solution)/shard_map/ppermute | solution.py:300
  58.2 1.0 %multiply_add_fusion = f32[1024,128]{1,0:T(8,128)} fusion(f32[1024,128]{1,0:T(8,128)S(1)} %get-tuple-element.33.rs_ref, f32[1024,128]{1,0:T(8,128)S(1)} %peer_product.11, f32[1024,128]{1,0:T(8,128)S(1)} %collective-permute-done.11, f32[1024,128]{1,0:T(8,128)S(1)} %copy-done, pred[1024]{0:T(1024)(128)(4,1)S(1)} %broadcast_compare_fusion), kind=kLoop, calls=%fused_computation | loop fusion | flops 655360 | bytes 2622464 | tf_op jit(solution)/shard_map/add | solution.py:372
  (22 shorter events, 4.5 us)
Async XLA Ops:
  1.0 6.7 %collective-permute-start.2 = (bf16[1040,128]{1,0:T(8,128)(2,1)S(1)}, bf16[1040,128]{1,0:T(8,128)(2,1)S(1)}, u32[]{:S(2)}, u32[]{:S(2)}) collective-permute-start(bf16[1040,128]{1,0:T(8,128)(2,1)S(1)} %pack.1.refs_0_), channel_id=1, source_target_pairs={{0,2},{1,4},{3,6},{5,8},{7,10},{9,12},{11,14},{13,15},{2,0},{4,1},... | collective-permute-start | bytes 798728 | tf_op jit(solution)/shard_map/ppermute | solution.py:297
  2.9 5.9 %collective-permute-start.1 = (bf16[1040,128]{1,0:T(8,128)(2,1)S(1)}, bf16[1040,128]{1,0:T(8,128)(2,1)S(1)}, u32[]{:S(2)}, u32[]{:S(2)}) collective-permute-start(bf16[1040,128]{1,0:T(8,128)(2,1)S(1)} %pack.1.refs_0_), channel_id=1, source_target_pairs={{2,4},{3,8},{5,6},{7,12},{9,10},{11,13},{0,1},{14,15},{4,2},{8,3},... | collective-permute-start | bytes 798728 | tf_op jit(solution)/shard_map/ppermute | solution.py:297
  2.9 12.4 %collective-permute-start = (bf16[1040,128]{1,0:T(8,128)(2,1)S(1)}, bf16[1040,128]{1,0:T(8,128)(2,1)S(1)}, u32[]{:S(2)}, u32[]{:S(2)}) collective-permute-start(bf16[1040,128]{1,0:T(8,128)(2,1)S(1)} %pack.1.refs_0_), channel_id=1, source_target_pairs={{0,6},{4,10},{7,8},{9,14},{2,3},{12,13},{1,5},{11,15},{6,0},{10,4}... | collective-permute-start | bytes 798728 | tf_op jit(solution)/shard_map/ppermute | solution.py:297
  8.8 11.2 %copy-start.1 = (s32[1024]{0:T(1024)S(1)}, s32[1024]{0:T(1024)}, u32[]{:S(2)}) copy-start(s32[1024]{0:T(1024)} %param.7) | copy-start | bytes 12292
  8.8 11.2 %copy-start = (f32[1024,128]{1,0:T(8,128)S(1)}, f32[1024,128]{1,0:T(8,128)}, u32[]{:S(2)}) copy-start(f32[1024,128]{1,0:T(8,128)} %param.6) | copy-start | bytes 1572868
  16.5 5.1 %collective-permute-start.3 = (f32[1024,128]{1,0:T(8,128)S(1)}, f32[1024,128]{1,0:T(8,128)S(1)}, u32[]{:S(2)}, u32[]{:S(2)}) collective-permute-start(f32[1024,128]{1,0:T(8,128)S(1)} %get-tuple-element.28.own_ref), channel_id=1, source_target_pairs={{0,1},{1,0},{2,3},{3,2},{4,5},{5,4},{6,7},{7,6},{8,9},{9,8},{10,11... | collective-permute-start | bytes 1572872 | tf_op jit(solution)/shard_map/ppermute | solution.py:300
  22.0 7.7 %collective-permute-start.6 = (bf16[1024,128]{1,0:T(8,128)(2,1)S(1)}, bf16[1024,128]{1,0:T(8,128)(2,1)S(1)}, u32[]{:S(2)}, u32[]{:S(2)}) collective-permute-start(bf16[1024,128]{1,0:T(8,128)(2,1)S(1)} %get-tuple-element.29.refs_2_), channel_id=1, source_target_pairs={{0,2},{1,4},{3,6},{5,8},{7,10},{9,12},{11,14},{13,15},{2,0},{4,1},... | collective-permute-start | bytes 786440 | tf_op jit(solution)/shard_map/ppermute | solution.py:297
  22.0 14.3 %collective-permute-start.5 = (bf16[1024,128]{1,0:T(8,128)(2,1)S(1)}, bf16[1024,128]{1,0:T(8,128)(2,1)S(1)}, u32[]{:S(2)}, u32[]{:S(2)}) collective-permute-start(bf16[1024,128]{1,0:T(8,128)(2,1)S(1)} %get-tuple-element.29.refs_2_), channel_id=1, source_target_pairs={{2,4},{3,8},{5,6},{7,12},{9,10},{11,13},{0,1},{14,15},{4,2},{8,3},... | collective-permute-start | bytes 786440 | tf_op jit(solution)/shard_map/ppermute | solution.py:297
  22.1 15.0 %collective-permute-start.4 = (bf16[1024,128]{1,0:T(8,128)(2,1)S(1)}, bf16[1024,128]{1,0:T(8,128)(2,1)S(1)}, u32[]{:S(2)}, u32[]{:S(2)}) collective-permute-start(bf16[1024,128]{1,0:T(8,128)(2,1)S(1)} %get-tuple-element.29.refs_2_), channel_id=1, source_target_pairs={{0,6},{4,10},{7,8},{9,14},{2,3},{12,13},{1,5},{11,15},{6,0},{10,4}... | collective-permute-start | bytes 786440 | tf_op jit(solution)/shard_map/ppermute | solution.py:297
  37.9 2.0 %collective-permute-start.7 = (f32[1024,128]{1,0:T(8,128)S(1)}, f32[1024,128]{1,0:T(8,128)S(1)}, u32[]{:S(2)}, u32[]{:S(2)}) collective-permute-start(f32[1024,128]{1,0:T(8,128)S(1)} %peer_product.8.own_ref), channel_id=1, source_target_pairs={{0,1},{1,0},{2,3},{3,2},{4,5},{5,4},{6,7},{7,6},{8,9},{9,8},{10,11... | collective-permute-start | bytes 1572872 | tf_op jit(solution)/shard_map/ppermute | solution.py:300
  40.1 7.8 %collective-permute-start.10 = (bf16[1024,128]{1,0:T(8,128)(2,1)S(1)}, bf16[1024,128]{1,0:T(8,128)(2,1)S(1)}, u32[]{:S(2)}, u32[]{:S(2)}) collective-permute-start(bf16[1024,128]{1,0:T(8,128)(2,1)S(1)} %state.1.refs_2_), channel_id=1, source_target_pairs={{0,2},{1,4},{3,6},{5,8},{7,10},{9,12},{11,14},{13,15},{2,0},{4,1},... | collective-permute-start | bytes 786440 | tf_op jit(solution)/shard_map/ppermute | solution.py:297
  40.2 9.5 %collective-permute-start.9 = (bf16[1024,128]{1,0:T(8,128)(2,1)S(1)}, bf16[1024,128]{1,0:T(8,128)(2,1)S(1)}, u32[]{:S(2)}, u32[]{:S(2)}) collective-permute-start(bf16[1024,128]{1,0:T(8,128)(2,1)S(1)} %state.1.refs_2_), channel_id=1, source_target_pairs={{2,4},{3,8},{5,6},{7,12},{9,10},{11,13},{0,1},{14,15},{4,2},{8,3},... | collective-permute-start | bytes 786440 | tf_op jit(solution)/shard_map/ppermute | solution.py:297
  41.9 11.4 %collective-permute-start.8 = (bf16[1024,128]{1,0:T(8,128)(2,1)S(1)}, bf16[1024,128]{1,0:T(8,128)(2,1)S(1)}, u32[]{:S(2)}, u32[]{:S(2)}) collective-permute-start(bf16[1024,128]{1,0:T(8,128)(2,1)S(1)} %state.1.refs_2_), channel_id=1, source_target_pairs={{0,6},{4,10},{7,8},{9,14},{2,3},{12,13},{1,5},{11,15},{6,0},{10,4}... | collective-permute-start | bytes 786440 | tf_op jit(solution)/shard_map/ppermute | solution.py:297
  54.0 4.1 %collective-permute-start.11 = (f32[1024,128]{1,0:T(8,128)S(1)}, f32[1024,128]{1,0:T(8,128)S(1)}, u32[]{:S(2)}, u32[]{:S(2)}) collective-permute-start(f32[1024,128]{1,0:T(8,128)S(1)} %peer_product.11), channel_id=1, source_target_pairs={{0,1},{1,0},{2,3},{3,2},{4,5},{5,4},{6,7},{7,6},{8,9},{9,8},{10,11... | collective-permute-start | bytes 1572872 | tf_op jit(solution)/shard_map/ppermute | solution.py:300

commit v5 on v4

--- a/solution.py
+++ b/solution.py
@@ -122,27 +122,24 @@
     return part
 
 
-def pack_kernel(blocks, slots, emb_hbm, cols_hbm, count_hbm, out_ref, cols_ref, count_ref, sems):
-    mols = emb_hbm.shape[0]
-    loads = [
-        pltpu.make_async_copy(emb_hbm, out_ref.at[pl.ds(0, mols), :], sems.at[0]),
-        pltpu.make_async_copy(cols_hbm, cols_ref, sems.at[1]),
-        pltpu.make_async_copy(count_hbm, count_ref, sems.at[2]),
-    ]
-    for load in loads:
-        load.start()
-    loads[1].wait()
-    loads[2].wait()
+def listing_table(blocks, slots, cols_ref, count_ref):
     first = lax.axis_index("row") * blocks
-    lane = lax.broadcasted_iota(jnp.int32, (TAIL, LANES), 1)
-    row = lax.broadcasted_iota(jnp.int32, (TAIL, LANES), 0)
-    table = jnp.zeros((TAIL, LANES), F32)
+    lane = lax.broadcasted_iota(jnp.int32, (8, LANES), 1)
+    row = lax.broadcasted_iota(jnp.int32, (8, LANES), 0)
+    table = jnp.zeros((8, LANES), F32)
     for b in range(blocks):
         for s in range(slots):
             offset = jnp.where(s < count_ref[b], cols_ref[b, s] - (first + b) + BAND, -1)
             table = jnp.where(jnp.logical_and(lane == offset, row == b), 1.0, table)
-    out_ref[pl.ds(mols, TAIL), :] = table.astype(BF16)
-    loads[0].wait()
+    return table
+
+
+def compact(column):
+    eye = lax.broadcasted_iota(jnp.int32, (LANES, LANES), 0) == lax.broadcasted_iota(jnp.int32, (LANES, LANES), 1)
+    rows = []
+    for k in range(column.shape[0] // LANES):
+        rows.append(jnp.sum(jnp.where(eye, column[k * LANES : (k + 1) * LANES], 0.0), axis=0, keepdims=True))
+    return jnp.concatenate(rows, axis=0)
 
 
 def tile_weights(hl, b, e, w_ref, at, s_ref, diagonal):
@@ -177,19 +174,31 @@
         ref[at, :] = value if start else ref[at, :] + value
 
 
-def own_weights_kernel(blocks, pack_ref, hl, w_ref, row_ref, col_ref, s_ref):
+def own_weights_kernel(dims, cols_hbm, count_hbm, own_hbm, *rest):
+    blocks, slots = dims
+    table_ref, hl, w_ref, row_ref, col_ref, s_ref, own_ref, cols_ref, count_ref, sems = rest
+    loads = [
+        pltpu.make_async_copy(cols_hbm, cols_ref, sems.at[0]),
+        pltpu.make_async_copy(count_hbm, count_ref, sems.at[1]),
+        pltpu.make_async_copy(own_hbm, own_ref, sems.at[2]),
+    ]
+    for load in loads:
+        load.start()
+    for load in loads:
+        load.wait()
     mols = hl.shape[0]
     size, width = mols // blocks, hl.shape[1] // 2
     c = lax.axis_index("col")
-    table = pack_ref[pl.ds(mols, TAIL), :].astype(F32)
+    table = listing_table(blocks, slots, cols_ref, count_ref)
+    table_ref[...] = table
     for b in range(blocks):
-        x = pack_ref[pl.ds(b * size, size), :].astype(F32)
+        x = own_ref[pl.ds(b * size, size), :].astype(F32)
         scale = lax.rsqrt(jnp.sum(x * x, axis=-1, keepdims=True) * (1.0 / width) + EPS)
         x = x * (scale * (2.0 * KERNEL_SCALE * LOG2E / width))
         high = x.astype(BF16)
         hl[pl.ds(b * size, size), :width] = high
         hl[pl.ds(b * size, size), width:] = (x - high.astype(F32)).astype(BF16)
-    e = pack_ref[pl.ds(pl.multiple_of(c * size, size), size), :]
+    e = own_ref[pl.ds(pl.multiple_of(c * size, size), size), :]
     for b in range(blocks):
         parts = tile_weights(hl, b, e, w_ref, b, s_ref, c == b)
         from_c = jnp.where(c == 0, table_entry(table, 0, b), table_entry(table, 1, b - 1))
@@ -197,7 +206,7 @@
         add_parts(col_ref, b * size, parts, from_c, True)
 
 
-def peer_weights_kernel(dims, offsets, pack_ref, peer_ref, hl, row_in, col_in, w_ref, *rest):
+def peer_weights_kernel(dims, offsets, table_ref, peer_ref, peer_table_ref, hl, row_in, col_in, w_ref, *rest):
     blocks, last = dims
     if last:
         deg_ref, row_ref, col_ref, s_ref = rest
@@ -207,8 +216,8 @@
     size = mols // blocks
     chips = peer_offset(offsets)
     valid = jnp.where(chips != 0, 1.0, 0.0)
-    own_table = pack_ref[pl.ds(mols, TAIL), :].astype(F32) * valid
-    peer_table = peer_ref[pl.ds(mols, TAIL), :].astype(F32) * valid
+    own_table = table_ref[...] * valid
+    peer_table = peer_table_ref[...] * valid
     row_ref[...] = row_in[...]
     col_ref[...] = col_in[...]
     for k in range(blocks):
@@ -219,27 +228,51 @@
             add_parts(row_ref, b * size, parts, table_entry(own_table, b, offset), False)
             add_parts(col_ref, b * size, parts, table_entry(peer_table, k, -offset), False)
     if last:
-        lane = lax.broadcasted_iota(jnp.int32, (size, LANES), 1)
-        for b in range(blocks):
-            at = pl.ds(b * size, size)
-            by_row = jnp.sum(row_ref[at, :], axis=-1, keepdims=True)
-            by_col = jnp.sum(col_ref[at, :], axis=-1, keepdims=True)
-            deg_ref[at, :] = jnp.where(lane < LANES // 2, by_row, by_col)
-
-
-def scale_kernel(own_ref, other_ref, seed_ref, scaled_ref, rs_ref, cs_ref):
-    total = lax.rsqrt(own_ref[...] + other_ref[...])
-    by_col = jnp.broadcast_to(total[:, LANES // 2 : LANES // 2 + 1], total.shape)
-    rs_ref[...] = jnp.broadcast_to(total[:, 0:1] * ALPHA, total.shape)
-    cs_ref[...] = by_col
-    scaled_ref[...] = (seed_ref[...] * by_col).astype(BF16)
-
-
-def product_kernel(blocks, offsets, pack_ref, w_ref, scaled_ref, *rest):
-    out_ref = rest[-1]
+        half = mols // LANES
+        for n, ref in enumerate((row_ref, col_ref)):
+            deg_ref[pl.ds(n * half, half), :] = compact(jnp.sum(ref[...], axis=-1, keepdims=True))
+
+
+def seeds_kernel(mask_ref, profile_ref, after_ref, seed_ref, bf16_ref):
+    del after_ref
+    columns = mask_ref[...].astype(F32).T
+    for k in range(mask_ref.shape[0]):
+        at = pl.ds(k * LANES, LANES)
+        seed = jnp.where(columns[:, k : k + 1] > 0.0, profile_ref[at, :], 0.0)
+        seed_ref[at, :] = seed
+        bf16_ref[at, :] = seed.astype(BF16)
+
+
+def degree_kernel(own_ref, other_ref, out_ref):
+    out_ref[...] = lax.rsqrt(own_ref[...] + other_ref[...])
+
+
+def expand_kernel(scales_ref, seed_ref, scaled_ref, rs_ref, cs_ref):
+    columns = scales_ref[...].T
+    half = scales_ref.shape[0] // 2
+    for k in range(half):
+        at = pl.ds(k * LANES, LANES)
+        by_col = jnp.broadcast_to(columns[:, half + k : half + k + 1], (LANES, LANES))
+        rs_ref[at, :] = jnp.broadcast_to(columns[:, k : k + 1] * ALPHA, (LANES, LANES))
+        cs_ref[at, :] = by_col
+        scaled_ref[at, :] = (seed_ref[at, :] * by_col).astype(BF16)
+
+
+def product_kernel(blocks, offsets, first, table_ref, w_ref, scaled_ref, *rest):
+    if first:
+        scales_ref, _, out_ref, product_ref = rest
+        columns = scales_ref[...].T
+        half = scales_ref.shape[0] // 2
+        for k in range(half):
+            at = pl.ds(k * LANES, LANES)
+            seed = scaled_ref[at, :].astype(F32)
+            product_ref[at, :] = (seed * columns[:, half + k : half + k + 1]).astype(BF16)
+        scaled_ref, rest = product_ref, rest[1:]
+    else:
+        out_ref = rest[-1]
     mols = scaled_ref.shape[0]
     size = mols // blocks
-    table = pack_ref[pl.ds(mols, TAIL), :].astype(F32)
+    table = table_ref[...]
     c = lax.axis_index("col")
     if offsets is not None:
         chips = peer_offset(offsets)
@@ -293,8 +326,11 @@
     bf16_rows = jax.ShapeDtypeStruct((mols, LANES), BF16)
     tile_flops = 4 * size * size * width
 
+    def to_peer(value, step):
+        return lax.ppermute(value, ("row", "col"), steps[step][0])
+
     def from_peers(value):
-        return [lax.ppermute(value, ("row", "col"), swaps) for swaps, _ in steps]
+        return [to_peer(value, step) for step in range(len(steps))]
 
     def other_core(value):
         return lax.ppermute(value, "col", [(0, 1), (1, 0)])
@@ -302,40 +338,47 @@
     def weights_of(tiles):
         return jax.ShapeDtypeStruct((tiles, size, size), BF16)
 
-    held = [pltpu.with_memory_space_constraint(t, pltpu.HBM) for t in (embeddings, tile_cols, tile_count)]
-    pack = kernel_call(
-        lambda *refs: pack_kernel(blocks, slots, *refs),
-        "pack",
-        held,
-        jax.ShapeDtypeStruct((mols + TAIL, LANES), BF16),
-        1,
+    chunks = mols // LANES
+    peer_emb = from_peers(embeddings)
+    one_tile = pltpu.VMEM((size, size), F32)
+    table, hl, own_weights, row_sum, col_sum = kernel_call(
+        lambda *refs: own_weights_kernel((blocks, slots), *refs),
+        "own_weights",
+        [pltpu.with_memory_space_constraint(t, pltpu.HBM) for t in (tile_cols, tile_count, embeddings)],
+        (
+            jax.ShapeDtypeStruct((8, LANES), F32),
+            jax.ShapeDtypeStruct((mols, 2 * width), BF16),
+            weights_of(blocks),
+            f32_rows,
+            f32_rows,
+        ),
+        blocks * tile_flops,
         [
+            one_tile,
+            pltpu.VMEM((mols, width), BF16),
             pltpu.SMEM(tile_cols.shape, jnp.int32),
             pltpu.SMEM(tile_count.shape, jnp.int32),
             pltpu.SemaphoreType.DMA((3,)),
         ],
         [HBM] * 3,
     )
-    peer_packs = from_peers(pack)
-    seed_rows = jnp.where(seed_mask[:, None] > 0, profiles, 0.0)
-    one_tile = pltpu.VMEM((size, size), F32)
-    hl, own_weights, row_sum, col_sum = kernel_call(
-        lambda *refs: own_weights_kernel(blocks, *refs),
-        "own_weights",
-        [pack],
-        (jax.ShapeDtypeStruct((mols, 2 * width), BF16), weights_of(blocks), f32_rows, f32_rows),
-        blocks * tile_flops,
-        [one_tile],
-    )
+    sent_table = table
     weights = [own_weights]
     for step, (_, offsets) in enumerate(steps):
         last = step + 1 == len(steps)
-        ins = [pack, peer_packs[step], hl, row_sum, col_sum]
+        if last:
+            seed_rows, seeds = kernel_call(
+                seeds_kernel, "seeds", [seed_mask.reshape(chunks, LANES), profiles, row_sum], (f32_rows, bf16_rows), 1
+            )
+            peer_seeds = from_peers(seeds)
+        peer_table = to_peer(sent_table, step)
+        ins = [table, peer_emb[step], peer_table, hl, row_sum, col_sum]
+        degrees = jax.ShapeDtypeStruct((2 * chunks, LANES), F32)
         out = kernel_call(
             lambda *refs, offsets=offsets, last=last: peer_weights_kernel((blocks, last), offsets, *refs),
             "peer_weights",
             ins,
-            (weights_of(blocks * blocks), f32_rows) if last else (weights_of(blocks * blocks), f32_rows, f32_rows),
+            (weights_of(blocks * blocks), degrees) if last else (weights_of(blocks * blocks), f32_rows, f32_rows),
             blocks * blocks * tile_flops,
             [pltpu.VMEM((mols, LANES), F32)] * 2 + [one_tile] if last else [one_tile],
         )
@@ -344,25 +387,32 @@
             degree = out[1]
         else:
             row_sum, col_sum = out[1:]
+            if step + 3 == len(steps):
+                sent_table, row_sum = lax.optimization_barrier((table, row_sum))
+    scales = kernel_call(degree_kernel, "degree", [degree, other_core(degree)], degrees, 1)
+    scales, peer_seeds[0] = lax.optimization_barrier((scales, peer_seeds[0]))
+    peer_scales = from_peers(scales)
     scaled, row_scale, col_scale = kernel_call(
-        scale_kernel, "scale", [degree, other_core(degree), seed_rows], (bf16_rows, f32_rows, f32_rows), 1
+        expand_kernel, "expand", [scales, seed_rows], (bf16_rows, f32_rows, f32_rows), 1
     )
     for iteration in range(ITERS):
-        peers = from_peers(scaled)
+        first = iteration == 0
+        peers = peer_seeds if first else from_peers(scaled)
         partial = kernel_call(
-            lambda *refs: product_kernel(blocks, None, *refs),
+            lambda *refs: product_kernel(blocks, None, False, *refs),
             "own_product",
-            [pack, weights[0], scaled],
+            [table, weights[0], scaled],
             f32_rows,
             blocks * tile_flops,
         )
         for step, (_, offsets) in enumerate(steps):
             partial = kernel_call(
-                lambda *refs, offsets=offsets: product_kernel(blocks, offsets, *refs),
+                lambda *refs, offsets=offsets, first=first: product_kernel(blocks, offsets, first, *refs),
                 "peer_product",
-                [pack, weights[1 + step], peers[step], partial],
+                [table, weights[1 + step], peers[step]] + [peer_scales[step]] * first + [partial],
                 f32_rows,
                 blocks * blocks * tile_flops,
+                [pltpu.VMEM((mols, LANES), BF16)] * first,
             )
         other = other_core(partial)
         if iteration + 1 < ITERS:

time: 59.4 us -> 67.1 us (1.13)
  the two profiles are of different devices: /device:TPU:17 before, /device:TPU:7 now
where the time goes in v5:
time: 67.1 us; the launch traced here: 66.9 us
  starting transfers between devices  29.1 us (43%)
  waiting for transfers between devices  24.2 us (36%)
  Pallas kernels  12.5 us (19%)
  other arithmetic  0.95 us (1%)
    ppermute x15, starting transfers between devices, to_peer(): return lax.ppermute(value, ('row', 'col'), steps[step][0])  23.8 us
    ppermute x15, waiting for transfers between devices, to_peer(): return lax.ppermute(value, ('row', 'col'), steps[step][0])  20 us
    pallas_call x16, Pallas kernels, kernel_call(): pl.pallas_call(body, out_shape=outs, in_specs=in_specs or [VMEM] * len(in...  12.5 us
    ppermute x3, starting transfers between devices, other_core(): return lax.ppermute(value, 'col', [(0, 1), (1, 0)])  5.29 us
    ppermute x3, waiting for transfers between devices, other_core(): return lax.ppermute(value, 'col', [(0, 1), (1, 0)])  4.21 us
  transfers between devices with their start and end apart: 18, of which 10 were waited for; matrix products, arithmetic and copies ran while one was open for 0% of the time, Pallas kernels for 16%

profile of v5, /device:TPU:7, one launch (start us, length us, event | category | flops | bytes accessed | tf_op | source)
XLA Modules:
  0.0 66.9 jit_solution(4477222006369761820)
XLA Ops:
  0.0 1.9 %collective-permute-start.1 = (bf16[1024,128]{1,0:T(8,128)(2,1)}, bf16[1024,128]{1,0:T(8,128)(2,1)S(1)}, u32[]{:S(2)}, u32[]{:S(2)}) collective-permute-start(bf16[1024,128]{1,0:T(8,128)(2,1)} %refs_2_.1), channel_id=1, source_target_pairs={{0,2},{1,4},{3,6},{5,8},{7,10},{9,12},{11,14},{13,15},{2,0},{4,1},... | collective-permute-start | bytes 786440 | tf_op jit(solution)/shard_map/ppermute | solution.py:330
  1.9 1.0 %collective-permute-start.4 = (bf16[1024,128]{1,0:T(8,128)(2,1)}, bf16[1024,128]{1,0:T(8,128)(2,1)S(1)}, u32[]{:S(2)}, u32[]{:S(2)}) collective-permute-start(bf16[1024,128]{1,0:T(8,128)(2,1)} %refs_2_.1), channel_id=1, source_target_pairs={{2,4},{3,8},{5,6},{7,12},{9,10},{11,13},{0,1},{14,15},{4,2},{8,3},... | collective-permute-start | bytes 786440 | tf_op jit(solution)/shard_map/ppermute | solution.py:330
  2.8 1.8 %own_weights.1 = (f32[8,128]{1,0:T(8,128)S(1)}, bf16[1024,256]{1,0:T(8,128)(2,1)S(1)}, bf16[2,512,512]{2,1,0:T(8,128)(2,1)S(1)}, f32[1024,128]{1,0:T(8,128)S(1)}, f32[1024,128]{1,0:T(8,128)S(1)}) custom-call(s32[2,13]{1,0:T(2,128)} %refs_0_.1, s32[2]{0:T(128)} %refs_1_.1, bf16[1024,128]{1,0:T(8,128)(2,1)} %refs_2_.1), custom_call_target="tpu_custom_call" | custom-call | flops 268435456 | bytes 1048576 | tf_op jit(solution)/shard_map/own_weights/pallas_call | solution.py:302
  4.6 0.9 %collective-permute-start.2 = (f32[8,128]{1,0:T(8,128)S(1)}, f32[8,128]{1,0:T(8,128)S(1)}, u32[]{:S(2)}, u32[]{:S(2)}) collective-permute-start(f32[8,128]{1,0:T(8,128)S(1)} %get-tuple-element.32.refs_0_), channel_id=1, source_target_pairs={{0,2},{1,4},{3,6},{5,8},{7,10},{9,12},{11,14},{13,15},{2,0},{4,1},... | collective-permute-start | bytes 12296 | tf_op jit(solution)/shard_map/ppermute | solution.py:330
  5.6 5.6 %collective-permute-done.2.refs_2_ = f32[8,128]{1,0:T(8,128)S(1)} collective-permute-done((f32[8,128]{1,0:T(8,128)S(1)}, f32[8,128]{1,0:T(8,128)S(1)}, u32[]{:S(2)}, u32[]{:S(2)}) %collective-permute-start.2) | collective-permute-done | bytes 4128 | tf_op jit(solution)/shard_map/ppermute | solution.py:330
  11.2 1.1 %peer_weights.3 = (bf16[4,512,512]{2,1,0:T(8,128)(2,1)S(1)}, f32[1024,128]{1,0:T(8,128)S(1)}, f32[1024,128]{1,0:T(8,128)S(1)}) custom-call(f32[8,128]{1,0:T(8,128)S(1)} %get-tuple-element.32.refs_0_, bf16[1024,128]{1,0:T(8,128)(2,1)S(1)} %collective-permute-done.1.refs_1_, f32[8,128]{1,0:T(8,128)S(1)} %collective-permute-done.2.refs_2_, ...), custom_call_target="tpu_custom_call" | custom-call | flops 536870912 | bytes 1048576 | tf_op jit(solution)/shard_map/peer_weights/pallas_call | solution.py:302
  12.4 5.6 %collective-permute-done.5.refs_2_ = f32[8,128]{1,0:T(8,128)S(1)} collective-permute-done((f32[8,128]{1,0:T(8,128)S(1)}, f32[8,128]{1,0:T(8,128)S(1)}, u32[]{:S(2)}, u32[]{:S(2)}) %collective-permute-start.5) | collective-permute-done | bytes 4128 | tf_op jit(solution)/shard_map/ppermute | solution.py:330
  18.0 1.1 %peer_weights.4 = (bf16[4,512,512]{2,1,0:T(8,128)(2,1)S(1)}, f32[1024,128]{1,0:T(8,128)S(1)}, f32[1024,128]{1,0:T(8,128)S(1)}) custom-call(f32[8,128]{1,0:T(8,128)S(1)} %get-tuple-element.32.refs_0_, bf16[1024,128]{1,0:T(8,128)(2,1)S(1)} %collective-permute-done.4.refs_1_, f32[8,128]{1,0:T(8,128)S(1)} %collective-permute-done.5.refs_2_, ...), custom_call_target="tpu_custom_call" | custom-call | flops 536870912 | bytes 1048576 | tf_op jit(solution)/shard_map/peer_weights/pallas_call | solution.py:302
  21.1 1.2 %collective-permute-done.3.refs_2_ = f32[8,128]{1,0:T(8,128)S(1)} collective-permute-done((f32[8,128]{1,0:T(8,128)S(1)}, f32[8,128]{1,0:T(8,128)S(1)}, u32[]{:S(2)}, u32[]{:S(2)}) %collective-permute-start.3) | collective-permute-done | bytes 4128 | tf_op jit(solution)/shard_map/ppermute | solution.py:330
  22.3 1.3 %peer_weights.5 = (bf16[4,512,512]{2,1,0:T(8,128)(2,1)S(1)}, f32[16,128]{1,0:T(8,128)S(1)}) custom-call(f32[8,128]{1,0:T(8,128)S(1)} %get-tuple-element.32.refs_0_, bf16[1024,128]{1,0:T(8,128)(2,1)S(1)} %collective-permute-done.refs_1_, f32[8,128]{1,0:T(8,128)S(1)} %collective-permute-done.3.refs_2_, bf16[1024,256]{1,0:T(8,128)(2,1)S(1)} %get-tuple-element.28.refs_3_, ...), custom_call_target="tpu_custom_call" | custom-call | flops 536870912 | bytes 1048576 | tf_op jit(solution)/shard_map/peer_weights/pallas_call | solution.py:302
  24.0 0.8 %collective-permute-done.7.other_ref = f32[16,128]{1,0:T(8,128)S(1)} collective-permute-done((f32[16,128]{1,0:T(8,128)S(1)}, f32[16,128]{1,0:T(8,128)S(1)}, u32[]{:S(2)}, u32[]{:S(2)}) %collective-permute-start.7) | collective-permute-done | bytes 8224 | tf_op jit(solution)/shard_map/ppermute | solution.py:336
  25.3 12.3 %collective-permute-start.12 = (f32[16,128]{1,0:T(8,128)S(1)}, f32[16,128]{1,0:T(8,128)S(1)}, u32[]{:S(2)}, u32[]{:S(2)}) collective-permute-start(f32[16,128]{1,0:T(8,128)S(1)} %degree.1.scales_ref), channel_id=1, source_target_pairs={{0,2},{1,4},{3,6},{5,8},{7,10},{9,12},{11,14},{13,15},{2,0},{4,1},... | collective-permute-start | bytes 24584 | tf_op jit(solution)/shard_map/ppermute | solution.py:330
  37.7 2.5 %collective-permute-start.11 = (f32[16,128]{1,0:T(8,128)S(1)}, f32[16,128]{1,0:T(8,128)S(1)}, u32[]{:S(2)}, u32[]{:S(2)}) collective-permute-start(f32[16,128]{1,0:T(8,128)S(1)} %degree.1.scales_ref), channel_id=1, source_target_pairs={{2,4},{3,8},{5,6},{7,12},{9,10},{11,13},{0,1},{14,15},{4,2},{8,3},... | collective-permute-start | bytes 24584 | tf_op jit(solution)/shard_map/ppermute | solution.py:330
  41.2 0.9 %peer_product.6.refs_4_ = f32[1024,128]{1,0:T(8,128)S(1)} custom-call(f32[8,128]{1,0:T(8,128)S(1)} %get-tuple-element.32.refs_0_, bf16[4,512,512]{2,1,0:T(8,128)(2,1)S(1)} %get-tuple-element.42.refs_1_, bf16[1024,128]{1,0:T(8,128)(2,1)S(1)} %collective-permute-done.8.refs_2_, f32[16,128]{1,0:T(8,128)S(1)} %collective-permute-done.12.refs_3_, ...), custom_call_target="tpu_custom_call" | custom-call | flops 536870912 | bytes 1048576 | tf_op jit(solution)/shard_map/peer_product/pallas_call | solution.py:302
  42.5 0.9 %peer_product.7.refs_4_ = f32[1024,128]{1,0:T(8,128)S(1)} custom-call(f32[8,128]{1,0:T(8,128)S(1)} %get-tuple-element.32.refs_0_, bf16[4,512,512]{2,1,0:T(8,128)(2,1)S(1)} %get-tuple-element.41.refs_1_, bf16[1024,128]{1,0:T(8,128)(2,1)S(1)} %collective-permute-done.10.refs_2_, f32[16,128]{1,0:T(8,128)S(1)} %collective-permute-done.11.refs_3_, ...), custom_call_target="tpu_custom_call" | custom-call | flops 536870912 | bytes 1048576 | tf_op jit(solution)/shard_map/peer_product/pallas_call | solution.py:302
  43.5 0.9 %peer_product.8.own_ref = f32[1024,128]{1,0:T(8,128)S(1)} custom-call(f32[8,128]{1,0:T(8,128)S(1)} %get-tuple-element.32.refs_0_, bf16[4,512,512]{2,1,0:T(8,128)(2,1)S(1)} %get-tuple-element.37.refs_1_, bf16[1024,128]{1,0:T(8,128)(2,1)S(1)} %collective-permute-done.6.refs_2_, f32[16,128]{1,0:T(8,128)S(1)} %collective-permute-done.9.refs_3_, ...), custom_call_target="tpu_custom_call" | custom-call | flops 536870912 | bytes 1048576 | tf_op jit(solution)/shard_map/peer_product/pallas_call | solution.py:302
  44.5 1.8 %collective-permute-done.13.other_ref = f32[1024,128]{1,0:T(8,128)S(1)} collective-permute-done((f32[1024,128]{1,0:T(8,128)S(1)}, f32[1024,128]{1,0:T(8,128)S(1)}, u32[]{:S(2)}, u32[]{:S(2)}) %collective-permute-start.13) | collective-permute-done | bytes 524320 | tf_op jit(solution)/shard_map/ppermute | solution.py:336
  46.5 2.2 %collective-permute-start.16 = (bf16[1024,128]{1,0:T(8,128)(2,1)S(1)}, bf16[1024,128]{1,0:T(8,128)(2,1)S(1)}, u32[]{:S(2)}, u32[]{:S(2)}) collective-permute-start(bf16[1024,128]{1,0:T(8,128)(2,1)S(1)} %state.1.refs_2_), channel_id=1, source_target_pairs={{0,2},{1,4},{3,6},{5,8},{7,10},{9,12},{11,14},{13,15},{2,0},{4,1},... | collective-permute-start | bytes 786440 | tf_op jit(solution)/shard_map/ppermute | solution.py:330
  48.7 1.3 %collective-permute-start.15 = (bf16[1024,128]{1,0:T(8,128)(2,1)S(1)}, bf16[1024,128]{1,0:T(8,128)(2,1)S(1)}, u32[]{:S(2)}, u32[]{:S(2)}) collective-permute-start(bf16[1024,128]{1,0:T(8,128)(2,1)S(1)} %state.1.refs_2_), channel_id=1, source_target_pairs={{2,4},{3,8},{5,6},{7,12},{9,10},{11,13},{0,1},{14,15},{4,2},{8,3},... | collective-permute-start | bytes 786440 | tf_op jit(solution)/shard_map/ppermute | solution.py:330
  50.5 2.8 %collective-permute-done.16.refs_2_ = bf16[1024,128]{1,0:T(8,128)(2,1)S(1)} collective-permute-done((bf16[1024,128]{1,0:T(8,128)(2,1)S(1)}, bf16[1024,128]{1,0:T(8,128)(2,1)S(1)}, u32[]{:S(2)}, u32[]{:S(2)}) %collective-permute-start.16) | collective-permute-done | bytes 262176 | tf_op jit(solution)/shard_map/ppermute | solution.py:330
  54.2 3.9 %collective-permute-done.15.refs_2_ = bf16[1024,128]{1,0:T(8,128)(2,1)S(1)} collective-permute-done((bf16[1024,128]{1,0:T(8,128)(2,1)S(1)}, bf16[1024,128]{1,0:T(8,128)(2,1)S(1)}, u32[]{:S(2)}, u32[]{:S(2)}) %collective-permute-start.15) | collective-permute-done | bytes 262176 | tf_op jit(solution)/shard_map/ppermute | solution.py:330
  59.7 4.7 %collective-permute-start.17 = (f32[1024,128]{1,0:T(8,128)S(1)}, f32[1024,128]{1,0:T(8,128)S(1)}, u32[]{:S(2)}, u32[]{:S(2)}) collective-permute-start(f32[1024,128]{1,0:T(8,128)S(1)} %peer_product.11), channel_id=1, source_target_pairs={{0,1},{1,0},{2,3},{3,2},{4,5},{5,4},{6,7},{7,6},{8,9},{9,8},{10,11... | collective-permute-start | bytes 1572872 | tf_op jit(solution)/shard_map/ppermute | solution.py:336
  64.4 1.5 %collective-permute-done.17 = f32[1024,128]{1,0:T(8,128)S(1)} collective-permute-done((f32[1024,128]{1,0:T(8,128)S(1)}, f32[1024,128]{1,0:T(8,128)S(1)}, u32[]{:S(2)}, u32[]{:S(2)}) %collective-permute-start.17) | collective-permute-done | bytes 524320 | tf_op jit(solution)/shard_map/ppermute | solution.py:336
  66.0 0.9 %multiply_add_fusion = f32[1024,128]{1,0:T(8,128)} fusion(f32[1024,128]{1,0:T(8,128)S(1)} %get-tuple-element.45.seed_ref, f32[1024,128]{1,0:T(8,128)S(1)} %get-tuple-element.47.rs_ref, f32[1024,128]{1,0:T(8,128)S(1)} %peer_product.11, f32[1024,128]{1,0:T(8,128)S(1)} %collective-permute-done.17), kind=kLoop, calls=%fused_computation | loop fusion | flops 524288 | bytes 2621440 | tf_op jit(solution)/shard_map/add | solution.py:422
  (33 shorter events, 7.7 us)
Async XLA Ops:
  0.0 11.2 %collective-permute-start.1 = (bf16[1024,128]{1,0:T(8,128)(2,1)}, bf16[1024,128]{1,0:T(8,128)(2,1)S(1)}, u32[]{:S(2)}, u32[]{:S(2)}) collective-permute-start(bf16[1024,128]{1,0:T(8,128)(2,1)} %refs_2_.1), channel_id=1, source_target_pairs={{0,2},{1,4},{3,6},{5,8},{7,10},{9,12},{11,14},{13,15},{2,0},{4,1},... | collective-permute-start | bytes 786440 | tf_op jit(solution)/shard_map/ppermute | solution.py:330
  1.9 10.5 %collective-permute-start.4 = (bf16[1024,128]{1,0:T(8,128)(2,1)}, bf16[1024,128]{1,0:T(8,128)(2,1)S(1)}, u32[]{:S(2)}, u32[]{:S(2)}) collective-permute-start(bf16[1024,128]{1,0:T(8,128)(2,1)} %refs_2_.1), channel_id=1, source_target_pairs={{2,4},{3,8},{5,6},{7,12},{9,10},{11,13},{0,1},{14,15},{4,2},{8,3},... | collective-permute-start | bytes 786440 | tf_op jit(solution)/shard_map/ppermute | solution.py:330
  4.6 14.5 %copy-start = (f32[1024,128]{1,0:T(8,128)S(1)}, f32[1024,128]{1,0:T(8,128)}, u32[]{:S(2)}) copy-start(f32[1024,128]{1,0:T(8,128)} %profile_ref.1) | copy-start | bytes 1572868
  4.6 14.5 %copy-start.1 = (s32[1024]{0:T(1024)S(1)}, s32[1024]{0:T(1024)}, u32[]{:S(2)}) copy-start(s32[1024]{0:T(1024)} %param.7) | copy-start | bytes 12292
  4.6 6.5 %collective-permute-start.2 = (f32[8,128]{1,0:T(8,128)S(1)}, f32[8,128]{1,0:T(8,128)S(1)}, u32[]{:S(2)}, u32[]{:S(2)}) collective-permute-start(f32[8,128]{1,0:T(8,128)S(1)} %get-tuple-element.32.refs_0_), channel_id=1, source_target_pairs={{0,2},{1,4},{3,6},{5,8},{7,10},{9,12},{11,14},{13,15},{2,0},{4,1},... | collective-permute-start | bytes 12296 | tf_op jit(solution)/shard_map/ppermute | solution.py:330
  5.5 15.6 %collective-permute-start = (bf16[1024,128]{1,0:T(8,128)(2,1)}, bf16[1024,128]{1,0:T(8,128)(2,1)S(1)}, u32[]{:S(2)}, u32[]{:S(2)}) collective-permute-start(bf16[1024,128]{1,0:T(8,128)(2,1)} %refs_2_.1), channel_id=1, source_target_pairs={{0,6},{4,10},{7,8},{9,14},{2,3},{12,13},{1,5},{11,15},{6,0},{10,4}... | collective-permute-start | bytes 786440 | tf_op jit(solution)/shard_map/ppermute | solution.py:330
  12.3 5.6 %collective-permute-start.5 = (f32[8,128]{1,0:T(8,128)S(1)}, f32[8,128]{1,0:T(8,128)S(1)}, u32[]{:S(2)}, u32[]{:S(2)}) collective-permute-start(f32[8,128]{1,0:T(8,128)S(1)} %get-tuple-element.32.refs_0_), channel_id=1, source_target_pairs={{2,4},{3,8},{5,6},{7,12},{9,10},{11,13},{0,1},{14,15},{4,2},{8,3},... | collective-permute-start | bytes 12296 | tf_op jit(solution)/shard_map/ppermute | solution.py:330
  19.5 5.9 %collective-permute-start.8 = (bf16[1024,128]{1,0:T(8,128)(2,1)S(1)}, bf16[1024,128]{1,0:T(8,128)(2,1)S(1)}, u32[]{:S(2)}, u32[]{:S(2)}) collective-permute-start(bf16[1024,128]{1,0:T(8,128)(2,1)S(1)} %get-tuple-element.38), channel_id=1, source_target_pairs={{0,2},{1,4},{3,6},{5,8},{7,10},{9,12},{11,14},{13,15},{2,0},{4,1},... | collective-permute-start | bytes 786440 | tf_op jit(solution)/shard_map/ppermute | solution.py:330
  19.8 22.3 %collective-permute-start.10 = (bf16[1024,128]{1,0:T(8,128)(2,1)S(1)}, bf16[1024,128]{1,0:T(8,128)(2,1)S(1)}, u32[]{:S(2)}, u32[]{:S(2)}) collective-permute-start(bf16[1024,128]{1,0:T(8,128)(2,1)S(1)} %get-tuple-element.38), channel_id=1, source_target_pairs={{2,4},{3,8},{5,6},{7,12},{9,10},{11,13},{0,1},{14,15},{4,2},{8,3},... | collective-permute-start | bytes 786440 | tf_op jit(solution)/shard_map/ppermute | solution.py:330
  20.3 23.1 %collective-permute-start.6 = (bf16[1024,128]{1,0:T(8,128)(2,1)S(1)}, bf16[1024,128]{1,0:T(8,128)(2,1)S(1)}, u32[]{:S(2)}, u32[]{:S(2)}) collective-permute-start(bf16[1024,128]{1,0:T(8,128)(2,1)S(1)} %get-tuple-element.38), channel_id=1, source_target_pairs={{0,6},{4,10},{7,8},{9,14},{2,3},{12,13},{1,5},{11,15},{6,0},{10,4}... | collective-permute-start | bytes 786440 | tf_op jit(solution)/shard_map/ppermute | solution.py:330
  21.1 1.2 %collective-permute-start.3 = (f32[8,128]{1,0:T(8,128)S(1)}, f32[8,128]{1,0:T(8,128)S(1)}, u32[]{:S(2)}, u32[]{:S(2)}) collective-permute-start(f32[8,128]{1,0:T(8,128)S(1)} %get-tuple-element.32.refs_0_), channel_id=1, source_target_pairs={{0,6},{4,10},{7,8},{9,14},{2,3},{12,13},{1,5},{11,15},{6,0},{10,4}... | collective-permute-start | bytes 12296 | tf_op jit(solution)/shard_map/ppermute | solution.py:330
  23.6 1.3 %collective-permute-start.7 = (f32[16,128]{1,0:T(8,128)S(1)}, f32[16,128]{1,0:T(8,128)S(1)}, u32[]{:S(2)}, u32[]{:S(2)}) collective-permute-start(f32[16,128]{1,0:T(8,128)S(1)} %get-tuple-element.39.own_ref), channel_id=1, source_target_pairs={{0,1},{1,0},{2,3},{3,2},{4,5},{5,4},{6,7},{7,6},{8,9},{9,8},{10,11... | collective-permute-start | bytes 24584 | tf_op jit(solution)/shard_map/ppermute | solution.py:336
  25.3 15.9 %collective-permute-start.12 = (f32[16,128]{1,0:T(8,128)S(1)}, f32[16,128]{1,0:T(8,128)S(1)}, u32[]{:S(2)}, u32[]{:S(2)}) collective-permute-start(f32[16,128]{1,0:T(8,128)S(1)} %degree.1.scales_ref), channel_id=1, source_target_pairs={{0,2},{1,4},{3,6},{5,8},{7,10},{9,12},{11,14},{13,15},{2,0},{4,1},... | collective-permute-start | bytes 24584 | tf_op jit(solution)/shard_map/ppermute | solution.py:330
  37.7 4.9 %collective-permute-start.11 = (f32[16,128]{1,0:T(8,128)S(1)}, f32[16,128]{1,0:T(8,128)S(1)}, u32[]{:S(2)}, u32[]{:S(2)}) collective-permute-start(f32[16,128]{1,0:T(8,128)S(1)} %degree.1.scales_ref), channel_id=1, source_target_pairs={{2,4},{3,8},{5,6},{7,12},{9,10},{11,13},{0,1},{14,15},{4,2},{8,3},... | collective-permute-start | bytes 24584 | tf_op jit(solution)/shard_map/ppermute | solution.py:330
  40.2 3.3 %collective-permute-start.9 = (f32[16,128]{1,0:T(8,128)S(1)}, f32[16,128]{1,0:T(8,128)S(1)}, u32[]{:S(2)}, u32[]{:S(2)}) collective-permute-start(f32[16,128]{1,0:T(8,128)S(1)} %degree.1.scales_ref), channel_id=1, source_target_pairs={{0,6},{4,10},{7,8},{9,14},{2,3},{12,13},{1,5},{11,15},{6,0},{10,4}... | collective-permute-start | bytes 24584 | tf_op jit(solution)/shard_map/ppermute | solution.py:330
  44.4 2.0 %collective-permute-start.13 = (f32[1024,128]{1,0:T(8,128)S(1)}, f32[1024,128]{1,0:T(8,128)S(1)}, u32[]{:S(2)}, u32[]{:S(2)}) collective-permute-start(f32[1024,128]{1,0:T(8,128)S(1)} %peer_product.8.own_ref), channel_id=1, source_target_pairs={{0,1},{1,0},{2,3},{3,2},{4,5},{5,4},{6,7},{7,6},{8,9},{9,8},{10,11... | collective-permute-start | bytes 1572872 | tf_op jit(solution)/shard_map/ppermute | solution.py:336
  46.5 6.9 %collective-permute-start.16 = (bf16[1024,128]{1,0:T(8,128)(2,1)S(1)}, bf16[1024,128]{1,0:T(8,128)(2,1)S(1)}, u32[]{:S(2)}, u32[]{:S(2)}) collective-permute-start(bf16[1024,128]{1,0:T(8,128)(2,1)S(1)} %state.1.refs_2_), channel_id=1, source_target_pairs={{0,2},{1,4},{3,6},{5,8},{7,10},{9,12},{11,14},{13,15},{2,0},{4,1},... | collective-permute-start | bytes 786440 | tf_op jit(solution)/shard_map/ppermute | solution.py:330
  48.7 9.4 %collective-permute-start.15 = (bf16[1024,128]{1,0:T(8,128)(2,1)S(1)}, bf16[1024,128]{1,0:T(8,128)(2,1)S(1)}, u32[]{:S(2)}, u32[]{:S(2)}) collective-permute-start(bf16[1024,128]{1,0:T(8,128)(2,1)S(1)} %state.1.refs_2_), channel_id=1, source_target_pairs={{2,4},{3,8},{5,6},{7,12},{9,10},{11,13},{0,1},{14,15},{4,2},{8,3},... | collective-permute-start | bytes 786440 | tf_op jit(solution)/shard_map/ppermute | solution.py:330
  50.0 8.9 %collective-permute-start.14 = (bf16[1024,128]{1,0:T(8,128)(2,1)S(1)}, bf16[1024,128]{1,0:T(8,128)(2,1)S(1)}, u32[]{:S(2)}, u32[]{:S(2)}) collective-permute-start(bf16[1024,128]{1,0:T(8,128)(2,1)S(1)} %state.1.refs_2_), channel_id=1, source_target_pairs={{0,6},{4,10},{7,8},{9,14},{2,3},{12,13},{1,5},{11,15},{6,0},{10,4}... | collective-permute-start | bytes 786440 | tf_op jit(solution)/shard_map/ppermute | solution.py:330
  59.7 6.3 %collective-permute-start.17 = (f32[1024,128]{1,0:T(8,128)S(1)}, f32[1024,128]{1,0:T(8,128)S(1)}, u32[]{:S(2)}, u32[]{:S(2)}) collective-permute-start(f32[1024,128]{1,0:T(8,128)S(1)} %peer_product.11), channel_id=1, source_target_pairs={{0,1},{1,0},{2,3},{3,2},{4,5},{5,4},{6,7},{7,6},{8,9},{9,8},{10,11... | collective-permute-start | bytes 1572872 | tf_op jit(solution)/shard_map/ppermute | solution.py:336

commit v6 on v4

--- a/solution.py
+++ b/solution.py
@@ -145,6 +145,14 @@
     loads[0].wait()
 
 
+def compact(column):
+    eye = lax.broadcasted_iota(jnp.int32, (LANES, LANES), 0) == lax.broadcasted_iota(jnp.int32, (LANES, LANES), 1)
+    rows = []
+    for k in range(column.shape[0] // LANES):
+        rows.append(jnp.sum(jnp.where(eye, column[k * LANES : (k + 1) * LANES], 0.0), axis=0, keepdims=True))
+    return jnp.concatenate(rows, axis=0)
+
+
 def tile_weights(hl, b, e, w_ref, at, s_ref, diagonal):
     size, width = e.shape
     x = e.astype(F32)
@@ -219,24 +227,48 @@
             add_parts(row_ref, b * size, parts, table_entry(own_table, b, offset), False)
             add_parts(col_ref, b * size, parts, table_entry(peer_table, k, -offset), False)
     if last:
-        lane = lax.broadcasted_iota(jnp.int32, (size, LANES), 1)
-        for b in range(blocks):
-            at = pl.ds(b * size, size)
-            by_row = jnp.sum(row_ref[at, :], axis=-1, keepdims=True)
-            by_col = jnp.sum(col_ref[at, :], axis=-1, keepdims=True)
-            deg_ref[at, :] = jnp.where(lane < LANES // 2, by_row, by_col)
-
-
-def scale_kernel(own_ref, other_ref, seed_ref, scaled_ref, rs_ref, cs_ref):
-    total = lax.rsqrt(own_ref[...] + other_ref[...])
-    by_col = jnp.broadcast_to(total[:, LANES // 2 : LANES // 2 + 1], total.shape)
-    rs_ref[...] = jnp.broadcast_to(total[:, 0:1] * ALPHA, total.shape)
-    cs_ref[...] = by_col
-    scaled_ref[...] = (seed_ref[...] * by_col).astype(BF16)
-
-
-def product_kernel(blocks, offsets, pack_ref, w_ref, scaled_ref, *rest):
-    out_ref = rest[-1]
+        half = mols // LANES
+        for n, ref in enumerate((row_ref, col_ref)):
+            deg_ref[pl.ds(n * half, half), :] = compact(jnp.sum(ref[...], axis=-1, keepdims=True))
+
+
+def seeds_kernel(mask_ref, profile_ref, after_ref, seed_ref, bf16_ref):
+    del after_ref
+    columns = mask_ref[...].astype(F32).T
+    for k in range(mask_ref.shape[0]):
+        at = pl.ds(k * LANES, LANES)
+        seed = jnp.where(columns[:, k : k + 1] > 0.0, profile_ref[at, :], 0.0)
+        seed_ref[at, :] = seed
+        bf16_ref[at, :] = seed.astype(BF16)
+
+
+def degree_kernel(own_ref, other_ref, out_ref):
+    out_ref[...] = lax.rsqrt(own_ref[...] + other_ref[...])
+
+
+def expand_kernel(scales_ref, seed_ref, scaled_ref, rs_ref, cs_ref):
+    columns = scales_ref[...].T
+    half = scales_ref.shape[0] // 2
+    for k in range(half):
+        at = pl.ds(k * LANES, LANES)
+        by_col = jnp.broadcast_to(columns[:, half + k : half + k + 1], (LANES, LANES))
+        rs_ref[at, :] = jnp.broadcast_to(columns[:, k : k + 1] * ALPHA, (LANES, LANES))
+        cs_ref[at, :] = by_col
+        scaled_ref[at, :] = (seed_ref[at, :] * by_col).astype(BF16)
+
+
+def product_kernel(blocks, offsets, first, pack_ref, w_ref, scaled_ref, *rest):
+    if first:
+        scales_ref, _, out_ref, product_ref = rest
+        columns = scales_ref[...].T
+        half = scales_ref.shape[0] // 2
+        for k in range(half):
+            at = pl.ds(k * LANES, LANES)
+            seed = scaled_ref[at, :].astype(F32)
+            product_ref[at, :] = (seed * columns[:, half + k : half + k + 1]).astype(BF16)
+        scaled_ref, rest = product_ref, rest[1:]
+    else:
+        out_ref = rest[-1]
     mols = scaled_ref.shape[0]
     size = mols // blocks
     table = pack_ref[pl.ds(mols, TAIL), :].astype(F32)
@@ -293,8 +325,11 @@
     bf16_rows = jax.ShapeDtypeStruct((mols, LANES), BF16)
     tile_flops = 4 * size * size * width
 
+    def to_peer(value, step):
+        return lax.ppermute(value, ("row", "col"), steps[step][0])
+
     def from_peers(value):
-        return [lax.ppermute(value, ("row", "col"), swaps) for swaps, _ in steps]
+        return [to_peer(value, step) for step in range(len(steps))]
 
     def other_core(value):
         return lax.ppermute(value, "col", [(0, 1), (1, 0)])
@@ -302,6 +337,7 @@
     def weights_of(tiles):
         return jax.ShapeDtypeStruct((tiles, size, size), BF16)
 
+    chunks = mols // LANES
     held = [pltpu.with_memory_space_constraint(t, pltpu.HBM) for t in (embeddings, tile_cols, tile_count)]
     pack = kernel_call(
         lambda *refs: pack_kernel(blocks, slots, *refs),
@@ -317,7 +353,6 @@
         [HBM] * 3,
     )
     peer_packs = from_peers(pack)
-    seed_rows = jnp.where(seed_mask[:, None] > 0, profiles, 0.0)
     one_tile = pltpu.VMEM((size, size), F32)
     hl, own_weights, row_sum, col_sum = kernel_call(
         lambda *refs: own_weights_kernel(blocks, *refs),
@@ -330,12 +365,18 @@
     weights = [own_weights]
     for step, (_, offsets) in enumerate(steps):
         last = step + 1 == len(steps)
+        if last:
+            seed_rows, seeds = kernel_call(
+                seeds_kernel, "seeds", [seed_mask.reshape(chunks, LANES), profiles, row_sum], (f32_rows, bf16_rows), 1
+            )
+            peer_seeds = from_peers(seeds)
         ins = [pack, peer_packs[step], hl, row_sum, col_sum]
+        degrees = jax.ShapeDtypeStruct((2 * chunks, LANES), F32)
         out = kernel_call(
             lambda *refs, offsets=offsets, last=last: peer_weights_kernel((blocks, last), offsets, *refs),
             "peer_weights",
             ins,
-            (weights_of(blocks * blocks), f32_rows) if last else (weights_of(blocks * blocks), f32_rows, f32_rows),
+            (weights_of(blocks * blocks), degrees) if last else (weights_of(blocks * blocks), f32_rows, f32_rows),
             blocks * blocks * tile_flops,
             [pltpu.VMEM((mols, LANES), F32)] * 2 + [one_tile] if last else [one_tile],
         )
@@ -344,13 +385,17 @@
             degree = out[1]
         else:
             row_sum, col_sum = out[1:]
+    scales = kernel_call(degree_kernel, "degree", [degree, other_core(degree)], degrees, 1)
+    scales, peer_seeds[0] = lax.optimization_barrier((scales, peer_seeds[0]))
+    peer_scales = from_peers(scales)
     scaled, row_scale, col_scale = kernel_call(
-        scale_kernel, "scale", [degree, other_core(degree), seed_rows], (bf16_rows, f32_rows, f32_rows), 1
+        expand_kernel, "expand", [scales, seed_rows], (bf16_rows, f32_rows, f32_rows), 1
     )
     for iteration in range(ITERS):
-        peers = from_peers(scaled)
+        first = iteration == 0
+        peers = peer_seeds if first else from_peers(scaled)
         partial = kernel_call(
-            lambda *refs: product_kernel(blocks, None, *refs),
+            lambda *refs: product_kernel(blocks, None, False, *refs),
             "own_product",
             [pack, weights[0], scaled],
             f32_rows,
@@ -358,11 +403,12 @@
         )
         for step, (_, offsets) in enumerate(steps):
             partial = kernel_call(
-                lambda *refs, offsets=offsets: product_kernel(blocks, offsets, *refs),
+                lambda *refs, offsets=offsets, first=first: product_kernel(blocks, offsets, first, *refs),
                 "peer_product",
-                [pack, weights[1 + step], peers[step], partial],
+                [pack, weights[1 + step], peers[step]] + [peer_scales[step]] * first + [partial],
                 f32_rows,
                 blocks * blocks * tile_flops,
+                [pltpu.VMEM((mols, LANES), BF16)] * first,
             )
         other = other_core(partial)
         if iteration + 1 < ITERS:

time: 59.4 us -> 55.7 us (0.938)
  the two profiles are of different devices: /device:TPU:17 before, /device:TPU:19 now
where the time goes in v6:
time: 55.7 us; the launch traced here: 55.5 us
  starting transfers between devices  24.3 us (44%)
  waiting for transfers between devices  17.9 us (32%)
  Pallas kernels  12.3 us (22%)
  other arithmetic  0.89 us (2%)
    ppermute x12, starting transfers between devices, to_peer(): return lax.ppermute(value, ('row', 'col'), steps[step][0])  19.5 us
    ppermute x12, waiting for transfers between devices, to_peer(): return lax.ppermute(value, ('row', 'col'), steps[step][0])  14 us
    pallas_call x17, Pallas kernels, kernel_call(): pl.pallas_call(body, out_shape=outs, in_specs=in_specs or [VMEM] * len(in...  12.3 us
    ppermute x3, starting transfers between devices, other_core(): return lax.ppermute(value, 'col', [(0, 1), (1, 0)])  4.8 us
    ppermute x3, waiting for transfers between devices, other_core(): return lax.ppermute(value, 'col', [(0, 1), (1, 0)])  3.9 us
  transfers between devices with their start and end apart: 15, of which 8 were waited for; matrix products, arithmetic and copies ran while one was open for 0% of the time, Pallas kernels for 17%

profile of v6, /device:TPU:19, one launch (start us, length us, event | category | flops | bytes accessed | tf_op | source)
XLA Modules:
  0.0 55.5 jit_solution(3880352969796695156)
XLA Ops:
  0.0 1.0 %pack.1.refs_0_ = bf16[1040,128]{1,0:T(8,128)(2,1)S(1)} custom-call(bf16[1024,128]{1,0:T(8,128)(2,1)} %refs_0_.1, s32[2,13]{1,0:T(2,128)} %refs_1_.1, s32[2]{0:T(128)} %refs_2_.1), custom_call_target="tpu_custom_call" | custom-call | flops 1 | bytes 1048576 | tf_op jit(solution)/shard_map/pack/pallas_call | solution.py:301
  1.0 1.9 %collective-permute-start.2 = (bf16[1040,128]{1,0:T(8,128)(2,1)S(1)}, bf16[1040,128]{1,0:T(8,128)(2,1)S(1)}, u32[]{:S(2)}, u32[]{:S(2)}) collective-permute-start(bf16[1040,128]{1,0:T(8,128)(2,1)S(1)} %pack.1.refs_0_), channel_id=1, source_target_pairs={{0,2},{1,4},{3,6},{5,8},{7,10},{9,12},{11,14},{13,15},{2,0},{4,1},... | collective-permute-start | bytes 798728 | tf_op jit(solution)/shard_map/ppermute | solution.py:329
  2.9 1.1 %collective-permute-start = (bf16[1040,128]{1,0:T(8,128)(2,1)S(1)}, bf16[1040,128]{1,0:T(8,128)(2,1)S(1)}, u32[]{:S(2)}, u32[]{:S(2)}) collective-permute-start(bf16[1040,128]{1,0:T(8,128)(2,1)S(1)} %pack.1.refs_0_), channel_id=1, source_target_pairs={{0,6},{4,10},{7,8},{9,14},{2,3},{12,13},{1,5},{11,15},{6,0},{10,4}... | collective-permute-start | bytes 798728 | tf_op jit(solution)/shard_map/ppermute | solution.py:329
  4.8 2.9 %collective-permute-done.2.refs_1_ = bf16[1040,128]{1,0:T(8,128)(2,1)S(1)} collective-permute-done((bf16[1040,128]{1,0:T(8,128)(2,1)S(1)}, bf16[1040,128]{1,0:T(8,128)(2,1)S(1)}, u32[]{:S(2)}, u32[]{:S(2)}) %collective-permute-start.2) | collective-permute-done | bytes 266272 | tf_op jit(solution)/shard_map/ppermute | solution.py:329
  7.7 1.1 %peer_weights.3 = (bf16[4,512,512]{2,1,0:T(8,128)(2,1)S(1)}, f32[1024,128]{1,0:T(8,128)S(1)}, f32[1024,128]{1,0:T(8,128)S(1)}) custom-call(bf16[1040,128]{1,0:T(8,128)(2,1)S(1)} %pack.1.refs_0_, bf16[1040,128]{1,0:T(8,128)(2,1)S(1)} %collective-permute-done.2.refs_1_, bf16[1024,256]{1,0:T(8,128)(2,1)S(1)} %get-tuple-element.24.refs_2_, ...), custom_call_target="tpu_custom_call" | custom-call | flops 536870912 | bytes 1048576 | tf_op jit(solution)/shard_map/peer_weights/pallas_call | solution.py:301
  8.8 1.1 %peer_weights.4 = (bf16[4,512,512]{2,1,0:T(8,128)(2,1)S(1)}, f32[1024,128]{1,0:T(8,128)S(1)}, f32[1024,128]{1,0:T(8,128)S(1)}) custom-call(bf16[1040,128]{1,0:T(8,128)(2,1)S(1)} %pack.1.refs_0_, bf16[1040,128]{1,0:T(8,128)(2,1)S(1)} %collective-permute-done.1.refs_1_, bf16[1024,256]{1,0:T(8,128)(2,1)S(1)} %get-tuple-element.24.refs_2_, ...), custom_call_target="tpu_custom_call" | custom-call | flops 536870912 | bytes 1048576 | tf_op jit(solution)/shard_map/peer_weights/pallas_call | solution.py:301
  10.3 5.5 %collective-permute-start.5 = (bf16[1024,128]{1,0:T(8,128)(2,1)S(1)}, bf16[1024,128]{1,0:T(8,128)(2,1)S(1)}, u32[]{:S(2)}, u32[]{:S(2)}) collective-permute-start(bf16[1024,128]{1,0:T(8,128)(2,1)S(1)} %get-tuple-element.32), channel_id=1, source_target_pairs={{0,2},{1,4},{3,6},{5,8},{7,10},{9,12},{11,14},{13,15},{2,0},{4,1},... | collective-permute-start | bytes 786440 | tf_op jit(solution)/shard_map/ppermute | solution.py:329
  15.8 1.8 %collective-permute-start.7 = (bf16[1024,128]{1,0:T(8,128)(2,1)S(1)}, bf16[1024,128]{1,0:T(8,128)(2,1)S(1)}, u32[]{:S(2)}, u32[]{:S(2)}) collective-permute-start(bf16[1024,128]{1,0:T(8,128)(2,1)S(1)} %get-tuple-element.32), channel_id=1, source_target_pairs={{2,4},{3,8},{5,6},{7,12},{9,10},{11,13},{0,1},{14,15},{4,2},{8,3},... | collective-permute-start | bytes 786440 | tf_op jit(solution)/shard_map/ppermute | solution.py:329
  18.0 1.3 %peer_weights.5 = (bf16[4,512,512]{2,1,0:T(8,128)(2,1)S(1)}, f32[16,128]{1,0:T(8,128)S(1)}) custom-call(bf16[1040,128]{1,0:T(8,128)(2,1)S(1)} %pack.1.refs_0_, bf16[1040,128]{1,0:T(8,128)(2,1)S(1)} %collective-permute-done.refs_1_, bf16[1024,256]{1,0:T(8,128)(2,1)S(1)} %get-tuple-element.24.refs_2_, f32[1024,128]{1,0:T(8,128)S(1)} %get-tuple-element.29.refs_3_.after_ref, ...), custom_call_target="tpu_custom_call" | custom-call | flops 536870912 | bytes 1048576 | tf_op jit(solution)/shard_map/peer_weights/pallas_call | solution.py:301
  21.0 1.5 %collective-permute-done.5.refs_2_ = bf16[1024,128]{1,0:T(8,128)(2,1)S(1)} collective-permute-done((bf16[1024,128]{1,0:T(8,128)(2,1)S(1)}, bf16[1024,128]{1,0:T(8,128)(2,1)S(1)}, u32[]{:S(2)}, u32[]{:S(2)}) %collective-permute-start.5) | collective-permute-done | bytes 262176 | tf_op jit(solution)/shard_map/ppermute | solution.py:329
  22.5 1.2 %collective-permute-start.8 = (f32[16,128]{1,0:T(8,128)S(1)}, f32[16,128]{1,0:T(8,128)S(1)}, u32[]{:S(2)}, u32[]{:S(2)}) collective-permute-start(f32[16,128]{1,0:T(8,128)S(1)} %degree.1.scales_ref), channel_id=1, source_target_pairs={{2,4},{3,8},{5,6},{7,12},{9,10},{11,13},{0,1},{14,15},{4,2},{8,3},... | collective-permute-start | bytes 24584 | tf_op jit(solution)/shard_map/ppermute | solution.py:329
  23.7 5.0 %collective-permute-start.6 = (f32[16,128]{1,0:T(8,128)S(1)}, f32[16,128]{1,0:T(8,128)S(1)}, u32[]{:S(2)}, u32[]{:S(2)}) collective-permute-start(f32[16,128]{1,0:T(8,128)S(1)} %degree.1.scales_ref), channel_id=1, source_target_pairs={{0,6},{4,10},{7,8},{9,14},{2,3},{12,13},{1,5},{11,15},{6,0},{10,4}... | collective-permute-start | bytes 24584 | tf_op jit(solution)/shard_map/ppermute | solution.py:329
  29.7 0.9 %peer_product.6.refs_4_ = f32[1024,128]{1,0:T(8,128)S(1)} custom-call(bf16[1040,128]{1,0:T(8,128)(2,1)S(1)} %pack.1.refs_0_, bf16[4,512,512]{2,1,0:T(8,128)(2,1)S(1)} %get-tuple-element.36.refs_1_, bf16[1024,128]{1,0:T(8,128)(2,1)S(1)} %collective-permute-done.5.refs_2_, f32[16,128]{1,0:T(8,128)S(1)} %collective-permute-done.9.refs_3_, ...), custom_call_target="tpu_custom_call" | custom-call | flops 536870912 | bytes 1048576 | tf_op jit(solution)/shard_map/peer_product/pallas_call | solution.py:301
  30.7 0.9 %peer_product.7.refs_4_ = f32[1024,128]{1,0:T(8,128)S(1)} custom-call(bf16[1040,128]{1,0:T(8,128)(2,1)S(1)} %pack.1.refs_0_, bf16[4,512,512]{2,1,0:T(8,128)(2,1)S(1)} %get-tuple-element.35.refs_1_, bf16[1024,128]{1,0:T(8,128)(2,1)S(1)} %collective-permute-done.7.refs_2_, f32[16,128]{1,0:T(8,128)S(1)} %collective-permute-done.8.refs_3_, ...), custom_call_target="tpu_custom_call" | custom-call | flops 536870912 | bytes 1048576 | tf_op jit(solution)/shard_map/peer_product/pallas_call | solution.py:301
  31.6 0.9 %peer_product.8.own_ref = f32[1024,128]{1,0:T(8,128)S(1)} custom-call(bf16[1040,128]{1,0:T(8,128)(2,1)S(1)} %pack.1.refs_0_, bf16[4,512,512]{2,1,0:T(8,128)(2,1)S(1)} %get-tuple-element.31.refs_1_, bf16[1024,128]{1,0:T(8,128)(2,1)S(1)} %collective-permute-done.3.refs_2_, f32[16,128]{1,0:T(8,128)S(1)} %collective-permute-done.6.refs_3_, ...), custom_call_target="tpu_custom_call" | custom-call | flops 536870912 | bytes 1048576 | tf_op jit(solution)/shard_map/peer_product/pallas_call | solution.py:301
  32.5 0.9 %collective-permute-start.10 = (f32[1024,128]{1,0:T(8,128)S(1)}, f32[1024,128]{1,0:T(8,128)S(1)}, u32[]{:S(2)}, u32[]{:S(2)}) collective-permute-start(f32[1024,128]{1,0:T(8,128)S(1)} %peer_product.8.own_ref), channel_id=1, source_target_pairs={{0,1},{1,0},{2,3},{3,2},{4,5},{5,4},{6,7},{7,6},{8,9},{9,8},{10,11... | collective-permute-start | bytes 1572872 | tf_op jit(solution)/shard_map/ppermute | solution.py:335
  33.4 1.5 %collective-permute-done.10.other_ref = f32[1024,128]{1,0:T(8,128)S(1)} collective-permute-done((f32[1024,128]{1,0:T(8,128)S(1)}, f32[1024,128]{1,0:T(8,128)S(1)}, u32[]{:S(2)}, u32[]{:S(2)}) %collective-permute-start.10) | collective-permute-done | bytes 524320 | tf_op jit(solution)/shard_map/ppermute | solution.py:335
  35.0 1.3 %collective-permute-start.13 = (bf16[1024,128]{1,0:T(8,128)(2,1)S(1)}, bf16[1024,128]{1,0:T(8,128)(2,1)S(1)}, u32[]{:S(2)}, u32[]{:S(2)}) collective-permute-start(bf16[1024,128]{1,0:T(8,128)(2,1)S(1)} %state.1.refs_2_), channel_id=1, source_target_pairs={{0,2},{1,4},{3,6},{5,8},{7,10},{9,12},{11,14},{13,15},{2,0},{4,1},... | collective-permute-start | bytes 786440 | tf_op jit(solution)/shard_map/ppermute | solution.py:329
  38.1 5.7 %collective-permute-done.13.refs_2_ = bf16[1024,128]{1,0:T(8,128)(2,1)S(1)} collective-permute-done((bf16[1024,128]{1,0:T(8,128)(2,1)S(1)}, bf16[1024,128]{1,0:T(8,128)(2,1)S(1)}, u32[]{:S(2)}, u32[]{:S(2)}) %collective-permute-start.13) | collective-permute-done | bytes 262176 | tf_op jit(solution)/shard_map/ppermute | solution.py:329
  44.7 1.0 %collective-permute-done.12.refs_2_ = bf16[1024,128]{1,0:T(8,128)(2,1)S(1)} collective-permute-done((bf16[1024,128]{1,0:T(8,128)(2,1)S(1)}, bf16[1024,128]{1,0:T(8,128)(2,1)S(1)}, u32[]{:S(2)}, u32[]{:S(2)}) %collective-permute-start.12) | collective-permute-done | bytes 262176 | tf_op jit(solution)/shard_map/ppermute | solution.py:329
  46.5 2.8 %collective-permute-done.11.refs_2_ = bf16[1024,128]{1,0:T(8,128)(2,1)S(1)} collective-permute-done((bf16[1024,128]{1,0:T(8,128)(2,1)S(1)}, bf16[1024,128]{1,0:T(8,128)(2,1)S(1)}, u32[]{:S(2)}, u32[]{:S(2)}) %collective-permute-start.11) | collective-permute-done | bytes 262176 | tf_op jit(solution)/shard_map/ppermute | solution.py:329
  50.1 3.0 %collective-permute-start.14 = (f32[1024,128]{1,0:T(8,128)S(1)}, f32[1024,128]{1,0:T(8,128)S(1)}, u32[]{:S(2)}, u32[]{:S(2)}) collective-permute-start(f32[1024,128]{1,0:T(8,128)S(1)} %peer_product.11), channel_id=1, source_target_pairs={{0,1},{1,0},{2,3},{3,2},{4,5},{5,4},{6,7},{7,6},{8,9},{9,8},{10,11... | collective-permute-start | bytes 1572872 | tf_op jit(solution)/shard_map/ppermute | solution.py:335
  53.1 1.5 %collective-permute-done.14 = f32[1024,128]{1,0:T(8,128)S(1)} collective-permute-done((f32[1024,128]{1,0:T(8,128)S(1)}, f32[1024,128]{1,0:T(8,128)S(1)}, u32[]{:S(2)}, u32[]{:S(2)}) %collective-permute-start.14) | collective-permute-done | bytes 524320 | tf_op jit(solution)/shard_map/ppermute | solution.py:335
  54.7 0.9 %multiply_add_fusion = f32[1024,128]{1,0:T(8,128)} fusion(f32[1024,128]{1,0:T(8,128)S(1)} %get-tuple-element.39.seed_ref, f32[1024,128]{1,0:T(8,128)S(1)} %get-tuple-element.41.rs_ref, f32[1024,128]{1,0:T(8,128)S(1)} %peer_product.11, f32[1024,128]{1,0:T(8,128)S(1)} %collective-permute-done.14), kind=kLoop, calls=%fused_computation | loop fusion | flops 524288 | bytes 2621440 | tf_op jit(solution)/shard_map/add | solution.py:418
  (28 shorter events, 8.5 us)
Async XLA Ops:
  1.0 6.7 %collective-permute-start.2 = (bf16[1040,128]{1,0:T(8,128)(2,1)S(1)}, bf16[1040,128]{1,0:T(8,128)(2,1)S(1)}, u32[]{:S(2)}, u32[]{:S(2)}) collective-permute-start(bf16[1040,128]{1,0:T(8,128)(2,1)S(1)} %pack.1.refs_0_), channel_id=1, source_target_pairs={{0,2},{1,4},{3,6},{5,8},{7,10},{9,12},{11,14},{13,15},{2,0},{4,1},... | collective-permute-start | bytes 798728 | tf_op jit(solution)/shard_map/ppermute | solution.py:329
  2.9 5.9 %collective-permute-start.1 = (bf16[1040,128]{1,0:T(8,128)(2,1)S(1)}, bf16[1040,128]{1,0:T(8,128)(2,1)S(1)}, u32[]{:S(2)}, u32[]{:S(2)}) collective-permute-start(bf16[1040,128]{1,0:T(8,128)(2,1)S(1)} %pack.1.refs_0_), channel_id=1, source_target_pairs={{2,4},{3,8},{5,6},{7,12},{9,10},{11,13},{0,1},{14,15},{4,2},{8,3},... | collective-permute-start | bytes 798728 | tf_op jit(solution)/shard_map/ppermute | solution.py:329
  2.9 15.1 %collective-permute-start = (bf16[1040,128]{1,0:T(8,128)(2,1)S(1)}, bf16[1040,128]{1,0:T(8,128)(2,1)S(1)}, u32[]{:S(2)}, u32[]{:S(2)}) collective-permute-start(bf16[1040,128]{1,0:T(8,128)(2,1)S(1)} %pack.1.refs_0_), channel_id=1, source_target_pairs={{0,6},{4,10},{7,8},{9,14},{2,3},{12,13},{1,5},{11,15},{6,0},{10,4}... | collective-permute-start | bytes 798728 | tf_op jit(solution)/shard_map/ppermute | solution.py:329
  7.7 2.3 %copy-start = (f32[1024,128]{1,0:T(8,128)S(1)}, f32[1024,128]{1,0:T(8,128)}, u32[]{:S(2)}) copy-start(f32[1024,128]{1,0:T(8,128)} %profile_ref.1) | copy-start | bytes 1572868
  7.7 2.3 %copy-start.1 = (s32[1024]{0:T(1024)S(1)}, s32[1024]{0:T(1024)}, u32[]{:S(2)}) copy-start(s32[1024]{0:T(1024)} %param.7) | copy-start | bytes 12292
  10.3 12.2 %collective-permute-start.5 = (bf16[1024,128]{1,0:T(8,128)(2,1)S(1)}, bf16[1024,128]{1,0:T(8,128)(2,1)S(1)}, u32[]{:S(2)}, u32[]{:S(2)}) collective-permute-start(bf16[1024,128]{1,0:T(8,128)(2,1)S(1)} %get-tuple-element.32), channel_id=1, source_target_pairs={{0,2},{1,4},{3,6},{5,8},{7,10},{9,12},{11,14},{13,15},{2,0},{4,1},... | collective-permute-start | bytes 786440 | tf_op jit(solution)/shard_map/ppermute | solution.py:329
  15.8 14.8 %collective-permute-start.7 = (bf16[1024,128]{1,0:T(8,128)(2,1)S(1)}, bf16[1024,128]{1,0:T(8,128)(2,1)S(1)}, u32[]{:S(2)}, u32[]{:S(2)}) collective-permute-start(bf16[1024,128]{1,0:T(8,128)(2,1)S(1)} %get-tuple-element.32), channel_id=1, source_target_pairs={{2,4},{3,8},{5,6},{7,12},{9,10},{11,13},{0,1},{14,15},{4,2},{8,3},... | collective-permute-start | bytes 786440 | tf_op jit(solution)/shard_map/ppermute | solution.py:329
  17.6 13.9 %collective-permute-start.3 = (bf16[1024,128]{1,0:T(8,128)(2,1)S(1)}, bf16[1024,128]{1,0:T(8,128)(2,1)S(1)}, u32[]{:S(2)}, u32[]{:S(2)}) collective-permute-start(bf16[1024,128]{1,0:T(8,128)(2,1)S(1)} %get-tuple-element.32), channel_id=1, source_target_pairs={{0,6},{4,10},{7,8},{9,14},{2,3},{12,13},{1,5},{11,15},{6,0},{10,4}... | collective-permute-start | bytes 786440 | tf_op jit(solution)/shard_map/ppermute | solution.py:329
  19.3 1.7 %collective-permute-start.4 = (f32[16,128]{1,0:T(8,128)S(1)}, f32[16,128]{1,0:T(8,128)S(1)}, u32[]{:S(2)}, u32[]{:S(2)}) collective-permute-start(f32[16,128]{1,0:T(8,128)S(1)} %get-tuple-element.33.own_ref), channel_id=1, source_target_pairs={{0,1},{1,0},{2,3},{3,2},{4,5},{5,4},{6,7},{7,6},{8,9},{9,8},{10,11... | collective-permute-start | bytes 24584 | tf_op jit(solution)/shard_map/ppermute | solution.py:335
  22.5 7.2 %collective-permute-start.9 = (f32[16,128]{1,0:T(8,128)S(1)}, f32[16,128]{1,0:T(8,128)S(1)}, u32[]{:S(2)}, u32[]{:S(2)}) collective-permute-start(f32[16,128]{1,0:T(8,128)S(1)} %degree.1.scales_ref), channel_id=1, source_target_pairs={{0,2},{1,4},{3,6},{5,8},{7,10},{9,12},{11,14},{13,15},{2,0},{4,1},... | collective-permute-start | bytes 24584 | tf_op jit(solution)/shard_map/ppermute | solution.py:329
  22.5 8.1 %collective-permute-start.8 = (f32[16,128]{1,0:T(8,128)S(1)}, f32[16,128]{1,0:T(8,128)S(1)}, u32[]{:S(2)}, u32[]{:S(2)}) collective-permute-start(f32[16,128]{1,0:T(8,128)S(1)} %degree.1.scales_ref), channel_id=1, source_target_pairs={{2,4},{3,8},{5,6},{7,12},{9,10},{11,13},{0,1},{14,15},{4,2},{8,3},... | collective-permute-start | bytes 24584 | tf_op jit(solution)/shard_map/ppermute | solution.py:329
  23.7 7.8 %collective-permute-start.6 = (f32[16,128]{1,0:T(8,128)S(1)}, f32[16,128]{1,0:T(8,128)S(1)}, u32[]{:S(2)}, u32[]{:S(2)}) collective-permute-start(f32[16,128]{1,0:T(8,128)S(1)} %degree.1.scales_ref), channel_id=1, source_target_pairs={{0,6},{4,10},{7,8},{9,14},{2,3},{12,13},{1,5},{11,15},{6,0},{10,4}... | collective-permute-start | bytes 24584 | tf_op jit(solution)/shard_map/ppermute | solution.py:329
  32.5 2.4 %collective-permute-start.10 = (f32[1024,128]{1,0:T(8,128)S(1)}, f32[1024,128]{1,0:T(8,128)S(1)}, u32[]{:S(2)}, u32[]{:S(2)}) collective-permute-start(f32[1024,128]{1,0:T(8,128)S(1)} %peer_product.8.own_ref), channel_id=1, source_target_pairs={{0,1},{1,0},{2,3},{3,2},{4,5},{5,4},{6,7},{7,6},{8,9},{9,8},{10,11... | collective-permute-start | bytes 1572872 | tf_op jit(solution)/shard_map/ppermute | solution.py:335
  35.0 8.8 %collective-permute-start.13 = (bf16[1024,128]{1,0:T(8,128)(2,1)S(1)}, bf16[1024,128]{1,0:T(8,128)(2,1)S(1)}, u32[]{:S(2)}, u32[]{:S(2)}) collective-permute-start(bf16[1024,128]{1,0:T(8,128)(2,1)S(1)} %state.1.refs_2_), channel_id=1, source_target_pairs={{0,2},{1,4},{3,6},{5,8},{7,10},{9,12},{11,14},{13,15},{2,0},{4,1},... | collective-permute-start | bytes 786440 | tf_op jit(solution)/shard_map/ppermute | solution.py:329
  36.3 9.4 %collective-permute-start.12 = (bf16[1024,128]{1,0:T(8,128)(2,1)S(1)}, bf16[1024,128]{1,0:T(8,128)(2,1)S(1)}, u32[]{:S(2)}, u32[]{:S(2)}) collective-permute-start(bf16[1024,128]{1,0:T(8,128)(2,1)S(1)} %state.1.refs_2_), channel_id=1, source_target_pairs={{2,4},{3,8},{5,6},{7,12},{9,10},{11,13},{0,1},{14,15},{4,2},{8,3},... | collective-permute-start | bytes 786440 | tf_op jit(solution)/shard_map/ppermute | solution.py:329
  36.8 12.5 %collective-permute-start.11 = (bf16[1024,128]{1,0:T(8,128)(2,1)S(1)}, bf16[1024,128]{1,0:T(8,128)(2,1)S(1)}, u32[]{:S(2)}, u32[]{:S(2)}) collective-permute-start(bf16[1024,128]{1,0:T(8,128)(2,1)S(1)} %state.1.refs_2_), channel_id=1, source_target_pairs={{0,6},{4,10},{7,8},{9,14},{2,3},{12,13},{1,5},{11,15},{6,0},{10,4}... | collective-permute-start | bytes 786440 | tf_op jit(solution)/shard_map/ppermute | solution.py:329
  50.1 4.6 %collective-permute-start.14 = (f32[1024,128]{1,0:T(8,128)S(1)}, f32[1024,128]{1,0:T(8,128)S(1)}, u32[]{:S(2)}, u32[]{:S(2)}) collective-permute-start(f32[1024,128]{1,0:T(8,128)S(1)} %peer_product.11), channel_id=1, source_target_pairs={{0,1},{1,0},{2,3},{3,2},{4,5},{5,4},{6,7},{7,6},{8,9},{9,8},{10,11... | collective-permute-start | bytes 1572872 | tf_op jit(solution)/shard_map/ppermute | solution.py:335

commit v7 on v6

--- a/solution.py
+++ b/solution.py
@@ -1,5 +1,3 @@
-import itertools
-
 import jax
 import jax.numpy as jnp
 from jax import lax
@@ -24,76 +22,85 @@
 PARAMS = pltpu.CompilerParams(vmem_limit_bytes=24 * 1024 * 1024)
 
 
-def search_steps(rows, reach):
-    if reach != 3 or rows < 8:
-        return None
-    edges = [(a, a + d) for a in range(rows) for d in range(1, reach + 1) if a + d < rows]
-
-    def solve(room):
-        chosen = []
-
-        def place(n):
-            done = edges[n][0] if n < len(edges) else rows
-            if any(room[chip][step] for chip in range(max(done - reach, 0), done) for step in range(reach)):
-                return False
-            if n == len(edges):
-                return True
-            a, b = edges[n]
-            for k in range(reach):
-                step = (b - a - 1 + k) % reach
-                if room[a][step] and room[b][step]:
-                    room[a][step] -= 1
-                    room[b][step] -= 1
-                    chosen.append(step)
-                    if place(n + 1):
-                        return True
-                    room[a][step] += 1
-                    room[b][step] += 1
-                    chosen.pop()
-            return False
-
-        return chosen if place(0) else None
-
-    best, best_moved = None, None
-    orders = list(itertools.permutations(range(reach)))
-    for low, near_low, high, near_high in itertools.product(orders, range(reach), orders, range(reach)):
-        room = [[2] * reach for _ in range(rows)]
-        for chip, way, order, near in ((0, 1, low, near_low), (rows - 1, -1, high, near_high)):
-            for k in range(reach):
-                room[chip][order[k]] = k
-            room[chip + way][near] = 0
-            room[chip + 2 * way][order[1]] = 1
-        chosen = solve(room)
-        if chosen is not None:
-            moved = sum(step != b - a - 1 for (a, b), step in zip(edges, chosen))
-            if best is None or moved < best_moved:
-                best, best_moved = chosen, moved
-    if best is None:
-        return None
-    return [[e for e, s in zip(edges, best) if s == step] for step in range(reach)]
-
-
-def swap_steps(rows, cols, reach):
-    chip_steps = search_steps(rows, reach)
-    if chip_steps is None:
-        chip_steps = [[(a, a + d) for a in range(rows - d)] for d in range(1, reach + 1)]
+FORWARD = (True, True, True)
+
+
+def distance_of(chip, device, cols):
+    return abs(chip - device // cols)
+
+
+def complete(moves, rows, cols, fixed):
+    moves = dict(moves)
+    sources = [n for n in range(rows * cols) if n not in moves]
+    targets = [n for n in range(rows * cols) if n not in moves.values()]
+    for s in list(sources):
+        other = [t for t in targets if t // cols == s // cols and t != s]
+        if other:
+            moves[s] = other[0]
+            sources.remove(s)
+            targets.remove(other[0])
+    for s in list(sources):
+        if s in targets:
+            y = s ^ 1
+            if fixed:
+                moves[s] = moves[y]
+                moves[y] = s
+            else:
+                z = next(n for n, t in moves.items() if t == y)
+                moves[z] = s
+                moves[s] = y
+            sources.remove(s)
+            targets.remove(s)
+    for s, t in zip(sources, targets):
+        moves[s] = t
+    return moves
+
+
+def landings(moves, origin, rows, cols, distance):
+    table = [[0] * rows for _ in range(cols)]
+    for s, t in moves.items():
+        if origin(s) is not None and distance_of(origin(s), t, cols) == distance:
+            table[t % cols][t // cols] = origin(s) - t // cols
+    return table
+
+
+def exchange_steps(rows, cols, reach):
     steps = []
-    for chip_pairs in chip_steps:
-        free = [list(range(cols)) for _ in range(rows)]
-        offsets = [[0] * rows for _ in range(cols)]
-        swaps = []
-        for a, b in chip_pairs:
-            core_a, core_b = free[a].pop(0), free[b].pop(0)
-            swaps.append((a * cols + core_a, b * cols + core_b))
-            offsets[core_a][a], offsets[core_b][b] = b - a, a - b
-        idle = []
-        for chip, cores in enumerate(free):
-            if len(cores) == 2:
-                swaps.append((chip * cols + cores[0], chip * cols + cores[1]))
-            else:
-                idle += [chip * cols + core for core in cores]
-        swaps += list(zip(idle[::2], idle[1::2]))
-        steps.append((swaps + [(b, a) for a, b in swaps], offsets))
+    for d in range(1, reach + 1):
+        if d < 3:
+            moves = {}
+            for a in range(rows - d):
+                core = a // d % cols
+                moves[a * cols + core] = (a + d) * cols + core
+                moves[(a + d) * cols + core] = a * cols + core
+            moves = complete(moves, rows, cols, False)
+            table = landings(moves, lambda s: s // cols, rows, cols, d)
+            steps.append((moves, table, moves))
+            continue
+        held = steps[d - 3][1]
+
+        def origin(s, held=held):
+            offset = held[s % cols][s // cols]
+            return s // cols + offset if offset else None
+
+        moves, taken = {}, [0] * rows
+        for s in range(rows * cols):
+            if origin(s) is not None:
+                t = s // cols + (2 if origin(s) < s // cols else -2)
+                if 0 <= t < rows:
+                    moves[s] = t * cols + taken[t]
+                    taken[t] += 1
+        moves = complete(moves, rows, cols, False)
+        table = landings(moves, origin, rows, cols, d)
+        direct, sent = {}, [0] * rows
+        for chip in range(rows):
+            for core in range(cols):
+                if table[core][chip]:
+                    source = chip + table[core][chip]
+                    direct[source * cols + sent[source]] = chip * cols + core
+                    sent[source] += 1
+        direct = complete(direct, rows, cols, True)
+        steps.append((moves, table, direct))
     return steps
 
 
@@ -318,18 +325,22 @@
     size = mols // blocks
     reach = (BAND + blocks - 1) // blocks
     assert blocks == 2 and cols == 2 and width == LANES and prof == LANES
-    steps = swap_steps(rows, cols, reach)
-    if len(steps) == 3:
-        steps = [steps[1], steps[0], steps[2]]
+    steps = exchange_steps(rows, cols, reach)
     f32_rows = jax.ShapeDtypeStruct((mols, LANES), F32)
     bf16_rows = jax.ShapeDtypeStruct((mols, LANES), BF16)
     tile_flops = 4 * size * size * width
 
     def to_peer(value, step):
-        return lax.ppermute(value, ("row", "col"), steps[step][0])
-
-    def from_peers(value):
-        return [to_peer(value, step) for step in range(len(steps))]
+        return lax.ppermute(value, ("row", "col"), list(steps[step][2].items()))
+
+    def from_peers(value, forward=False):
+        pieces = []
+        for step, (moves, _, _) in enumerate(steps):
+            if forward and step > 1:
+                pieces.append(lax.ppermute(pieces[step - 2], ("row", "col"), list(moves.items())))
+            else:
+                pieces.append(to_peer(value, step))
+        return pieces
 
     def other_core(value):
         return lax.ppermute(value, "col", [(0, 1), (1, 0)])
@@ -352,7 +363,7 @@
         ],
         [HBM] * 3,
     )
-    peer_packs = from_peers(pack)
+    peer_packs = from_peers(pack, FORWARD[0])
     one_tile = pltpu.VMEM((size, size), F32)
     hl, own_weights, row_sum, col_sum = kernel_call(
         lambda *refs: own_weights_kernel(blocks, *refs),
@@ -362,14 +373,15 @@
         blocks * tile_flops,
         [one_tile],
     )
-    weights = [own_weights]
-    for step, (_, offsets) in enumerate(steps):
-        last = step + 1 == len(steps)
-        if last:
+    weights = [own_weights] + [None] * len(steps)
+    for rank, step in enumerate([1, 0, 2]):
+        offsets = steps[step][1]
+        last = rank + 1 == len(steps)
+        if rank == 0:
             seed_rows, seeds = kernel_call(
                 seeds_kernel, "seeds", [seed_mask.reshape(chunks, LANES), profiles, row_sum], (f32_rows, bf16_rows), 1
             )
-            peer_seeds = from_peers(seeds)
+            peer_seeds = from_peers(seeds, FORWARD[1])
         ins = [pack, peer_packs[step], hl, row_sum, col_sum]
         degrees = jax.ShapeDtypeStruct((2 * chunks, LANES), F32)
         out = kernel_call(
@@ -380,20 +392,21 @@
             blocks * blocks * tile_flops,
             [pltpu.VMEM((mols, LANES), F32)] * 2 + [one_tile] if last else [one_tile],
         )
-        weights.append(out[0])
+        weights[1 + step] = out[0]
         if last:
             degree = out[1]
         else:
             row_sum, col_sum = out[1:]
     scales = kernel_call(degree_kernel, "degree", [degree, other_core(degree)], degrees, 1)
-    scales, peer_seeds[0] = lax.optimization_barrier((scales, peer_seeds[0]))
-    peer_scales = from_peers(scales)
+    peer_scales = [to_peer(scales, step) for step in range(len(steps) - 1)]
+    held_scales, peer_seeds[0] = lax.optimization_barrier((scales, peer_seeds[0]))
+    peer_scales.append(to_peer(held_scales, len(steps) - 1))
     scaled, row_scale, col_scale = kernel_call(
         expand_kernel, "expand", [scales, seed_rows], (bf16_rows, f32_rows, f32_rows), 1
     )
     for iteration in range(ITERS):
         first = iteration == 0
-        peers = peer_seeds if first else from_peers(scaled)
+        peers = peer_seeds if first else from_peers(scaled, FORWARD[2])
         partial = kernel_call(
             lambda *refs: product_kernel(blocks, None, False, *refs),
             "own_product",
@@ -401,7 +414,8 @@
             f32_rows,
             blocks * tile_flops,
         )
-        for step, (_, offsets) in enumerate(steps):
+        for step in [1, 0, 2]:
+            offsets = steps[step][1]
             partial = kernel_call(
                 lambda *refs, offsets=offsets, first=first: product_kernel(blocks, offsets, first, *refs),
                 "peer_product",

time: 55.7 us -> 51.8 us (0.930)
  the two profiles are of different devices: /device:TPU:19 before, /device:TPU:0 now
where the time goes in v7:
time: 51.8 us; the launch traced here: 51.6 us
  waiting for transfers between devices  21.8 us (42%)
  starting transfers between devices  14.6 us (28%)
  Pallas kernels  12.4 us (24%)
  local copies, waits for them, and re-layouts  1.72 us (3%)
  other arithmetic  0.89 us (2%)
    ppermute x9, starting transfers between devices, to_peer(): return lax.ppermute(value, ('row', 'col'), list(steps[step][2].items()))  14.4 us
    ppermute x9, waiting for transfers between devices, to_peer(): return lax.ppermute(value, ('row', 'col'), list(steps[step][2].items()))  12.6 us
    pallas_call x17, Pallas kernels, kernel_call(): pl.pallas_call(body, out_shape=outs, in_specs=in_specs or [VMEM] * len(in...  12.4 us
    ppermute x3, waiting for transfers between devices, other_core(): return lax.ppermute(value, 'col', [(0, 1), (1, 0)])  4.95 us
    ppermute x3, waiting for transfers between devices, from_peers(): lax.ppermute(pieces[step - 2], ('row', 'col'), list(moves.items()))  4.3 us
    unnamed x4, local copies, waits for them, and re-layouts  1.72 us
  transfers between devices with their start and end apart: 15, of which 8 were waited for; matrix products, arithmetic and copies ran while one was open for 0% of the time, Pallas kernels for 19%

profile of v7, /device:TPU:0, one launch (start us, length us, event | category | flops | bytes accessed | tf_op | source)
XLA Modules:
  0.0 51.6 jit_solution(7784690406129189369)
XLA Ops:
  0.0 1.0 %pack.1.refs_0_ = bf16[1040,128]{1,0:T(8,128)(2,1)S(1)} custom-call(bf16[1024,128]{1,0:T(8,128)(2,1)} %refs_0_.1, s32[2,13]{1,0:T(2,128)} %refs_1_.1, s32[2]{0:T(128)} %refs_2_.1), custom_call_target="tpu_custom_call" | custom-call | flops 1 | bytes 1048576 | tf_op jit(solution)/shard_map/pack/pallas_call | solution.py:308
  1.0 3.0 %collective-permute-start = (bf16[1040,128]{1,0:T(8,128)(2,1)S(1)}, bf16[1040,128]{1,0:T(8,128)(2,1)S(1)}, u32[]{:S(2)}, u32[]{:S(2)}) collective-permute-start(bf16[1040,128]{1,0:T(8,128)(2,1)S(1)} %pack.1.refs_0_), channel_id=1, source_target_pairs={{0,2},{2,1},{3,5},{5,3},{4,6},{6,4},{7,9},{9,7},{8,10},{10,8},{11,... | collective-permute-start | bytes 798728 | tf_op jit(solution)/shard_map/ppermute | solution.py:334
  4.0 1.6 %collective-permute-start.2 = (bf16[1040,128]{1,0:T(8,128)(2,1)S(1)}, bf16[1040,128]{1,0:T(8,128)(2,1)S(1)}, u32[]{:S(2)}, u32[]{:S(2)}) collective-permute-start(bf16[1040,128]{1,0:T(8,128)(2,1)S(1)} %pack.1.refs_0_), channel_id=1, source_target_pairs={{0,4},{4,1},{2,6},{6,3},{5,9},{9,5},{7,11},{11,7},{8,13},{12,8},{1... | collective-permute-start | bytes 798728 | tf_op jit(solution)/shard_map/ppermute | solution.py:334
  6.4 1.0 %copy-done = f32[1024,128]{1,0:T(8,128)S(1)} copy-done((f32[1024,128]{1,0:T(8,128)S(1)}, f32[1024,128]{1,0:T(8,128)}, u32[]{:S(2)}) %copy-start) | copy-done | bytes 524312
  9.0 2.7 %collective-permute-done.refs_1_ = bf16[1040,128]{1,0:T(8,128)(2,1)S(1)} collective-permute-done((bf16[1040,128]{1,0:T(8,128)(2,1)S(1)}, bf16[1040,128]{1,0:T(8,128)(2,1)S(1)}, u32[]{:S(2)}, u32[]{:S(2)}) %collective-permute-start) | collective-permute-done | bytes 266272 | tf_op jit(solution)/shard_map/ppermute | solution.py:334
  11.7 2.0 %collective-permute-start.8 = (bf16[1024,128]{1,0:T(8,128)(2,1)S(1)}, bf16[1024,128]{1,0:T(8,128)(2,1)S(1)}, u32[]{:S(2)}, u32[]{:S(2)}) collective-permute-start(bf16[1024,128]{1,0:T(8,128)(2,1)S(1)} %get-tuple-element.32), channel_id=1, source_target_pairs={{0,4},{4,1},{2,6},{6,3},{5,9},{9,5},{7,11},{11,7},{8,13},{12,8},{1... | collective-permute-start | bytes 786440 | tf_op jit(solution)/shard_map/ppermute | solution.py:334
  13.7 2.4 %collective-permute-done.3.refs_2_ = bf16[1024,128]{1,0:T(8,128)(2,1)S(1)} collective-permute-done((bf16[1024,128]{1,0:T(8,128)(2,1)S(1)}, bf16[1024,128]{1,0:T(8,128)(2,1)S(1)}, u32[]{:S(2)}, u32[]{:S(2)}) %collective-permute-start.3) | collective-permute-done | bytes 262176 | tf_op jit(solution)/shard_map/ppermute | solution.py:334
  16.2 1.1 %peer_weights.3 = (bf16[4,512,512]{2,1,0:T(8,128)(2,1)S(1)}, f32[1024,128]{1,0:T(8,128)S(1)}, f32[1024,128]{1,0:T(8,128)S(1)}) custom-call(bf16[1040,128]{1,0:T(8,128)(2,1)S(1)} %pack.1.refs_0_, bf16[1040,128]{1,0:T(8,128)(2,1)S(1)} %collective-permute-done.2.refs_1_, bf16[1024,256]{1,0:T(8,128)(2,1)S(1)} %get-tuple-element.24.refs_2_, ...), custom_call_target="tpu_custom_call" | custom-call | flops 536870912 | bytes 1048576 | tf_op jit(solution)/shard_map/peer_weights/pallas_call | solution.py:308
  17.3 1.1 %peer_weights.4 = (bf16[4,512,512]{2,1,0:T(8,128)(2,1)S(1)}, f32[1024,128]{1,0:T(8,128)S(1)}, f32[1024,128]{1,0:T(8,128)S(1)}) custom-call(bf16[1040,128]{1,0:T(8,128)(2,1)S(1)} %pack.1.refs_0_, bf16[1040,128]{1,0:T(8,128)(2,1)S(1)} %collective-permute-done.refs_1_, bf16[1024,256]{1,0:T(8,128)(2,1)S(1)} %get-tuple-element.24.refs_2_, ...), custom_call_target="tpu_custom_call" | custom-call | flops 536870912 | bytes 1048576 | tf_op jit(solution)/shard_map/peer_weights/pallas_call | solution.py:308
  18.5 1.3 %peer_weights.5 = (bf16[4,512,512]{2,1,0:T(8,128)(2,1)S(1)}, f32[16,128]{1,0:T(8,128)S(1)}) custom-call(bf16[1040,128]{1,0:T(8,128)(2,1)S(1)} %pack.1.refs_0_, bf16[1040,128]{1,0:T(8,128)(2,1)S(1)} %collective-permute-done.1.refs_1_, bf16[1024,256]{1,0:T(8,128)(2,1)S(1)} %get-tuple-element.24.refs_2_, f32[1024,128]{1,0:T(8,128)S(1)} %get-tuple-element.29.refs_3_, ...), custom_call_target="tpu_custom_call" | custom-call | flops 536870912 | bytes 1048576 | tf_op jit(solution)/shard_map/peer_weights/pallas_call | solution.py:308
  19.8 1.2 %collective-permute-done.5.other_ref = f32[16,128]{1,0:T(8,128)S(1)} collective-permute-done((f32[16,128]{1,0:T(8,128)S(1)}, f32[16,128]{1,0:T(8,128)S(1)}, u32[]{:S(2)}, u32[]{:S(2)}) %collective-permute-start.5) | collective-permute-done | bytes 8224 | tf_op jit(solution)/shard_map/ppermute | solution.py:346
  21.0 3.9 %collective-permute-start.9 = (f32[16,128]{1,0:T(8,128)S(1)}, f32[16,128]{1,0:T(8,128)S(1)}, u32[]{:S(2)}, u32[]{:S(2)}) collective-permute-start(f32[16,128]{1,0:T(8,128)S(1)} %degree.1.scales_ref), channel_id=1, source_target_pairs={{0,4},{4,1},{2,6},{6,3},{5,9},{9,5},{7,11},{11,7},{8,13},{12,8},{1... | collective-permute-start | bytes 24584 | tf_op jit(solution)/shard_map/ppermute | solution.py:334
  24.9 1.7 %collective-permute-start.7 = (f32[16,128]{1,0:T(8,128)S(1)}, f32[16,128]{1,0:T(8,128)S(1)}, u32[]{:S(2)}, u32[]{:S(2)}) collective-permute-start(f32[16,128]{1,0:T(8,128)S(1)} %degree.1.scales_ref), channel_id=1, source_target_pairs={{0,2},{2,1},{3,5},{5,3},{4,6},{6,4},{7,9},{9,7},{8,10},{10,8},{11,... | collective-permute-start | bytes 24584 | tf_op jit(solution)/shard_map/ppermute | solution.py:334
  27.7 0.9 %peer_product.6.refs_4_ = f32[1024,128]{1,0:T(8,128)S(1)} custom-call(bf16[1040,128]{1,0:T(8,128)(2,1)S(1)} %pack.1.refs_0_, bf16[4,512,512]{2,1,0:T(8,128)(2,1)S(1)} %get-tuple-element.37.refs_1_, bf16[1024,128]{1,0:T(8,128)(2,1)S(1)} %collective-permute-done.8.refs_2_, f32[16,128]{1,0:T(8,128)S(1)} %collective-permute-done.9.refs_3_, ...), custom_call_target="tpu_custom_call" | custom-call | flops 536870912 | bytes 1048576 | tf_op jit(solution)/shard_map/peer_product/pallas_call | solution.py:308
  28.6 0.9 %peer_product.7.refs_4_ = f32[1024,128]{1,0:T(8,128)S(1)} custom-call(bf16[1040,128]{1,0:T(8,128)(2,1)S(1)} %pack.1.refs_0_, bf16[4,512,512]{2,1,0:T(8,128)(2,1)S(1)} %get-tuple-element.35.refs_1_, bf16[1024,128]{1,0:T(8,128)(2,1)S(1)} %collective-permute-done.3.refs_2_, f32[16,128]{1,0:T(8,128)S(1)} %collective-permute-done.7.refs_3_, ...), custom_call_target="tpu_custom_call" | custom-call | flops 536870912 | bytes 1048576 | tf_op jit(solution)/shard_map/peer_product/pallas_call | solution.py:308
  29.5 2.2 %collective-permute-done.6.refs_3_ = f32[16,128]{1,0:T(8,128)S(1)} collective-permute-done((f32[16,128]{1,0:T(8,128)S(1)}, f32[16,128]{1,0:T(8,128)S(1)}, u32[]{:S(2)}, u32[]{:S(2)}) %collective-permute-start.6) | collective-permute-done | bytes 8224 | tf_op jit(solution)/shard_map/ppermute | solution.py:334
  31.7 0.9 %peer_product.8.own_ref = f32[1024,128]{1,0:T(8,128)S(1)} custom-call(bf16[1040,128]{1,0:T(8,128)(2,1)S(1)} %pack.1.refs_0_, bf16[4,512,512]{2,1,0:T(8,128)(2,1)S(1)} %get-tuple-element.31.refs_1_, bf16[1024,128]{1,0:T(8,128)(2,1)S(1)} %collective-permute-done.4.refs_2_, f32[16,128]{1,0:T(8,128)S(1)} %collective-permute-done.6.refs_3_, ...), custom_call_target="tpu_custom_call" | custom-call | flops 536870912 | bytes 1048576 | tf_op jit(solution)/shard_map/peer_product/pallas_call | solution.py:308
  32.7 1.9 %collective-permute-done.10.other_ref = f32[1024,128]{1,0:T(8,128)S(1)} collective-permute-done((f32[1024,128]{1,0:T(8,128)S(1)}, f32[1024,128]{1,0:T(8,128)S(1)}, u32[]{:S(2)}, u32[]{:S(2)}) %collective-permute-start.10) | collective-permute-done | bytes 524320 | tf_op jit(solution)/shard_map/ppermute | solution.py:346
  34.8 1.5 %collective-permute-start.13 = (bf16[1024,128]{1,0:T(8,128)(2,1)S(1)}, bf16[1024,128]{1,0:T(8,128)(2,1)S(1)}, u32[]{:S(2)}, u32[]{:S(2)}) collective-permute-start(bf16[1024,128]{1,0:T(8,128)(2,1)S(1)} %state.1.refs_2_), channel_id=1, source_target_pairs={{0,4},{4,1},{2,6},{6,3},{5,9},{9,5},{7,11},{11,7},{8,13},{12,8},{1... | collective-permute-start | bytes 786440 | tf_op jit(solution)/shard_map/ppermute | solution.py:334
  36.3 5.2 %collective-permute-done.11.refs_2_ = bf16[1024,128]{1,0:T(8,128)(2,1)S(1)} collective-permute-done((bf16[1024,128]{1,0:T(8,128)(2,1)S(1)}, bf16[1024,128]{1,0:T(8,128)(2,1)S(1)}, u32[]{:S(2)}, u32[]{:S(2)}) %collective-permute-start.11) | collective-permute-done | bytes 262176 | tf_op jit(solution)/shard_map/ppermute | solution.py:334
  42.8 0.8 %peer_product.10.refs_3_ = f32[1024,128]{1,0:T(8,128)S(1)} custom-call(bf16[1040,128]{1,0:T(8,128)(2,1)S(1)} %pack.1.refs_0_, bf16[4,512,512]{2,1,0:T(8,128)(2,1)S(1)} %get-tuple-element.35.refs_1_, bf16[1024,128]{1,0:T(8,128)(2,1)S(1)} %collective-permute-done.11.refs_2_, f32[1024,128]{1,0:T(8,128)S(1)} %peer_product.9.refs_3_), custom_call_target="tpu_custom_call" | custom-call | flops 536870912 | bytes 1048576 | tf_op jit(solution)/shard_map/peer_product/pallas_call | solution.py:308
  43.7 4.3 %collective-permute-done.12.refs_2_ = bf16[1024,128]{1,0:T(8,128)(2,1)S(1)} collective-permute-done((bf16[1024,128]{1,0:T(8,128)(2,1)S(1)}, bf16[1024,128]{1,0:T(8,128)(2,1)S(1)}, u32[]{:S(2)}, u32[]{:S(2)}) %collective-permute-start.12) | collective-permute-done | bytes 262176 | tf_op jit(solution)/shard_map/ppermute | solution.py:340
  48.8 1.9 %collective-permute-done.14 = f32[1024,128]{1,0:T(8,128)S(1)} collective-permute-done((f32[1024,128]{1,0:T(8,128)S(1)}, f32[1024,128]{1,0:T(8,128)S(1)}, u32[]{:S(2)}, u32[]{:S(2)}) %collective-permute-start.14) | collective-permute-done | bytes 524320 | tf_op jit(solution)/shard_map/ppermute | solution.py:346
  50.7 0.9 %multiply_add_fusion = f32[1024,128]{1,0:T(8,128)} fusion(f32[1024,128]{1,0:T(8,128)S(1)} %get-tuple-element.39.seed_ref, f32[1024,128]{1,0:T(8,128)S(1)} %get-tuple-element.41.rs_ref, f32[1024,128]{1,0:T(8,128)S(1)} %peer_product.11, f32[1024,128]{1,0:T(8,128)S(1)} %collective-permute-done.14), kind=kLoop, calls=%fused_computation | loop fusion | flops 524288 | bytes 2621440 | tf_op jit(solution)/shard_map/add | solution.py:432
  (28 shorter events, 6.0 us)
Async XLA Ops:
  1.0 10.7 %collective-permute-start = (bf16[1040,128]{1,0:T(8,128)(2,1)S(1)}, bf16[1040,128]{1,0:T(8,128)(2,1)S(1)}, u32[]{:S(2)}, u32[]{:S(2)}) collective-permute-start(bf16[1040,128]{1,0:T(8,128)(2,1)S(1)} %pack.1.refs_0_), channel_id=1, source_target_pairs={{0,2},{2,1},{3,5},{5,3},{4,6},{6,4},{7,9},{9,7},{8,10},{10,8},{11,... | collective-permute-start | bytes 798728 | tf_op jit(solution)/shard_map/ppermute | solution.py:334
  4.0 12.2 %collective-permute-start.2 = (bf16[1040,128]{1,0:T(8,128)(2,1)S(1)}, bf16[1040,128]{1,0:T(8,128)(2,1)S(1)}, u32[]{:S(2)}, u32[]{:S(2)}) collective-permute-start(bf16[1040,128]{1,0:T(8,128)(2,1)S(1)} %pack.1.refs_0_), channel_id=1, source_target_pairs={{0,4},{4,1},{2,6},{6,3},{5,9},{9,5},{7,11},{11,7},{8,13},{12,8},{1... | collective-permute-start | bytes 798728 | tf_op jit(solution)/shard_map/ppermute | solution.py:334
  6.4 1.0 %copy-start = (f32[1024,128]{1,0:T(8,128)S(1)}, f32[1024,128]{1,0:T(8,128)}, u32[]{:S(2)}) copy-start(f32[1024,128]{1,0:T(8,128)} %profile_ref.1) | copy-start | bytes 1572868
  7.4 0.7 %copy-start.1 = (s32[1024]{0:T(1024)S(1)}, s32[1024]{0:T(1024)}, u32[]{:S(2)}) copy-start(s32[1024]{0:T(1024)} %param.7) | copy-start | bytes 12292
  8.4 7.7 %collective-permute-start.3 = (bf16[1024,128]{1,0:T(8,128)(2,1)S(1)}, bf16[1024,128]{1,0:T(8,128)(2,1)S(1)}, u32[]{:S(2)}, u32[]{:S(2)}) collective-permute-start(bf16[1024,128]{1,0:T(8,128)(2,1)S(1)} %get-tuple-element.32), channel_id=1, source_target_pairs={{0,2},{2,1},{3,5},{5,3},{4,6},{6,4},{7,9},{9,7},{8,10},{10,8},{11,... | collective-permute-start | bytes 786440 | tf_op jit(solution)/shard_map/ppermute | solution.py:334
  11.7 6.8 %collective-permute-start.1 = (bf16[1040,128]{1,0:T(8,128)(2,1)S(1)}, bf16[1040,128]{1,0:T(8,128)(2,1)S(1)}, u32[]{:S(2)}, u32[]{:S(2)}) collective-permute-start(bf16[1040,128]{1,0:T(8,128)(2,1)S(1)} %collective-permute-done.refs_1_), channel_id=1, source_target_pairs={{2,6},{4,0},{5,8},{6,10},{7,3},{8,4},{9,13},{10,14},{11,7},{12,9},... | collective-permute-start | bytes 798728 | tf_op jit(solution)/shard_map/ppermute | solution.py:340
  11.7 16.0 %collective-permute-start.8 = (bf16[1024,128]{1,0:T(8,128)(2,1)S(1)}, bf16[1024,128]{1,0:T(8,128)(2,1)S(1)}, u32[]{:S(2)}, u32[]{:S(2)}) collective-permute-start(bf16[1024,128]{1,0:T(8,128)(2,1)S(1)} %get-tuple-element.32), channel_id=1, source_target_pairs={{0,4},{4,1},{2,6},{6,3},{5,9},{9,5},{7,11},{11,7},{8,13},{12,8},{1... | collective-permute-start | bytes 786440 | tf_op jit(solution)/shard_map/ppermute | solution.py:334
  16.2 13.3 %collective-permute-start.4 = (bf16[1024,128]{1,0:T(8,128)(2,1)S(1)}, bf16[1024,128]{1,0:T(8,128)(2,1)S(1)}, u32[]{:S(2)}, u32[]{:S(2)}) collective-permute-start(bf16[1024,128]{1,0:T(8,128)(2,1)S(1)} %collective-permute-done.3.refs_2_), channel_id=1, source_target_pairs={{2,6},{4,0},{5,8},{6,10},{7,3},{8,4},{9,13},{10,14},{11,7},{12,9},... | collective-permute-start | bytes 786440 | tf_op jit(solution)/shard_map/ppermute | solution.py:340
  19.8 1.2 %collective-permute-start.5 = (f32[16,128]{1,0:T(8,128)S(1)}, f32[16,128]{1,0:T(8,128)S(1)}, u32[]{:S(2)}, u32[]{:S(2)}) collective-permute-start(f32[16,128]{1,0:T(8,128)S(1)} %get-tuple-element.33.own_ref), channel_id=1, source_target_pairs={{0,1},{1,0},{2,3},{3,2},{4,5},{5,4},{6,7},{7,6},{8,9},{9,8},{10,11... | collective-permute-start | bytes 24584 | tf_op jit(solution)/shard_map/ppermute | solution.py:346
  21.0 6.7 %collective-permute-start.9 = (f32[16,128]{1,0:T(8,128)S(1)}, f32[16,128]{1,0:T(8,128)S(1)}, u32[]{:S(2)}, u32[]{:S(2)}) collective-permute-start(f32[16,128]{1,0:T(8,128)S(1)} %degree.1.scales_ref), channel_id=1, source_target_pairs={{0,4},{4,1},{2,6},{6,3},{5,9},{9,5},{7,11},{11,7},{8,13},{12,8},{1... | collective-permute-start | bytes 24584 | tf_op jit(solution)/shard_map/ppermute | solution.py:334
  24.9 3.7 %collective-permute-start.7 = (f32[16,128]{1,0:T(8,128)S(1)}, f32[16,128]{1,0:T(8,128)S(1)}, u32[]{:S(2)}, u32[]{:S(2)}) collective-permute-start(f32[16,128]{1,0:T(8,128)S(1)} %degree.1.scales_ref), channel_id=1, source_target_pairs={{0,2},{2,1},{3,5},{5,3},{4,6},{6,4},{7,9},{9,7},{8,10},{10,8},{11,... | collective-permute-start | bytes 24584 | tf_op jit(solution)/shard_map/ppermute | solution.py:334
  27.1 4.6 %collective-permute-start.6 = (f32[16,128]{1,0:T(8,128)S(1)}, f32[16,128]{1,0:T(8,128)S(1)}, u32[]{:S(2)}, u32[]{:S(2)}) collective-permute-start(f32[16,128]{1,0:T(8,128)S(1)} %degree.1.scales_ref), channel_id=1, source_target_pairs={{6,0},{8,3},{10,11},{0,1},{12,7},{2,8},{14,15},{4,5},{7,13},{9,14}... | collective-permute-start | bytes 24584 | tf_op jit(solution)/shard_map/ppermute | solution.py:334
  32.6 2.0 %collective-permute-start.10 = (f32[1024,128]{1,0:T(8,128)S(1)}, f32[1024,128]{1,0:T(8,128)S(1)}, u32[]{:S(2)}, u32[]{:S(2)}) collective-permute-start(f32[1024,128]{1,0:T(8,128)S(1)} %peer_product.8.own_ref), channel_id=1, source_target_pairs={{0,1},{1,0},{2,3},{3,2},{4,5},{5,4},{6,7},{7,6},{8,9},{9,8},{10,11... | collective-permute-start | bytes 1572872 | tf_op jit(solution)/shard_map/ppermute | solution.py:346
  34.7 6.8 %collective-permute-start.11 = (bf16[1024,128]{1,0:T(8,128)(2,1)S(1)}, bf16[1024,128]{1,0:T(8,128)(2,1)S(1)}, u32[]{:S(2)}, u32[]{:S(2)}) collective-permute-start(bf16[1024,128]{1,0:T(8,128)(2,1)S(1)} %state.1.refs_2_), channel_id=1, source_target_pairs={{0,2},{2,1},{3,5},{5,3},{4,6},{6,4},{7,9},{9,7},{8,10},{10,8},{11,... | collective-permute-start | bytes 786440 | tf_op jit(solution)/shard_map/ppermute | solution.py:334
  34.8 7.2 %collective-permute-start.13 = (bf16[1024,128]{1,0:T(8,128)(2,1)S(1)}, bf16[1024,128]{1,0:T(8,128)(2,1)S(1)}, u32[]{:S(2)}, u32[]{:S(2)}) collective-permute-start(bf16[1024,128]{1,0:T(8,128)(2,1)S(1)} %state.1.refs_2_), channel_id=1, source_target_pairs={{0,4},{4,1},{2,6},{6,3},{5,9},{9,5},{7,11},{11,7},{8,13},{12,8},{1... | collective-permute-start | bytes 786440 | tf_op jit(solution)/shard_map/ppermute | solution.py:334
  41.5 6.5 %collective-permute-start.12 = (bf16[1024,128]{1,0:T(8,128)(2,1)S(1)}, bf16[1024,128]{1,0:T(8,128)(2,1)S(1)}, u32[]{:S(2)}, u32[]{:S(2)}) collective-permute-start(bf16[1024,128]{1,0:T(8,128)(2,1)S(1)} %collective-permute-done.11.refs_2_), channel_id=1, source_target_pairs={{2,6},{4,0},{5,8},{6,10},{7,3},{8,4},{9,13},{10,14},{11,7},{12,9},... | collective-permute-start | bytes 786440 | tf_op jit(solution)/shard_map/ppermute | solution.py:340
  48.8 2.0 %collective-permute-start.14 = (f32[1024,128]{1,0:T(8,128)S(1)}, f32[1024,128]{1,0:T(8,128)S(1)}, u32[]{:S(2)}, u32[]{:S(2)}) collective-permute-start(f32[1024,128]{1,0:T(8,128)S(1)} %peer_product.11), channel_id=1, source_target_pairs={{0,1},{1,0},{2,3},{3,2},{4,5},{5,4},{6,7},{7,6},{8,9},{9,8},{10,11... | collective-permute-start | bytes 1572872 | tf_op jit(solution)/shard_map/ppermute | solution.py:346

commit v8 on v7

--- a/solution.py
+++ b/solution.py
@@ -296,11 +296,11 @@
             s = scaled_ref[pl.ds(k * size, size), :].astype(F32)
             s = (s * table_entry(table, b, offset)).astype(BF16)
             total = total + jnp.dot(w_ref[k * blocks + b], s, preferred_element_type=F32)
-        out_ref[at, :] = total
+        out_ref[at, :] = total.astype(out_ref.dtype)
 
 
 def state_kernel(own_ref, other_ref, rs_ref, seed_ref, cs_ref, out_ref):
-    state = (own_ref[...] + other_ref[...]) * rs_ref[...] + (1.0 - ALPHA) * seed_ref[...]
+    state = (own_ref[...].astype(F32) + other_ref[...].astype(F32)) * rs_ref[...] + (1.0 - ALPHA) * seed_ref[...]
     out_ref[...] = (state * cs_ref[...]).astype(BF16)
 
 
@@ -416,11 +416,12 @@
         )
         for step in [1, 0, 2]:
             offsets = steps[step][1]
+            final = step + 1 == len(steps)
             partial = kernel_call(
                 lambda *refs, offsets=offsets, first=first: product_kernel(blocks, offsets, first, *refs),
                 "peer_product",
                 [pack, weights[1 + step], peers[step]] + [peer_scales[step]] * first + [partial],
-                f32_rows,
+                bf16_rows if final else f32_rows,
                 blocks * blocks * tile_flops,
                 [pltpu.VMEM((mols, LANES), BF16)] * first,
             )
@@ -429,7 +430,7 @@
             scaled = kernel_call(
                 state_kernel, "state", [partial, other, row_scale, seed_rows, col_scale], bf16_rows, 1
             )
-    return (partial + other) * row_scale + (1.0 - ALPHA) * seed_rows
+    return (partial.astype(F32) + other.astype(F32)) * row_scale + (1.0 - ALPHA) * seed_rows
 
 
 def solution(mesh):

time: 51.8 us -> 51.1 us (0.986)
  waiting for transfers between devices: 21.8 us -> 21.1 us
    ppermute x3, waiting for transfers between devices: 4.95 us -> 4.2 us  [other_core(): return lax.ppermute(value, 'col', [(0, 1), (1, 0)])]
where the time goes in v8:
time: 51.1 us; the launch traced here: 50.9 us
  waiting for transfers between devices  21.1 us (41%)
  starting transfers between devices  14.6 us (29%)
  Pallas kernels  12.4 us (24%)
  local copies, waits for them, and re-layouts  1.72 us (3%)
  other arithmetic  0.9 us (2%)
    ppermute x9, starting transfers between devices, to_peer(): return lax.ppermute(value, ('row', 'col'), list(steps[step][2].items()))  14.4 us
    ppermute x9, waiting for transfers between devices, to_peer(): return lax.ppermute(value, ('row', 'col'), list(steps[step][2].items()))  12.6 us
    pallas_call x17, Pallas kernels, kernel_call(): pl.pallas_call(body, out_shape=outs, in_specs=in_specs or [VMEM] * len(in...  12.4 us
    ppermute x3, waiting for transfers between devices, from_peers(): lax.ppermute(pieces[step - 2], ('row', 'col'), list(moves.items()))  4.31 us
    ppermute x3, waiting for transfers between devices, other_core(): return lax.ppermute(value, 'col', [(0, 1), (1, 0)])  4.2 us
    unnamed x4, local copies, waits for them, and re-layouts  1.72 us
  transfers between devices with their start and end apart: 15, of which 8 were waited for; matrix products, arithmetic and copies ran while one was open for 0% of the time, Pallas kernels for 19%

profile of v8, /device:TPU:0, one launch (start us, length us, event | category | flops | bytes accessed | tf_op | source)
XLA Modules:
  0.0 50.9 jit_solution(8473785811527868261)
XLA Ops:
  0.0 1.0 %pack.1.refs_0_ = bf16[1040,128]{1,0:T(8,128)(2,1)S(1)} custom-call(bf16[1024,128]{1,0:T(8,128)(2,1)} %refs_0_.1, s32[2,13]{1,0:T(2,128)} %refs_1_.1, s32[2]{0:T(128)} %refs_2_.1), custom_call_target="tpu_custom_call" | custom-call | flops 1 | bytes 1048576 | tf_op jit(solution)/shard_map/pack/pallas_call | solution.py:308
  1.0 3.0 %collective-permute-start = (bf16[1040,128]{1,0:T(8,128)(2,1)S(1)}, bf16[1040,128]{1,0:T(8,128)(2,1)S(1)}, u32[]{:S(2)}, u32[]{:S(2)}) collective-permute-start(bf16[1040,128]{1,0:T(8,128)(2,1)S(1)} %pack.1.refs_0_), channel_id=1, source_target_pairs={{0,2},{2,1},{3,5},{5,3},{4,6},{6,4},{7,9},{9,7},{8,10},{10,8},{11,... | collective-permute-start | bytes 798728 | tf_op jit(solution)/shard_map/ppermute | solution.py:334
  4.0 1.6 %collective-permute-start.2 = (bf16[1040,128]{1,0:T(8,128)(2,1)S(1)}, bf16[1040,128]{1,0:T(8,128)(2,1)S(1)}, u32[]{:S(2)}, u32[]{:S(2)}) collective-permute-start(bf16[1040,128]{1,0:T(8,128)(2,1)S(1)} %pack.1.refs_0_), channel_id=1, source_target_pairs={{0,4},{4,1},{2,6},{6,3},{5,9},{9,5},{7,11},{11,7},{8,13},{12,8},{1... | collective-permute-start | bytes 798728 | tf_op jit(solution)/shard_map/ppermute | solution.py:334
  6.4 1.0 %copy-done = f32[1024,128]{1,0:T(8,128)S(1)} copy-done((f32[1024,128]{1,0:T(8,128)S(1)}, f32[1024,128]{1,0:T(8,128)}, u32[]{:S(2)}) %copy-start) | copy-done | bytes 524312
  9.0 2.7 %collective-permute-done.refs_1_ = bf16[1040,128]{1,0:T(8,128)(2,1)S(1)} collective-permute-done((bf16[1040,128]{1,0:T(8,128)(2,1)S(1)}, bf16[1040,128]{1,0:T(8,128)(2,1)S(1)}, u32[]{:S(2)}, u32[]{:S(2)}) %collective-permute-start) | collective-permute-done | bytes 266272 | tf_op jit(solution)/shard_map/ppermute | solution.py:334
  11.7 2.0 %collective-permute-start.8 = (bf16[1024,128]{1,0:T(8,128)(2,1)S(1)}, bf16[1024,128]{1,0:T(8,128)(2,1)S(1)}, u32[]{:S(2)}, u32[]{:S(2)}) collective-permute-start(bf16[1024,128]{1,0:T(8,128)(2,1)S(1)} %get-tuple-element.32), channel_id=1, source_target_pairs={{0,4},{4,1},{2,6},{6,3},{5,9},{9,5},{7,11},{11,7},{8,13},{12,8},{1... | collective-permute-start | bytes 786440 | tf_op jit(solution)/shard_map/ppermute | solution.py:334
  13.7 2.4 %collective-permute-done.3.refs_2_ = bf16[1024,128]{1,0:T(8,128)(2,1)S(1)} collective-permute-done((bf16[1024,128]{1,0:T(8,128)(2,1)S(1)}, bf16[1024,128]{1,0:T(8,128)(2,1)S(1)}, u32[]{:S(2)}, u32[]{:S(2)}) %collective-permute-start.3) | collective-permute-done | bytes 262176 | tf_op jit(solution)/shard_map/ppermute | solution.py:334
  16.2 1.1 %peer_weights.3 = (bf16[4,512,512]{2,1,0:T(8,128)(2,1)S(1)}, f32[1024,128]{1,0:T(8,128)S(1)}, f32[1024,128]{1,0:T(8,128)S(1)}) custom-call(bf16[1040,128]{1,0:T(8,128)(2,1)S(1)} %pack.1.refs_0_, bf16[1040,128]{1,0:T(8,128)(2,1)S(1)} %collective-permute-done.2.refs_1_, bf16[1024,256]{1,0:T(8,128)(2,1)S(1)} %get-tuple-element.24.refs_2_, ...), custom_call_target="tpu_custom_call" | custom-call | flops 536870912 | bytes 1048576 | tf_op jit(solution)/shard_map/peer_weights/pallas_call | solution.py:308
  17.3 1.1 %peer_weights.4 = (bf16[4,512,512]{2,1,0:T(8,128)(2,1)S(1)}, f32[1024,128]{1,0:T(8,128)S(1)}, f32[1024,128]{1,0:T(8,128)S(1)}) custom-call(bf16[1040,128]{1,0:T(8,128)(2,1)S(1)} %pack.1.refs_0_, bf16[1040,128]{1,0:T(8,128)(2,1)S(1)} %collective-permute-done.refs_1_, bf16[1024,256]{1,0:T(8,128)(2,1)S(1)} %get-tuple-element.24.refs_2_, ...), custom_call_target="tpu_custom_call" | custom-call | flops 536870912 | bytes 1048576 | tf_op jit(solution)/shard_map/peer_weights/pallas_call | solution.py:308
  18.5 1.3 %peer_weights.5 = (bf16[4,512,512]{2,1,0:T(8,128)(2,1)S(1)}, f32[16,128]{1,0:T(8,128)S(1)}) custom-call(bf16[1040,128]{1,0:T(8,128)(2,1)S(1)} %pack.1.refs_0_, bf16[1040,128]{1,0:T(8,128)(2,1)S(1)} %collective-permute-done.1.refs_1_, bf16[1024,256]{1,0:T(8,128)(2,1)S(1)} %get-tuple-element.24.refs_2_, f32[1024,128]{1,0:T(8,128)S(1)} %get-tuple-element.29.refs_3_, ...), custom_call_target="tpu_custom_call" | custom-call | flops 536870912 | bytes 1048576 | tf_op jit(solution)/shard_map/peer_weights/pallas_call | solution.py:308
  19.8 1.2 %collective-permute-done.5.other_ref = f32[16,128]{1,0:T(8,128)S(1)} collective-permute-done((f32[16,128]{1,0:T(8,128)S(1)}, f32[16,128]{1,0:T(8,128)S(1)}, u32[]{:S(2)}, u32[]{:S(2)}) %collective-permute-start.5) | collective-permute-done | bytes 8224 | tf_op jit(solution)/shard_map/ppermute | solution.py:346
  21.0 3.9 %collective-permute-start.9 = (f32[16,128]{1,0:T(8,128)S(1)}, f32[16,128]{1,0:T(8,128)S(1)}, u32[]{:S(2)}, u32[]{:S(2)}) collective-permute-start(f32[16,128]{1,0:T(8,128)S(1)} %degree.1.scales_ref), channel_id=1, source_target_pairs={{0,4},{4,1},{2,6},{6,3},{5,9},{9,5},{7,11},{11,7},{8,13},{12,8},{1... | collective-permute-start | bytes 24584 | tf_op jit(solution)/shard_map/ppermute | solution.py:334
  24.9 1.7 %collective-permute-start.7 = (f32[16,128]{1,0:T(8,128)S(1)}, f32[16,128]{1,0:T(8,128)S(1)}, u32[]{:S(2)}, u32[]{:S(2)}) collective-permute-start(f32[16,128]{1,0:T(8,128)S(1)} %degree.1.scales_ref), channel_id=1, source_target_pairs={{0,2},{2,1},{3,5},{5,3},{4,6},{6,4},{7,9},{9,7},{8,10},{10,8},{11,... | collective-permute-start | bytes 24584 | tf_op jit(solution)/shard_map/ppermute | solution.py:334
  27.7 0.9 %peer_product.6.refs_4_ = f32[1024,128]{1,0:T(8,128)S(1)} custom-call(bf16[1040,128]{1,0:T(8,128)(2,1)S(1)} %pack.1.refs_0_, bf16[4,512,512]{2,1,0:T(8,128)(2,1)S(1)} %get-tuple-element.37.refs_1_, bf16[1024,128]{1,0:T(8,128)(2,1)S(1)} %collective-permute-done.8.refs_2_, f32[16,128]{1,0:T(8,128)S(1)} %collective-permute-done.9.refs_3_, ...), custom_call_target="tpu_custom_call" | custom-call | flops 536870912 | bytes 1048576 | tf_op jit(solution)/shard_map/peer_product/pallas_call | solution.py:308
  28.6 0.9 %peer_product.7.refs_4_ = f32[1024,128]{1,0:T(8,128)S(1)} custom-call(bf16[1040,128]{1,0:T(8,128)(2,1)S(1)} %pack.1.refs_0_, bf16[4,512,512]{2,1,0:T(8,128)(2,1)S(1)} %get-tuple-element.35.refs_1_, bf16[1024,128]{1,0:T(8,128)(2,1)S(1)} %collective-permute-done.3.refs_2_, f32[16,128]{1,0:T(8,128)S(1)} %collective-permute-done.7.refs_3_, ...), custom_call_target="tpu_custom_call" | custom-call | flops 536870912 | bytes 1048576 | tf_op jit(solution)/shard_map/peer_product/pallas_call | solution.py:308
  29.5 2.2 %collective-permute-done.6.refs_3_ = f32[16,128]{1,0:T(8,128)S(1)} collective-permute-done((f32[16,128]{1,0:T(8,128)S(1)}, f32[16,128]{1,0:T(8,128)S(1)}, u32[]{:S(2)}, u32[]{:S(2)}) %collective-permute-start.6) | collective-permute-done | bytes 8224 | tf_op jit(solution)/shard_map/ppermute | solution.py:334
  31.7 0.9 %peer_product.8.own_ref = bf16[1024,128]{1,0:T(8,128)(2,1)S(1)} custom-call(bf16[1040,128]{1,0:T(8,128)(2,1)S(1)} %pack.1.refs_0_, bf16[4,512,512]{2,1,0:T(8,128)(2,1)S(1)} %get-tuple-element.31.refs_1_, bf16[1024,128]{1,0:T(8,128)(2,1)S(1)} %collective-permute-done.4.refs_2_, f32[16,128]{1,0:T(8,128)S(1)} %collective-permute-done.6.refs_3_, ...), custom_call_target="tpu_custom_call" | custom-call | flops 536870912 | bytes 1048576 | tf_op jit(solution)/shard_map/peer_product/pallas_call | solution.py:308
  32.7 1.5 %collective-permute-done.10.other_ref = bf16[1024,128]{1,0:T(8,128)(2,1)S(1)} collective-permute-done((bf16[1024,128]{1,0:T(8,128)(2,1)S(1)}, bf16[1024,128]{1,0:T(8,128)(2,1)S(1)}, u32[]{:S(2)}, u32[]{:S(2)}) %collective-permute-start.10) | collective-permute-done | bytes 262176 | tf_op jit(solution)/shard_map/ppermute | solution.py:346
  34.4 1.5 %collective-permute-start.13 = (bf16[1024,128]{1,0:T(8,128)(2,1)S(1)}, bf16[1024,128]{1,0:T(8,128)(2,1)S(1)}, u32[]{:S(2)}, u32[]{:S(2)}) collective-permute-start(bf16[1024,128]{1,0:T(8,128)(2,1)S(1)} %state.1.refs_2_), channel_id=1, source_target_pairs={{0,4},{4,1},{2,6},{6,3},{5,9},{9,5},{7,11},{11,7},{8,13},{12,8},{1... | collective-permute-start | bytes 786440 | tf_op jit(solution)/shard_map/ppermute | solution.py:334
  35.9 5.2 %collective-permute-done.11.refs_2_ = bf16[1024,128]{1,0:T(8,128)(2,1)S(1)} collective-permute-done((bf16[1024,128]{1,0:T(8,128)(2,1)S(1)}, bf16[1024,128]{1,0:T(8,128)(2,1)S(1)}, u32[]{:S(2)}, u32[]{:S(2)}) %collective-permute-start.11) | collective-permute-done | bytes 262176 | tf_op jit(solution)/shard_map/ppermute | solution.py:334
  42.5 0.8 %peer_product.10.refs_3_ = f32[1024,128]{1,0:T(8,128)S(1)} custom-call(bf16[1040,128]{1,0:T(8,128)(2,1)S(1)} %pack.1.refs_0_, bf16[4,512,512]{2,1,0:T(8,128)(2,1)S(1)} %get-tuple-element.35.refs_1_, bf16[1024,128]{1,0:T(8,128)(2,1)S(1)} %collective-permute-done.11.refs_2_, f32[1024,128]{1,0:T(8,128)S(1)} %peer_product.9.refs_3_), custom_call_target="tpu_custom_call" | custom-call | flops 536870912 | bytes 1048576 | tf_op jit(solution)/shard_map/peer_product/pallas_call | solution.py:308
  43.3 4.3 %collective-permute-done.12.refs_2_ = bf16[1024,128]{1,0:T(8,128)(2,1)S(1)} collective-permute-done((bf16[1024,128]{1,0:T(8,128)(2,1)S(1)}, bf16[1024,128]{1,0:T(8,128)(2,1)S(1)}, u32[]{:S(2)}, u32[]{:S(2)}) %collective-permute-start.12) | collective-permute-done | bytes 262176 | tf_op jit(solution)/shard_map/ppermute | solution.py:340
  48.5 1.5 %collective-permute-done.14 = bf16[1024,128]{1,0:T(8,128)(2,1)S(1)} collective-permute-done((bf16[1024,128]{1,0:T(8,128)(2,1)S(1)}, bf16[1024,128]{1,0:T(8,128)(2,1)S(1)}, u32[]{:S(2)}, u32[]{:S(2)}) %collective-permute-start.14) | collective-permute-done | bytes 262176 | tf_op jit(solution)/shard_map/ppermute | solution.py:346
  50.0 0.9 %multiply_add_fusion = f32[1024,128]{1,0:T(8,128)} fusion(f32[1024,128]{1,0:T(8,128)S(1)} %get-tuple-element.39.seed_ref, f32[1024,128]{1,0:T(8,128)S(1)} %get-tuple-element.41.rs_ref, bf16[1024,128]{1,0:T(8,128)(2,1)S(1)} %collective-permute-done.14, bf16[1024,128]{1,0:T(8,128)(2,1)S(1)} %peer_product.11), kind=kLoop, calls=%fused_computation | loop fusion | flops 786432 | bytes 2097152 | tf_op jit(solution)/shard_map/add | solution.py:433
  (28 shorter events, 6.0 us)
Async XLA Ops:
  1.0 10.7 %collective-permute-start = (bf16[1040,128]{1,0:T(8,128)(2,1)S(1)}, bf16[1040,128]{1,0:T(8,128)(2,1)S(1)}, u32[]{:S(2)}, u32[]{:S(2)}) collective-permute-start(bf16[1040,128]{1,0:T(8,128)(2,1)S(1)} %pack.1.refs_0_), channel_id=1, source_target_pairs={{0,2},{2,1},{3,5},{5,3},{4,6},{6,4},{7,9},{9,7},{8,10},{10,8},{11,... | collective-permute-start | bytes 798728 | tf_op jit(solution)/shard_map/ppermute | solution.py:334
  4.0 12.2 %collective-permute-start.2 = (bf16[1040,128]{1,0:T(8,128)(2,1)S(1)}, bf16[1040,128]{1,0:T(8,128)(2,1)S(1)}, u32[]{:S(2)}, u32[]{:S(2)}) collective-permute-start(bf16[1040,128]{1,0:T(8,128)(2,1)S(1)} %pack.1.refs_0_), channel_id=1, source_target_pairs={{0,4},{4,1},{2,6},{6,3},{5,9},{9,5},{7,11},{11,7},{8,13},{12,8},{1... | collective-permute-start | bytes 798728 | tf_op jit(solution)/shard_map/ppermute | solution.py:334
  6.4 1.0 %copy-start = (f32[1024,128]{1,0:T(8,128)S(1)}, f32[1024,128]{1,0:T(8,128)}, u32[]{:S(2)}) copy-start(f32[1024,128]{1,0:T(8,128)} %profile_ref.1) | copy-start | bytes 1572868
  7.4 0.7 %copy-start.1 = (s32[1024]{0:T(1024)S(1)}, s32[1024]{0:T(1024)}, u32[]{:S(2)}) copy-start(s32[1024]{0:T(1024)} %param.7) | copy-start | bytes 12292
  8.4 7.7 %collective-permute-start.3 = (bf16[1024,128]{1,0:T(8,128)(2,1)S(1)}, bf16[1024,128]{1,0:T(8,128)(2,1)S(1)}, u32[]{:S(2)}, u32[]{:S(2)}) collective-permute-start(bf16[1024,128]{1,0:T(8,128)(2,1)S(1)} %get-tuple-element.32), channel_id=1, source_target_pairs={{0,2},{2,1},{3,5},{5,3},{4,6},{6,4},{7,9},{9,7},{8,10},{10,8},{11,... | collective-permute-start | bytes 786440 | tf_op jit(solution)/shard_map/ppermute | solution.py:334
  11.7 6.8 %collective-permute-start.1 = (bf16[1040,128]{1,0:T(8,128)(2,1)S(1)}, bf16[1040,128]{1,0:T(8,128)(2,1)S(1)}, u32[]{:S(2)}, u32[]{:S(2)}) collective-permute-start(bf16[1040,128]{1,0:T(8,128)(2,1)S(1)} %collective-permute-done.refs_1_), channel_id=1, source_target_pairs={{2,6},{4,0},{5,8},{6,10},{7,3},{8,4},{9,13},{10,14},{11,7},{12,9},... | collective-permute-start | bytes 798728 | tf_op jit(solution)/shard_map/ppermute | solution.py:340
  11.7 16.0 %collective-permute-start.8 = (bf16[1024,128]{1,0:T(8,128)(2,1)S(1)}, bf16[1024,128]{1,0:T(8,128)(2,1)S(1)}, u32[]{:S(2)}, u32[]{:S(2)}) collective-permute-start(bf16[1024,128]{1,0:T(8,128)(2,1)S(1)} %get-tuple-element.32), channel_id=1, source_target_pairs={{0,4},{4,1},{2,6},{6,3},{5,9},{9,5},{7,11},{11,7},{8,13},{12,8},{1... | collective-permute-start | bytes 786440 | tf_op jit(solution)/shard_map/ppermute | solution.py:334
  16.2 13.3 %collective-permute-start.4 = (bf16[1024,128]{1,0:T(8,128)(2,1)S(1)}, bf16[1024,128]{1,0:T(8,128)(2,1)S(1)}, u32[]{:S(2)}, u32[]{:S(2)}) collective-permute-start(bf16[1024,128]{1,0:T(8,128)(2,1)S(1)} %collective-permute-done.3.refs_2_), channel_id=1, source_target_pairs={{2,6},{4,0},{5,8},{6,10},{7,3},{8,4},{9,13},{10,14},{11,7},{12,9},... | collective-permute-start | bytes 786440 | tf_op jit(solution)/shard_map/ppermute | solution.py:340
  19.8 1.2 %collective-permute-start.5 = (f32[16,128]{1,0:T(8,128)S(1)}, f32[16,128]{1,0:T(8,128)S(1)}, u32[]{:S(2)}, u32[]{:S(2)}) collective-permute-start(f32[16,128]{1,0:T(8,128)S(1)} %get-tuple-element.33.own_ref), channel_id=1, source_target_pairs={{0,1},{1,0},{2,3},{3,2},{4,5},{5,4},{6,7},{7,6},{8,9},{9,8},{10,11... | collective-permute-start | bytes 24584 | tf_op jit(solution)/shard_map/ppermute | solution.py:346
  21.0 6.7 %collective-permute-start.9 = (f32[16,128]{1,0:T(8,128)S(1)}, f32[16,128]{1,0:T(8,128)S(1)}, u32[]{:S(2)}, u32[]{:S(2)}) collective-permute-start(f32[16,128]{1,0:T(8,128)S(1)} %degree.1.scales_ref), channel_id=1, source_target_pairs={{0,4},{4,1},{2,6},{6,3},{5,9},{9,5},{7,11},{11,7},{8,13},{12,8},{1... | collective-permute-start | bytes 24584 | tf_op jit(solution)/shard_map/ppermute | solution.py:334
  24.9 3.7 %collective-permute-start.7 = (f32[16,128]{1,0:T(8,128)S(1)}, f32[16,128]{1,0:T(8,128)S(1)}, u32[]{:S(2)}, u32[]{:S(2)}) collective-permute-start(f32[16,128]{1,0:T(8,128)S(1)} %degree.1.scales_ref), channel_id=1, source_target_pairs={{0,2},{2,1},{3,5},{5,3},{4,6},{6,4},{7,9},{9,7},{8,10},{10,8},{11,... | collective-permute-start | bytes 24584 | tf_op jit(solution)/shard_map/ppermute | solution.py:334
  27.1 4.6 %collective-permute-start.6 = (f32[16,128]{1,0:T(8,128)S(1)}, f32[16,128]{1,0:T(8,128)S(1)}, u32[]{:S(2)}, u32[]{:S(2)}) collective-permute-start(f32[16,128]{1,0:T(8,128)S(1)} %degree.1.scales_ref), channel_id=1, source_target_pairs={{6,0},{8,3},{10,11},{0,1},{12,7},{2,8},{14,15},{4,5},{7,13},{9,14}... | collective-permute-start | bytes 24584 | tf_op jit(solution)/shard_map/ppermute | solution.py:334
  32.6 1.6 %collective-permute-start.10 = (bf16[1024,128]{1,0:T(8,128)(2,1)S(1)}, bf16[1024,128]{1,0:T(8,128)(2,1)S(1)}, u32[]{:S(2)}, u32[]{:S(2)}) collective-permute-start(bf16[1024,128]{1,0:T(8,128)(2,1)S(1)} %peer_product.8.own_ref), channel_id=1, source_target_pairs={{0,1},{1,0},{2,3},{3,2},{4,5},{5,4},{6,7},{7,6},{8,9},{9,8},{10,11... | collective-permute-start | bytes 786440 | tf_op jit(solution)/shard_map/ppermute | solution.py:346
  34.4 6.8 %collective-permute-start.11 = (bf16[1024,128]{1,0:T(8,128)(2,1)S(1)}, bf16[1024,128]{1,0:T(8,128)(2,1)S(1)}, u32[]{:S(2)}, u32[]{:S(2)}) collective-permute-start(bf16[1024,128]{1,0:T(8,128)(2,1)S(1)} %state.1.refs_2_), channel_id=1, source_target_pairs={{0,2},{2,1},{3,5},{5,3},{4,6},{6,4},{7,9},{9,7},{8,10},{10,8},{11,... | collective-permute-start | bytes 786440 | tf_op jit(solution)/shard_map/ppermute | solution.py:334
  34.4 7.2 %collective-permute-start.13 = (bf16[1024,128]{1,0:T(8,128)(2,1)S(1)}, bf16[1024,128]{1,0:T(8,128)(2,1)S(1)}, u32[]{:S(2)}, u32[]{:S(2)}) collective-permute-start(bf16[1024,128]{1,0:T(8,128)(2,1)S(1)} %state.1.refs_2_), channel_id=1, source_target_pairs={{0,4},{4,1},{2,6},{6,3},{5,9},{9,5},{7,11},{11,7},{8,13},{12,8},{1... | collective-permute-start | bytes 786440 | tf_op jit(solution)/shard_map/ppermute | solution.py:334
  41.1 6.5 %collective-permute-start.12 = (bf16[1024,128]{1,0:T(8,128)(2,1)S(1)}, bf16[1024,128]{1,0:T(8,128)(2,1)S(1)}, u32[]{:S(2)}, u32[]{:S(2)}) collective-permute-start(bf16[1024,128]{1,0:T(8,128)(2,1)S(1)} %collective-permute-done.11.refs_2_), channel_id=1, source_target_pairs={{2,6},{4,0},{5,8},{6,10},{7,3},{8,4},{9,13},{10,14},{11,7},{12,9},... | collective-permute-start | bytes 786440 | tf_op jit(solution)/shard_map/ppermute | solution.py:340
  48.4 1.6 %collective-permute-start.14 = (bf16[1024,128]{1,0:T(8,128)(2,1)S(1)}, bf16[1024,128]{1,0:T(8,128)(2,1)S(1)}, u32[]{:S(2)}, u32[]{:S(2)}) collective-permute-start(bf16[1024,128]{1,0:T(8,128)(2,1)S(1)} %peer_product.11), channel_id=1, source_target_pairs={{0,1},{1,0},{2,3},{3,2},{4,5},{5,4},{6,7},{7,6},{8,9},{9,8},{10,11... | collective-permute-start | bytes 786440 | tf_op jit(solution)/shard_map/ppermute | solution.py:346

commit v9 on v8

--- a/solution.py
+++ b/solution.py
@@ -381,7 +381,7 @@
             seed_rows, seeds = kernel_call(
                 seeds_kernel, "seeds", [seed_mask.reshape(chunks, LANES), profiles, row_sum], (f32_rows, bf16_rows), 1
             )
-            peer_seeds = from_peers(seeds, FORWARD[1])
+            peer_seeds = [to_peer(seeds, step) for step in range(min(2, len(steps)))]
         ins = [pack, peer_packs[step], hl, row_sum, col_sum]
         degrees = jax.ShapeDtypeStruct((2 * chunks, LANES), F32)
         out = kernel_call(
@@ -397,12 +397,16 @@
             degree = out[1]
         else:
             row_sum, col_sum = out[1:]
+        if rank == 0:
+            held_seeds, row_sum = lax.optimization_barrier((peer_seeds[0], row_sum))
+            peer_seeds.append(lax.ppermute(held_seeds, ("row", "col"), list(steps[2][0].items())))
     scales = kernel_call(degree_kernel, "degree", [degree, other_core(degree)], degrees, 1)
     peer_scales = [to_peer(scales, step) for step in range(len(steps) - 1)]
     held_scales, peer_seeds[0] = lax.optimization_barrier((scales, peer_seeds[0]))
     peer_scales.append(to_peer(held_scales, len(steps) - 1))
+    own_scales, peer_seeds[1] = lax.optimization_barrier((scales, peer_seeds[1]))
     scaled, row_scale, col_scale = kernel_call(
-        expand_kernel, "expand", [scales, seed_rows], (bf16_rows, f32_rows, f32_rows), 1
+        expand_kernel, "expand", [own_scales, seed_rows], (bf16_rows, f32_rows, f32_rows), 1
     )
     for iteration in range(ITERS):
         first = iteration == 0
@@ -414,6 +418,9 @@
             f32_rows,
             blocks * tile_flops,
         )
+        if not first:
+            held, partial = lax.optimization_barrier((scaled, partial))
+            peers[1] = to_peer(held, 1)
         for step in [1, 0, 2]:
             offsets = steps[step][1]
             final = step + 1 == len(steps)

time: 51.1 us -> 49.9 us (0.977)
  waiting for transfers between devices: 21.1 us -> 20 us
    ppermute x9, waiting for transfers between devices: 12.6 us -> 10.2 us  [to_peer(): return lax.ppermute(value, ('row', 'col'), list(steps[step][2].items()))]
    ppermute x3 -> x2, waiting for transfers between devices: 4.31 us -> 5.62 us  [from_peers(): lax.ppermute(pieces[step - 2], ('row', 'col'), list(moves.items()))]
  transfers between devices with their start and end apart: 15 -> 15, of which waited for: 8 -> 9; matrix products, arithmetic and copies ran while one was open for 0% -> 0% of each run, Pallas kernels for 19% -> 19%
where the time goes in v9:
time: 49.9 us; the launch traced here: 49.7 us
  waiting for transfers between devices  20 us (40%)
  starting transfers between devices  14.5 us (29%)
  Pallas kernels  12.4 us (25%)
  local copies, waits for them, and re-layouts  1.72 us (3%)
  other arithmetic  0.9 us (2%)
    ppermute x9, starting transfers between devices, to_peer(): return lax.ppermute(value, ('row', 'col'), list(steps[step][2].items()))  14.3 us
    pallas_call x17, Pallas kernels, kernel_call(): pl.pallas_call(body, out_shape=outs, in_specs=in_specs or [VMEM] * len(in...  12.4 us
    ppermute x9, waiting for transfers between devices, to_peer(): return lax.ppermute(value, ('row', 'col'), list(steps[step][2].items()))  10.2 us
    ppermute x2, waiting for transfers between devices, from_peers(): lax.ppermute(pieces[step - 2], ('row', 'col'), list(moves.items()))  5.62 us
    ppermute x3, waiting for transfers between devices, other_core(): return lax.ppermute(value, 'col', [(0, 1), (1, 0)])  4.2 us
    unnamed x4, local copies, waits for them, and re-layouts  1.72 us
  transfers between devices with their start and end apart: 15, of which 9 were waited for; matrix products, arithmetic and copies ran while one was open for 0% of the time, Pallas kernels for 19%

profile of v9, /device:TPU:0, one launch (start us, length us, event | category | flops | bytes accessed | tf_op | source)
XLA Modules:
  0.0 49.7 jit_solution(8881240692793007470)
XLA Ops:
  0.0 1.0 %pack.1.refs_0_ = bf16[1040,128]{1,0:T(8,128)(2,1)S(1)} custom-call(bf16[1024,128]{1,0:T(8,128)(2,1)} %refs_0_.1, s32[2,13]{1,0:T(2,128)} %refs_1_.1, s32[2]{0:T(128)} %refs_2_.1), custom_call_target="tpu_custom_call" | custom-call | flops 1 | bytes 1048576 | tf_op jit(solution)/shard_map/pack/pallas_call | solution.py:308
  1.0 3.0 %collective-permute-start = (bf16[1040,128]{1,0:T(8,128)(2,1)S(1)}, bf16[1040,128]{1,0:T(8,128)(2,1)S(1)}, u32[]{:S(2)}, u32[]{:S(2)}) collective-permute-start(bf16[1040,128]{1,0:T(8,128)(2,1)S(1)} %pack.1.refs_0_), channel_id=1, source_target_pairs={{0,2},{2,1},{3,5},{5,3},{4,6},{6,4},{7,9},{9,7},{8,10},{10,8},{11,... | collective-permute-start | bytes 798728 | tf_op jit(solution)/shard_map/ppermute | solution.py:334
  4.0 1.6 %collective-permute-start.3 = (bf16[1040,128]{1,0:T(8,128)(2,1)S(1)}, bf16[1040,128]{1,0:T(8,128)(2,1)S(1)}, u32[]{:S(2)}, u32[]{:S(2)}) collective-permute-start(bf16[1040,128]{1,0:T(8,128)(2,1)S(1)} %pack.1.refs_0_), channel_id=1, source_target_pairs={{0,4},{4,1},{2,6},{6,3},{5,9},{9,5},{7,11},{11,7},{8,13},{12,8},{1... | collective-permute-start | bytes 798728 | tf_op jit(solution)/shard_map/ppermute | solution.py:334
  6.4 1.0 %copy-done = f32[1024,128]{1,0:T(8,128)S(1)} copy-done((f32[1024,128]{1,0:T(8,128)S(1)}, f32[1024,128]{1,0:T(8,128)}, u32[]{:S(2)}) %copy-start) | copy-done | bytes 524312
  9.0 2.7 %collective-permute-done.refs_1_ = bf16[1040,128]{1,0:T(8,128)(2,1)S(1)} collective-permute-done((bf16[1040,128]{1,0:T(8,128)(2,1)S(1)}, bf16[1040,128]{1,0:T(8,128)(2,1)S(1)}, u32[]{:S(2)}, u32[]{:S(2)}) %collective-permute-start) | collective-permute-done | bytes 266272 | tf_op jit(solution)/shard_map/ppermute | solution.py:334
  11.7 2.0 %collective-permute-start.8 = (bf16[1024,128]{1,0:T(8,128)(2,1)S(1)}, bf16[1024,128]{1,0:T(8,128)(2,1)S(1)}, u32[]{:S(2)}, u32[]{:S(2)}) collective-permute-start(bf16[1024,128]{1,0:T(8,128)(2,1)S(1)} %get-tuple-element.32), channel_id=1, source_target_pairs={{0,4},{4,1},{2,6},{6,3},{5,9},{9,5},{7,11},{11,7},{8,13},{12,8},{1... | collective-permute-start | bytes 786440 | tf_op jit(solution)/shard_map/ppermute | solution.py:334
  13.7 1.1 %peer_weights.3 = (bf16[4,512,512]{2,1,0:T(8,128)(2,1)S(1)}, f32[1024,128]{1,0:T(8,128)S(1)}, f32[1024,128]{1,0:T(8,128)S(1)}) custom-call(bf16[1040,128]{1,0:T(8,128)(2,1)S(1)} %pack.1.refs_0_, bf16[1040,128]{1,0:T(8,128)(2,1)S(1)} %collective-permute-done.3.refs_1_, bf16[1024,256]{1,0:T(8,128)(2,1)S(1)} %get-tuple-element.30.refs_2_, ...), custom_call_target="tpu_custom_call" | custom-call | flops 536870912 | bytes 1048576 | tf_op jit(solution)/shard_map/peer_weights/pallas_call | solution.py:308
  14.9 1.3 %collective-permute-done.2.refs_2_ = bf16[1024,128]{1,0:T(8,128)(2,1)S(1)} collective-permute-done((bf16[1024,128]{1,0:T(8,128)(2,1)S(1)}, bf16[1024,128]{1,0:T(8,128)(2,1)S(1)}, u32[]{:S(2)}, u32[]{:S(2)}) %collective-permute-start.2) | collective-permute-done | bytes 262176 | tf_op jit(solution)/shard_map/ppermute | solution.py:334
  16.2 1.1 %peer_weights.4 = (bf16[4,512,512]{2,1,0:T(8,128)(2,1)S(1)}, f32[1024,128]{1,0:T(8,128)S(1)}, f32[1024,128]{1,0:T(8,128)S(1)}) custom-call(bf16[1040,128]{1,0:T(8,128)(2,1)S(1)} %pack.1.refs_0_, bf16[1040,128]{1,0:T(8,128)(2,1)S(1)} %collective-permute-done.refs_1_, bf16[1024,256]{1,0:T(8,128)(2,1)S(1)} %get-tuple-element.30.refs_2_, ...), custom_call_target="tpu_custom_call" | custom-call | flops 536870912 | bytes 1048576 | tf_op jit(solution)/shard_map/peer_weights/pallas_call | solution.py:308
  18.1 1.2 %peer_weights.5 = (bf16[4,512,512]{2,1,0:T(8,128)(2,1)S(1)}, f32[16,128]{1,0:T(8,128)S(1)}) custom-call(bf16[1040,128]{1,0:T(8,128)(2,1)S(1)} %pack.1.refs_0_, bf16[1040,128]{1,0:T(8,128)(2,1)S(1)} %collective-permute-done.1.refs_1_, bf16[1024,256]{1,0:T(8,128)(2,1)S(1)} %get-tuple-element.30.refs_2_, f32[1024,128]{1,0:T(8,128)S(1)} %get-tuple-element.37.refs_3_, ...), custom_call_target="tpu_custom_call" | custom-call | flops 536870912 | bytes 1048576 | tf_op jit(solution)/shard_map/peer_weights/pallas_call | solution.py:308
  19.4 1.2 %collective-permute-done.5.other_ref = f32[16,128]{1,0:T(8,128)S(1)} collective-permute-done((f32[16,128]{1,0:T(8,128)S(1)}, f32[16,128]{1,0:T(8,128)S(1)}, u32[]{:S(2)}, u32[]{:S(2)}) %collective-permute-start.5) | collective-permute-done | bytes 8224 | tf_op jit(solution)/shard_map/ppermute | solution.py:346
  20.6 4.0 %collective-permute-start.9 = (f32[16,128]{1,0:T(8,128)S(1)}, f32[16,128]{1,0:T(8,128)S(1)}, u32[]{:S(2)}, u32[]{:S(2)}) collective-permute-start(f32[16,128]{1,0:T(8,128)S(1)} %degree.1.scales_ref), channel_id=1, source_target_pairs={{0,4},{4,1},{2,6},{6,3},{5,9},{9,5},{7,11},{11,7},{8,13},{12,8},{1... | collective-permute-start | bytes 24584 | tf_op jit(solution)/shard_map/ppermute | solution.py:334
  24.6 0.9 %collective-permute-start.7 = (f32[16,128]{1,0:T(8,128)S(1)}, f32[16,128]{1,0:T(8,128)S(1)}, u32[]{:S(2)}, u32[]{:S(2)}) collective-permute-start(f32[16,128]{1,0:T(8,128)S(1)} %degree.1.scales_ref), channel_id=1, source_target_pairs={{0,2},{2,1},{3,5},{5,3},{4,6},{6,4},{7,9},{9,7},{8,10},{10,8},{11,... | collective-permute-start | bytes 24584 | tf_op jit(solution)/shard_map/ppermute | solution.py:334
  26.5 0.9 %peer_product.6.refs_4_ = f32[1024,128]{1,0:T(8,128)S(1)} custom-call(bf16[1040,128]{1,0:T(8,128)(2,1)S(1)} %pack.1.refs_0_, bf16[4,512,512]{2,1,0:T(8,128)(2,1)S(1)} %get-tuple-element.45.refs_1_, bf16[1024,128]{1,0:T(8,128)(2,1)S(1)} %collective-permute-done.8.refs_2_, f32[16,128]{1,0:T(8,128)S(1)} %collective-permute-done.9.refs_3_, ...), custom_call_target="tpu_custom_call" | custom-call | flops 536870912 | bytes 1048576 | tf_op jit(solution)/shard_map/peer_product/pallas_call | solution.py:308
  27.4 0.9 %peer_product.7.refs_4_ = f32[1024,128]{1,0:T(8,128)S(1)} custom-call(bf16[1040,128]{1,0:T(8,128)(2,1)S(1)} %pack.1.refs_0_, bf16[4,512,512]{2,1,0:T(8,128)(2,1)S(1)} %get-tuple-element.43.refs_1_, bf16[1024,128]{1,0:T(8,128)(2,1)S(1)} %collective-permute-done.2.refs_2_, f32[16,128]{1,0:T(8,128)S(1)} %collective-permute-done.7.refs_3_, ...), custom_call_target="tpu_custom_call" | custom-call | flops 536870912 | bytes 1048576 | tf_op jit(solution)/shard_map/peer_product/pallas_call | solution.py:308
  28.3 1.7 %collective-permute-done.6.refs_3_ = f32[16,128]{1,0:T(8,128)S(1)} collective-permute-done((f32[16,128]{1,0:T(8,128)S(1)}, f32[16,128]{1,0:T(8,128)S(1)}, u32[]{:S(2)}, u32[]{:S(2)}) %collective-permute-start.6) | collective-permute-done | bytes 8224 | tf_op jit(solution)/shard_map/ppermute | solution.py:334
  30.0 0.9 %peer_product.8.own_ref = bf16[1024,128]{1,0:T(8,128)(2,1)S(1)} custom-call(bf16[1040,128]{1,0:T(8,128)(2,1)S(1)} %pack.1.refs_0_, bf16[4,512,512]{2,1,0:T(8,128)(2,1)S(1)} %get-tuple-element.39.refs_1_, bf16[1024,128]{1,0:T(8,128)(2,1)S(1)} %collective-permute-done.4.refs_2_, f32[16,128]{1,0:T(8,128)S(1)} %collective-permute-done.6.refs_3_, ...), custom_call_target="tpu_custom_call" | custom-call | flops 536870912 | bytes 1048576 | tf_op jit(solution)/shard_map/peer_product/pallas_call | solution.py:308
  31.0 1.5 %collective-permute-done.10.other_ref = bf16[1024,128]{1,0:T(8,128)(2,1)S(1)} collective-permute-done((bf16[1024,128]{1,0:T(8,128)(2,1)S(1)}, bf16[1024,128]{1,0:T(8,128)(2,1)S(1)}, u32[]{:S(2)}, u32[]{:S(2)}) %collective-permute-start.10) | collective-permute-done | bytes 262176 | tf_op jit(solution)/shard_map/ppermute | solution.py:346
  33.7 1.8 %collective-permute-start.13 = (bf16[1024,128]{1,0:T(8,128)(2,1)S(1)}, bf16[1024,128]{1,0:T(8,128)(2,1)S(1)}, u32[]{:S(2)}, u32[]{:S(2)}) collective-permute-start(bf16[1024,128]{1,0:T(8,128)(2,1)S(1)} %state.1.refs_2_), channel_id=1, source_target_pairs={{0,4},{4,1},{2,6},{6,3},{5,9},{9,5},{7,11},{11,7},{8,13},{12,8},{1... | collective-permute-start | bytes 786440 | tf_op jit(solution)/shard_map/ppermute | solution.py:334
  35.5 4.4 %collective-permute-done.11.refs_2_ = bf16[1024,128]{1,0:T(8,128)(2,1)S(1)} collective-permute-done((bf16[1024,128]{1,0:T(8,128)(2,1)S(1)}, bf16[1024,128]{1,0:T(8,128)(2,1)S(1)}, u32[]{:S(2)}, u32[]{:S(2)}) %collective-permute-start.11) | collective-permute-done | bytes 262176 | tf_op jit(solution)/shard_map/ppermute | solution.py:334
  40.7 0.8 %peer_product.10.refs_3_ = f32[1024,128]{1,0:T(8,128)S(1)} custom-call(bf16[1040,128]{1,0:T(8,128)(2,1)S(1)} %pack.1.refs_0_, bf16[4,512,512]{2,1,0:T(8,128)(2,1)S(1)} %get-tuple-element.43.refs_1_, bf16[1024,128]{1,0:T(8,128)(2,1)S(1)} %collective-permute-done.11.refs_2_, f32[1024,128]{1,0:T(8,128)S(1)} %peer_product.9.refs_3_), custom_call_target="tpu_custom_call" | custom-call | flops 536870912 | bytes 1048576 | tf_op jit(solution)/shard_map/peer_product/pallas_call | solution.py:308
  41.5 4.8 %collective-permute-done.12.refs_2_ = bf16[1024,128]{1,0:T(8,128)(2,1)S(1)} collective-permute-done((bf16[1024,128]{1,0:T(8,128)(2,1)S(1)}, bf16[1024,128]{1,0:T(8,128)(2,1)S(1)}, u32[]{:S(2)}, u32[]{:S(2)}) %collective-permute-start.12) | collective-permute-done | bytes 262176 | tf_op jit(solution)/shard_map/ppermute | solution.py:340
  47.3 1.5 %collective-permute-done.14 = bf16[1024,128]{1,0:T(8,128)(2,1)S(1)} collective-permute-done((bf16[1024,128]{1,0:T(8,128)(2,1)S(1)}, bf16[1024,128]{1,0:T(8,128)(2,1)S(1)}, u32[]{:S(2)}, u32[]{:S(2)}) %collective-permute-start.14) | collective-permute-done | bytes 262176 | tf_op jit(solution)/shard_map/ppermute | solution.py:346
  48.8 0.9 %multiply_add_fusion = f32[1024,128]{1,0:T(8,128)} fusion(f32[1024,128]{1,0:T(8,128)S(1)} %get-tuple-element.49.seed_ref, f32[1024,128]{1,0:T(8,128)S(1)} %get-tuple-element.51.rs_ref, bf16[1024,128]{1,0:T(8,128)(2,1)S(1)} %collective-permute-done.14, bf16[1024,128]{1,0:T(8,128)(2,1)S(1)} %peer_product.11), kind=kLoop, calls=%fused_computation | loop fusion | flops 786432 | bytes 2097152 | tf_op jit(solution)/shard_map/add | solution.py:440
  (28 shorter events, 7.2 us)
Async XLA Ops:
  1.0 10.7 %collective-permute-start = (bf16[1040,128]{1,0:T(8,128)(2,1)S(1)}, bf16[1040,128]{1,0:T(8,128)(2,1)S(1)}, u32[]{:S(2)}, u32[]{:S(2)}) collective-permute-start(bf16[1040,128]{1,0:T(8,128)(2,1)S(1)} %pack.1.refs_0_), channel_id=1, source_target_pairs={{0,2},{2,1},{3,5},{5,3},{4,6},{6,4},{7,9},{9,7},{8,10},{10,8},{11,... | collective-permute-start | bytes 798728 | tf_op jit(solution)/shard_map/ppermute | solution.py:334
  4.0 9.7 %collective-permute-start.3 = (bf16[1040,128]{1,0:T(8,128)(2,1)S(1)}, bf16[1040,128]{1,0:T(8,128)(2,1)S(1)}, u32[]{:S(2)}, u32[]{:S(2)}) collective-permute-start(bf16[1040,128]{1,0:T(8,128)(2,1)S(1)} %pack.1.refs_0_), channel_id=1, source_target_pairs={{0,4},{4,1},{2,6},{6,3},{5,9},{9,5},{7,11},{11,7},{8,13},{12,8},{1... | collective-permute-start | bytes 798728 | tf_op jit(solution)/shard_map/ppermute | solution.py:334
  6.4 1.0 %copy-start = (f32[1024,128]{1,0:T(8,128)S(1)}, f32[1024,128]{1,0:T(8,128)}, u32[]{:S(2)}) copy-start(f32[1024,128]{1,0:T(8,128)} %profile_ref.1) | copy-start | bytes 1572868
  7.4 0.7 %copy-start.1 = (s32[1024]{0:T(1024)S(1)}, s32[1024]{0:T(1024)}, u32[]{:S(2)}) copy-start(s32[1024]{0:T(1024)} %param.7) | copy-start | bytes 12292
  8.4 7.7 %collective-permute-start.2 = (bf16[1024,128]{1,0:T(8,128)(2,1)S(1)}, bf16[1024,128]{1,0:T(8,128)(2,1)S(1)}, u32[]{:S(2)}, u32[]{:S(2)}) collective-permute-start(bf16[1024,128]{1,0:T(8,128)(2,1)S(1)} %get-tuple-element.32), channel_id=1, source_target_pairs={{0,2},{2,1},{3,5},{5,3},{4,6},{6,4},{7,9},{9,7},{8,10},{10,8},{11,... | collective-permute-start | bytes 786440 | tf_op jit(solution)/shard_map/ppermute | solution.py:334
  11.7 6.4 %collective-permute-start.1 = (bf16[1040,128]{1,0:T(8,128)(2,1)S(1)}, bf16[1040,128]{1,0:T(8,128)(2,1)S(1)}, u32[]{:S(2)}, u32[]{:S(2)}) collective-permute-start(bf16[1040,128]{1,0:T(8,128)(2,1)S(1)} %collective-permute-done.refs_1_), channel_id=1, source_target_pairs={{2,6},{4,0},{5,8},{6,10},{7,3},{8,4},{9,13},{10,14},{11,7},{12,9},... | collective-permute-start | bytes 798728 | tf_op jit(solution)/shard_map/ppermute | solution.py:340
  11.7 13.8 %collective-permute-start.8 = (bf16[1024,128]{1,0:T(8,128)(2,1)S(1)}, bf16[1024,128]{1,0:T(8,128)(2,1)S(1)}, u32[]{:S(2)}, u32[]{:S(2)}) collective-permute-start(bf16[1024,128]{1,0:T(8,128)(2,1)S(1)} %get-tuple-element.32), channel_id=1, source_target_pairs={{0,4},{4,1},{2,6},{6,3},{5,9},{9,5},{7,11},{11,7},{8,13},{12,8},{1... | collective-permute-start | bytes 786440 | tf_op jit(solution)/shard_map/ppermute | solution.py:334
  16.2 12.1 %collective-permute-start.4 = (bf16[1024,128]{1,0:T(8,128)(2,1)S(1)}, bf16[1024,128]{1,0:T(8,128)(2,1)S(1)}, u32[]{:S(2)}, u32[]{:S(2)}) collective-permute-start(bf16[1024,128]{1,0:T(8,128)(2,1)S(1)} %collective-permute-done.2.refs_2_), channel_id=1, source_target_pairs={{2,6},{4,0},{5,8},{6,10},{7,3},{8,4},{9,13},{10,14},{11,7},{12,9},... | collective-permute-start | bytes 786440 | tf_op jit(solution)/shard_map/ppermute | solution.py:402
  19.4 1.2 %collective-permute-start.5 = (f32[16,128]{1,0:T(8,128)S(1)}, f32[16,128]{1,0:T(8,128)S(1)}, u32[]{:S(2)}, u32[]{:S(2)}) collective-permute-start(f32[16,128]{1,0:T(8,128)S(1)} %get-tuple-element.41.own_ref), channel_id=1, source_target_pairs={{0,1},{1,0},{2,3},{3,2},{4,5},{5,4},{6,7},{7,6},{8,9},{9,8},{10,11... | collective-permute-start | bytes 24584 | tf_op jit(solution)/shard_map/ppermute | solution.py:346
  20.6 5.9 %collective-permute-start.9 = (f32[16,128]{1,0:T(8,128)S(1)}, f32[16,128]{1,0:T(8,128)S(1)}, u32[]{:S(2)}, u32[]{:S(2)}) collective-permute-start(f32[16,128]{1,0:T(8,128)S(1)} %degree.1.scales_ref), channel_id=1, source_target_pairs={{0,4},{4,1},{2,6},{6,3},{5,9},{9,5},{7,11},{11,7},{8,13},{12,8},{1... | collective-permute-start | bytes 24584 | tf_op jit(solution)/shard_map/ppermute | solution.py:334
  24.6 2.8 %collective-permute-start.7 = (f32[16,128]{1,0:T(8,128)S(1)}, f32[16,128]{1,0:T(8,128)S(1)}, u32[]{:S(2)}, u32[]{:S(2)}) collective-permute-start(f32[16,128]{1,0:T(8,128)S(1)} %degree.1.scales_ref), channel_id=1, source_target_pairs={{0,2},{2,1},{3,5},{5,3},{4,6},{6,4},{7,9},{9,7},{8,10},{10,8},{11,... | collective-permute-start | bytes 24584 | tf_op jit(solution)/shard_map/ppermute | solution.py:334
  25.5 4.6 %collective-permute-start.6 = (f32[16,128]{1,0:T(8,128)S(1)}, f32[16,128]{1,0:T(8,128)S(1)}, u32[]{:S(2)}, u32[]{:S(2)}) collective-permute-start(f32[16,128]{1,0:T(8,128)S(1)} %degree.1.scales_ref), channel_id=1, source_target_pairs={{6,0},{8,3},{10,11},{0,1},{12,7},{2,8},{14,15},{4,5},{7,13},{9,14}... | collective-permute-start | bytes 24584 | tf_op jit(solution)/shard_map/ppermute | solution.py:334
  30.9 1.6 %collective-permute-start.10 = (bf16[1024,128]{1,0:T(8,128)(2,1)S(1)}, bf16[1024,128]{1,0:T(8,128)(2,1)S(1)}, u32[]{:S(2)}, u32[]{:S(2)}) collective-permute-start(bf16[1024,128]{1,0:T(8,128)(2,1)S(1)} %peer_product.8.own_ref), channel_id=1, source_target_pairs={{0,1},{1,0},{2,3},{3,2},{4,5},{5,4},{6,7},{7,6},{8,9},{9,8},{10,11... | collective-permute-start | bytes 786440 | tf_op jit(solution)/shard_map/ppermute | solution.py:346
  32.7 7.2 %collective-permute-start.11 = (bf16[1024,128]{1,0:T(8,128)(2,1)S(1)}, bf16[1024,128]{1,0:T(8,128)(2,1)S(1)}, u32[]{:S(2)}, u32[]{:S(2)}) collective-permute-start(bf16[1024,128]{1,0:T(8,128)(2,1)S(1)} %state.1.refs_2_), channel_id=1, source_target_pairs={{0,2},{2,1},{3,5},{5,3},{4,6},{6,4},{7,9},{9,7},{8,10},{10,8},{11,... | collective-permute-start | bytes 786440 | tf_op jit(solution)/shard_map/ppermute | solution.py:334
  33.7 6.2 %collective-permute-start.13 = (bf16[1024,128]{1,0:T(8,128)(2,1)S(1)}, bf16[1024,128]{1,0:T(8,128)(2,1)S(1)}, u32[]{:S(2)}, u32[]{:S(2)}) collective-permute-start(bf16[1024,128]{1,0:T(8,128)(2,1)S(1)} %state.1.refs_2_), channel_id=1, source_target_pairs={{0,4},{4,1},{2,6},{6,3},{5,9},{9,5},{7,11},{11,7},{8,13},{12,8},{1... | collective-permute-start | bytes 786440 | tf_op jit(solution)/shard_map/ppermute | solution.py:334
  39.9 6.5 %collective-permute-start.12 = (bf16[1024,128]{1,0:T(8,128)(2,1)S(1)}, bf16[1024,128]{1,0:T(8,128)(2,1)S(1)}, u32[]{:S(2)}, u32[]{:S(2)}) collective-permute-start(bf16[1024,128]{1,0:T(8,128)(2,1)S(1)} %collective-permute-done.11.refs_2_), channel_id=1, source_target_pairs={{2,6},{4,0},{5,8},{6,10},{7,3},{8,4},{9,13},{10,14},{11,7},{12,9},... | collective-permute-start | bytes 786440 | tf_op jit(solution)/shard_map/ppermute | solution.py:340
  47.2 1.6 %collective-permute-start.14 = (bf16[1024,128]{1,0:T(8,128)(2,1)S(1)}, bf16[1024,128]{1,0:T(8,128)(2,1)S(1)}, u32[]{:S(2)}, u32[]{:S(2)}) collective-permute-start(bf16[1024,128]{1,0:T(8,128)(2,1)S(1)} %peer_product.11), channel_id=1, source_target_pairs={{0,1},{1,0},{2,3},{3,2},{4,5},{5,4},{6,7},{7,6},{8,9},{9,8},{10,11... | collective-permute-start | bytes 786440 | tf_op jit(solution)/shard_map/ppermute | solution.py:346

commit v10 on v9

--- a/solution.py
+++ b/solution.py
@@ -304,12 +304,26 @@
     out_ref[...] = (state * cs_ref[...]).astype(BF16)
 
 
-def kernel_call(body, name, ins, outs, flops, scratch=(), in_specs=None):
+def spread_kernel(own_ref, other_ref, rs_ref, seed_ref, out_hbm, out_ref, sems):
+    chunks = sems.shape[0]
+    size = out_ref.shape[0] // chunks
+    copies = []
+    for n in range(chunks):
+        at = pl.ds(n * size, size)
+        total = own_ref[at, :].astype(F32) + other_ref[at, :].astype(F32)
+        out_ref[at, :] = total * rs_ref[at, :] + (1.0 - ALPHA) * seed_ref[at, :]
+        copies.append(pltpu.make_async_copy(out_ref.at[at, :], out_hbm.at[at, :], sems.at[n]))
+        copies[-1].start()
+    for copy in copies:
+        copy.wait()
+
+
+def kernel_call(body, name, ins, outs, flops, scratch=(), in_specs=None, out_specs=None):
     return pl.pallas_call(
         body,
         out_shape=outs,
         in_specs=in_specs or [VMEM] * len(ins),
-        out_specs=jax.tree.map(lambda _: VMEM, outs),
+        out_specs=out_specs or jax.tree.map(lambda _: VMEM, outs),
         scratch_shapes=scratch,
         compiler_params=PARAMS,
         cost_estimate=pl.CostEstimate(flops=flops, bytes_accessed=1 << 20, transcendentals=0),
@@ -437,7 +451,15 @@
             scaled = kernel_call(
                 state_kernel, "state", [partial, other, row_scale, seed_rows, col_scale], bf16_rows, 1
             )
-    return (partial.astype(F32) + other.astype(F32)) * row_scale + (1.0 - ALPHA) * seed_rows
+    return kernel_call(
+        spread_kernel,
+        "spread",
+        [partial, other, row_scale, seed_rows],
+        pltpu.HBM((mols, LANES), F32),
+        1,
+        [pltpu.VMEM((mols, LANES), F32), pltpu.SemaphoreType.DMA((4,))],
+        out_specs=HBM,
+    )
 
 
 def solution(mesh):

time: 49.9 us -> 49.8 us (level)
  other arithmetic: 0.9 us -> 0 us
  Pallas kernels: 12.4 us -> 13.2 us
    add x1 -> x0, other arithmetic: 0.9 us -> none  [shards(): (partial.astype(F32) + other.astype(F32)) * row_scale]
    pallas_call x17 -> x18, Pallas kernels: 12.4 us -> 13.2 us  [kernel_call(): pl.pallas_call(body, out_shape=outs, in_specs=in_specs or [VMEM] * len(in...]
where the time goes in v10:
time: 49.8 us; the launch traced here: 49.6 us
  waiting for transfers between devices  20 us (40%)
  starting transfers between devices  14.5 us (29%)
  Pallas kernels  13.2 us (27%)
  local copies, waits for them, and re-layouts  1.72 us (3%)
    ppermute x9, starting transfers between devices, to_peer(): return lax.ppermute(value, ('row', 'col'), list(steps[step][2].items()))  14.3 us
    pallas_call x18, Pallas kernels, kernel_call(): pl.pallas_call(body, out_shape=outs, in_specs=in_specs or [VMEM] * len(in...  13.2 us
    ppermute x9, waiting for transfers between devices, to_peer(): return lax.ppermute(value, ('row', 'col'), list(steps[step][2].items()))  10.2 us
    ppermute x2, waiting for transfers between devices, from_peers(): lax.ppermute(pieces[step - 2], ('row', 'col'), list(moves.items()))  5.62 us
    ppermute x3, waiting for transfers between devices, other_core(): return lax.ppermute(value, 'col', [(0, 1), (1, 0)])  4.2 us
    unnamed x4, local copies, waits for them, and re-layouts  1.72 us
  transfers between devices with their start and end apart: 15, of which 9 were waited for; matrix products, arithmetic and copies ran while one was open for 0% of the time, Pallas kernels for 19%

profile of v10, /device:TPU:0, one launch (start us, length us, event | category | flops | bytes accessed | tf_op | source)
XLA Modules:
  0.0 49.6 jit_solution(11404738369517095775)
XLA Ops:
  0.0 1.0 %pack.1.refs_0_ = bf16[1040,128]{1,0:T(8,128)(2,1)S(1)} custom-call(bf16[1024,128]{1,0:T(8,128)(2,1)} %refs_0_.1, s32[2,13]{1,0:T(2,128)} %refs_1_.1, s32[2]{0:T(128)} %refs_2_.1), custom_call_target="tpu_custom_call" | custom-call | flops 1 | bytes 1048576 | tf_op jit(solution)/shard_map/pack/pallas_call | solution.py:322
  1.0 3.0 %collective-permute-start = (bf16[1040,128]{1,0:T(8,128)(2,1)S(1)}, bf16[1040,128]{1,0:T(8,128)(2,1)S(1)}, u32[]{:S(2)}, u32[]{:S(2)}) collective-permute-start(bf16[1040,128]{1,0:T(8,128)(2,1)S(1)} %pack.1.refs_0_), channel_id=1, source_target_pairs={{0,2},{2,1},{3,5},{5,3},{4,6},{6,4},{7,9},{9,7},{8,10},{10,8},{11,... | collective-permute-start | bytes 798728 | tf_op jit(solution)/shard_map/ppermute | solution.py:348
  4.0 1.6 %collective-permute-start.3 = (bf16[1040,128]{1,0:T(8,128)(2,1)S(1)}, bf16[1040,128]{1,0:T(8,128)(2,1)S(1)}, u32[]{:S(2)}, u32[]{:S(2)}) collective-permute-start(bf16[1040,128]{1,0:T(8,128)(2,1)S(1)} %pack.1.refs_0_), channel_id=1, source_target_pairs={{0,4},{4,1},{2,6},{6,3},{5,9},{9,5},{7,11},{11,7},{8,13},{12,8},{1... | collective-permute-start | bytes 798728 | tf_op jit(solution)/shard_map/ppermute | solution.py:348
  6.4 1.0 %copy-done = f32[1024,128]{1,0:T(8,128)S(1)} copy-done((f32[1024,128]{1,0:T(8,128)S(1)}, f32[1024,128]{1,0:T(8,128)}, u32[]{:S(2)}) %copy-start) | copy-done | bytes 524312
  9.0 2.7 %collective-permute-done.refs_1_ = bf16[1040,128]{1,0:T(8,128)(2,1)S(1)} collective-permute-done((bf16[1040,128]{1,0:T(8,128)(2,1)S(1)}, bf16[1040,128]{1,0:T(8,128)(2,1)S(1)}, u32[]{:S(2)}, u32[]{:S(2)}) %collective-permute-start) | collective-permute-done | bytes 266272 | tf_op jit(solution)/shard_map/ppermute | solution.py:348
  11.7 2.0 %collective-permute-start.8 = (bf16[1024,128]{1,0:T(8,128)(2,1)S(1)}, bf16[1024,128]{1,0:T(8,128)(2,1)S(1)}, u32[]{:S(2)}, u32[]{:S(2)}) collective-permute-start(bf16[1024,128]{1,0:T(8,128)(2,1)S(1)} %get-tuple-element.32), channel_id=1, source_target_pairs={{0,4},{4,1},{2,6},{6,3},{5,9},{9,5},{7,11},{11,7},{8,13},{12,8},{1... | collective-permute-start | bytes 786440 | tf_op jit(solution)/shard_map/ppermute | solution.py:348
  13.7 1.1 %peer_weights.3 = (bf16[4,512,512]{2,1,0:T(8,128)(2,1)S(1)}, f32[1024,128]{1,0:T(8,128)S(1)}, f32[1024,128]{1,0:T(8,128)S(1)}) custom-call(bf16[1040,128]{1,0:T(8,128)(2,1)S(1)} %pack.1.refs_0_, bf16[1040,128]{1,0:T(8,128)(2,1)S(1)} %collective-permute-done.3.refs_1_, bf16[1024,256]{1,0:T(8,128)(2,1)S(1)} %get-tuple-element.30.refs_2_, ...), custom_call_target="tpu_custom_call" | custom-call | flops 536870912 | bytes 1048576 | tf_op jit(solution)/shard_map/peer_weights/pallas_call | solution.py:322
  14.9 1.3 %collective-permute-done.2.refs_2_ = bf16[1024,128]{1,0:T(8,128)(2,1)S(1)} collective-permute-done((bf16[1024,128]{1,0:T(8,128)(2,1)S(1)}, bf16[1024,128]{1,0:T(8,128)(2,1)S(1)}, u32[]{:S(2)}, u32[]{:S(2)}) %collective-permute-start.2) | collective-permute-done | bytes 262176 | tf_op jit(solution)/shard_map/ppermute | solution.py:348
  16.2 1.1 %peer_weights.4 = (bf16[4,512,512]{2,1,0:T(8,128)(2,1)S(1)}, f32[1024,128]{1,0:T(8,128)S(1)}, f32[1024,128]{1,0:T(8,128)S(1)}) custom-call(bf16[1040,128]{1,0:T(8,128)(2,1)S(1)} %pack.1.refs_0_, bf16[1040,128]{1,0:T(8,128)(2,1)S(1)} %collective-permute-done.refs_1_, bf16[1024,256]{1,0:T(8,128)(2,1)S(1)} %get-tuple-element.30.refs_2_, ...), custom_call_target="tpu_custom_call" | custom-call | flops 536870912 | bytes 1048576 | tf_op jit(solution)/shard_map/peer_weights/pallas_call | solution.py:322
  18.1 1.2 %peer_weights.5 = (bf16[4,512,512]{2,1,0:T(8,128)(2,1)S(1)}, f32[16,128]{1,0:T(8,128)S(1)}) custom-call(bf16[1040,128]{1,0:T(8,128)(2,1)S(1)} %pack.1.refs_0_, bf16[1040,128]{1,0:T(8,128)(2,1)S(1)} %collective-permute-done.1.refs_1_, bf16[1024,256]{1,0:T(8,128)(2,1)S(1)} %get-tuple-element.30.refs_2_, f32[1024,128]{1,0:T(8,128)S(1)} %get-tuple-element.37.refs_3_, ...), custom_call_target="tpu_custom_call" | custom-call | flops 536870912 | bytes 1048576 | tf_op jit(solution)/shard_map/peer_weights/pallas_call | solution.py:322
  19.4 1.2 %collective-permute-done.5.other_ref = f32[16,128]{1,0:T(8,128)S(1)} collective-permute-done((f32[16,128]{1,0:T(8,128)S(1)}, f32[16,128]{1,0:T(8,128)S(1)}, u32[]{:S(2)}, u32[]{:S(2)}) %collective-permute-start.5) | collective-permute-done | bytes 8224 | tf_op jit(solution)/shard_map/ppermute | solution.py:360
  20.6 4.0 %collective-permute-start.9 = (f32[16,128]{1,0:T(8,128)S(1)}, f32[16,128]{1,0:T(8,128)S(1)}, u32[]{:S(2)}, u32[]{:S(2)}) collective-permute-start(f32[16,128]{1,0:T(8,128)S(1)} %degree.1.scales_ref), channel_id=1, source_target_pairs={{0,4},{4,1},{2,6},{6,3},{5,9},{9,5},{7,11},{11,7},{8,13},{12,8},{1... | collective-permute-start | bytes 24584 | tf_op jit(solution)/shard_map/ppermute | solution.py:348
  24.6 0.9 %collective-permute-start.7 = (f32[16,128]{1,0:T(8,128)S(1)}, f32[16,128]{1,0:T(8,128)S(1)}, u32[]{:S(2)}, u32[]{:S(2)}) collective-permute-start(f32[16,128]{1,0:T(8,128)S(1)} %degree.1.scales_ref), channel_id=1, source_target_pairs={{0,2},{2,1},{3,5},{5,3},{4,6},{6,4},{7,9},{9,7},{8,10},{10,8},{11,... | collective-permute-start | bytes 24584 | tf_op jit(solution)/shard_map/ppermute | solution.py:348
  26.5 0.9 %peer_product.6.refs_4_ = f32[1024,128]{1,0:T(8,128)S(1)} custom-call(bf16[1040,128]{1,0:T(8,128)(2,1)S(1)} %pack.1.refs_0_, bf16[4,512,512]{2,1,0:T(8,128)(2,1)S(1)} %get-tuple-element.45.refs_1_, bf16[1024,128]{1,0:T(8,128)(2,1)S(1)} %collective-permute-done.8.refs_2_, f32[16,128]{1,0:T(8,128)S(1)} %collective-permute-done.9.refs_3_, ...), custom_call_target="tpu_custom_call" | custom-call | flops 536870912 | bytes 1048576 | tf_op jit(solution)/shard_map/peer_product/pallas_call | solution.py:322
  27.4 0.9 %peer_product.7.refs_4_ = f32[1024,128]{1,0:T(8,128)S(1)} custom-call(bf16[1040,128]{1,0:T(8,128)(2,1)S(1)} %pack.1.refs_0_, bf16[4,512,512]{2,1,0:T(8,128)(2,1)S(1)} %get-tuple-element.43.refs_1_, bf16[1024,128]{1,0:T(8,128)(2,1)S(1)} %collective-permute-done.2.refs_2_, f32[16,128]{1,0:T(8,128)S(1)} %collective-permute-done.7.refs_3_, ...), custom_call_target="tpu_custom_call" | custom-call | flops 536870912 | bytes 1048576 | tf_op jit(solution)/shard_map/peer_product/pallas_call | solution.py:322
  28.3 1.7 %collective-permute-done.6.refs_3_ = f32[16,128]{1,0:T(8,128)S(1)} collective-permute-done((f32[16,128]{1,0:T(8,128)S(1)}, f32[16,128]{1,0:T(8,128)S(1)}, u32[]{:S(2)}, u32[]{:S(2)}) %collective-permute-start.6) | collective-permute-done | bytes 8224 | tf_op jit(solution)/shard_map/ppermute | solution.py:348
  30.0 0.9 %peer_product.8.own_ref = bf16[1024,128]{1,0:T(8,128)(2,1)S(1)} custom-call(bf16[1040,128]{1,0:T(8,128)(2,1)S(1)} %pack.1.refs_0_, bf16[4,512,512]{2,1,0:T(8,128)(2,1)S(1)} %get-tuple-element.39.refs_1_, bf16[1024,128]{1,0:T(8,128)(2,1)S(1)} %collective-permute-done.4.refs_2_, f32[16,128]{1,0:T(8,128)S(1)} %collective-permute-done.6.refs_3_, ...), custom_call_target="tpu_custom_call" | custom-call | flops 536870912 | bytes 1048576 | tf_op jit(solution)/shard_map/peer_product/pallas_call | solution.py:322
  31.0 1.5 %collective-permute-done.10.other_ref = bf16[1024,128]{1,0:T(8,128)(2,1)S(1)} collective-permute-done((bf16[1024,128]{1,0:T(8,128)(2,1)S(1)}, bf16[1024,128]{1,0:T(8,128)(2,1)S(1)}, u32[]{:S(2)}, u32[]{:S(2)}) %collective-permute-start.10) | collective-permute-done | bytes 262176 | tf_op jit(solution)/shard_map/ppermute | solution.py:360
  33.7 1.8 %collective-permute-start.13 = (bf16[1024,128]{1,0:T(8,128)(2,1)S(1)}, bf16[1024,128]{1,0:T(8,128)(2,1)S(1)}, u32[]{:S(2)}, u32[]{:S(2)}) collective-permute-start(bf16[1024,128]{1,0:T(8,128)(2,1)S(1)} %state.1.refs_2_), channel_id=1, source_target_pairs={{0,4},{4,1},{2,6},{6,3},{5,9},{9,5},{7,11},{11,7},{8,13},{12,8},{1... | collective-permute-start | bytes 786440 | tf_op jit(solution)/shard_map/ppermute | solution.py:348
  35.5 4.4 %collective-permute-done.11.refs_2_ = bf16[1024,128]{1,0:T(8,128)(2,1)S(1)} collective-permute-done((bf16[1024,128]{1,0:T(8,128)(2,1)S(1)}, bf16[1024,128]{1,0:T(8,128)(2,1)S(1)}, u32[]{:S(2)}, u32[]{:S(2)}) %collective-permute-start.11) | collective-permute-done | bytes 262176 | tf_op jit(solution)/shard_map/ppermute | solution.py:348
  40.7 0.8 %peer_product.10.refs_3_ = f32[1024,128]{1,0:T(8,128)S(1)} custom-call(bf16[1040,128]{1,0:T(8,128)(2,1)S(1)} %pack.1.refs_0_, bf16[4,512,512]{2,1,0:T(8,128)(2,1)S(1)} %get-tuple-element.43.refs_1_, bf16[1024,128]{1,0:T(8,128)(2,1)S(1)} %collective-permute-done.11.refs_2_, f32[1024,128]{1,0:T(8,128)S(1)} %peer_product.9.refs_3_), custom_call_target="tpu_custom_call" | custom-call | flops 536870912 | bytes 1048576 | tf_op jit(solution)/shard_map/peer_product/pallas_call | solution.py:322
  41.5 4.8 %collective-permute-done.12.refs_2_ = bf16[1024,128]{1,0:T(8,128)(2,1)S(1)} collective-permute-done((bf16[1024,128]{1,0:T(8,128)(2,1)S(1)}, bf16[1024,128]{1,0:T(8,128)(2,1)S(1)}, u32[]{:S(2)}, u32[]{:S(2)}) %collective-permute-start.12) | collective-permute-done | bytes 262176 | tf_op jit(solution)/shard_map/ppermute | solution.py:354
  47.3 1.5 %collective-permute-done.14.other_ref = bf16[1024,128]{1,0:T(8,128)(2,1)S(1)} collective-permute-done((bf16[1024,128]{1,0:T(8,128)(2,1)S(1)}, bf16[1024,128]{1,0:T(8,128)(2,1)S(1)}, u32[]{:S(2)}, u32[]{:S(2)}) %collective-permute-start.14) | collective-permute-done | bytes 262176 | tf_op jit(solution)/shard_map/ppermute | solution.py:360
  48.8 0.9 %spread.1 = f32[1024,128]{1,0:T(8,128)} custom-call(bf16[1024,128]{1,0:T(8,128)(2,1)S(1)} %peer_product.11.own_ref, bf16[1024,128]{1,0:T(8,128)(2,1)S(1)} %collective-permute-done.14.other_ref, f32[1024,128]{1,0:T(8,128)S(1)} %get-tuple-element.51.rs_ref, f32[1024,128]{1,0:T(8,128)S(1)} %get-tuple-element.49.seed_ref), custom_call_target="tpu_custom_call" | custom-call | flops 1 | bytes 1048576 | tf_op jit(solution)/shard_map/spread/pallas_call | solution.py:322
  (28 shorter events, 7.2 us)
Async XLA Ops:
  1.0 10.7 %collective-permute-start = (bf16[1040,128]{1,0:T(8,128)(2,1)S(1)}, bf16[1040,128]{1,0:T(8,128)(2,1)S(1)}, u32[]{:S(2)}, u32[]{:S(2)}) collective-permute-start(bf16[1040,128]{1,0:T(8,128)(2,1)S(1)} %pack.1.refs_0_), channel_id=1, source_target_pairs={{0,2},{2,1},{3,5},{5,3},{4,6},{6,4},{7,9},{9,7},{8,10},{10,8},{11,... | collective-permute-start | bytes 798728 | tf_op jit(solution)/shard_map/ppermute | solution.py:348
  4.0 9.7 %collective-permute-start.3 = (bf16[1040,128]{1,0:T(8,128)(2,1)S(1)}, bf16[1040,128]{1,0:T(8,128)(2,1)S(1)}, u32[]{:S(2)}, u32[]{:S(2)}) collective-permute-start(bf16[1040,128]{1,0:T(8,128)(2,1)S(1)} %pack.1.refs_0_), channel_id=1, source_target_pairs={{0,4},{4,1},{2,6},{6,3},{5,9},{9,5},{7,11},{11,7},{8,13},{12,8},{1... | collective-permute-start | bytes 798728 | tf_op jit(solution)/shard_map/ppermute | solution.py:348
  6.4 1.0 %copy-start = (f32[1024,128]{1,0:T(8,128)S(1)}, f32[1024,128]{1,0:T(8,128)}, u32[]{:S(2)}) copy-start(f32[1024,128]{1,0:T(8,128)} %profile_ref.1) | copy-start | bytes 1572868
  7.4 0.7 %copy-start.1 = (s32[1024]{0:T(1024)S(1)}, s32[1024]{0:T(1024)}, u32[]{:S(2)}) copy-start(s32[1024]{0:T(1024)} %param.7) | copy-start | bytes 12292
  8.4 7.7 %collective-permute-start.2 = (bf16[1024,128]{1,0:T(8,128)(2,1)S(1)}, bf16[1024,128]{1,0:T(8,128)(2,1)S(1)}, u32[]{:S(2)}, u32[]{:S(2)}) collective-permute-start(bf16[1024,128]{1,0:T(8,128)(2,1)S(1)} %get-tuple-element.32), channel_id=1, source_target_pairs={{0,2},{2,1},{3,5},{5,3},{4,6},{6,4},{7,9},{9,7},{8,10},{10,8},{11,... | collective-permute-start | bytes 786440 | tf_op jit(solution)/shard_map/ppermute | solution.py:348
  11.7 6.4 %collective-permute-start.1 = (bf16[1040,128]{1,0:T(8,128)(2,1)S(1)}, bf16[1040,128]{1,0:T(8,128)(2,1)S(1)}, u32[]{:S(2)}, u32[]{:S(2)}) collective-permute-start(bf16[1040,128]{1,0:T(8,128)(2,1)S(1)} %collective-permute-done.refs_1_), channel_id=1, source_target_pairs={{2,6},{4,0},{5,8},{6,10},{7,3},{8,4},{9,13},{10,14},{11,7},{12,9},... | collective-permute-start | bytes 798728 | tf_op jit(solution)/shard_map/ppermute | solution.py:354
  11.7 13.8 %collective-permute-start.8 = (bf16[1024,128]{1,0:T(8,128)(2,1)S(1)}, bf16[1024,128]{1,0:T(8,128)(2,1)S(1)}, u32[]{:S(2)}, u32[]{:S(2)}) collective-permute-start(bf16[1024,128]{1,0:T(8,128)(2,1)S(1)} %get-tuple-element.32), channel_id=1, source_target_pairs={{0,4},{4,1},{2,6},{6,3},{5,9},{9,5},{7,11},{11,7},{8,13},{12,8},{1... | collective-permute-start | bytes 786440 | tf_op jit(solution)/shard_map/ppermute | solution.py:348
  16.2 12.1 %collective-permute-start.4 = (bf16[1024,128]{1,0:T(8,128)(2,1)S(1)}, bf16[1024,128]{1,0:T(8,128)(2,1)S(1)}, u32[]{:S(2)}, u32[]{:S(2)}) collective-permute-start(bf16[1024,128]{1,0:T(8,128)(2,1)S(1)} %collective-permute-done.2.refs_2_), channel_id=1, source_target_pairs={{2,6},{4,0},{5,8},{6,10},{7,3},{8,4},{9,13},{10,14},{11,7},{12,9},... | collective-permute-start | bytes 786440 | tf_op jit(solution)/shard_map/ppermute | solution.py:416
  19.4 1.2 %collective-permute-start.5 = (f32[16,128]{1,0:T(8,128)S(1)}, f32[16,128]{1,0:T(8,128)S(1)}, u32[]{:S(2)}, u32[]{:S(2)}) collective-permute-start(f32[16,128]{1,0:T(8,128)S(1)} %get-tuple-element.41.own_ref), channel_id=1, source_target_pairs={{0,1},{1,0},{2,3},{3,2},{4,5},{5,4},{6,7},{7,6},{8,9},{9,8},{10,11... | collective-permute-start | bytes 24584 | tf_op jit(solution)/shard_map/ppermute | solution.py:360
  20.6 5.9 %collective-permute-start.9 = (f32[16,128]{1,0:T(8,128)S(1)}, f32[16,128]{1,0:T(8,128)S(1)}, u32[]{:S(2)}, u32[]{:S(2)}) collective-permute-start(f32[16,128]{1,0:T(8,128)S(1)} %degree.1.scales_ref), channel_id=1, source_target_pairs={{0,4},{4,1},{2,6},{6,3},{5,9},{9,5},{7,11},{11,7},{8,13},{12,8},{1... | collective-permute-start | bytes 24584 | tf_op jit(solution)/shard_map/ppermute | solution.py:348
  24.6 2.8 %collective-permute-start.7 = (f32[16,128]{1,0:T(8,128)S(1)}, f32[16,128]{1,0:T(8,128)S(1)}, u32[]{:S(2)}, u32[]{:S(2)}) collective-permute-start(f32[16,128]{1,0:T(8,128)S(1)} %degree.1.scales_ref), channel_id=1, source_target_pairs={{0,2},{2,1},{3,5},{5,3},{4,6},{6,4},{7,9},{9,7},{8,10},{10,8},{11,... | collective-permute-start | bytes 24584 | tf_op jit(solution)/shard_map/ppermute | solution.py:348
  25.5 4.6 %collective-permute-start.6 = (f32[16,128]{1,0:T(8,128)S(1)}, f32[16,128]{1,0:T(8,128)S(1)}, u32[]{:S(2)}, u32[]{:S(2)}) collective-permute-start(f32[16,128]{1,0:T(8,128)S(1)} %degree.1.scales_ref), channel_id=1, source_target_pairs={{6,0},{8,3},{10,11},{0,1},{12,7},{2,8},{14,15},{4,5},{7,13},{9,14}... | collective-permute-start | bytes 24584 | tf_op jit(solution)/shard_map/ppermute | solution.py:348
  30.9 1.6 %collective-permute-start.10 = (bf16[1024,128]{1,0:T(8,128)(2,1)S(1)}, bf16[1024,128]{1,0:T(8,128)(2,1)S(1)}, u32[]{:S(2)}, u32[]{:S(2)}) collective-permute-start(bf16[1024,128]{1,0:T(8,128)(2,1)S(1)} %peer_product.8.own_ref), channel_id=1, source_target_pairs={{0,1},{1,0},{2,3},{3,2},{4,5},{5,4},{6,7},{7,6},{8,9},{9,8},{10,11... | collective-permute-start | bytes 786440 | tf_op jit(solution)/shard_map/ppermute | solution.py:360
  32.7 7.2 %collective-permute-start.11 = (bf16[1024,128]{1,0:T(8,128)(2,1)S(1)}, bf16[1024,128]{1,0:T(8,128)(2,1)S(1)}, u32[]{:S(2)}, u32[]{:S(2)}) collective-permute-start(bf16[1024,128]{1,0:T(8,128)(2,1)S(1)} %state.1.refs_2_), channel_id=1, source_target_pairs={{0,2},{2,1},{3,5},{5,3},{4,6},{6,4},{7,9},{9,7},{8,10},{10,8},{11,... | collective-permute-start | bytes 786440 | tf_op jit(solution)/shard_map/ppermute | solution.py:348
  33.7 6.2 %collective-permute-start.13 = (bf16[1024,128]{1,0:T(8,128)(2,1)S(1)}, bf16[1024,128]{1,0:T(8,128)(2,1)S(1)}, u32[]{:S(2)}, u32[]{:S(2)}) collective-permute-start(bf16[1024,128]{1,0:T(8,128)(2,1)S(1)} %state.1.refs_2_), channel_id=1, source_target_pairs={{0,4},{4,1},{2,6},{6,3},{5,9},{9,5},{7,11},{11,7},{8,13},{12,8},{1... | collective-permute-start | bytes 786440 | tf_op jit(solution)/shard_map/ppermute | solution.py:348
  39.9 6.5 %collective-permute-start.12 = (bf16[1024,128]{1,0:T(8,128)(2,1)S(1)}, bf16[1024,128]{1,0:T(8,128)(2,1)S(1)}, u32[]{:S(2)}, u32[]{:S(2)}) collective-permute-start(bf16[1024,128]{1,0:T(8,128)(2,1)S(1)} %collective-permute-done.11.refs_2_), channel_id=1, source_target_pairs={{2,6},{4,0},{5,8},{6,10},{7,3},{8,4},{9,13},{10,14},{11,7},{12,9},... | collective-permute-start | bytes 786440 | tf_op jit(solution)/shard_map/ppermute | solution.py:354
  47.2 1.6 %collective-permute-start.14 = (bf16[1024,128]{1,0:T(8,128)(2,1)S(1)}, bf16[1024,128]{1,0:T(8,128)(2,1)S(1)}, u32[]{:S(2)}, u32[]{:S(2)}) collective-permute-start(bf16[1024,128]{1,0:T(8,128)(2,1)S(1)} %peer_product.11.own_ref), channel_id=1, source_target_pairs={{0,1},{1,0},{2,3},{3,2},{4,5},{5,4},{6,7},{7,6},{8,9},{9,8},{10,11... | collective-permute-start | bytes 786440 | tf_op jit(solution)/shard_map/ppermute | solution.py:360

commit v11 on v9

--- a/solution.py
+++ b/solution.py
@@ -184,12 +184,12 @@
     return parts
 
 
-def add_parts(ref, first, parts, mask, start):
+def add_parts(ref, first, parts, mask, source):
     rows = parts[0].shape[0]
     for k, part in enumerate(parts):
         at = pl.ds(first + k * rows, rows)
         value = part * mask
-        ref[at, :] = value if start else ref[at, :] + value
+        ref[at, :] = value if source is None else source[at, :] + value
 
 
 def own_weights_kernel(blocks, pack_ref, hl, w_ref, row_ref, col_ref, s_ref):
@@ -208,8 +208,8 @@
     for b in range(blocks):
         parts = tile_weights(hl, b, e, w_ref, b, s_ref, c == b)
         from_c = jnp.where(c == 0, table_entry(table, 0, b), table_entry(table, 1, b - 1))
-        add_parts(row_ref, b * size, parts, table_entry(table, b, c - b), True)
-        add_parts(col_ref, b * size, parts, from_c, True)
+        add_parts(row_ref, b * size, parts, table_entry(table, b, c - b), None)
+        add_parts(col_ref, b * size, parts, from_c, None)
 
 
 def peer_weights_kernel(dims, offsets, pack_ref, peer_ref, hl, row_in, col_in, w_ref, *rest):
@@ -224,15 +224,13 @@
     valid = jnp.where(chips != 0, 1.0, 0.0)
     own_table = pack_ref[pl.ds(mols, TAIL), :].astype(F32) * valid
     peer_table = peer_ref[pl.ds(mols, TAIL), :].astype(F32) * valid
-    row_ref[...] = row_in[...]
-    col_ref[...] = col_in[...]
     for k in range(blocks):
         e = peer_ref[pl.ds(k * size, size), :]
         for b in range(blocks):
             offset = chips * blocks + (k - b)
             parts = tile_weights(hl, b, e, w_ref, k * blocks + b, s_ref, None)
-            add_parts(row_ref, b * size, parts, table_entry(own_table, b, offset), False)
-            add_parts(col_ref, b * size, parts, table_entry(peer_table, k, -offset), False)
+            add_parts(row_ref, b * size, parts, table_entry(own_table, b, offset), row_in if k == 0 else row_ref)
+            add_parts(col_ref, b * size, parts, table_entry(peer_table, k, -offset), col_in if k == 0 else col_ref)
     if last:
         half = mols // LANES
         for n, ref in enumerate((row_ref, col_ref)):

time: 49.9 us -> 49.9 us (level)
  no operation moved by 1% of the time
where the time goes in v11:
time: 49.9 us; the launch traced here: 49.7 us
  waiting for transfers between devices  20 us (40%)
  starting transfers between devices  14.5 us (29%)
  Pallas kernels  12.4 us (25%)
  local copies, waits for them, and re-layouts  1.72 us (3%)
  other arithmetic  0.9 us (2%)
    ppermute x9, starting transfers between devices, to_peer(): return lax.ppermute(value, ('row', 'col'), list(steps[step][2].items()))  14.3 us
    pallas_call x17, Pallas kernels, kernel_call(): pl.pallas_call(body, out_shape=outs, in_specs=in_specs or [VMEM] * len(in...  12.4 us
    ppermute x9, waiting for transfers between devices, to_peer(): return lax.ppermute(value, ('row', 'col'), list(steps[step][2].items()))  10.2 us
    ppermute x2, waiting for transfers between devices, from_peers(): lax.ppermute(pieces[step - 2], ('row', 'col'), list(moves.items()))  5.63 us
    ppermute x3, waiting for transfers between devices, other_core(): return lax.ppermute(value, 'col', [(0, 1), (1, 0)])  4.2 us
    unnamed x4, local copies, waits for them, and re-layouts  1.72 us
  transfers between devices with their start and end apart: 15, of which 9 were waited for; matrix products, arithmetic and copies ran while one was open for 0% of the time, Pallas kernels for 19%

profile of v11, /device:TPU:0, one launch (start us, length us, event | category | flops | bytes accessed | tf_op | source)
XLA Modules:
  0.0 49.7 jit_solution(13376079191998917403)
XLA Ops:
  0.0 1.0 %pack.1.refs_0_ = bf16[1040,128]{1,0:T(8,128)(2,1)S(1)} custom-call(bf16[1024,128]{1,0:T(8,128)(2,1)} %refs_0_.1, s32[2,13]{1,0:T(2,128)} %refs_1_.1, s32[2]{0:T(128)} %refs_2_.1), custom_call_target="tpu_custom_call" | custom-call | flops 1 | bytes 1048576 | tf_op jit(solution)/shard_map/pack/pallas_call | solution.py:306
  1.0 3.0 %collective-permute-start = (bf16[1040,128]{1,0:T(8,128)(2,1)S(1)}, bf16[1040,128]{1,0:T(8,128)(2,1)S(1)}, u32[]{:S(2)}, u32[]{:S(2)}) collective-permute-start(bf16[1040,128]{1,0:T(8,128)(2,1)S(1)} %pack.1.refs_0_), channel_id=1, source_target_pairs={{0,2},{2,1},{3,5},{5,3},{4,6},{6,4},{7,9},{9,7},{8,10},{10,8},{11,... | collective-permute-start | bytes 798728 | tf_op jit(solution)/shard_map/ppermute | solution.py:332
  4.0 1.6 %collective-permute-start.3 = (bf16[1040,128]{1,0:T(8,128)(2,1)S(1)}, bf16[1040,128]{1,0:T(8,128)(2,1)S(1)}, u32[]{:S(2)}, u32[]{:S(2)}) collective-permute-start(bf16[1040,128]{1,0:T(8,128)(2,1)S(1)} %pack.1.refs_0_), channel_id=1, source_target_pairs={{0,4},{4,1},{2,6},{6,3},{5,9},{9,5},{7,11},{11,7},{8,13},{12,8},{1... | collective-permute-start | bytes 798728 | tf_op jit(solution)/shard_map/ppermute | solution.py:332
  6.4 1.0 %copy-done = f32[1024,128]{1,0:T(8,128)S(1)} copy-done((f32[1024,128]{1,0:T(8,128)S(1)}, f32[1024,128]{1,0:T(8,128)}, u32[]{:S(2)}) %copy-start) | copy-done | bytes 524312
  9.0 2.7 %collective-permute-done.refs_1_ = bf16[1040,128]{1,0:T(8,128)(2,1)S(1)} collective-permute-done((bf16[1040,128]{1,0:T(8,128)(2,1)S(1)}, bf16[1040,128]{1,0:T(8,128)(2,1)S(1)}, u32[]{:S(2)}, u32[]{:S(2)}) %collective-permute-start) | collective-permute-done | bytes 266272 | tf_op jit(solution)/shard_map/ppermute | solution.py:332
  11.7 2.0 %collective-permute-start.8 = (bf16[1024,128]{1,0:T(8,128)(2,1)S(1)}, bf16[1024,128]{1,0:T(8,128)(2,1)S(1)}, u32[]{:S(2)}, u32[]{:S(2)}) collective-permute-start(bf16[1024,128]{1,0:T(8,128)(2,1)S(1)} %get-tuple-element.32), channel_id=1, source_target_pairs={{0,4},{4,1},{2,6},{6,3},{5,9},{9,5},{7,11},{11,7},{8,13},{12,8},{1... | collective-permute-start | bytes 786440 | tf_op jit(solution)/shard_map/ppermute | solution.py:332
  13.7 1.1 %peer_weights.3 = (bf16[4,512,512]{2,1,0:T(8,128)(2,1)S(1)}, f32[1024,128]{1,0:T(8,128)S(1)}, f32[1024,128]{1,0:T(8,128)S(1)}) custom-call(bf16[1040,128]{1,0:T(8,128)(2,1)S(1)} %pack.1.refs_0_, bf16[1040,128]{1,0:T(8,128)(2,1)S(1)} %collective-permute-done.3.refs_1_, bf16[1024,256]{1,0:T(8,128)(2,1)S(1)} %get-tuple-element.30.refs_2_, ...), custom_call_target="tpu_custom_call" | custom-call | flops 536870912 | bytes 1048576 | tf_op jit(solution)/shard_map/peer_weights/pallas_call | solution.py:306
  14.9 1.3 %collective-permute-done.2.refs_2_ = bf16[1024,128]{1,0:T(8,128)(2,1)S(1)} collective-permute-done((bf16[1024,128]{1,0:T(8,128)(2,1)S(1)}, bf16[1024,128]{1,0:T(8,128)(2,1)S(1)}, u32[]{:S(2)}, u32[]{:S(2)}) %collective-permute-start.2) | collective-permute-done | bytes 262176 | tf_op jit(solution)/shard_map/ppermute | solution.py:332
  16.2 1.1 %peer_weights.4 = (bf16[4,512,512]{2,1,0:T(8,128)(2,1)S(1)}, f32[1024,128]{1,0:T(8,128)S(1)}, f32[1024,128]{1,0:T(8,128)S(1)}) custom-call(bf16[1040,128]{1,0:T(8,128)(2,1)S(1)} %pack.1.refs_0_, bf16[1040,128]{1,0:T(8,128)(2,1)S(1)} %collective-permute-done.refs_1_, bf16[1024,256]{1,0:T(8,128)(2,1)S(1)} %get-tuple-element.30.refs_2_, ...), custom_call_target="tpu_custom_call" | custom-call | flops 536870912 | bytes 1048576 | tf_op jit(solution)/shard_map/peer_weights/pallas_call | solution.py:306
  18.1 1.2 %peer_weights.5 = (bf16[4,512,512]{2,1,0:T(8,128)(2,1)S(1)}, f32[16,128]{1,0:T(8,128)S(1)}) custom-call(bf16[1040,128]{1,0:T(8,128)(2,1)S(1)} %pack.1.refs_0_, bf16[1040,128]{1,0:T(8,128)(2,1)S(1)} %collective-permute-done.1.refs_1_, bf16[1024,256]{1,0:T(8,128)(2,1)S(1)} %get-tuple-element.30.refs_2_, f32[1024,128]{1,0:T(8,128)S(1)} %get-tuple-element.37.refs_3_, ...), custom_call_target="tpu_custom_call" | custom-call | flops 536870912 | bytes 1048576 | tf_op jit(solution)/shard_map/peer_weights/pallas_call | solution.py:306
  19.4 1.2 %collective-permute-done.5.other_ref = f32[16,128]{1,0:T(8,128)S(1)} collective-permute-done((f32[16,128]{1,0:T(8,128)S(1)}, f32[16,128]{1,0:T(8,128)S(1)}, u32[]{:S(2)}, u32[]{:S(2)}) %collective-permute-start.5) | collective-permute-done | bytes 8224 | tf_op jit(solution)/shard_map/ppermute | solution.py:344
  20.6 4.0 %collective-permute-start.9 = (f32[16,128]{1,0:T(8,128)S(1)}, f32[16,128]{1,0:T(8,128)S(1)}, u32[]{:S(2)}, u32[]{:S(2)}) collective-permute-start(f32[16,128]{1,0:T(8,128)S(1)} %degree.1.scales_ref), channel_id=1, source_target_pairs={{0,4},{4,1},{2,6},{6,3},{5,9},{9,5},{7,11},{11,7},{8,13},{12,8},{1... | collective-permute-start | bytes 24584 | tf_op jit(solution)/shard_map/ppermute | solution.py:332
  24.6 0.9 %collective-permute-start.7 = (f32[16,128]{1,0:T(8,128)S(1)}, f32[16,128]{1,0:T(8,128)S(1)}, u32[]{:S(2)}, u32[]{:S(2)}) collective-permute-start(f32[16,128]{1,0:T(8,128)S(1)} %degree.1.scales_ref), channel_id=1, source_target_pairs={{0,2},{2,1},{3,5},{5,3},{4,6},{6,4},{7,9},{9,7},{8,10},{10,8},{11,... | collective-permute-start | bytes 24584 | tf_op jit(solution)/shard_map/ppermute | solution.py:332
  26.5 0.9 %peer_product.6.refs_4_ = f32[1024,128]{1,0:T(8,128)S(1)} custom-call(bf16[1040,128]{1,0:T(8,128)(2,1)S(1)} %pack.1.refs_0_, bf16[4,512,512]{2,1,0:T(8,128)(2,1)S(1)} %get-tuple-element.45.refs_1_, bf16[1024,128]{1,0:T(8,128)(2,1)S(1)} %collective-permute-done.8.refs_2_, f32[16,128]{1,0:T(8,128)S(1)} %collective-permute-done.9.refs_3_, ...), custom_call_target="tpu_custom_call" | custom-call | flops 536870912 | bytes 1048576 | tf_op jit(solution)/shard_map/peer_product/pallas_call | solution.py:306
  27.4 0.9 %peer_product.7.refs_4_ = f32[1024,128]{1,0:T(8,128)S(1)} custom-call(bf16[1040,128]{1,0:T(8,128)(2,1)S(1)} %pack.1.refs_0_, bf16[4,512,512]{2,1,0:T(8,128)(2,1)S(1)} %get-tuple-element.43.refs_1_, bf16[1024,128]{1,0:T(8,128)(2,1)S(1)} %collective-permute-done.2.refs_2_, f32[16,128]{1,0:T(8,128)S(1)} %collective-permute-done.7.refs_3_, ...), custom_call_target="tpu_custom_call" | custom-call | flops 536870912 | bytes 1048576 | tf_op jit(solution)/shard_map/peer_product/pallas_call | solution.py:306
  28.3 1.7 %collective-permute-done.6.refs_3_ = f32[16,128]{1,0:T(8,128)S(1)} collective-permute-done((f32[16,128]{1,0:T(8,128)S(1)}, f32[16,128]{1,0:T(8,128)S(1)}, u32[]{:S(2)}, u32[]{:S(2)}) %collective-permute-start.6) | collective-permute-done | bytes 8224 | tf_op jit(solution)/shard_map/ppermute | solution.py:332
  30.0 0.9 %peer_product.8.own_ref = bf16[1024,128]{1,0:T(8,128)(2,1)S(1)} custom-call(bf16[1040,128]{1,0:T(8,128)(2,1)S(1)} %pack.1.refs_0_, bf16[4,512,512]{2,1,0:T(8,128)(2,1)S(1)} %get-tuple-element.39.refs_1_, bf16[1024,128]{1,0:T(8,128)(2,1)S(1)} %collective-permute-done.4.refs_2_, f32[16,128]{1,0:T(8,128)S(1)} %collective-permute-done.6.refs_3_, ...), custom_call_target="tpu_custom_call" | custom-call | flops 536870912 | bytes 1048576 | tf_op jit(solution)/shard_map/peer_product/pallas_call | solution.py:306
  31.0 1.5 %collective-permute-done.10.other_ref = bf16[1024,128]{1,0:T(8,128)(2,1)S(1)} collective-permute-done((bf16[1024,128]{1,0:T(8,128)(2,1)S(1)}, bf16[1024,128]{1,0:T(8,128)(2,1)S(1)}, u32[]{:S(2)}, u32[]{:S(2)}) %collective-permute-start.10) | collective-permute-done | bytes 262176 | tf_op jit(solution)/shard_map/ppermute | solution.py:344
  33.7 1.8 %collective-permute-start.13 = (bf16[1024,128]{1,0:T(8,128)(2,1)S(1)}, bf16[1024,128]{1,0:T(8,128)(2,1)S(1)}, u32[]{:S(2)}, u32[]{:S(2)}) collective-permute-start(bf16[1024,128]{1,0:T(8,128)(2,1)S(1)} %state.1.refs_2_), channel_id=1, source_target_pairs={{0,4},{4,1},{2,6},{6,3},{5,9},{9,5},{7,11},{11,7},{8,13},{12,8},{1... | collective-permute-start | bytes 786440 | tf_op jit(solution)/shard_map/ppermute | solution.py:332
  35.5 4.4 %collective-permute-done.11.refs_2_ = bf16[1024,128]{1,0:T(8,128)(2,1)S(1)} collective-permute-done((bf16[1024,128]{1,0:T(8,128)(2,1)S(1)}, bf16[1024,128]{1,0:T(8,128)(2,1)S(1)}, u32[]{:S(2)}, u32[]{:S(2)}) %collective-permute-start.11) | collective-permute-done | bytes 262176 | tf_op jit(solution)/shard_map/ppermute | solution.py:332
  40.7 0.8 %peer_product.10.refs_3_ = f32[1024,128]{1,0:T(8,128)S(1)} custom-call(bf16[1040,128]{1,0:T(8,128)(2,1)S(1)} %pack.1.refs_0_, bf16[4,512,512]{2,1,0:T(8,128)(2,1)S(1)} %get-tuple-element.43.refs_1_, bf16[1024,128]{1,0:T(8,128)(2,1)S(1)} %collective-permute-done.11.refs_2_, f32[1024,128]{1,0:T(8,128)S(1)} %peer_product.9.refs_3_), custom_call_target="tpu_custom_call" | custom-call | flops 536870912 | bytes 1048576 | tf_op jit(solution)/shard_map/peer_product/pallas_call | solution.py:306
  41.5 4.8 %collective-permute-done.12.refs_2_ = bf16[1024,128]{1,0:T(8,128)(2,1)S(1)} collective-permute-done((bf16[1024,128]{1,0:T(8,128)(2,1)S(1)}, bf16[1024,128]{1,0:T(8,128)(2,1)S(1)}, u32[]{:S(2)}, u32[]{:S(2)}) %collective-permute-start.12) | collective-permute-done | bytes 262176 | tf_op jit(solution)/shard_map/ppermute | solution.py:338
  47.3 1.5 %collective-permute-done.14 = bf16[1024,128]{1,0:T(8,128)(2,1)S(1)} collective-permute-done((bf16[1024,128]{1,0:T(8,128)(2,1)S(1)}, bf16[1024,128]{1,0:T(8,128)(2,1)S(1)}, u32[]{:S(2)}, u32[]{:S(2)}) %collective-permute-start.14) | collective-permute-done | bytes 262176 | tf_op jit(solution)/shard_map/ppermute | solution.py:344
  48.8 0.9 %multiply_add_fusion = f32[1024,128]{1,0:T(8,128)} fusion(f32[1024,128]{1,0:T(8,128)S(1)} %get-tuple-element.49.seed_ref, f32[1024,128]{1,0:T(8,128)S(1)} %get-tuple-element.51.rs_ref, bf16[1024,128]{1,0:T(8,128)(2,1)S(1)} %collective-permute-done.14, bf16[1024,128]{1,0:T(8,128)(2,1)S(1)} %peer_product.11), kind=kLoop, calls=%fused_computation | loop fusion | flops 786432 | bytes 2097152 | tf_op jit(solution)/shard_map/add | solution.py:438
  (28 shorter events, 7.2 us)
Async XLA Ops:
  1.0 10.7 %collective-permute-start = (bf16[1040,128]{1,0:T(8,128)(2,1)S(1)}, bf16[1040,128]{1,0:T(8,128)(2,1)S(1)}, u32[]{:S(2)}, u32[]{:S(2)}) collective-permute-start(bf16[1040,128]{1,0:T(8,128)(2,1)S(1)} %pack.1.refs_0_), channel_id=1, source_target_pairs={{0,2},{2,1},{3,5},{5,3},{4,6},{6,4},{7,9},{9,7},{8,10},{10,8},{11,... | collective-permute-start | bytes 798728 | tf_op jit(solution)/shard_map/ppermute | solution.py:332
  4.0 9.7 %collective-permute-start.3 = (bf16[1040,128]{1,0:T(8,128)(2,1)S(1)}, bf16[1040,128]{1,0:T(8,128)(2,1)S(1)}, u32[]{:S(2)}, u32[]{:S(2)}) collective-permute-start(bf16[1040,128]{1,0:T(8,128)(2,1)S(1)} %pack.1.refs_0_), channel_id=1, source_target_pairs={{0,4},{4,1},{2,6},{6,3},{5,9},{9,5},{7,11},{11,7},{8,13},{12,8},{1... | collective-permute-start | bytes 798728 | tf_op jit(solution)/shard_map/ppermute | solution.py:332
  6.4 1.0 %copy-start = (f32[1024,128]{1,0:T(8,128)S(1)}, f32[1024,128]{1,0:T(8,128)}, u32[]{:S(2)}) copy-start(f32[1024,128]{1,0:T(8,128)} %profile_ref.1) | copy-start | bytes 1572868
  7.4 0.7 %copy-start.1 = (s32[1024]{0:T(1024)S(1)}, s32[1024]{0:T(1024)}, u32[]{:S(2)}) copy-start(s32[1024]{0:T(1024)} %param.7) | copy-start | bytes 12292
  8.4 7.7 %collective-permute-start.2 = (bf16[1024,128]{1,0:T(8,128)(2,1)S(1)}, bf16[1024,128]{1,0:T(8,128)(2,1)S(1)}, u32[]{:S(2)}, u32[]{:S(2)}) collective-permute-start(bf16[1024,128]{1,0:T(8,128)(2,1)S(1)} %get-tuple-element.32), channel_id=1, source_target_pairs={{0,2},{2,1},{3,5},{5,3},{4,6},{6,4},{7,9},{9,7},{8,10},{10,8},{11,... | collective-permute-start | bytes 786440 | tf_op jit(solution)/shard_map/ppermute | solution.py:332
  11.7 6.4 %collective-permute-start.1 = (bf16[1040,128]{1,0:T(8,128)(2,1)S(1)}, bf16[1040,128]{1,0:T(8,128)(2,1)S(1)}, u32[]{:S(2)}, u32[]{:S(2)}) collective-permute-start(bf16[1040,128]{1,0:T(8,128)(2,1)S(1)} %collective-permute-done.refs_1_), channel_id=1, source_target_pairs={{2,6},{4,0},{5,8},{6,10},{7,3},{8,4},{9,13},{10,14},{11,7},{12,9},... | collective-permute-start | bytes 798728 | tf_op jit(solution)/shard_map/ppermute | solution.py:338
  11.7 13.8 %collective-permute-start.8 = (bf16[1024,128]{1,0:T(8,128)(2,1)S(1)}, bf16[1024,128]{1,0:T(8,128)(2,1)S(1)}, u32[]{:S(2)}, u32[]{:S(2)}) collective-permute-start(bf16[1024,128]{1,0:T(8,128)(2,1)S(1)} %get-tuple-element.32), channel_id=1, source_target_pairs={{0,4},{4,1},{2,6},{6,3},{5,9},{9,5},{7,11},{11,7},{8,13},{12,8},{1... | collective-permute-start | bytes 786440 | tf_op jit(solution)/shard_map/ppermute | solution.py:332
  16.2 12.1 %collective-permute-start.4 = (bf16[1024,128]{1,0:T(8,128)(2,1)S(1)}, bf16[1024,128]{1,0:T(8,128)(2,1)S(1)}, u32[]{:S(2)}, u32[]{:S(2)}) collective-permute-start(bf16[1024,128]{1,0:T(8,128)(2,1)S(1)} %collective-permute-done.2.refs_2_), channel_id=1, source_target_pairs={{2,6},{4,0},{5,8},{6,10},{7,3},{8,4},{9,13},{10,14},{11,7},{12,9},... | collective-permute-start | bytes 786440 | tf_op jit(solution)/shard_map/ppermute | solution.py:400
  19.4 1.2 %collective-permute-start.5 = (f32[16,128]{1,0:T(8,128)S(1)}, f32[16,128]{1,0:T(8,128)S(1)}, u32[]{:S(2)}, u32[]{:S(2)}) collective-permute-start(f32[16,128]{1,0:T(8,128)S(1)} %get-tuple-element.41.own_ref), channel_id=1, source_target_pairs={{0,1},{1,0},{2,3},{3,2},{4,5},{5,4},{6,7},{7,6},{8,9},{9,8},{10,11... | collective-permute-start | bytes 24584 | tf_op jit(solution)/shard_map/ppermute | solution.py:344
  20.6 5.9 %collective-permute-start.9 = (f32[16,128]{1,0:T(8,128)S(1)}, f32[16,128]{1,0:T(8,128)S(1)}, u32[]{:S(2)}, u32[]{:S(2)}) collective-permute-start(f32[16,128]{1,0:T(8,128)S(1)} %degree.1.scales_ref), channel_id=1, source_target_pairs={{0,4},{4,1},{2,6},{6,3},{5,9},{9,5},{7,11},{11,7},{8,13},{12,8},{1... | collective-permute-start | bytes 24584 | tf_op jit(solution)/shard_map/ppermute | solution.py:332
  24.6 2.8 %collective-permute-start.7 = (f32[16,128]{1,0:T(8,128)S(1)}, f32[16,128]{1,0:T(8,128)S(1)}, u32[]{:S(2)}, u32[]{:S(2)}) collective-permute-start(f32[16,128]{1,0:T(8,128)S(1)} %degree.1.scales_ref), channel_id=1, source_target_pairs={{0,2},{2,1},{3,5},{5,3},{4,6},{6,4},{7,9},{9,7},{8,10},{10,8},{11,... | collective-permute-start | bytes 24584 | tf_op jit(solution)/shard_map/ppermute | solution.py:332
  25.5 4.6 %collective-permute-start.6 = (f32[16,128]{1,0:T(8,128)S(1)}, f32[16,128]{1,0:T(8,128)S(1)}, u32[]{:S(2)}, u32[]{:S(2)}) collective-permute-start(f32[16,128]{1,0:T(8,128)S(1)} %degree.1.scales_ref), channel_id=1, source_target_pairs={{6,0},{8,3},{10,11},{0,1},{12,7},{2,8},{14,15},{4,5},{7,13},{9,14}... | collective-permute-start | bytes 24584 | tf_op jit(solution)/shard_map/ppermute | solution.py:332
  30.9 1.6 %collective-permute-start.10 = (bf16[1024,128]{1,0:T(8,128)(2,1)S(1)}, bf16[1024,128]{1,0:T(8,128)(2,1)S(1)}, u32[]{:S(2)}, u32[]{:S(2)}) collective-permute-start(bf16[1024,128]{1,0:T(8,128)(2,1)S(1)} %peer_product.8.own_ref), channel_id=1, source_target_pairs={{0,1},{1,0},{2,3},{3,2},{4,5},{5,4},{6,7},{7,6},{8,9},{9,8},{10,11... | collective-permute-start | bytes 786440 | tf_op jit(solution)/shard_map/ppermute | solution.py:344
  32.7 7.2 %collective-permute-start.11 = (bf16[1024,128]{1,0:T(8,128)(2,1)S(1)}, bf16[1024,128]{1,0:T(8,128)(2,1)S(1)}, u32[]{:S(2)}, u32[]{:S(2)}) collective-permute-start(bf16[1024,128]{1,0:T(8,128)(2,1)S(1)} %state.1.refs_2_), channel_id=1, source_target_pairs={{0,2},{2,1},{3,5},{5,3},{4,6},{6,4},{7,9},{9,7},{8,10},{10,8},{11,... | collective-permute-start | bytes 786440 | tf_op jit(solution)/shard_map/ppermute | solution.py:332
  33.7 6.2 %collective-permute-start.13 = (bf16[1024,128]{1,0:T(8,128)(2,1)S(1)}, bf16[1024,128]{1,0:T(8,128)(2,1)S(1)}, u32[]{:S(2)}, u32[]{:S(2)}) collective-permute-start(bf16[1024,128]{1,0:T(8,128)(2,1)S(1)} %state.1.refs_2_), channel_id=1, source_target_pairs={{0,4},{4,1},{2,6},{6,3},{5,9},{9,5},{7,11},{11,7},{8,13},{12,8},{1... | collective-permute-start | bytes 786440 | tf_op jit(solution)/shard_map/ppermute | solution.py:332
  39.9 6.5 %collective-permute-start.12 = (bf16[1024,128]{1,0:T(8,128)(2,1)S(1)}, bf16[1024,128]{1,0:T(8,128)(2,1)S(1)}, u32[]{:S(2)}, u32[]{:S(2)}) collective-permute-start(bf16[1024,128]{1,0:T(8,128)(2,1)S(1)} %collective-permute-done.11.refs_2_), channel_id=1, source_target_pairs={{2,6},{4,0},{5,8},{6,10},{7,3},{8,4},{9,13},{10,14},{11,7},{12,9},... | collective-permute-start | bytes 786440 | tf_op jit(solution)/shard_map/ppermute | solution.py:338
  47.2 1.6 %collective-permute-start.14 = (bf16[1024,128]{1,0:T(8,128)(2,1)S(1)}, bf16[1024,128]{1,0:T(8,128)(2,1)S(1)}, u32[]{:S(2)}, u32[]{:S(2)}) collective-permute-start(bf16[1024,128]{1,0:T(8,128)(2,1)S(1)} %peer_product.11), channel_id=1, source_target_pairs={{0,1},{1,0},{2,3},{3,2},{4,5},{5,4},{6,7},{7,6},{8,9},{9,8},{10,11... | collective-permute-start | bytes 786440 | tf_op jit(solution)/shard_map/ppermute | solution.py:344
